TPU v7x, 512 devices: a whole 4x4x16 slice. The times are simulated.
512 devices in a mesh: dp: 8 (over y, core), expert: 64 (over x, z).
Axes of the slice: x: 4, y: 4, z: 16, core: 2. Of those that a mesh axis runs over, the one named last changes fastest.
Arguments:
- grad_out: bfloat16 [32768, 4096], P('expert', 'dp'), may hold values from -30 to 30
- hidden: bfloat16 [32768, 2, 1024], P('expert', None, 'dp'), may hold values from -24 to 24
- gate_prob: float32 [32768, 2], P('expert'), may hold values from 0.05 to 1
- expert_ids: int32 [32768, 2], P('expert'), may hold values from 0 to 63, all different within a row; in each aligned block of 512 rows (0 to 511, 512 to 1023, ...) at most 20 rows name the same one
- weights: bfloat16 [64, 1024, 4096], P('expert', None, 'dp'), may hold values from -0.1875 to 0.1875
Outputs:
- hidden_grad: bfloat16 [32768, 2, 1024], P('expert', None, 'dp')
- update: float32 [64, 1024, 4096], P('expert', None, 'dp')
Inputs may be any that keep to these rules, and one draw needn't show every extreme that they name: `expert_ids`: among the 512 tokens of one index of expert, no expert is named by more than 20 choices, a bound that some block reaches; the 2 experts of a token differ.
All inputs are finite; a program needn't handle non-finite values.
Results may differ from a plain program's by a relative error of at most 0.019.
Values may be sent and summed in bfloat16 or wider, within the bound.
No kernel may reach another device: no remote copies, remote signals or barrier semaphores. Data moves between devices by JAX's collectives and lax.ppermute only.
A program may use at most 64 MiB of HBM per device.

v0:
```python
import jax
import jax.numpy as jnp
from jax import lax
from jax.sharding import PartitionSpec as P

D = 4096


def slot_numbers(route_ids, capacity, expert_count):
    flat_ids = route_ids.reshape(-1)
    one_hot = (flat_ids[:, None] == jnp.arange(expert_count, dtype=jnp.int32)[None, :]).astype(
        jnp.int32
    )
    before = jnp.cumsum(one_hot, axis=0) - one_hot
    rank_in = jnp.sum(before * one_hot, axis=1)
    return flat_ids * capacity + rank_in


def gram_sum(matrix_part):
    partial_gram = jnp.dot(matrix_part, matrix_part.T, preferred_element_type=jnp.float32)
    return lax.psum(partial_gram.astype(jnp.bfloat16), "dp").astype(jnp.float32)


def place_slots(slot_index, values, slot_count):
    empty_rows = jnp.zeros((slot_count,) + values.shape[1:], values.dtype)
    return empty_rows.at[slot_index].set(values)


def per_device(grad_out, hidden, gate_prob, expert_ids, weights):
    tokens, width_part = grad_out.shape
    top_count = expert_ids.shape[1]
    experts = lax.axis_size("expert")
    capacity = 5 * tokens * top_count // (4 * experts)
    total_slots = experts * capacity
    pair_count = tokens * top_count
    slot_index = slot_numbers(expert_ids, capacity, experts)
    token_of = jnp.arange(pair_count, dtype=jnp.int32) // top_count
    send_grad = place_slots(slot_index, grad_out[token_of], total_slots).reshape(
        experts, capacity, width_part
    )
    scaled_part = (gate_prob[:, :, None] * hidden.astype(jnp.float32)).astype(jnp.bfloat16)
    whole_scaled = lax.all_gather(scaled_part, "dp", axis=2, tiled=True)
    send_scaled = place_slots(
        slot_index, whole_scaled.reshape(pair_count, -1), total_slots
    ).reshape(experts, capacity, -1)
    got_grad, got_scaled = (
        lax.all_to_all(send_grad, "expert", split_axis=0, concat_axis=0, tiled=True),
        lax.all_to_all(send_scaled, "expert", split_axis=0, concat_axis=0, tiled=True),
    )
    got_grad = got_grad.reshape(total_slots, width_part)
    got_scaled = got_scaled.reshape(total_slots, -1)
    weight_part = weights[0]
    gradient = lax.dot_general(
        got_scaled, got_grad, (((0,), (0,)), ((), ())), preferred_element_type=jnp.float32
    )
    back_term = lax.dot_general(
        got_grad, weight_part, (((1,), (1,)), ((), ())), preferred_element_type=jnp.float32
    )
    flat_prob = gate_prob.reshape(-1)
    summed = lax.psum_scatter(
        back_term.astype(jnp.bfloat16), "dp", scatter_dimension=1, tiled=True
    ).astype(jnp.float32)
    returned = lax.all_to_all(
        summed.reshape(experts, capacity, -1).astype(jnp.bfloat16),
        "expert",
        split_axis=0,
        concat_axis=0,
        tiled=True,
    ).astype(jnp.float32)
    picked = returned.reshape(total_slots, -1)[slot_index]
    hidden_grad = (flat_prob[:, None] * picked).astype(jnp.bfloat16).reshape(tokens, top_count, -1)
    grad_bf16 = gradient.astype(jnp.bfloat16)
    gram_first = gram_sum(grad_bf16)
    norm_sq = jnp.sqrt(jnp.sum(gram_first * gram_first)) + 1e-06
    current = (grad_bf16.astype(jnp.float32) * lax.rsqrt(norm_sq)).astype(jnp.bfloat16)
    gram_now = (gram_first / norm_sq).astype(jnp.bfloat16)
    following = current.astype(jnp.float32)
    for sweep_number in range(2):
        if sweep_number > 0:
            gram_now = gram_sum(current).astype(jnp.bfloat16)
        following = 1.5 * current.astype(jnp.float32) - 0.5 * jnp.dot(
            gram_now, current, preferred_element_type=jnp.float32
        )
        current = following.astype(jnp.bfloat16)
    update = following * D**0.5
    return (hidden_grad, update[None])


def solution(mesh):
    in_specs = (
        P("expert", "dp"),
        P("expert", None, "dp"),
        P("expert", None),
        P("expert", None),
        P("expert", None, "dp"),
    )
    out_specs = (P("expert", None, "dp"), P("expert", None, "dp"))
    return jax.shard_map(
        per_device, mesh=mesh, in_specs=in_specs, out_specs=out_specs, check_vma=False
    )
```

profile of v0, /device:TPU:1, one launch (start us, length us, event | category | flops | bytes accessed | tf_op | source)
XLA Modules:
  0.0 625.0 jit_solution(6197987789082699378)
XLA Ops:
  7.2 0.8 broadcast_multiply_fusion
  8.0 0.8 copy.19
  9.6 18.0 %reduce-window.6 = s32[64,8,128]{2,1,0:T(8,128)S(1)} reduce-window(s32[64,8,128]{2,1,0:T(8,128)S(1)} %fusion.21, s32[]{:T(128)} %constant.16.clone.1), window={size=1x1x128 pad=0_0x0_0x127_0}, to_apply=%region_0.0 | reduce-window | flops 8323072 | bytes 524292 | tf_op jit(solution)/shard_map/reduce-window
  28.2 12.8 %scatter_custom_fusion = bf16[1280,512]{1,0:T(8,128)(2,1)S(1)} fusion(s32[1024]{0:T(1024)S(1)} %bitcast.46, bf16[512,512]{1,0:T(8,128)(2,1)} %param.5, s32[1024]{0:T(1024)S(1)} %broadcast_clamp_fusion.1, bf16[]{:T(256)} %constant.13.clone.1), kind=kCustom, calls=%fused_computation.22 | custom fusion | bytes 1311232 | tf_op jit(solution)/shard_map/scatter | solution.py:26
  41.0 1.3 reshape.124
  42.3 89.4 %all_to_all.15 = bf16[64,20,512]{2,1,0:T(8,128)(2,1)S(1)} all-to-all(bf16[64,20,512]{2,1,0:T(8,128)(2,1)} %reshape.124), channel_id=1, replica_groups=mesh['dp'=8,'expert'=64] {'expert'}, dimensions={0} | all-to-all | bytes 2621440 | tf_op jit(solution)/shard_map/all_to_all | solution.py:47
  131.7 1.2 reshape.125
  132.9 4.4 convolution_convert_fusion
  137.3 4.4 copy.25
  141.7 39.6 %reduce-scatter.4.cloned.1.call-done = bf16[128,1280]{1,0:T(8,128)(2,1)} async-done(((bf16[1024,1280]{1,0:T(8,128)(2,1)}), bf16[128,1280]{1,0:T(8,128)(2,1)}) %reduce-scatter.4.cloned.1.call-update) | async-done | bytes 327696
  181.3 1.2 copy.26
  182.5 0.8 convert_element_type.61
  183.3 14.5 %all-to-all-start.1 = ((bf16[64,20,128]{2,1,0:T(8,128)(2,1)}), bf16[64,20,128]{2,1,0:T(8,128)(2,1)}, u32[]{:S(2)}, u32[]{:S(2)}) async-start(bf16[64,20,128]{2,1,0:T(8,128)(2,1)} %convert_element_type.61), calls=%async_computation.1 | async-start | bytes 786432 | tf_op jit(solution)/shard_map/all_to_all | solution.py:63
  198.1 20.6 %all-to-all-done.1 = bf16[64,20,128]{2,1,0:T(8,128)(2,1)} async-done(((bf16[64,20,128]{2,1,0:T(8,128)(2,1)}), bf16[64,20,128]{2,1,0:T(8,128)(2,1)}, u32[]{:S(2)}, u32[]{:S(2)}) %all-to-all-start.1) | async-done | bytes 327712 | tf_op jit(solution)/shard_map/all_to_all | solution.py:63
  218.7 1.1 reshape.131
  219.8 4.0 gather_fusion
  223.8 2.4 multiply_convert_fusion.2
  226.5 41.5 %all-gather.2.cloned.1.call-done = bf16[512,2,1024]{2,1,0:T(2,128)(2,1)} async-done(((bf16[512,2,128]{2,1,0:T(2,128)(2,1)}), bf16[512,2,1024]{2,1,0:T(2,128)(2,1)}) %all-gather.2.cloned.1.call-update) | async-done | bytes 2097168 | tf_op jit(solution)/shard_map/all_gather | solution.py:42
  268.0 4.1 reshape.160
  272.1 7.8 %scatter_custom_fusion.1 = bf16[1280,1024]{1,0:T(8,128)(2,1)} fusion(s32[1024]{0:T(1024)S(1)} %bitcast.48, bf16[1024,1024]{1,0:T(8,128)(2,1)} %reshape.160, bf16[]{:T(256)} %constant.13.clone.1), kind=kCustom, calls=%fused_computation.19 | custom fusion | bytes 2621952 | tf_op jit(solution)/shard_map/scatter | solution.py:26
  279.9 5.2 reshape.129
  285.1 156.4 %all_to_all.16 = bf16[64,20,1024]{2,1,0:T(8,128)(2,1)S(1)} all-to-all(bf16[64,20,1024]{2,1,0:T(8,128)(2,1)} %reshape.129), channel_id=1, replica_groups=mesh['dp'=8,'expert'=64] {'expert'}, dimensions={0} | all-to-all | bytes 5242880 | tf_op jit(solution)/shard_map/all_to_all | solution.py:48
  441.5 2.9 bitcast_convert_fusion
  444.4 1.0 copy-done.3
  445.4 2.6 convolution_convert_fusion.2
  448.3 74.4 %all-reduce.3.cloned.1.call-done = bf16[1024,1024]{1,0:T(8,128)(2,1)} async-done(((bf16[1024,1024]{1,0:T(8,128)(2,1)}), bf16[1024,1024]{1,0:T(8,128)(2,1)}) %all-reduce.3.cloned.1.call-update) | async-done | bytes 2097168 | tf_op jit(solution)/shard_map/psum | solution.py:21
  522.7 3.4 fusion
  526.9 2.9 subtract_convert_fusion
  529.8 1.0 copy-done.4
  530.8 2.6 convolution_convert_fusion.1
  533.4 80.9 %all-reduce.5.cloned.1.call-done = bf16[1024,1024]{1,0:T(8,128)(2,1)} async-done(((bf16[1024,1024]{1,0:T(8,128)(2,1)}), bf16[1024,1024]{1,0:T(8,128)(2,1)}) %all-reduce.5.cloned.1.call-update) | async-done | bytes 2097168 | tf_op jit(solution)/shard_map/psum | solution.py:21
  614.3 4.2 multiply_bitcast_fusion
  (35 shorter events, 2.1 us)
Async XLA Ops:
  7.2 125.7 %copy-start = (bf16[1,1024,512]{2,1,0:T(8,128)(2,1)S(1)}, bf16[1,1024,512]{2,1,0:T(8,128)(2,1)}, u32[]{:S(2)}) copy-start(bf16[1,1024,512]{2,1,0:T(8,128)(2,1)} %param.9) | copy-start | bytes 3145732
  7.2 174.1 %reduce-scatter.4.cloned.1.call-start = ((), (), s32[]{:S(2)}) async-start(), calls=%async_computation.7 | async-start | bytes 2949120
  141.7 56.2 %copy-start.2 = (f32[512,2]{0,1:T(2,128)S(1)}, f32[512,2]{0,1:T(2,128)}, u32[]{:S(2)}) copy-start(f32[512,2]{0,1:T(2,128)} %param.7) | copy-start | bytes 12292
  183.3 35.4 %all-to-all-start.1 = ((bf16[64,20,128]{2,1,0:T(8,128)(2,1)}), bf16[64,20,128]{2,1,0:T(8,128)(2,1)}, u32[]{:S(2)}, u32[]{:S(2)}) async-start(bf16[64,20,128]{2,1,0:T(8,128)(2,1)} %convert_element_type.61), calls=%async_computation.1 | async-start | bytes 786432 | tf_op jit(solution)/shard_map/all_to_all | solution.py:63
  197.9 70.2 %all-gather.2.cloned.1.call-start = ((), (), s32[]{:S(2)}) async-start(), calls=%async_computation.4 | async-start | bytes 2359296 | tf_op jit(solution)/shard_map/all_gather | solution.py:42
  226.3 296.4 %all-reduce.3.cloned.1.call-start = ((), (), s32[]{:S(2)}) async-start(), calls=%async_computation.5 | async-start | bytes 4194304 | tf_op jit(solution)/shard_map/psum | solution.py:21
  444.4 1.0 copy-start.3
  448.0 166.3 %all-reduce.5.cloned.1.call-start = ((), (), s32[]{:S(2)}) async-start(), calls=%async_computation.6 | async-start | bytes 4194304 | tf_op jit(solution)/shard_map/psum | solution.py:21
  522.7 4.2 copy-start.1
  529.8 1.0 copy-start.4
  533.4 80.9 %copy-start.5 = (bf16[1024,512]{1,0:T(8,128)(2,1)S(1)}, bf16[1024,512]{1,0:T(8,128)(2,1)}, u32[]{:S(2)}) copy-start(bf16[1024,512]{1,0:T(8,128)(2,1)} %copy-done.4) | copy-start | bytes 3145732
Sparse Core Ops, SparseCore 0:
  141.8 39.4 reduce-scatter.3
  226.4 41.6 all-gather.1
  448.1 74.5 all-reduce.2
  533.6 80.7 all-reduce.4
where the time goes:
time: 627 us; the launch traced here: 625 us
  waiting for transfers between devices  257 us (41%)
  blocking collectives  246 us (39%)
  local copies, waits for them, and re-layouts  47.8 us (8%)
  other arithmetic  24.9 us (4%)
  matrix products  19.6 us (3%)
  starting transfers between devices  15.1 us (2%)
  between operations  14.7 us (2%)
    all_to_all x1, blocking collectives, per_device(): lax.all_to_all(send_scaled, 'expert', split_axis=0, concat_axis=0, tiled=...  156 us
    psum x2, waiting for transfers between devices, gram_sum(): return lax.psum(partial_gram.astype(jnp.bfloat16), 'dp').astype(jnp.float32)  155 us
    all_to_all x1, blocking collectives, per_device(): lax.all_to_all(send_grad, 'expert', split_axis=0, concat_axis=0, tiled=True)  89.4 us
    all_gather x1, waiting for transfers between devices, per_device(): whole_scaled = lax.all_gather(scaled_part, 'dp', axis=2, tiled=True)  41.5 us
    unnamed x5, waiting for transfers between devices  39.7 us
    all_to_all x1, waiting for transfers between devices, per_device(): lax.all_to_all(summed.reshape(experts, capacity, -1).astype(jnp.bfloat16)...  20.6 us
    scatter x2, local copies, waits for them, and re-layouts, place_slots(): return empty_rows.at[slot_index].set(values)  20.6 us
    another operation x3, other arithmetic  18.2 us
  transfers between devices with their start and end apart: 5, of which 5 were waited for; matrix products, arithmetic and copies ran while one was open for 0% of the time, Pallas kernels for 0%

commit v1 on v0

v1 whole, which is shorter than its diff:
```python
import jax
import jax.numpy as jnp
from jax import lax
from jax.experimental import pallas as pl
from jax.experimental.pallas import tpu as pltpu
from jax.sharding import Mesh, PartitionSpec as P

EXPERT = ("x", "z")
VMEM_LIMIT = 50 * 1024 * 1024
BF16 = jnp.bfloat16
F32 = jnp.float32


def full_spec():
    return pl.BlockSpec(memory_space=pltpu.VMEM)


def smem_spec():
    return pl.BlockSpec(memory_space=pltpu.SMEM)


def shift_y(value, step, size):
    return lax.ppermute(value, "y", [(i, (i + step) % size) for i in range(size)])


def swap_core(value):
    return lax.ppermute(value, "c", [(0, 1), (1, 0)])


def nt_dot(left, right):
    return lax.dot_general(left, right, (((1,), (1,)), ((), ())), preferred_element_type=F32)


def grad_kernel(spot_ref, own_ref, other_ref, rows_ref, gradb_ref, pack_own_ref, pack_other_ref, wide_ref):
    blocks = gradb_ref.shape[0] // 128
    y_size = blocks // 2
    for d in range(blocks):
        spot = spot_ref[d]

        @pl.when(spot < y_size)
        def _():
            wide_ref[:, d * 128 : (d + 1) * 128] = own_ref[spot]

        @pl.when(spot >= y_size)
        def _():
            wide_ref[:, d * 128 : (d + 1) * 128] = other_ref[spot - y_size]

    gradient = lax.dot_general(
        wide_ref[...], rows_ref[...], (((0,), (0,)), ((), ())), preferred_element_type=F32
    )
    gradb = gradient.astype(BF16)
    gradb_ref[...] = gradb
    gram = nt_dot(gradb, gradb).astype(BF16)
    half = blocks // 2
    for d in range(blocks):
        rows = slice(d * 128, (d + 1) * 128)
        pieces = []
        for k in range(half):
            j = (d + k) % blocks
            pieces.append(gram[rows, j * 128 : (j + 1) * 128])
        i = d % half
        top = i * 128 + (64 if d >= half else 0)
        pieces.append(gram[top : top + 64, (i + half) * 128 : (i + half + 1) * 128])
        spot = spot_ref[blocks + d]

        def put(ref, at):
            for k in range(half):
                ref[at, k * 128 : (k + 1) * 128, :] = pieces[k]
            ref[at, half * 128 : half * 128 + 64, :] = pieces[half]

        @pl.when(spot < y_size)
        def _():
            put(pack_own_ref, spot)

        @pl.when(spot >= y_size)
        def _():
            put(pack_other_ref, spot - y_size)


def back_kernel(spot_ref, rows_ref, weight_ref, own_ref, other_ref):
    blocks = weight_ref.shape[0] // 128
    y_size = blocks // 2
    term = nt_dot(rows_ref[...], weight_ref[...]).astype(BF16)
    for d in range(blocks):
        spot = spot_ref[blocks + d]
        piece = term[:, d * 128 : (d + 1) * 128]

        @pl.when(spot < y_size)
        def _():
            own_ref[spot] = piece

        @pl.when(spot >= y_size)
        def _():
            other_ref[spot - y_size] = piece


def ortho_kernel(width, spot_ref, own_ref, other_ref, gradb_ref, out_ref, gram_ref):
    blocks = gradb_ref.shape[0] // 128
    y_size = blocks // 2
    half = blocks // 2
    for d in range(blocks):
        spot = spot_ref[d]

        def place(ref, at):
            for k in range(half):
                j = (d + k) % blocks
                block = ref[at, k * 128 : (k + 1) * 128, :]
                gram_ref[d * 128 : (d + 1) * 128, j * 128 : (j + 1) * 128] = block
                if k > 0:
                    gram_ref[j * 128 : (j + 1) * 128, d * 128 : (d + 1) * 128] = block.T
            i = d % half
            top = i * 128 + (64 if d >= half else 0)
            gram_ref[top : top + 64, (i + half) * 128 : (i + half + 1) * 128] = ref[
                at, half * 128 : half * 128 + 64, :
            ]

        @pl.when(spot < y_size)
        def _():
            place(own_ref, spot)

        @pl.when(spot >= y_size)
        def _():
            place(other_ref, spot - y_size)

    for i in range(half):
        upper = gram_ref[i * 128 : (i + 1) * 128, (i + half) * 128 : (i + half + 1) * 128]
        gram_ref[(i + half) * 128 : (i + half + 1) * 128, i * 128 : (i + 1) * 128] = upper.T

    gram = gram_ref[...]
    wide = gram.astype(F32)
    norm_sq = jnp.sqrt(jnp.sum(wide * wide, keepdims=True)) + 1e-06
    inverse = 1.0 / norm_sq
    first = (gradb_ref[...].astype(F32) * lax.rsqrt(norm_sq)).astype(BF16)

    def apply(value):
        return jnp.dot(gram, value, preferred_element_type=F32) * inverse

    second = (1.5 * first.astype(F32) - 0.5 * apply(first)).astype(BF16)
    power_one = apply(second)
    power_two = apply(power_one.astype(BF16))
    power_three = apply(power_two.astype(BF16))
    total = 1.5 * second.astype(F32) - 0.5 * (2.25 * power_one - 1.5 * power_two + 0.25 * power_three)
    out_ref[0] = total * width**0.5


def call(kernel, outs, ins, scratch=()):
    return pl.pallas_call(
        kernel,
        out_shape=outs,
        in_specs=[smem_spec()] + [full_spec()] * (len(ins) - 1),
        out_specs=jax.tree.map(lambda _: full_spec(), outs),
        scratch_shapes=list(scratch),
        compiler_params=pltpu.CompilerParams(vmem_limit_bytes=VMEM_LIMIT),
    )(*ins)


def per_device(grad_out, hidden, gate_prob, expert_ids, weights):
    tokens, width_part = grad_out.shape
    top_count = expert_ids.shape[1]
    unit_part = hidden.shape[2]
    units = weights.shape[1]
    experts = lax.axis_size("x") * lax.axis_size("z")
    y_size = lax.axis_size("y")
    dp = y_size * 2
    width = width_part * dp
    capacity = 5 * tokens * top_count // (4 * experts)
    total_slots = experts * capacity
    pair_count = tokens * top_count
    y = lax.axis_index("y")
    c = lax.axis_index("c")
    block = jnp.arange(dp, dtype=jnp.int32)
    other_core = (block % 2) ^ c
    came_from = other_core * y_size + (y - block // 2) % y_size
    goes_to = other_core * y_size + (block // 2 - y) % y_size
    spots = jnp.concatenate([came_from, goes_to]).astype(jnp.int32)

    flat_ids = expert_ids.T.reshape(1, pair_count)
    named = (jnp.arange(experts, dtype=jnp.int32)[:, None] == flat_ids).astype(BF16)
    order = jnp.arange(pair_count, dtype=jnp.int32)
    earlier = (order[:, None] < order[None, :]).astype(BF16)
    before = jnp.dot(named, earlier, preferred_element_type=F32)
    rank_in = jnp.sum(before * named.astype(F32), axis=0, keepdims=True).astype(jnp.int32)
    slot_index = flat_ids * capacity + rank_in
    chosen = (jnp.arange(total_slots, dtype=jnp.int32)[:, None] == slot_index).astype(BF16)
    chosen_token = chosen[:, :tokens] + chosen[:, tokens:]

    scaled_part = (gate_prob[:, :, None] * hidden.astype(F32)).astype(BF16)
    scaled_part = scaled_part.transpose(1, 0, 2).reshape(pair_count, unit_part)
    send_scaled = jnp.dot(chosen, scaled_part, preferred_element_type=F32).astype(BF16)
    got_scaled = lax.all_to_all(
        send_scaled.reshape(experts, capacity, unit_part), EXPERT, split_axis=0, concat_axis=0, tiled=True
    ).reshape(total_slots, unit_part)

    send_grad = jnp.dot(chosen_token, grad_out, preferred_element_type=F32).astype(BF16)
    send_grad = (
        send_grad.reshape(experts, capacity, 2, width_part // 2)
        .transpose(0, 2, 1, 3)
        .reshape(experts, 2 * capacity, width_part // 2)
    )
    got_grad = lax.all_to_all(send_grad, EXPERT, split_axis=0, concat_axis=0, tiled=True)
    got_grad = (
        got_grad.reshape(experts, 2, capacity, width_part // 2)
        .transpose(0, 2, 1, 3)
        .reshape(total_slots, width_part)
    )

    gathered = jnp.stack([got_scaled] + [shift_y(got_scaled, k, y_size) for k in range(1, y_size)])
    gathered_other = swap_core(gathered)

    pack_rows = units // 2 + 64
    packs = jax.ShapeDtypeStruct((y_size, pack_rows, 128), BF16)
    grad_bf16, pack_own, pack_other = call(
        grad_kernel,
        (jax.ShapeDtypeStruct((units, width_part), BF16), packs, packs),
        (spots, gathered, gathered_other, got_grad),
        (pltpu.VMEM((total_slots, units), BF16),),
    )

    def reduce_dp(own, other):
        both = (own.astype(F32) + swap_core(other).astype(F32)).astype(BF16)
        parts = [both[0]] + [shift_y(both[k], k, y_size) for k in range(1, y_size)]
        total = parts[0].astype(F32)
        for part in parts[1:]:
            total = total + part.astype(F32)
        return total.astype(BF16)

    pack = reduce_dp(pack_own, pack_other)
    pack_all = jnp.stack([pack] + [shift_y(pack, k, y_size) for k in range(1, y_size)])
    pack_all_other = swap_core(pack_all)
    update = call(
        lambda *refs: ortho_kernel(width, *refs),
        jax.ShapeDtypeStruct((1, units, width_part), F32),
        (spots, pack_all, pack_all_other, grad_bf16),
        (pltpu.VMEM((units, units), BF16),),
    )

    terms = jax.ShapeDtypeStruct((y_size, total_slots, unit_part), BF16)
    term_own, term_other = call(back_kernel, (terms, terms), (spots, got_grad, weights[0]))
    summed = reduce_dp(term_own, term_other)
    returned = lax.all_to_all(
        summed.reshape(experts, capacity, unit_part), EXPERT, split_axis=0, concat_axis=0, tiled=True
    ).reshape(total_slots, unit_part)
    picked = lax.dot_general(chosen, returned, (((0,), (0,)), ((), ())), preferred_element_type=F32)
    picked = picked.reshape(top_count, tokens, unit_part).transpose(1, 0, 2)
    hidden_grad = (gate_prob[:, :, None] * picked).astype(BF16)
    return (hidden_grad, update)


def solution(mesh):
    dp, experts = mesh.devices.shape
    x_size = 4
    split = Mesh(
        mesh.devices.reshape(dp // 2, 2, x_size, experts // x_size), ("y", "c", "x", "z")
    )
    rows, cols = ("x", "z"), ("y", "c")
    in_specs = (P(rows, cols), P(rows, None, cols), P(rows, None), P(rows, None), P(rows, None, cols))
    out_specs = (P(rows, None, cols), P(rows, None, cols))
    return jax.shard_map(per_device, mesh=split, in_specs=in_specs, out_specs=out_specs, check_vma=False)
```

time: 627 us -> 216 us (0.34)
  blocking collectives: 246 us -> 0 us
  waiting for transfers between devices: 257 us -> 85.9 us
  starting transfers between devices: 15.1 us -> 93.1 us
  local copies, waits for them, and re-layouts: 47.8 us -> 10.5 us
  other arithmetic: 24.9 us -> 3.27 us
  Pallas kernels: 0 us -> 17.9 us
  matrix products: 19.6 us -> 3.08 us
  between operations: 14.7 us -> 1.06 us
    all_to_all x2 -> x0, blocking collectives: 246 us -> none  [the longest x1 156 us: per_device(): lax.all_to_all(send_scaled, 'expert', split_axis=0, concat_axis=0, tiled=...]
    psum x2 -> x0, waiting for transfers between devices: 155 us -> none  [gram_sum(): return lax.psum(partial_gram.astype(jnp.bfloat16), 'dp').astype(jnp.float32)]
    ppermute x0 -> x16, starting transfers between devices: none -> 59.8 us  [the longest x12 41.2 us: shift_y(): lax.ppermute(value, 'y', [(i, (i + step) % size) for i in range(size)])]
    all_gather x1 -> x0, waiting for transfers between devices: 41.5 us -> none  [per_device(): whole_scaled = lax.all_gather(scaled_part, 'dp', axis=2, tiled=True)]
    unnamed x5 -> x0, waiting for transfers between devices: 39.7 us -> none
    all_to_all x1 -> x3, waiting for transfers between devices: 20.6 us -> 55.7 us  [the longest x1 35.5 us: per_device(): lax.all_to_all(send_grad, EXPERT, split_axis=0, concat_axis=0, tiled=True)]
    ppermute x0 -> x16, waiting for transfers between devices: none -> 30.2 us  [the longest x12 29.4 us: shift_y(): lax.ppermute(value, 'y', [(i, (i + step) % size) for i in range(size)])]
    scatter x2 -> x0, local copies, waits for them, and re-layouts: 20.6 us -> none  [place_slots(): return empty_rows.at[slot_index].set(values)]
  transfers between devices with their start and end apart: 5 -> 19, of which waited for: 5 -> 12; matrix products, arithmetic and copies ran while one was open for 0% -> 5% of each run, Pallas kernels for 0% -> 8%
where the time goes in v1:
time: 216 us; the launch traced here: 215 us
  starting transfers between devices  93.1 us (43%)
  waiting for transfers between devices  85.9 us (40%)
  Pallas kernels  17.9 us (8%)
  local copies, waits for them, and re-layouts  10.5 us (5%)
  other arithmetic  3.27 us (2%)
  matrix products  3.08 us (1%)
    ppermute x12, starting transfers between devices, shift_y(): lax.ppermute(value, 'y', [(i, (i + step) % size) for i in range(size)])  41.2 us
    all_to_all x1, waiting for transfers between devices, per_device(): lax.all_to_all(send_grad, EXPERT, split_axis=0, concat_axis=0, tiled=True)  35.5 us
    ppermute x12, waiting for transfers between devices, shift_y(): lax.ppermute(value, 'y', [(i, (i + step) % size) for i in range(size)])  29.4 us
    all_to_all x1, waiting for transfers between devices, per_device(): lax.all_to_all(send_scaled.reshape(experts, capacity, unit_part), EXPERT,...  20.2 us
    all_to_all x1, starting transfers between devices, per_device(): lax.all_to_all(send_scaled.reshape(experts, capacity, unit_part), EXPERT,...  19.1 us
    ppermute x4, starting transfers between devices, swap_core(): return lax.ppermute(value, 'c', [(0, 1), (1, 0)])  18.6 us
    pallas_call x3, Pallas kernels, call(): pl.pallas_call(kernel, out_shape=outs, in_specs=[smem_spec()] + [full_spe...  17.9 us
    all_to_all x1, starting transfers between devices, per_device(): lax.all_to_all(send_grad, EXPERT, split_axis=0, concat_axis=0, tiled=True)  7.81 us
  transfers between devices with their start and end apart: 19, of which 12 were waited for; matrix products, arithmetic and copies ran while one was open for 5% of the time, Pallas kernels for 8%

profile of v1, /device:TPU:1, one launch (start us, length us, event | category | flops | bytes accessed | tf_op | source)
XLA Modules:
  0.0 214.7 jit_solution(7945436283628602982)
XLA Ops:
  3.9 19.1 %all-to-all-start.2 = ((bf16[64,20,128]{2,1,0:T(8,128)(2,1)}), bf16[64,20,128]{2,1,0:T(8,128)(2,1)S(1)}, u32[]{:S(2)}, u32[]{:S(2)}) async-start(bf16[64,20,128]{2,1,0:T(8,128)(2,1)} %reshape.87), calls=%async_computation.2 | async-start | bytes 786432 | tf_op jit(solution)/shard_map/all_to_all | solution.py:190
  25.7 1.8 copy.14
  27.5 20.2 %all-to-all-done.2 = bf16[64,20,128]{2,1,0:T(8,128)(2,1)S(1)} async-done(((bf16[64,20,128]{2,1,0:T(8,128)(2,1)}), bf16[64,20,128]{2,1,0:T(8,128)(2,1)S(1)}, u32[]{:S(2)}, u32[]{:S(2)}) %all-to-all-start.2) | async-done | bytes 327712 | tf_op jit(solution)/shard_map/all_to_all | solution.py:190
  47.7 7.8 %all-to-all-start = ((bf16[64,40,256]{2,1,0:T(8,128)(2,1)}), bf16[64,40,256]{2,1,0:T(8,128)(2,1)}, u32[]{:S(2)}, u32[]{:S(2)}) async-start(bf16[64,40,256]{2,1,0:T(8,128)(2,1)} %copy.14), calls=%async_computation | async-start | bytes 2621440 | tf_op jit(solution)/shard_map/all_to_all | solution.py:200
  55.6 3.2 %collective-permute-start.4 = (bf16[1280,128]{1,0:T(8,128)(2,1)S(1)}, bf16[1280,128]{1,0:T(8,128)(2,1)S(1)}, u32[]{:S(2)}, u32[]{:S(2)}) collective-permute-start(bf16[1280,128]{1,0:T(8,128)(2,1)S(1)} %reshape.88), channel_id=1, source_target_pairs={{0,128},{128,256},{256,384},{384,0},{1,129},{129,257},{257,385},{3... | collective-permute-start | bytes 983048 | tf_op jit(solution)/shard_map/ppermute | solution.py:23
  58.9 4.5 %collective-permute-start.5 = (bf16[1280,128]{1,0:T(8,128)(2,1)S(1)}, bf16[1280,128]{1,0:T(8,128)(2,1)S(1)}, u32[]{:S(2)}, u32[]{:S(2)}) collective-permute-start(bf16[1280,128]{1,0:T(8,128)(2,1)S(1)} %reshape.88), channel_id=1, source_target_pairs={{0,256},{128,384},{256,0},{384,128},{1,257},{129,385},{257,1},{385... | collective-permute-start | bytes 983048 | tf_op jit(solution)/shard_map/ppermute | solution.py:23
  63.4 3.0 %collective-permute-start.6 = (bf16[1280,128]{1,0:T(8,128)(2,1)S(1)}, bf16[1280,128]{1,0:T(8,128)(2,1)S(1)}, u32[]{:S(2)}, u32[]{:S(2)}) collective-permute-start(bf16[1280,128]{1,0:T(8,128)(2,1)S(1)} %reshape.88), channel_id=1, source_target_pairs={{0,384},{128,0},{256,128},{384,256},{1,385},{129,1},{257,129},{385... | collective-permute-start | bytes 983048 | tf_op jit(solution)/shard_map/ppermute | solution.py:23
  66.6 8.2 %collective-permute-done.5 = bf16[1280,128]{1,0:T(8,128)(2,1)S(1)} collective-permute-done((bf16[1280,128]{1,0:T(8,128)(2,1)S(1)}, bf16[1280,128]{1,0:T(8,128)(2,1)S(1)}, u32[]{:S(2)}, u32[]{:S(2)}) %collective-permute-start.5) | collective-permute-done | bytes 327712 | tf_op jit(solution)/shard_map/ppermute | solution.py:23
  74.8 1.4 collective-permute-done.6
  76.3 4.2 %collective-permute-start.7 = (bf16[4,1280,128]{2,1,0:T(8,128)(2,1)S(1)}, bf16[4,1280,128]{2,1,0:T(8,128)(2,1)}, u32[]{:S(2)}, u32[]{:S(2)}) collective-permute-start(bf16[4,1280,128]{2,1,0:T(8,128)(2,1)S(1)} %pad_maximum_fusion.own_ref), channel_id=1, source_target_pairs={{0,64},{64,0},{1,65},{65,1},{2,66},{66,2},{3,67},{67,3},{4,68},{68... | collective-permute-start | bytes 3932168 | tf_op jit(solution)/shard_map/ppermute | solution.py:27
  80.5 35.5 %all-to-all-done = bf16[64,40,256]{2,1,0:T(8,128)(2,1)} async-done(((bf16[64,40,256]{2,1,0:T(8,128)(2,1)}), bf16[64,40,256]{2,1,0:T(8,128)(2,1)}, u32[]{:S(2)}, u32[]{:S(2)}) %all-to-all-start) | async-done | bytes 1310752 | tf_op jit(solution)/shard_map/all_to_all | solution.py:200
  116.0 1.6 copy.15
  119.0 1.4 copy.20
  120.3 3.5 %shard_map.68 = (bf16[4,1280,128]{2,1,0:T(8,128)(2,1)S(1)}, bf16[4,1280,128]{2,1,0:T(8,128)(2,1)S(1)}) custom-call(s32[16]{0:T(128)S(1)} %pad_add_fusion.spot_ref.refs_0_, bf16[1280,512]{1,0:T(8,128)(2,1)} %bitcast.57, bf16[1024,512]{1,0:T(8,128)(2,1)S(1)} %bitcast.56), custom_call_target="tpu_custom_call" | custom-call | tf_op jit(solution)/shard_map/pallas_call | solution.py:147
  123.8 7.6 %collective-permute-start = (bf16[4,1280,128]{2,1,0:T(8,128)(2,1)S(1)}, bf16[4,1280,128]{2,1,0:T(8,128)(2,1)S(1)}, u32[]{:S(2)}, u32[]{:S(2)}) collective-permute-start(bf16[4,1280,128]{2,1,0:T(8,128)(2,1)S(1)} %get-tuple-element.8), channel_id=1, source_target_pairs={{0,64},{64,0},{1,65},{65,1},{2,66},{66,2},{3,67},{67,3},{4,68},{68... | collective-permute-start | bytes 3932168 | tf_op jit(solution)/shard_map/ppermute | solution.py:27
  131.4 5.5 %shard_map.69 = (bf16[1024,512]{1,0:T(8,128)(2,1)S(1)}, bf16[4,576,128]{2,1,0:T(8,128)(2,1)S(1)}, bf16[4,576,128]{2,1,0:T(8,128)(2,1)S(1)}) custom-call(s32[16]{0:T(128)S(1)} %pad_add_fusion.spot_ref.refs_0_, bf16[4,1280,128]{2,1,0:T(8,128)(2,1)S(1)} %pad_maximum_fusion.own_ref, bf16[4,1280,128]{2,1,0:T(8,128)(2,1)} %collective-permute-done.7.other_ref, ...), custom_call_target="tpu_custom_call" | custom-call | tf_op jit(solution)/shard_map/pallas_call | solution.py:147
  136.9 1.9 collective-permute-start.8
  139.3 3.2 %collective-permute-start.1 = (bf16[1280,128]{1,0:T(8,128)(2,1)S(1)}, bf16[1280,128]{1,0:T(8,128)(2,1)S(1)}, u32[]{:S(2)}, u32[]{:S(2)}) collective-permute-start(bf16[1280,128]{1,0:T(8,128)(2,1)S(1)} %get-tuple-element.18), channel_id=1, source_target_pairs={{0,128},{128,256},{256,384},{384,0},{1,129},{129,257},{257,385},{3... | collective-permute-start | bytes 983048 | tf_op jit(solution)/shard_map/ppermute | solution.py:23
  142.5 4.5 %collective-permute-start.2 = (bf16[1280,128]{1,0:T(8,128)(2,1)S(1)}, bf16[1280,128]{1,0:T(8,128)(2,1)S(1)}, u32[]{:S(2)}, u32[]{:S(2)}) collective-permute-start(bf16[1280,128]{1,0:T(8,128)(2,1)S(1)} %get-tuple-element.20), channel_id=1, source_target_pairs={{0,256},{128,384},{256,0},{384,128},{1,257},{129,385},{257,1},{385... | collective-permute-start | bytes 983048 | tf_op jit(solution)/shard_map/ppermute | solution.py:23
  147.0 3.0 %collective-permute-start.3 = (bf16[1280,128]{1,0:T(8,128)(2,1)S(1)}, bf16[1280,128]{1,0:T(8,128)(2,1)S(1)}, u32[]{:S(2)}, u32[]{:S(2)}) collective-permute-start(bf16[1280,128]{1,0:T(8,128)(2,1)S(1)} %get-tuple-element.19), channel_id=1, source_target_pairs={{0,384},{128,0},{256,128},{384,256},{1,385},{129,1},{257,129},{385... | collective-permute-start | bytes 983048 | tf_op jit(solution)/shard_map/ppermute | solution.py:23
  151.3 8.1 %collective-permute-done.2 = bf16[1280,128]{1,0:T(8,128)(2,1)S(1)} collective-permute-done((bf16[1280,128]{1,0:T(8,128)(2,1)S(1)}, bf16[1280,128]{1,0:T(8,128)(2,1)S(1)}, u32[]{:S(2)}, u32[]{:S(2)}) %collective-permute-start.2) | collective-permute-done | bytes 327712 | tf_op jit(solution)/shard_map/ppermute | solution.py:23
  161.6 6.3 %all-to-all-start.1 = ((bf16[64,20,128]{2,1,0:T(8,128)(2,1)}), bf16[64,20,128]{2,1,0:T(8,128)(2,1)S(1)}, u32[]{:S(2)}, u32[]{:S(2)}) async-start(bf16[64,20,128]{2,1,0:T(8,128)(2,1)} %reshape.84), calls=%async_computation.1 | async-start | bytes 786432 | tf_op jit(solution)/shard_map/all_to_all | solution.py:240
  168.0 4.8 %collective-permute-start.10 = (bf16[576,128]{1,0:T(8,128)(2,1)S(1)}, bf16[576,128]{1,0:T(8,128)(2,1)S(1)}, u32[]{:S(2)}, u32[]{:S(2)}) collective-permute-start(bf16[576,128]{1,0:T(8,128)(2,1)S(1)} %get-tuple-element.23), channel_id=1, source_target_pairs={{0,256},{128,384},{256,0},{384,128},{1,257},{129,385},{257,1},{385... | collective-permute-start | bytes 442376 | tf_op jit(solution)/shard_map/ppermute | solution.py:23
  172.7 4.7 %collective-permute-start.11 = (bf16[576,128]{1,0:T(8,128)(2,1)S(1)}, bf16[576,128]{1,0:T(8,128)(2,1)S(1)}, u32[]{:S(2)}, u32[]{:S(2)}) collective-permute-start(bf16[576,128]{1,0:T(8,128)(2,1)S(1)} %get-tuple-element.22), channel_id=1, source_target_pairs={{0,384},{128,0},{256,128},{384,256},{1,385},{129,1},{257,129},{385... | collective-permute-start | bytes 442376 | tf_op jit(solution)/shard_map/ppermute | solution.py:23
  177.4 1.9 collective-permute-start.9
  179.8 5.0 %collective-permute-done.9 = bf16[576,128]{1,0:T(8,128)(2,1)S(1)} collective-permute-done((bf16[576,128]{1,0:T(8,128)(2,1)S(1)}, bf16[576,128]{1,0:T(8,128)(2,1)S(1)}, u32[]{:S(2)}, u32[]{:S(2)}) %collective-permute-start.9) | collective-permute-done | bytes 147488 | tf_op jit(solution)/shard_map/ppermute | solution.py:23
  184.9 1.9 collective-permute-start.12
  186.9 2.4 %collective-permute-start.13 = (bf16[576,128]{1,0:T(8,128)(2,1)S(1)}, bf16[576,128]{1,0:T(8,128)(2,1)S(1)}, u32[]{:S(2)}, u32[]{:S(2)}) collective-permute-start(bf16[576,128]{1,0:T(8,128)(2,1)S(1)} %fusion.15), channel_id=1, source_target_pairs={{0,256},{128,384},{256,0},{384,128},{1,257},{129,385},{257,1},{385... | collective-permute-start | bytes 442376 | tf_op jit(solution)/shard_map/ppermute | solution.py:23
  189.2 4.1 %collective-permute-start.14 = (bf16[576,128]{1,0:T(8,128)(2,1)S(1)}, bf16[576,128]{1,0:T(8,128)(2,1)S(1)}, u32[]{:S(2)}, u32[]{:S(2)}) collective-permute-start(bf16[576,128]{1,0:T(8,128)(2,1)S(1)} %fusion.15), channel_id=1, source_target_pairs={{0,384},{128,0},{256,128},{384,256},{1,385},{129,1},{257,129},{385... | collective-permute-start | bytes 442376 | tf_op jit(solution)/shard_map/ppermute | solution.py:23
  194.5 2.8 %collective-permute-done.14 = bf16[576,128]{1,0:T(8,128)(2,1)S(1)} collective-permute-done((bf16[576,128]{1,0:T(8,128)(2,1)S(1)}, bf16[576,128]{1,0:T(8,128)(2,1)S(1)}, u32[]{:S(2)}, u32[]{:S(2)}) %collective-permute-start.14) | collective-permute-done | bytes 147488 | tf_op jit(solution)/shard_map/ppermute | solution.py:23
  197.4 4.9 %collective-permute-start.15 = (bf16[4,576,128]{2,1,0:T(8,128)(2,1)S(1)}, bf16[4,576,128]{2,1,0:T(8,128)(2,1)S(1)}, u32[]{:S(2)}, u32[]{:S(2)}) collective-permute-start(bf16[4,576,128]{2,1,0:T(8,128)(2,1)S(1)} %pad_maximum_fusion.1.refs_1_), channel_id=1, source_target_pairs={{0,64},{64,0},{1,65},{65,1},{2,66},{66,2},{3,67},{67,3},{4,68},{68... | collective-permute-start | bytes 1769480 | tf_op jit(solution)/shard_map/ppermute | solution.py:27
  203.9 8.9 %shard_map.70 = f32[1,1024,512]{2,1,0:T(8,128)} custom-call(s32[16]{0:T(128)S(1)} %pad_add_fusion.spot_ref.refs_0_, bf16[4,576,128]{2,1,0:T(8,128)(2,1)S(1)} %pad_maximum_fusion.1.refs_1_, bf16[4,576,128]{2,1,0:T(8,128)(2,1)S(1)} %collective-permute-done.15.refs_2_, bf16[1024,512]{1,0:T(8,128)(2,1)S(1)} %get-tuple-element.11.refs_3_), custom_call_target="tpu_custom_call" | custom-call | tf_op jit(solution)/shard_map/pallas_call | solution.py:147
  (48 shorter events, 16.8 us)
Async XLA Ops:
  0.6 23.6 %copy-start = (bf16[512,512]{1,0:T(8,128)(2,1)S(1)}, bf16[512,512]{1,0:T(8,128)(2,1)}, u32[]{:S(2)}) copy-start(bf16[512,512]{1,0:T(8,128)(2,1)} %param.5) | copy-start | bytes 1572868
  0.6 1.2 copy-start.2
  0.7 1.2 copy-start.3
  3.9 43.9 %all-to-all-start.2 = ((bf16[64,20,128]{2,1,0:T(8,128)(2,1)}), bf16[64,20,128]{2,1,0:T(8,128)(2,1)S(1)}, u32[]{:S(2)}, u32[]{:S(2)}) async-start(bf16[64,20,128]{2,1,0:T(8,128)(2,1)} %reshape.87), calls=%async_computation.2 | async-start | bytes 786432 | tf_op jit(solution)/shard_map/all_to_all | solution.py:190
  47.7 68.3 %all-to-all-start = ((bf16[64,40,256]{2,1,0:T(8,128)(2,1)}), bf16[64,40,256]{2,1,0:T(8,128)(2,1)}, u32[]{:S(2)}, u32[]{:S(2)}) async-start(bf16[64,40,256]{2,1,0:T(8,128)(2,1)} %copy.14), calls=%async_computation | async-start | bytes 2621440 | tf_op jit(solution)/shard_map/all_to_all | solution.py:200
  55.6 10.9 %collective-permute-start.4 = (bf16[1280,128]{1,0:T(8,128)(2,1)S(1)}, bf16[1280,128]{1,0:T(8,128)(2,1)S(1)}, u32[]{:S(2)}, u32[]{:S(2)}) collective-permute-start(bf16[1280,128]{1,0:T(8,128)(2,1)S(1)} %reshape.88), channel_id=1, source_target_pairs={{0,128},{128,256},{256,384},{384,0},{1,129},{129,257},{257,385},{3... | collective-permute-start | bytes 983048 | tf_op jit(solution)/shard_map/ppermute | solution.py:23
  58.9 15.9 %collective-permute-start.5 = (bf16[1280,128]{1,0:T(8,128)(2,1)S(1)}, bf16[1280,128]{1,0:T(8,128)(2,1)S(1)}, u32[]{:S(2)}, u32[]{:S(2)}) collective-permute-start(bf16[1280,128]{1,0:T(8,128)(2,1)S(1)} %reshape.88), channel_id=1, source_target_pairs={{0,256},{128,384},{256,0},{384,128},{1,257},{129,385},{257,1},{385... | collective-permute-start | bytes 983048 | tf_op jit(solution)/shard_map/ppermute | solution.py:23
  63.4 12.7 %collective-permute-start.6 = (bf16[1280,128]{1,0:T(8,128)(2,1)S(1)}, bf16[1280,128]{1,0:T(8,128)(2,1)S(1)}, u32[]{:S(2)}, u32[]{:S(2)}) collective-permute-start(bf16[1280,128]{1,0:T(8,128)(2,1)S(1)} %reshape.88), channel_id=1, source_target_pairs={{0,384},{128,0},{256,128},{384,256},{1,385},{129,1},{257,129},{385... | collective-permute-start | bytes 983048 | tf_op jit(solution)/shard_map/ppermute | solution.py:23
  76.3 55.1 %collective-permute-start.7 = (bf16[4,1280,128]{2,1,0:T(8,128)(2,1)S(1)}, bf16[4,1280,128]{2,1,0:T(8,128)(2,1)}, u32[]{:S(2)}, u32[]{:S(2)}) collective-permute-start(bf16[4,1280,128]{2,1,0:T(8,128)(2,1)S(1)} %pad_maximum_fusion.own_ref), channel_id=1, source_target_pairs={{0,64},{64,0},{1,65},{65,1},{2,66},{66,2},{3,67},{67,3},{4,68},{68... | collective-permute-start | bytes 3932168 | tf_op jit(solution)/shard_map/ppermute | solution.py:27
  119.0 1.4 copy-start.1
  123.8 15.0 %collective-permute-start = (bf16[4,1280,128]{2,1,0:T(8,128)(2,1)S(1)}, bf16[4,1280,128]{2,1,0:T(8,128)(2,1)S(1)}, u32[]{:S(2)}, u32[]{:S(2)}) collective-permute-start(bf16[4,1280,128]{2,1,0:T(8,128)(2,1)S(1)} %get-tuple-element.8), channel_id=1, source_target_pairs={{0,64},{64,0},{1,65},{65,1},{2,66},{66,2},{3,67},{67,3},{4,68},{68... | collective-permute-start | bytes 3932168 | tf_op jit(solution)/shard_map/ppermute | solution.py:27
  136.9 13.1 %collective-permute-start.8 = (bf16[4,576,128]{2,1,0:T(8,128)(2,1)S(1)}, bf16[4,576,128]{2,1,0:T(8,128)(2,1)S(1)}, u32[]{:S(2)}, u32[]{:S(2)}) collective-permute-start(bf16[4,576,128]{2,1,0:T(8,128)(2,1)S(1)} %get-tuple-element.10), channel_id=1, source_target_pairs={{0,64},{64,0},{1,65},{65,1},{2,66},{66,2},{3,67},{67,3},{4,68},{68... | collective-permute-start | bytes 1769480 | tf_op jit(solution)/shard_map/ppermute | solution.py:27
  139.3 12.0 %collective-permute-start.1 = (bf16[1280,128]{1,0:T(8,128)(2,1)S(1)}, bf16[1280,128]{1,0:T(8,128)(2,1)S(1)}, u32[]{:S(2)}, u32[]{:S(2)}) collective-permute-start(bf16[1280,128]{1,0:T(8,128)(2,1)S(1)} %get-tuple-element.18), channel_id=1, source_target_pairs={{0,128},{128,256},{256,384},{384,0},{1,129},{129,257},{257,385},{3... | collective-permute-start | bytes 983048 | tf_op jit(solution)/shard_map/ppermute | solution.py:23
  142.5 16.9 %collective-permute-start.2 = (bf16[1280,128]{1,0:T(8,128)(2,1)S(1)}, bf16[1280,128]{1,0:T(8,128)(2,1)S(1)}, u32[]{:S(2)}, u32[]{:S(2)}) collective-permute-start(bf16[1280,128]{1,0:T(8,128)(2,1)S(1)} %get-tuple-element.20), channel_id=1, source_target_pairs={{0,256},{128,384},{256,0},{384,128},{1,257},{129,385},{257,1},{385... | collective-permute-start | bytes 983048 | tf_op jit(solution)/shard_map/ppermute | solution.py:23
  147.0 13.6 %collective-permute-start.3 = (bf16[1280,128]{1,0:T(8,128)(2,1)S(1)}, bf16[1280,128]{1,0:T(8,128)(2,1)S(1)}, u32[]{:S(2)}, u32[]{:S(2)}) collective-permute-start(bf16[1280,128]{1,0:T(8,128)(2,1)S(1)} %get-tuple-element.19), channel_id=1, source_target_pairs={{0,384},{128,0},{256,128},{384,256},{1,385},{129,1},{257,129},{385... | collective-permute-start | bytes 983048 | tf_op jit(solution)/shard_map/ppermute | solution.py:23
  161.6 51.2 %all-to-all-start.1 = ((bf16[64,20,128]{2,1,0:T(8,128)(2,1)}), bf16[64,20,128]{2,1,0:T(8,128)(2,1)S(1)}, u32[]{:S(2)}, u32[]{:S(2)}) async-start(bf16[64,20,128]{2,1,0:T(8,128)(2,1)} %reshape.84), calls=%async_computation.1 | async-start | bytes 786432 | tf_op jit(solution)/shard_map/all_to_all | solution.py:240
  168.0 11.4 %collective-permute-start.10 = (bf16[576,128]{1,0:T(8,128)(2,1)S(1)}, bf16[576,128]{1,0:T(8,128)(2,1)S(1)}, u32[]{:S(2)}, u32[]{:S(2)}) collective-permute-start(bf16[576,128]{1,0:T(8,128)(2,1)S(1)} %get-tuple-element.23), channel_id=1, source_target_pairs={{0,256},{128,384},{256,0},{384,128},{1,257},{129,385},{257,1},{385... | collective-permute-start | bytes 442376 | tf_op jit(solution)/shard_map/ppermute | solution.py:23
  172.7 7.1 %collective-permute-start.11 = (bf16[576,128]{1,0:T(8,128)(2,1)S(1)}, bf16[576,128]{1,0:T(8,128)(2,1)S(1)}, u32[]{:S(2)}, u32[]{:S(2)}) collective-permute-start(bf16[576,128]{1,0:T(8,128)(2,1)S(1)} %get-tuple-element.22), channel_id=1, source_target_pairs={{0,384},{128,0},{256,128},{384,256},{1,385},{129,1},{257,129},{385... | collective-permute-start | bytes 442376 | tf_op jit(solution)/shard_map/ppermute | solution.py:23
  177.4 7.4 %collective-permute-start.9 = (bf16[576,128]{1,0:T(8,128)(2,1)S(1)}, bf16[576,128]{1,0:T(8,128)(2,1)S(1)}, u32[]{:S(2)}, u32[]{:S(2)}) collective-permute-start(bf16[576,128]{1,0:T(8,128)(2,1)S(1)} %get-tuple-element.21), channel_id=1, source_target_pairs={{0,128},{128,256},{256,384},{384,0},{1,129},{129,257},{257,385},{3... | collective-permute-start | bytes 442376 | tf_op jit(solution)/shard_map/ppermute | solution.py:23
  184.9 8.4 %collective-permute-start.12 = (bf16[576,128]{1,0:T(8,128)(2,1)S(1)}, bf16[576,128]{1,0:T(8,128)(2,1)S(1)}, u32[]{:S(2)}, u32[]{:S(2)}) collective-permute-start(bf16[576,128]{1,0:T(8,128)(2,1)S(1)} %fusion.15), channel_id=1, source_target_pairs={{0,128},{128,256},{256,384},{384,0},{1,129},{129,257},{257,385},{3... | collective-permute-start | bytes 442376 | tf_op jit(solution)/shard_map/ppermute | solution.py:23
  186.9 7.7 %collective-permute-start.13 = (bf16[576,128]{1,0:T(8,128)(2,1)S(1)}, bf16[576,128]{1,0:T(8,128)(2,1)S(1)}, u32[]{:S(2)}, u32[]{:S(2)}) collective-permute-start(bf16[576,128]{1,0:T(8,128)(2,1)S(1)} %fusion.15), channel_id=1, source_target_pairs={{0,256},{128,384},{256,0},{384,128},{1,257},{129,385},{257,1},{385... | collective-permute-start | bytes 442376 | tf_op jit(solution)/shard_map/ppermute | solution.py:23
  189.2 8.1 %collective-permute-start.14 = (bf16[576,128]{1,0:T(8,128)(2,1)S(1)}, bf16[576,128]{1,0:T(8,128)(2,1)S(1)}, u32[]{:S(2)}, u32[]{:S(2)}) collective-permute-start(bf16[576,128]{1,0:T(8,128)(2,1)S(1)} %fusion.15), channel_id=1, source_target_pairs={{0,384},{128,0},{256,128},{384,256},{1,385},{129,1},{257,129},{385... | collective-permute-start | bytes 442376 | tf_op jit(solution)/shard_map/ppermute | solution.py:23
  197.4 6.5 %collective-permute-start.15 = (bf16[4,576,128]{2,1,0:T(8,128)(2,1)S(1)}, bf16[4,576,128]{2,1,0:T(8,128)(2,1)S(1)}, u32[]{:S(2)}, u32[]{:S(2)}) collective-permute-start(bf16[4,576,128]{2,1,0:T(8,128)(2,1)S(1)} %pad_maximum_fusion.1.refs_1_), channel_id=1, source_target_pairs={{0,64},{64,0},{1,65},{65,1},{2,66},{66,2},{3,67},{67,3},{4,68},{68... | collective-permute-start | bytes 1769480 | tf_op jit(solution)/shard_map/ppermute | solution.py:27

commit v2 on v1

--- a/solution.py
+++ b/solution.py
@@ -6,7 +6,7 @@
 from jax.sharding import Mesh, PartitionSpec as P
 
 EXPERT = ("x", "z")
-VMEM_LIMIT = 50 * 1024 * 1024
+VMEM_LIMIT = 24 * 1024 * 1024
 BF16 = jnp.bfloat16
 F32 = jnp.float32
 
@@ -31,9 +31,104 @@
     return lax.dot_general(left, right, (((1,), (1,)), ((), ())), preferred_element_type=F32)
 
 
-def grad_kernel(spot_ref, own_ref, other_ref, rows_ref, gradb_ref, pack_own_ref, pack_other_ref, wide_ref):
+def one_hot(rows, index):
+    return jnp.where(rows == index, 1.0, 0.0).astype(BF16)
+
+
+def row_numbers(count):
+    return lax.broadcasted_iota(jnp.int32, (count, 1), 0)
+
+
+def first_send_kernel(main_ref, left_ref, scaled_ref, grad_ref, out_ref):
+    experts = out_ref.shape[0]
+    tokens, width_part = grad_ref.shape
+    chosen = one_hot(row_numbers(experts * 16), main_ref[...])
+    scaled = scaled_ref[...]
+    part = jnp.dot(chosen, scaled, preferred_element_type=F32).astype(BF16)
+    out_ref[:, 0:16, :] = part.reshape(experts, 16, 128)
+    chosen_token = chosen[:, :tokens] + chosen[:, tokens:]
+    rows = jnp.dot(chosen_token, grad_ref[...], preferred_element_type=F32).astype(BF16)
+    blocks = width_part // 128
+    for b in range(blocks):
+        out_ref[:, 16 * (b + 1) : 16 * (b + 2), :] = rows[:, b * 128 : (b + 1) * 128].reshape(experts, 16, 128)
+    left = one_hot(row_numbers(experts * 8), left_ref[...])
+    part = jnp.dot(left, scaled, preferred_element_type=F32)
+    out_ref[:, 16 * (blocks + 1) :, :] = part.reshape(experts, 8, 128).astype(BF16)
+
+
+def second_send_kernel(index_ref, grad_ref, out_ref):
+    experts = out_ref.shape[0]
+    tokens, width_part = grad_ref.shape
+    number = row_numbers(experts * 16)
+    chosen = one_hot(number - number % 16 + number % 4, index_ref[...])
+    chosen_token = chosen[:, :tokens] + chosen[:, tokens:]
+    rows = jnp.dot(chosen_token, grad_ref[...], preferred_element_type=F32)
+    column = (number % 16) // 4
+    total = jnp.zeros((experts * 16, 128), F32)
+    for b in range(width_part // 128):
+        total = jnp.where(column == b, rows[:, b * 128 : (b + 1) * 128], total)
+    out_ref[...] = total.astype(BF16).reshape(experts, 16, 128)
+
+
+def unpack_kernel(got_ref, out_ref):
+    experts, rows, _ = got_ref.shape
+    out_ref[: experts * 16] = got_ref[:, 0:16, :].reshape(experts * 16, 128)
+    tail = got_ref[:, rows - 8 :, :].astype(F32).reshape(experts * 8, 128).astype(BF16)
+    number = row_numbers(experts * 4)
+    source = lax.broadcasted_iota(jnp.int32, (1, experts * 8), 1)
+    take = one_hot(number // 4 * 8 + number % 4, source)
+    out_ref[experts * 16 :] = jnp.dot(take, tail, preferred_element_type=F32).astype(BF16)
+
+
+def put_piece(spot, y_size, own_ref, other_ref, piece):
+    @pl.when(spot < y_size)
+    def _():
+        own_ref[spot] = piece
+
+    @pl.when(spot >= y_size)
+    def _():
+        other_ref[spot - y_size] = piece
+
+
+def main_rows(got_ref, rows_ref):
+    experts = got_ref.shape[0]
+    for b in range(rows_ref.shape[1] // 128):
+        rows_ref[: experts * 16, b * 128 : (b + 1) * 128] = got_ref[
+            :, 16 * (b + 1) : 16 * (b + 2), :
+        ].reshape(experts * 16, 128)
+
+
+def back_main_kernel(spot_ref, got_ref, weight_ref, own_ref, other_ref, rows_ref):
+    blocks = weight_ref.shape[0] // 128
+    y_size = blocks // 2
+    main_rows(got_ref, rows_ref)
+    term = nt_dot(rows_ref[...], weight_ref[...]).astype(BF16)
+    for d in range(blocks):
+        put_piece(spot_ref[blocks + d], y_size, own_ref, other_ref, term[:, d * 128 : (d + 1) * 128])
+
+
+def back_left_kernel(spot_ref, got_ref, weight_ref, own_ref, other_ref, rows_ref):
+    blocks = weight_ref.shape[0] // 128
+    y_size = blocks // 2
+    experts = got_ref.shape[0]
+    got = got_ref[...].reshape(experts * 16, 128)
+    number = row_numbers(experts * 4)
+    source = lax.broadcasted_iota(jnp.int32, (1, experts * 16), 1)
+    for b in range(rows_ref.shape[1] // 128):
+        take = one_hot(number // 4 * 16 + b * 4 + number % 4, source)
+        rows_ref[:, b * 128 : (b + 1) * 128] = jnp.dot(take, got, preferred_element_type=F32).astype(BF16)
+    term = nt_dot(rows_ref[...], weight_ref[...]).astype(BF16)
+    for d in range(blocks):
+        put_piece(spot_ref[blocks + d], y_size, own_ref, other_ref, term[:, d * 128 : (d + 1) * 128])
+
+
+def grad_kernel(
+    spot_ref, own_ref, other_ref, got_ref, left_ref, gradb_ref, pack_own_ref, pack_other_ref, wide_ref, rows_ref
+):
     blocks = gradb_ref.shape[0] // 128
     y_size = blocks // 2
+    main_rows(got_ref, rows_ref)
+    rows_ref[got_ref.shape[0] * 16 :] = left_ref[...]
     for d in range(blocks):
         spot = spot_ref[d]
 
@@ -75,23 +170,6 @@
         @pl.when(spot >= y_size)
         def _():
             put(pack_other_ref, spot - y_size)
-
-
-def back_kernel(spot_ref, rows_ref, weight_ref, own_ref, other_ref):
-    blocks = weight_ref.shape[0] // 128
-    y_size = blocks // 2
-    term = nt_dot(rows_ref[...], weight_ref[...]).astype(BF16)
-    for d in range(blocks):
-        spot = spot_ref[blocks + d]
-        piece = term[:, d * 128 : (d + 1) * 128]
-
-        @pl.when(spot < y_size)
-        def _():
-            own_ref[spot] = piece
-
-        @pl.when(spot >= y_size)
-        def _():
-            other_ref[spot - y_size] = piece
 
 
 def ortho_kernel(width, spot_ref, own_ref, other_ref, gradb_ref, out_ref, gram_ref):
@@ -143,11 +221,11 @@
     out_ref[0] = total * width**0.5
 
 
-def call(kernel, outs, ins, scratch=()):
+def call(kernel, outs, ins, scratch=(), scalars=1):
     return pl.pallas_call(
         kernel,
         out_shape=outs,
-        in_specs=[smem_spec()] + [full_spec()] * (len(ins) - 1),
+        in_specs=[smem_spec()] * scalars + [full_spec()] * (len(ins) - scalars),
         out_specs=jax.tree.map(lambda _: full_spec(), outs),
         scratch_shapes=list(scratch),
         compiler_params=pltpu.CompilerParams(vmem_limit_bytes=VMEM_LIMIT),
@@ -180,41 +258,41 @@
     earlier = (order[:, None] < order[None, :]).astype(BF16)
     before = jnp.dot(named, earlier, preferred_element_type=F32)
     rank_in = jnp.sum(before * named.astype(F32), axis=0, keepdims=True).astype(jnp.int32)
-    slot_index = flat_ids * capacity + rank_in
-    chosen = (jnp.arange(total_slots, dtype=jnp.int32)[:, None] == slot_index).astype(BF16)
-    chosen_token = chosen[:, :tokens] + chosen[:, tokens:]
+    late = rank_in >= 16
+    main_index = jnp.where(late, -1, flat_ids * 16 + rank_in)
+    left_index = jnp.where(late, flat_ids * 8 + rank_in - 16, -1)
+    second_index = jnp.where(late, flat_ids * 16 + rank_in - 16, -1)
 
     scaled_part = (gate_prob[:, :, None] * hidden.astype(F32)).astype(BF16)
     scaled_part = scaled_part.transpose(1, 0, 2).reshape(pair_count, unit_part)
-    send_scaled = jnp.dot(chosen, scaled_part, preferred_element_type=F32).astype(BF16)
-    got_scaled = lax.all_to_all(
-        send_scaled.reshape(experts, capacity, unit_part), EXPERT, split_axis=0, concat_axis=0, tiled=True
-    ).reshape(total_slots, unit_part)
-
-    send_grad = jnp.dot(chosen_token, grad_out, preferred_element_type=F32).astype(BF16)
-    send_grad = (
-        send_grad.reshape(experts, capacity, 2, width_part // 2)
-        .transpose(0, 2, 1, 3)
-        .reshape(experts, 2 * capacity, width_part // 2)
-    )
-    got_grad = lax.all_to_all(send_grad, EXPERT, split_axis=0, concat_axis=0, tiled=True)
-    got_grad = (
-        got_grad.reshape(experts, 2, capacity, width_part // 2)
-        .transpose(0, 2, 1, 3)
-        .reshape(total_slots, width_part)
-    )
-
+    column_blocks = width_part // 128
+    first_rows = 16 * (column_blocks + 1) + 8
+
+    def exchange(value):
+        return lax.all_to_all(value, EXPERT, split_axis=0, concat_axis=0, tiled=True)
+
+    got_main = exchange(
+        call(
+            first_send_kernel,
+            jax.ShapeDtypeStruct((experts, first_rows, 128), BF16),
+            (main_index, left_index, scaled_part, grad_out),
+            scalars=0,
+        )
+    )
+    got_left = exchange(
+        call(
+            second_send_kernel,
+            jax.ShapeDtypeStruct((experts, 4 * column_blocks, 128), BF16),
+            (second_index, grad_out),
+            scalars=0,
+        )
+    )
+
+    got_scaled = call(
+        unpack_kernel, jax.ShapeDtypeStruct((total_slots, unit_part), BF16), (got_main,), scalars=0
+    )
     gathered = jnp.stack([got_scaled] + [shift_y(got_scaled, k, y_size) for k in range(1, y_size)])
     gathered_other = swap_core(gathered)
-
-    pack_rows = units // 2 + 64
-    packs = jax.ShapeDtypeStruct((y_size, pack_rows, 128), BF16)
-    grad_bf16, pack_own, pack_other = call(
-        grad_kernel,
-        (jax.ShapeDtypeStruct((units, width_part), BF16), packs, packs),
-        (spots, gathered, gathered_other, got_grad),
-        (pltpu.VMEM((total_slots, units), BF16),),
-    )
 
     def reduce_dp(own, other):
         both = (own.astype(F32) + swap_core(other).astype(F32)).astype(BF16)
@@ -224,6 +302,48 @@
             total = total + part.astype(F32)
         return total.astype(BF16)
 
+    def terms(count):
+        return jax.ShapeDtypeStruct((y_size, count, unit_part), BF16)
+
+    weight_part = weights[0]
+    main_count = experts * 16
+    left_count = total_slots - main_count
+    main_own, main_other = call(
+        back_main_kernel,
+        (terms(main_count), terms(main_count)),
+        (spots, got_main, weight_part),
+        (pltpu.VMEM((main_count, width_part), BF16),),
+    )
+    summed_main = reduce_dp(main_own, main_other)
+    left_own, left_other, left_rows = call(
+        back_left_kernel,
+        (terms(left_count), terms(left_count), jax.ShapeDtypeStruct((left_count, width_part), BF16)),
+        (spots, got_left, weight_part),
+    )
+    summed_left = reduce_dp(left_own, left_other)
+    returned = exchange(
+        jnp.concatenate(
+            [
+                summed_main.reshape(experts, 16, unit_part),
+                summed_left.reshape(experts, capacity - 16, unit_part),
+            ],
+            axis=1,
+        )
+    ).reshape(total_slots, unit_part)
+    slot_index = flat_ids * capacity + rank_in
+    chosen = (jnp.arange(total_slots, dtype=jnp.int32)[:, None] == slot_index).astype(BF16)
+    picked = lax.dot_general(chosen, returned, (((0,), (0,)), ((), ())), preferred_element_type=F32)
+    picked = picked.reshape(top_count, tokens, unit_part).transpose(1, 0, 2)
+    hidden_grad = (gate_prob[:, :, None] * picked).astype(BF16)
+
+    pack_rows = units // 2 + 64
+    packs = jax.ShapeDtypeStruct((y_size, pack_rows, 128), BF16)
+    grad_bf16, pack_own, pack_other = call(
+        grad_kernel,
+        (jax.ShapeDtypeStruct((units, width_part), BF16), packs, packs),
+        (spots, gathered, gathered_other, got_main, left_rows),
+        (pltpu.VMEM((total_slots, units), BF16), pltpu.VMEM((total_slots, width_part), BF16)),
+    )
     pack = reduce_dp(pack_own, pack_other)
     pack_all = jnp.stack([pack] + [shift_y(pack, k, y_size) for k in range(1, y_size)])
     pack_all_other = swap_core(pack_all)
@@ -233,16 +353,6 @@
         (spots, pack_all, pack_all_other, grad_bf16),
         (pltpu.VMEM((units, units), BF16),),
     )
-
-    terms = jax.ShapeDtypeStruct((y_size, total_slots, unit_part), BF16)
-    term_own, term_other = call(back_kernel, (terms, terms), (spots, got_grad, weights[0]))
-    summed = reduce_dp(term_own, term_other)
-    returned = lax.all_to_all(
-        summed.reshape(experts, capacity, unit_part), EXPERT, split_axis=0, concat_axis=0, tiled=True
-    ).reshape(total_slots, unit_part)
-    picked = lax.dot_general(chosen, returned, (((0,), (0,)), ((), ())), preferred_element_type=F32)
-    picked = picked.reshape(top_count, tokens, unit_part).transpose(1, 0, 2)
-    hidden_grad = (gate_prob[:, :, None] * picked).astype(BF16)
     return (hidden_grad, update)
 
 

time: 216 us -> 237 us (1.097)
  starting transfers between devices: 93.1 us -> 105 us
  waiting for transfers between devices: 85.9 us -> 94.1 us
  local copies, waits for them, and re-layouts: 10.5 us -> 3.1 us
  Pallas kernels: 17.9 us -> 23.6 us
  other arithmetic: 3.27 us -> 6.07 us
    all_to_all x3, starting transfers between devices: 33.2 us -> 45.9 us  [exchange(): lax.all_to_all(value, EXPERT, split_axis=0, concat_axis=0, tiled=True)]
    all_to_all x3, waiting for transfers between devices: 55.7 us -> 66.7 us  [exchange(): lax.all_to_all(value, EXPERT, split_axis=0, concat_axis=0, tiled=True)]
    pallas_call x3 -> x7, Pallas kernels: 17.9 us -> 23.6 us  [call(): pl.pallas_call(kernel, out_shape=outs, in_specs=[smem_spec()] * scalars +...]
    ppermute x4 -> x5, starting transfers between devices: 18.6 us -> 14.1 us  [swap_core(): return lax.ppermute(value, 'c', [(0, 1), (1, 0)])]
    reshape x7 -> x1, local copies, waits for them, and re-layouts: 4.22 us -> 0.07 us  [per_device(): returned = exchange(jnp.concatenate([summed_main.reshape(experts, 16, uni...]
    ppermute x12 -> x15, waiting for transfers between devices: 29.4 us -> 25.9 us  [shift_y(): lax.ppermute(value, 'y', [(i, (i + step) % size) for i in range(size)])]
    ppermute x12 -> x15, starting transfers between devices: 41.2 us -> 44.5 us  [shift_y(): lax.ppermute(value, 'y', [(i, (i + step) % size) for i in range(size)])]
  transfers between devices with their start and end apart: 19 -> 23, of which waited for: 12 -> 8; matrix products, arithmetic and copies ran while one was open for 5% -> 3% of each run, Pallas kernels for 8% -> 5%
where the time goes in v2:
time: 237 us; the launch traced here: 234 us
  starting transfers between devices  105 us (44%)
  waiting for transfers between devices  94.1 us (40%)
  Pallas kernels  23.6 us (10%)
  other arithmetic  6.07 us (3%)
  local copies, waits for them, and re-layouts  3.1 us (1%)
    all_to_all x3, waiting for transfers between devices, exchange(): lax.all_to_all(value, EXPERT, split_axis=0, concat_axis=0, tiled=True)  66.7 us
    all_to_all x3, starting transfers between devices, exchange(): lax.all_to_all(value, EXPERT, split_axis=0, concat_axis=0, tiled=True)  45.9 us
    ppermute x15, starting transfers between devices, shift_y(): lax.ppermute(value, 'y', [(i, (i + step) % size) for i in range(size)])  44.5 us
    ppermute x15, waiting for transfers between devices, shift_y(): lax.ppermute(value, 'y', [(i, (i + step) % size) for i in range(size)])  25.9 us
    pallas_call x7, Pallas kernels, call(): pl.pallas_call(kernel, out_shape=outs, in_specs=[smem_spec()] * scalars +...  23.6 us
    ppermute x5, starting transfers between devices, swap_core(): return lax.ppermute(value, 'c', [(0, 1), (1, 0)])  14.1 us
  transfers between devices with their start and end apart: 23, of which 8 were waited for; matrix products, arithmetic and copies ran while one was open for 3% of the time, Pallas kernels for 5%

profile of v2, /device:TPU:1, one launch (start us, length us, event | category | flops | bytes accessed | tf_op | source)
XLA Modules:
  0.0 233.8 jit_solution(3715071763598879865)
XLA Ops:
  2.8 2.7 %shard_map.68 = bf16[64,88,128]{2,1,0:T(8,128)(2,1)} custom-call(s32[1,1024]{1,0:T(1,128)S(1)} %get-tuple-element.31.main_ref, s32[1,1024]{1,0:T(1,128)S(1)} %get-tuple-element.33.left_ref, bf16[1024,128]{1,0:T(8,128)(2,1)S(1)} %bitcast.77, bf16[512,512]{1,0:T(8,128)(2,1)S(1)} %copy-done.2), custom_call_target="tpu_custom_call" | custom-call | tf_op jit(solution)/shard_map/pallas_call | solution.py:225
  5.5 19.1 %all-to-all-start = ((bf16[64,88,128]{2,1,0:T(8,128)(2,1)}), bf16[64,88,128]{2,1,0:T(8,128)(2,1)S(1)}, u32[]{:S(2)}, u32[]{:S(2)}) async-start(bf16[64,88,128]{2,1,0:T(8,128)(2,1)} %shard_map.68), calls=%async_computation | async-start | bytes 2883584 | tf_op jit(solution)/shard_map/all_to_all | solution.py:272
  26.1 63.9 %all-to-all-done.got_ref = bf16[64,88,128]{2,1,0:T(8,128)(2,1)S(1)} async-done(((bf16[64,88,128]{2,1,0:T(8,128)(2,1)}), bf16[64,88,128]{2,1,0:T(8,128)(2,1)S(1)}, u32[]{:S(2)}, u32[]{:S(2)}) %all-to-all-start) | async-done | bytes 1441824 | tf_op jit(solution)/shard_map/all_to_all | solution.py:272
  90.0 12.2 %all-to-all-start.1 = ((bf16[64,16,128]{2,1,0:T(8,128)(2,1)}), bf16[64,16,128]{2,1,0:T(8,128)(2,1)S(1)}, u32[]{:S(2)}, u32[]{:S(2)}) async-start(bf16[64,16,128]{2,1,0:T(8,128)(2,1)} %shard_map.70), calls=%async_computation.1 | async-start | bytes 524288 | tf_op jit(solution)/shard_map/all_to_all | solution.py:272
  102.4 4.6 %collective-permute-start.10 = (bf16[1280,128]{1,0:T(8,128)(2,1)S(1)}, bf16[1280,128]{1,0:T(8,128)(2,1)}, u32[]{:S(2)}, u32[]{:S(2)}) collective-permute-start(bf16[1280,128]{1,0:T(8,128)(2,1)S(1)} %shard_map.72), channel_id=1, source_target_pairs={{0,384},{128,0},{256,128},{384,256},{1,385},{129,1},{257,129},{385... | collective-permute-start | bytes 983048 | tf_op jit(solution)/shard_map/ppermute | solution.py:23
  107.1 2.3 collective-permute-start.9
  109.3 2.6 %collective-permute-start.8 = (bf16[1280,128]{1,0:T(8,128)(2,1)S(1)}, bf16[1280,128]{1,0:T(8,128)(2,1)}, u32[]{:S(2)}, u32[]{:S(2)}) collective-permute-start(bf16[1280,128]{1,0:T(8,128)(2,1)S(1)} %shard_map.72), channel_id=1, source_target_pairs={{0,128},{128,256},{256,384},{384,0},{1,129},{129,257},{257,385},{3... | collective-permute-start | bytes 983048 | tf_op jit(solution)/shard_map/ppermute | solution.py:23
  112.0 3.3 %shard_map.69 = (bf16[4,1024,128]{2,1,0:T(8,128)(2,1)S(1)}, bf16[4,1024,128]{2,1,0:T(8,128)(2,1)}) custom-call(s32[16]{0:T(128)S(1)} %pad_add_fusion.spot_ref.refs_0_, bf16[64,88,128]{2,1,0:T(8,128)(2,1)S(1)} %all-to-all-done.got_ref, bf16[1024,512]{1,0:T(8,128)(2,1)S(1)} %bitcast.74), custom_call_target="tpu_custom_call" | custom-call | tf_op jit(solution)/shard_map/pallas_call | solution.py:225
  115.3 3.6 %collective-permute-start = (bf16[4,1024,128]{2,1,0:T(8,128)(2,1)}, bf16[4,1024,128]{2,1,0:T(8,128)(2,1)}, u32[]{:S(2)}, u32[]{:S(2)}) collective-permute-start(bf16[4,1024,128]{2,1,0:T(8,128)(2,1)} %get-tuple-element.11), channel_id=1, source_target_pairs={{0,64},{64,0},{1,65},{65,1},{2,66},{66,2},{3,67},{67,3},{4,68},{68... | collective-permute-start | bytes 3145736 | tf_op jit(solution)/shard_map/ppermute | solution.py:27
  119.0 8.3 %collective-permute-done.8 = bf16[1280,128]{1,0:T(8,128)(2,1)} collective-permute-done((bf16[1280,128]{1,0:T(8,128)(2,1)S(1)}, bf16[1280,128]{1,0:T(8,128)(2,1)}, u32[]{:S(2)}, u32[]{:S(2)}) %collective-permute-start.8) | collective-permute-done | bytes 327712 | tf_op jit(solution)/shard_map/ppermute | solution.py:23
  128.6 2.4 %collective-permute-start.11 = (bf16[4,1280,128]{2,1,0:T(8,128)(2,1)S(1)}, bf16[4,1280,128]{2,1,0:T(8,128)(2,1)}, u32[]{:S(2)}, u32[]{:S(2)}) collective-permute-start(bf16[4,1280,128]{2,1,0:T(8,128)(2,1)S(1)} %pad_maximum_fusion.own_ref), channel_id=1, source_target_pairs={{0,64},{64,0},{1,65},{65,1},{2,66},{66,2},{3,67},{67,3},{4,68},{68... | collective-permute-start | bytes 3932168 | tf_op jit(solution)/shard_map/ppermute | solution.py:27
  137.5 2.2 collective-permute-start.7
  139.7 2.3 collective-permute-start.6
  142.0 2.7 %collective-permute-start.5 = (bf16[256,128]{1,0:T(8,128)(2,1)S(1)}, bf16[256,128]{1,0:T(8,128)(2,1)S(1)}, u32[]{:S(2)}, u32[]{:S(2)}) collective-permute-start(bf16[256,128]{1,0:T(8,128)(2,1)S(1)} %get-tuple-element.28), channel_id=1, source_target_pairs={{0,128},{128,256},{256,384},{384,0},{1,129},{129,257},{257,385},{3... | collective-permute-start | bytes 196616 | tf_op jit(solution)/shard_map/ppermute | solution.py:23
  146.2 5.3 %shard_map.73 = (bf16[1024,512]{1,0:T(8,128)(2,1)S(1)}, bf16[4,576,128]{2,1,0:T(8,128)(2,1)S(1)}, bf16[4,576,128]{2,1,0:T(8,128)(2,1)S(1)}) custom-call(s32[16]{0:T(128)S(1)} %pad_add_fusion.spot_ref.refs_0_, bf16[4,1280,128]{2,1,0:T(8,128)(2,1)S(1)} %pad_maximum_fusion.own_ref, bf16[4,1280,128]{2,1,0:T(8,128)(2,1)} %collective-permute-done.11.other_ref, ...), custom_call_target="tpu_custom_call" | custom-call | tf_op jit(solution)/shard_map/pallas_call | solution.py:225
  151.6 2.6 %collective-permute-start.12 = (bf16[4,576,128]{2,1,0:T(8,128)(2,1)S(1)}, bf16[4,576,128]{2,1,0:T(8,128)(2,1)S(1)}, u32[]{:S(2)}, u32[]{:S(2)}) collective-permute-start(bf16[4,576,128]{2,1,0:T(8,128)(2,1)S(1)} %get-tuple-element.16), channel_id=1, source_target_pairs={{0,64},{64,0},{1,65},{65,1},{2,66},{66,2},{3,67},{67,3},{4,68},{68... | collective-permute-start | bytes 1769480 | tf_op jit(solution)/shard_map/ppermute | solution.py:27
  154.3 4.3 %collective-permute-start.3 = (bf16[1024,128]{1,0:T(8,128)(2,1)S(1)}, bf16[1024,128]{1,0:T(8,128)(2,1)S(1)}, u32[]{:S(2)}, u32[]{:S(2)}) collective-permute-start(bf16[1024,128]{1,0:T(8,128)(2,1)S(1)} %get-tuple-element.23), channel_id=1, source_target_pairs={{0,384},{128,0},{256,128},{384,256},{1,385},{129,1},{257,129},{385... | collective-permute-start | bytes 786440 | tf_op jit(solution)/shard_map/ppermute | solution.py:23
  158.6 3.4 %collective-permute-start.2 = (bf16[1024,128]{1,0:T(8,128)(2,1)S(1)}, bf16[1024,128]{1,0:T(8,128)(2,1)S(1)}, u32[]{:S(2)}, u32[]{:S(2)}) collective-permute-start(bf16[1024,128]{1,0:T(8,128)(2,1)S(1)} %get-tuple-element.24), channel_id=1, source_target_pairs={{0,256},{128,384},{256,0},{384,128},{1,257},{129,385},{257,1},{385... | collective-permute-start | bytes 786440 | tf_op jit(solution)/shard_map/ppermute | solution.py:23
  162.0 2.8 %collective-permute-start.1 = (bf16[1024,128]{1,0:T(8,128)(2,1)S(1)}, bf16[1024,128]{1,0:T(8,128)(2,1)S(1)}, u32[]{:S(2)}, u32[]{:S(2)}) collective-permute-start(bf16[1024,128]{1,0:T(8,128)(2,1)S(1)} %get-tuple-element.22), channel_id=1, source_target_pairs={{0,128},{128,256},{256,384},{384,0},{1,129},{129,257},{257,385},{3... | collective-permute-start | bytes 786440 | tf_op jit(solution)/shard_map/ppermute | solution.py:23
  164.8 5.0 %collective-permute-done.3 = bf16[1024,128]{1,0:T(8,128)(2,1)S(1)} collective-permute-done((bf16[1024,128]{1,0:T(8,128)(2,1)S(1)}, bf16[1024,128]{1,0:T(8,128)(2,1)S(1)}, u32[]{:S(2)}, u32[]{:S(2)}) %collective-permute-start.3) | collective-permute-done | bytes 262176 | tf_op jit(solution)/shard_map/ppermute | solution.py:23
  169.7 6.1 %collective-permute-done.1 = bf16[1024,128]{1,0:T(8,128)(2,1)S(1)} collective-permute-done((bf16[1024,128]{1,0:T(8,128)(2,1)S(1)}, bf16[1024,128]{1,0:T(8,128)(2,1)S(1)}, u32[]{:S(2)}, u32[]{:S(2)}) %collective-permute-start.1) | collective-permute-done | bytes 262176 | tf_op jit(solution)/shard_map/ppermute | solution.py:23
  178.1 3.4 %collective-permute-start.14 = (bf16[576,128]{1,0:T(8,128)(2,1)S(1)}, bf16[576,128]{1,0:T(8,128)(2,1)S(1)}, u32[]{:S(2)}, u32[]{:S(2)}) collective-permute-start(bf16[576,128]{1,0:T(8,128)(2,1)S(1)} %get-tuple-element.27), channel_id=1, source_target_pairs={{0,256},{128,384},{256,0},{384,128},{1,257},{129,385},{257,1},{385... | collective-permute-start | bytes 442376 | tf_op jit(solution)/shard_map/ppermute | solution.py:23
  181.5 2.7 %collective-permute-start.13 = (bf16[576,128]{1,0:T(8,128)(2,1)S(1)}, bf16[576,128]{1,0:T(8,128)(2,1)S(1)}, u32[]{:S(2)}, u32[]{:S(2)}) collective-permute-start(bf16[576,128]{1,0:T(8,128)(2,1)S(1)} %get-tuple-element.25), channel_id=1, source_target_pairs={{0,128},{128,256},{256,384},{384,0},{1,129},{129,257},{257,385},{3... | collective-permute-start | bytes 442376 | tf_op jit(solution)/shard_map/ppermute | solution.py:23
  185.0 14.6 %all-to-all-start.2 = ((bf16[64,20,128]{2,1,0:T(8,128)(2,1)}), bf16[64,20,128]{2,1,0:T(8,128)(2,1)S(1)}, u32[]{:S(2)}, u32[]{:S(2)}) async-start(bf16[64,20,128]{2,1,0:T(8,128)(2,1)} %pad_maximum_fusion.2), calls=%async_computation.2 | async-start | bytes 786432 | tf_op jit(solution)/shard_map/all_to_all | solution.py:272
  199.7 3.7 %collective-permute-start.18 = (bf16[576,128]{1,0:T(8,128)(2,1)S(1)}, bf16[576,128]{1,0:T(8,128)(2,1)S(1)}, u32[]{:S(2)}, u32[]{:S(2)}) collective-permute-start(bf16[576,128]{1,0:T(8,128)(2,1)S(1)} %fusion.10), channel_id=1, source_target_pairs={{0,384},{128,0},{256,128},{384,256},{1,385},{129,1},{257,129},{385... | collective-permute-start | bytes 442376 | tf_op jit(solution)/shard_map/ppermute | solution.py:23
  203.5 2.8 %collective-permute-start.17 = (bf16[576,128]{1,0:T(8,128)(2,1)S(1)}, bf16[576,128]{1,0:T(8,128)(2,1)S(1)}, u32[]{:S(2)}, u32[]{:S(2)}) collective-permute-start(bf16[576,128]{1,0:T(8,128)(2,1)S(1)} %fusion.10), channel_id=1, source_target_pairs={{0,256},{128,384},{256,0},{384,128},{1,257},{129,385},{257,1},{385... | collective-permute-start | bytes 442376 | tf_op jit(solution)/shard_map/ppermute | solution.py:23
  206.3 2.8 %collective-permute-start.16 = (bf16[576,128]{1,0:T(8,128)(2,1)S(1)}, bf16[576,128]{1,0:T(8,128)(2,1)S(1)}, u32[]{:S(2)}, u32[]{:S(2)}) collective-permute-start(bf16[576,128]{1,0:T(8,128)(2,1)S(1)} %fusion.10), channel_id=1, source_target_pairs={{0,128},{128,256},{256,384},{384,0},{1,129},{129,257},{257,385},{3... | collective-permute-start | bytes 442376 | tf_op jit(solution)/shard_map/ppermute | solution.py:23
  209.1 2.1 collective-permute-done.17
  211.2 4.5 %collective-permute-done.16 = bf16[576,128]{1,0:T(8,128)(2,1)S(1)} collective-permute-done((bf16[576,128]{1,0:T(8,128)(2,1)S(1)}, bf16[576,128]{1,0:T(8,128)(2,1)S(1)}, u32[]{:S(2)}, u32[]{:S(2)}) %collective-permute-start.16) | collective-permute-done | bytes 147488 | tf_op jit(solution)/shard_map/ppermute | solution.py:23
  215.7 3.6 %collective-permute-start.19 = (bf16[4,576,128]{2,1,0:T(8,128)(2,1)S(1)}, bf16[4,576,128]{2,1,0:T(8,128)(2,1)S(1)}, u32[]{:S(2)}, u32[]{:S(2)}) collective-permute-start(bf16[4,576,128]{2,1,0:T(8,128)(2,1)S(1)} %pad_maximum_fusion.1.refs_1_), channel_id=1, source_target_pairs={{0,64},{64,0},{1,65},{65,1},{2,66},{66,2},{3,67},{67,3},{4,68},{68... | collective-permute-start | bytes 1769480 | tf_op jit(solution)/shard_map/ppermute | solution.py:27
  220.1 2.8 %all-to-all-done.2 = bf16[64,20,128]{2,1,0:T(8,128)(2,1)S(1)} async-done(((bf16[64,20,128]{2,1,0:T(8,128)(2,1)}), bf16[64,20,128]{2,1,0:T(8,128)(2,1)S(1)}, u32[]{:S(2)}, u32[]{:S(2)}) %all-to-all-start.2) | async-done | bytes 327712 | tf_op jit(solution)/shard_map/all_to_all | solution.py:272
  224.8 8.9 %shard_map.74 = f32[1,1024,512]{2,1,0:T(8,128)} custom-call(s32[16]{0:T(128)S(1)} %pad_add_fusion.spot_ref.refs_0_, bf16[4,576,128]{2,1,0:T(8,128)(2,1)S(1)} %pad_maximum_fusion.1.refs_1_, bf16[4,576,128]{2,1,0:T(8,128)(2,1)S(1)} %collective-permute-done.19.refs_2_, bf16[1024,512]{1,0:T(8,128)(2,1)S(1)} %copy-done.4), custom_call_target="tpu_custom_call" | custom-call | tf_op jit(solution)/shard_map/pallas_call | solution.py:225
  (66 shorter events, 19.2 us)
Async XLA Ops:
  0.6 1.9 copy-start.7
  0.6 1.9 copy-start.8
  0.6 2.2 copy-start.2
  5.5 84.5 %all-to-all-start = ((bf16[64,88,128]{2,1,0:T(8,128)(2,1)}), bf16[64,88,128]{2,1,0:T(8,128)(2,1)S(1)}, u32[]{:S(2)}, u32[]{:S(2)}) async-start(bf16[64,88,128]{2,1,0:T(8,128)(2,1)} %shard_map.68), calls=%async_computation | async-start | bytes 2883584 | tf_op jit(solution)/shard_map/all_to_all | solution.py:272
  26.1 86.0 %copy-start = (bf16[1,1024,512]{2,1,0:T(8,128)(2,1)S(1)}, bf16[1,1024,512]{2,1,0:T(8,128)(2,1)}, u32[]{:S(2)}) copy-start(bf16[1,1024,512]{2,1,0:T(8,128)(2,1)} %param.9) | copy-start | bytes 3145732
  90.0 41.0 %all-to-all-start.1 = ((bf16[64,16,128]{2,1,0:T(8,128)(2,1)}), bf16[64,16,128]{2,1,0:T(8,128)(2,1)S(1)}, u32[]{:S(2)}, u32[]{:S(2)}) async-start(bf16[64,16,128]{2,1,0:T(8,128)(2,1)} %shard_map.70), calls=%async_computation.1 | async-start | bytes 524288 | tf_op jit(solution)/shard_map/all_to_all | solution.py:272
  102.4 16.5 %collective-permute-start.10 = (bf16[1280,128]{1,0:T(8,128)(2,1)S(1)}, bf16[1280,128]{1,0:T(8,128)(2,1)}, u32[]{:S(2)}, u32[]{:S(2)}) collective-permute-start(bf16[1280,128]{1,0:T(8,128)(2,1)S(1)} %shard_map.72), channel_id=1, source_target_pairs={{0,384},{128,0},{256,128},{384,256},{1,385},{129,1},{257,129},{385... | collective-permute-start | bytes 983048 | tf_op jit(solution)/shard_map/ppermute | solution.py:23
  107.1 11.9 %collective-permute-start.9 = (bf16[1280,128]{1,0:T(8,128)(2,1)S(1)}, bf16[1280,128]{1,0:T(8,128)(2,1)}, u32[]{:S(2)}, u32[]{:S(2)}) collective-permute-start(bf16[1280,128]{1,0:T(8,128)(2,1)S(1)} %shard_map.72), channel_id=1, source_target_pairs={{0,256},{128,384},{256,0},{384,128},{1,257},{129,385},{257,1},{385... | collective-permute-start | bytes 983048 | tf_op jit(solution)/shard_map/ppermute | solution.py:23
  109.3 17.9 %collective-permute-start.8 = (bf16[1280,128]{1,0:T(8,128)(2,1)S(1)}, bf16[1280,128]{1,0:T(8,128)(2,1)}, u32[]{:S(2)}, u32[]{:S(2)}) collective-permute-start(bf16[1280,128]{1,0:T(8,128)(2,1)S(1)} %shard_map.72), channel_id=1, source_target_pairs={{0,128},{128,256},{256,384},{384,0},{1,129},{129,257},{257,385},{3... | collective-permute-start | bytes 983048 | tf_op jit(solution)/shard_map/ppermute | solution.py:23
  115.3 13.2 %copy-start.5 = (bf16[4,1024,128]{2,1,0:T(8,128)(2,1)}, bf16[4,1024,128]{2,1,0:T(8,128)(2,1)S(1)}, u32[]{:S(2)}) copy-start(bf16[4,1024,128]{2,1,0:T(8,128)(2,1)S(1)} %get-tuple-element.10) | copy-start | bytes 3145732
  115.3 29.4 %collective-permute-start = (bf16[4,1024,128]{2,1,0:T(8,128)(2,1)}, bf16[4,1024,128]{2,1,0:T(8,128)(2,1)}, u32[]{:S(2)}, u32[]{:S(2)}) collective-permute-start(bf16[4,1024,128]{2,1,0:T(8,128)(2,1)} %get-tuple-element.11), channel_id=1, source_target_pairs={{0,64},{64,0},{1,65},{65,1},{2,66},{66,2},{3,67},{67,3},{4,68},{68... | collective-permute-start | bytes 3145736 | tf_op jit(solution)/shard_map/ppermute | solution.py:27
  128.6 17.7 %collective-permute-start.11 = (bf16[4,1280,128]{2,1,0:T(8,128)(2,1)S(1)}, bf16[4,1280,128]{2,1,0:T(8,128)(2,1)}, u32[]{:S(2)}, u32[]{:S(2)}) collective-permute-start(bf16[4,1280,128]{2,1,0:T(8,128)(2,1)S(1)} %pad_maximum_fusion.own_ref), channel_id=1, source_target_pairs={{0,64},{64,0},{1,65},{65,1},{2,66},{66,2},{3,67},{67,3},{4,68},{68... | collective-permute-start | bytes 3932168 | tf_op jit(solution)/shard_map/ppermute | solution.py:27
  131.0 1.2 copy-start.1
  132.2 12.5 %copy-start.6 = (bf16[4,1024,128]{2,1,0:T(8,128)(2,1)S(1)}, bf16[4,1024,128]{2,1,0:T(8,128)(2,1)}, u32[]{:S(2)}) copy-start(bf16[4,1024,128]{2,1,0:T(8,128)(2,1)} %copy-done.5) | copy-start | bytes 3145732
  133.9 3.4 %collective-permute-start.4 = (bf16[4,256,128]{2,1,0:T(8,128)(2,1)S(1)}, bf16[4,256,128]{2,1,0:T(8,128)(2,1)S(1)}, u32[]{:S(2)}, u32[]{:S(2)}) collective-permute-start(bf16[4,256,128]{2,1,0:T(8,128)(2,1)S(1)} %get-tuple-element.13), channel_id=1, source_target_pairs={{0,64},{64,0},{1,65},{65,1},{2,66},{66,2},{3,67},{67,3},{4,68},{68... | collective-permute-start | bytes 786440 | tf_op jit(solution)/shard_map/ppermute | solution.py:27
  137.5 21.1 %collective-permute-start.7 = (bf16[256,128]{1,0:T(8,128)(2,1)S(1)}, bf16[256,128]{1,0:T(8,128)(2,1)S(1)}, u32[]{:S(2)}, u32[]{:S(2)}) collective-permute-start(bf16[256,128]{1,0:T(8,128)(2,1)S(1)} %get-tuple-element.29), channel_id=1, source_target_pairs={{0,384},{128,0},{256,128},{384,256},{1,385},{129,1},{257,129},{385... | collective-permute-start | bytes 196616 | tf_op jit(solution)/shard_map/ppermute | solution.py:23
  139.7 22.2 %collective-permute-start.6 = (bf16[256,128]{1,0:T(8,128)(2,1)S(1)}, bf16[256,128]{1,0:T(8,128)(2,1)S(1)}, u32[]{:S(2)}, u32[]{:S(2)}) collective-permute-start(bf16[256,128]{1,0:T(8,128)(2,1)S(1)} %get-tuple-element.30), channel_id=1, source_target_pairs={{0,256},{128,384},{256,0},{384,128},{1,257},{129,385},{257,1},{385... | collective-permute-start | bytes 196616 | tf_op jit(solution)/shard_map/ppermute | solution.py:23
  142.0 22.8 %collective-permute-start.5 = (bf16[256,128]{1,0:T(8,128)(2,1)S(1)}, bf16[256,128]{1,0:T(8,128)(2,1)S(1)}, u32[]{:S(2)}, u32[]{:S(2)}) collective-permute-start(bf16[256,128]{1,0:T(8,128)(2,1)S(1)} %get-tuple-element.28), channel_id=1, source_target_pairs={{0,128},{128,256},{256,384},{384,0},{1,129},{129,257},{257,385},{3... | collective-permute-start | bytes 196616 | tf_op jit(solution)/shard_map/ppermute | solution.py:23
  151.5 24.4 %copy-start.3 = (bf16[1024,512]{1,0:T(8,128)(2,1)}, bf16[1024,512]{1,0:T(8,128)(2,1)S(1)}, u32[]{:S(2)}) copy-start(bf16[1024,512]{1,0:T(8,128)(2,1)S(1)} %get-tuple-element.17.refs_3_) | copy-start | bytes 3145732
  151.6 24.4 %collective-permute-start.12 = (bf16[4,576,128]{2,1,0:T(8,128)(2,1)S(1)}, bf16[4,576,128]{2,1,0:T(8,128)(2,1)S(1)}, u32[]{:S(2)}, u32[]{:S(2)}) collective-permute-start(bf16[4,576,128]{2,1,0:T(8,128)(2,1)S(1)} %get-tuple-element.16), channel_id=1, source_target_pairs={{0,64},{64,0},{1,65},{65,1},{2,66},{66,2},{3,67},{67,3},{4,68},{68... | collective-permute-start | bytes 1769480 | tf_op jit(solution)/shard_map/ppermute | solution.py:27
  154.3 15.5 %collective-permute-start.3 = (bf16[1024,128]{1,0:T(8,128)(2,1)S(1)}, bf16[1024,128]{1,0:T(8,128)(2,1)S(1)}, u32[]{:S(2)}, u32[]{:S(2)}) collective-permute-start(bf16[1024,128]{1,0:T(8,128)(2,1)S(1)} %get-tuple-element.23), channel_id=1, source_target_pairs={{0,384},{128,0},{256,128},{384,256},{1,385},{129,1},{257,129},{385... | collective-permute-start | bytes 786440 | tf_op jit(solution)/shard_map/ppermute | solution.py:23
  158.6 11.2 %collective-permute-start.2 = (bf16[1024,128]{1,0:T(8,128)(2,1)S(1)}, bf16[1024,128]{1,0:T(8,128)(2,1)S(1)}, u32[]{:S(2)}, u32[]{:S(2)}) collective-permute-start(bf16[1024,128]{1,0:T(8,128)(2,1)S(1)} %get-tuple-element.24), channel_id=1, source_target_pairs={{0,256},{128,384},{256,0},{384,128},{1,257},{129,385},{257,1},{385... | collective-permute-start | bytes 786440 | tf_op jit(solution)/shard_map/ppermute | solution.py:23
  162.0 13.9 %collective-permute-start.1 = (bf16[1024,128]{1,0:T(8,128)(2,1)S(1)}, bf16[1024,128]{1,0:T(8,128)(2,1)S(1)}, u32[]{:S(2)}, u32[]{:S(2)}) collective-permute-start(bf16[1024,128]{1,0:T(8,128)(2,1)S(1)} %get-tuple-element.22), channel_id=1, source_target_pairs={{0,128},{128,256},{256,384},{384,0},{1,129},{129,257},{257,385},{3... | collective-permute-start | bytes 786440 | tf_op jit(solution)/shard_map/ppermute | solution.py:23
  176.2 23.4 %collective-permute-start.15 = (bf16[576,128]{1,0:T(8,128)(2,1)S(1)}, bf16[576,128]{1,0:T(8,128)(2,1)S(1)}, u32[]{:S(2)}, u32[]{:S(2)}) collective-permute-start(bf16[576,128]{1,0:T(8,128)(2,1)S(1)} %get-tuple-element.26), channel_id=1, source_target_pairs={{0,384},{128,0},{256,128},{384,256},{1,385},{129,1},{257,129},{385... | collective-permute-start | bytes 442376 | tf_op jit(solution)/shard_map/ppermute | solution.py:23
  178.1 21.5 %collective-permute-start.14 = (bf16[576,128]{1,0:T(8,128)(2,1)S(1)}, bf16[576,128]{1,0:T(8,128)(2,1)S(1)}, u32[]{:S(2)}, u32[]{:S(2)}) collective-permute-start(bf16[576,128]{1,0:T(8,128)(2,1)S(1)} %get-tuple-element.27), channel_id=1, source_target_pairs={{0,256},{128,384},{256,0},{384,128},{1,257},{129,385},{257,1},{385... | collective-permute-start | bytes 442376 | tf_op jit(solution)/shard_map/ppermute | solution.py:23
  181.5 18.1 %collective-permute-start.13 = (bf16[576,128]{1,0:T(8,128)(2,1)S(1)}, bf16[576,128]{1,0:T(8,128)(2,1)S(1)}, u32[]{:S(2)}, u32[]{:S(2)}) collective-permute-start(bf16[576,128]{1,0:T(8,128)(2,1)S(1)} %get-tuple-element.25), channel_id=1, source_target_pairs={{0,128},{128,256},{256,384},{384,0},{1,129},{129,257},{257,385},{3... | collective-permute-start | bytes 442376 | tf_op jit(solution)/shard_map/ppermute | solution.py:23
  185.0 37.9 %all-to-all-start.2 = ((bf16[64,20,128]{2,1,0:T(8,128)(2,1)}), bf16[64,20,128]{2,1,0:T(8,128)(2,1)S(1)}, u32[]{:S(2)}, u32[]{:S(2)}) async-start(bf16[64,20,128]{2,1,0:T(8,128)(2,1)} %pad_maximum_fusion.2), calls=%async_computation.2 | async-start | bytes 786432 | tf_op jit(solution)/shard_map/all_to_all | solution.py:272
  199.7 9.4 %collective-permute-start.18 = (bf16[576,128]{1,0:T(8,128)(2,1)S(1)}, bf16[576,128]{1,0:T(8,128)(2,1)S(1)}, u32[]{:S(2)}, u32[]{:S(2)}) collective-permute-start(bf16[576,128]{1,0:T(8,128)(2,1)S(1)} %fusion.10), channel_id=1, source_target_pairs={{0,384},{128,0},{256,128},{384,256},{1,385},{129,1},{257,129},{385... | collective-permute-start | bytes 442376 | tf_op jit(solution)/shard_map/ppermute | solution.py:23
  203.5 7.7 %collective-permute-start.17 = (bf16[576,128]{1,0:T(8,128)(2,1)S(1)}, bf16[576,128]{1,0:T(8,128)(2,1)S(1)}, u32[]{:S(2)}, u32[]{:S(2)}) collective-permute-start(bf16[576,128]{1,0:T(8,128)(2,1)S(1)} %fusion.10), channel_id=1, source_target_pairs={{0,256},{128,384},{256,0},{384,128},{1,257},{129,385},{257,1},{385... | collective-permute-start | bytes 442376 | tf_op jit(solution)/shard_map/ppermute | solution.py:23
  206.3 9.3 %collective-permute-start.16 = (bf16[576,128]{1,0:T(8,128)(2,1)S(1)}, bf16[576,128]{1,0:T(8,128)(2,1)S(1)}, u32[]{:S(2)}, u32[]{:S(2)}) collective-permute-start(bf16[576,128]{1,0:T(8,128)(2,1)S(1)} %fusion.10), channel_id=1, source_target_pairs={{0,128},{128,256},{256,384},{384,0},{1,129},{129,257},{257,385},{3... | collective-permute-start | bytes 442376 | tf_op jit(solution)/shard_map/ppermute | solution.py:23
  215.7 9.1 %collective-permute-start.19 = (bf16[4,576,128]{2,1,0:T(8,128)(2,1)S(1)}, bf16[4,576,128]{2,1,0:T(8,128)(2,1)S(1)}, u32[]{:S(2)}, u32[]{:S(2)}) collective-permute-start(bf16[4,576,128]{2,1,0:T(8,128)(2,1)S(1)} %pad_maximum_fusion.1.refs_1_), channel_id=1, source_target_pairs={{0,64},{64,0},{1,65},{65,1},{2,66},{66,2},{3,67},{67,3},{4,68},{68... | collective-permute-start | bytes 1769480 | tf_op jit(solution)/shard_map/ppermute | solution.py:27
  223.0 1.9 copy-start.4

commit v3 on v1

--- a/solution.py
+++ b/solution.py
@@ -6,7 +6,7 @@
 from jax.sharding import Mesh, PartitionSpec as P
 
 EXPERT = ("x", "z")
-VMEM_LIMIT = 50 * 1024 * 1024
+MIB = 1024 * 1024
 BF16 = jnp.bfloat16
 F32 = jnp.float32
 
@@ -31,25 +31,111 @@
     return lax.dot_general(left, right, (((1,), (1,)), ((), ())), preferred_element_type=F32)
 
 
-def grad_kernel(spot_ref, own_ref, other_ref, rows_ref, gradb_ref, pack_own_ref, pack_other_ref, wide_ref):
-    blocks = gradb_ref.shape[0] // 128
+def one_hot(rows, index):
+    return jnp.where(rows == index, 1.0, 0.0).astype(BF16)
+
+
+def row_numbers(count):
+    return lax.broadcasted_iota(jnp.int32, (count, 1), 0)
+
+
+def send_kernel(main_ref, left_ref, scaled_ref, grad_ref, out_ref):
+    experts, height, _ = out_ref.shape
+    tokens, width_part = grad_ref.shape
+    blocks = width_part // 128
+    main = 16 * (blocks + 1)
+    tail = height - main
+    scaled = scaled_ref[...]
+    grad = grad_ref[...]
+    chosen = one_hot(row_numbers(experts * 16), main_ref[...])
+    part = jnp.dot(chosen, scaled, preferred_element_type=F32).astype(BF16)
+    out_ref[:, 0:16, :] = part.reshape(experts, 16, 128)
+    chosen_token = chosen[:, :tokens] + chosen[:, tokens:]
+    rows = jnp.dot(chosen_token, grad, preferred_element_type=F32).astype(BF16)
+    for b in range(blocks):
+        out_ref[:, 16 * (b + 1) : 16 * (b + 2), :] = rows[:, b * 128 : (b + 1) * 128].reshape(experts, 16, 128)
+    expert = lax.broadcasted_iota(jnp.int32, (experts, tail, 1), 0)
+    place = lax.broadcasted_iota(jnp.int32, (experts, tail, 1), 1)
+    number = (expert * tail + (place & 3)).reshape(experts * tail, 1)
+    kind = (place >> 2).reshape(experts * tail, 1)
+    chosen = one_hot(number, left_ref[...])
+    part = jnp.dot(chosen, scaled, preferred_element_type=F32)
+    total = jnp.where(kind == 0, part, 0.0)
+    chosen_token = chosen[:, :tokens] + chosen[:, tokens:]
+    rows = jnp.dot(chosen_token, grad, preferred_element_type=F32)
+    for b in range(blocks):
+        total = jnp.where(kind == b + 1, rows[:, b * 128 : (b + 1) * 128], total)
+    out_ref[:, main:, :] = total.reshape(experts, tail, 128).astype(BF16)
+
+
+def tail_rows(tail, kind, experts, height):
+    number = row_numbers(experts * 4)
+    source = lax.broadcasted_iota(jnp.int32, (1, experts * height), 1)
+    take = one_hot((number >> 2) * height + kind * 4 + (number & 3), source)
+    return jnp.dot(take, tail, preferred_element_type=F32).astype(BF16)
+
+
+def unpack_kernel(got_ref, out_ref):
+    experts, height, _ = got_ref.shape
+    main = (height // 16 - 1) * 16
+    tail = got_ref[:, main:, :].astype(F32).reshape(experts * (height - main), 128).astype(BF16)
+    left = tail_rows(tail, 0, experts, height - main)
+    for k in range(out_ref.shape[0]):
+        out_ref[k, : experts * 16] = got_ref[:, 0:16, :].reshape(experts * 16, 128)
+        out_ref[k, experts * 16 :] = left
+
+
+def put_piece(spot, y_size, own_ref, other_ref, piece):
+    @pl.when(spot < y_size)
+    def _():
+        own_ref[spot] = piece
+
+    @pl.when(spot >= y_size)
+    def _():
+        other_ref[spot - y_size] = piece
+
+
+def back_kernel(spot_ref, got_ref, weight_ref, own_ref, other_ref, rows_ref):
+    blocks = weight_ref.shape[0] // 128
     y_size = blocks // 2
+    experts, height, _ = got_ref.shape
+    columns = rows_ref.shape[1] // 128
+    main = 16 * (columns + 1)
+    tail = got_ref[:, main:, :].astype(F32).reshape(experts * (height - main), 128).astype(BF16)
+    for b in range(columns):
+        lanes = slice(b * 128, (b + 1) * 128)
+        rows_ref[: experts * 16, lanes] = got_ref[:, 16 * (b + 1) : 16 * (b + 2), :].reshape(experts * 16, 128)
+        rows_ref[experts * 16 :, lanes] = tail_rows(tail, b + 1, experts, height - main)
+    term = nt_dot(rows_ref[...], weight_ref[...]).astype(BF16)
     for d in range(blocks):
-        spot = spot_ref[d]
-
-        @pl.when(spot < y_size)
-        def _():
-            wide_ref[:, d * 128 : (d + 1) * 128] = own_ref[spot]
-
-        @pl.when(spot >= y_size)
-        def _():
-            wide_ref[:, d * 128 : (d + 1) * 128] = other_ref[spot - y_size]
-
-    gradient = lax.dot_general(
+        put_piece(spot_ref[d], y_size, own_ref, other_ref, term[:, d * 128 : (d + 1) * 128])
+
+
+def add_kernel(own_ref, other_ref, after_ref, out_ref):
+    out_ref[...] = (own_ref[...].astype(F32) + other_ref[...].astype(F32)).astype(BF16)
+
+
+def gather_half(part_ref, rows_ref, wide_ref):
+    for k in range(part_ref.shape[0]):
+        wide_ref[:, k * 128 : (k + 1) * 128] = part_ref[k]
+    return lax.dot_general(
         wide_ref[...], rows_ref[...], (((0,), (0,)), ((), ())), preferred_element_type=F32
-    )
-    gradb = gradient.astype(BF16)
-    gradb_ref[...] = gradb
+    ).astype(BF16)
+
+
+def grad_half_kernel(part_ref, rows_ref, half_ref, wide_ref):
+    half_ref[...] = gather_half(part_ref, rows_ref, wide_ref).reshape(half_ref.shape)
+
+
+def grad_kernel(spot_ref, own_half_ref, part_ref, rows_ref, gradb_ref, pack_own_ref, pack_other_ref, wide_ref):
+    blocks = gradb_ref.shape[0]
+    y_size = blocks // 2
+    core = spot_ref[3 * blocks]
+    other_half = gather_half(part_ref, rows_ref, wide_ref)
+    for k in range(y_size):
+        gradb_ref[2 * k + core] = own_half_ref[k]
+        gradb_ref[2 * k + 1 - core] = other_half[k * 128 : (k + 1) * 128]
+    gradb = gradb_ref[...].reshape(blocks * 128, gradb_ref.shape[2])
     gram = nt_dot(gradb, gradb).astype(BF16)
     half = blocks // 2
     for d in range(blocks):
@@ -77,29 +163,12 @@
             put(pack_other_ref, spot - y_size)
 
 
-def back_kernel(spot_ref, rows_ref, weight_ref, own_ref, other_ref):
-    blocks = weight_ref.shape[0] // 128
-    y_size = blocks // 2
-    term = nt_dot(rows_ref[...], weight_ref[...]).astype(BF16)
-    for d in range(blocks):
-        spot = spot_ref[blocks + d]
-        piece = term[:, d * 128 : (d + 1) * 128]
-
-        @pl.when(spot < y_size)
-        def _():
-            own_ref[spot] = piece
-
-        @pl.when(spot >= y_size)
-        def _():
-            other_ref[spot - y_size] = piece
-
-
 def ortho_kernel(width, spot_ref, own_ref, other_ref, gradb_ref, out_ref, gram_ref):
-    blocks = gradb_ref.shape[0] // 128
+    blocks = gradb_ref.shape[0]
     y_size = blocks // 2
     half = blocks // 2
     for d in range(blocks):
-        spot = spot_ref[d]
+        spot = spot_ref[2 * blocks + d]
 
         def place(ref, at):
             for k in range(half):
@@ -130,7 +199,8 @@
     wide = gram.astype(F32)
     norm_sq = jnp.sqrt(jnp.sum(wide * wide, keepdims=True)) + 1e-06
     inverse = 1.0 / norm_sq
-    first = (gradb_ref[...].astype(F32) * lax.rsqrt(norm_sq)).astype(BF16)
+    gradb = gradb_ref[...].reshape(blocks * 128, gradb_ref.shape[2])
+    first = (gradb.astype(F32) * lax.rsqrt(norm_sq)).astype(BF16)
 
     def apply(value):
         return jnp.dot(gram, value, preferred_element_type=F32) * inverse
@@ -143,14 +213,15 @@
     out_ref[0] = total * width**0.5
 
 
-def call(kernel, outs, ins, scratch=()):
+def call(kernel, outs, ins, scratch=(), scalars=1, loose=0, vmem=24):
     return pl.pallas_call(
         kernel,
         out_shape=outs,
-        in_specs=[smem_spec()] + [full_spec()] * (len(ins) - 1),
+        in_specs=[smem_spec()] * scalars + [full_spec()] * (len(ins) - scalars - loose)
+        + [pl.BlockSpec(memory_space=pl.ANY)] * loose,
         out_specs=jax.tree.map(lambda _: full_spec(), outs),
         scratch_shapes=list(scratch),
-        compiler_params=pltpu.CompilerParams(vmem_limit_bytes=VMEM_LIMIT),
+        compiler_params=pltpu.CompilerParams(vmem_limit_bytes=vmem * MIB),
     )(*ins)
 
 
@@ -170,9 +241,10 @@
     c = lax.axis_index("c")
     block = jnp.arange(dp, dtype=jnp.int32)
     other_core = (block % 2) ^ c
+    stands_at = other_core * y_size + block // 2
+    goes_to = other_core * y_size + (block // 2 - y) % y_size
     came_from = other_core * y_size + (y - block // 2) % y_size
-    goes_to = other_core * y_size + (block // 2 - y) % y_size
-    spots = jnp.concatenate([came_from, goes_to]).astype(jnp.int32)
+    spots = jnp.concatenate([stands_at, goes_to, came_from, jnp.full((1,), c)]).astype(jnp.int32)
 
     flat_ids = expert_ids.T.reshape(1, pair_count)
     named = (jnp.arange(experts, dtype=jnp.int32)[:, None] == flat_ids).astype(BF16)
@@ -180,40 +252,70 @@
     earlier = (order[:, None] < order[None, :]).astype(BF16)
     before = jnp.dot(named, earlier, preferred_element_type=F32)
     rank_in = jnp.sum(before * named.astype(F32), axis=0, keepdims=True).astype(jnp.int32)
+    late = rank_in >= 16
+    main_index = jnp.where(late, -1, flat_ids * 16 + rank_in)
+    column_blocks = width_part // 128
+    tail = -(-4 * (column_blocks + 1) // 8) * 8
+    left_index = jnp.where(late, flat_ids * tail + rank_in - 16, -1)
+
+    scaled_part = (gate_prob[:, :, None] * hidden.astype(F32)).astype(BF16)
+    scaled_part = scaled_part.transpose(1, 0, 2).reshape(pair_count, unit_part)
+
+    def exchange(value, axes):
+        return lax.all_to_all(value, axes, split_axis=0, concat_axis=0, tiled=True)
+
+    sent = call(
+        send_kernel,
+        jax.ShapeDtypeStruct((experts, 16 * (column_blocks + 1) + tail, 128), BF16),
+        (main_index, left_index, scaled_part, grad_out),
+        scalars=0,
+    )
+    got = exchange(sent, EXPERT)
+
+    dp_parts = jax.ShapeDtypeStruct((y_size, total_slots, unit_part), BF16)
+    gathered = exchange(call(unpack_kernel, dp_parts, (got,), scalars=0, vmem=8), "y")
+    gathered_other = swap_core(gathered)
+    term_own, term_other, rows = call(
+        back_kernel,
+        (dp_parts, dp_parts, jax.ShapeDtypeStruct((total_slots, width_part), BF16)),
+        (spots, got, weights[0]),
+        vmem=20,
+    )
+    both = call(add_kernel, dp_parts, (term_own, swap_core(term_other), gathered), scalars=0, loose=1, vmem=8)
+    summed = jnp.sum(exchange(both, "y").astype(F32), axis=0).astype(BF16)
+    main_count = experts * 16
+    returned = exchange(
+        jnp.concatenate(
+            [
+                summed[:main_count].reshape(experts, 16, unit_part),
+                summed[main_count:].reshape(experts, capacity - 16, unit_part),
+            ],
+            axis=1,
+        ),
+        EXPERT,
+    ).reshape(total_slots, unit_part)
     slot_index = flat_ids * capacity + rank_in
     chosen = (jnp.arange(total_slots, dtype=jnp.int32)[:, None] == slot_index).astype(BF16)
-    chosen_token = chosen[:, :tokens] + chosen[:, tokens:]
-
-    scaled_part = (gate_prob[:, :, None] * hidden.astype(F32)).astype(BF16)
-    scaled_part = scaled_part.transpose(1, 0, 2).reshape(pair_count, unit_part)
-    send_scaled = jnp.dot(chosen, scaled_part, preferred_element_type=F32).astype(BF16)
-    got_scaled = lax.all_to_all(
-        send_scaled.reshape(experts, capacity, unit_part), EXPERT, split_axis=0, concat_axis=0, tiled=True
-    ).reshape(total_slots, unit_part)
-
-    send_grad = jnp.dot(chosen_token, grad_out, preferred_element_type=F32).astype(BF16)
-    send_grad = (
-        send_grad.reshape(experts, capacity, 2, width_part // 2)
-        .transpose(0, 2, 1, 3)
-        .reshape(experts, 2 * capacity, width_part // 2)
-    )
-    got_grad = lax.all_to_all(send_grad, EXPERT, split_axis=0, concat_axis=0, tiled=True)
-    got_grad = (
-        got_grad.reshape(experts, 2, capacity, width_part // 2)
-        .transpose(0, 2, 1, 3)
-        .reshape(total_slots, width_part)
-    )
-
-    gathered = jnp.stack([got_scaled] + [shift_y(got_scaled, k, y_size) for k in range(1, y_size)])
-    gathered_other = swap_core(gathered)
-
-    pack_rows = units // 2 + 64
-    packs = jax.ShapeDtypeStruct((y_size, pack_rows, 128), BF16)
+    picked = lax.dot_general(chosen, returned, (((0,), (0,)), ((), ())), preferred_element_type=F32)
+    picked = picked.reshape(top_count, tokens, unit_part).transpose(1, 0, 2)
+    hidden_grad = (gate_prob[:, :, None] * picked).astype(BF16)
+
+    wide = pltpu.VMEM((total_slots, units // 2), BF16)
+    own_half = call(
+        grad_half_kernel,
+        jax.ShapeDtypeStruct((y_size, 128, width_part), BF16),
+        (gathered, rows),
+        (wide,),
+        scalars=0,
+        vmem=10,
+    )
+    packs = jax.ShapeDtypeStruct((y_size, units // 2 + 64, 128), BF16)
     grad_bf16, pack_own, pack_other = call(
         grad_kernel,
-        (jax.ShapeDtypeStruct((units, width_part), BF16), packs, packs),
-        (spots, gathered, gathered_other, got_grad),
-        (pltpu.VMEM((total_slots, units), BF16),),
+        (jax.ShapeDtypeStruct((dp, 128, width_part), BF16), packs, packs),
+        (spots, own_half, gathered_other, rows),
+        (wide,),
+        vmem=20,
     )
 
     def reduce_dp(own, other):
@@ -233,16 +335,6 @@
         (spots, pack_all, pack_all_other, grad_bf16),
         (pltpu.VMEM((units, units), BF16),),
     )
-
-    terms = jax.ShapeDtypeStruct((y_size, total_slots, unit_part), BF16)
-    term_own, term_other = call(back_kernel, (terms, terms), (spots, got_grad, weights[0]))
-    summed = reduce_dp(term_own, term_other)
-    returned = lax.all_to_all(
-        summed.reshape(experts, capacity, unit_part), EXPERT, split_axis=0, concat_axis=0, tiled=True
-    ).reshape(total_slots, unit_part)
-    picked = lax.dot_general(chosen, returned, (((0,), (0,)), ((), ())), preferred_element_type=F32)
-    picked = picked.reshape(top_count, tokens, unit_part).transpose(1, 0, 2)
-    hidden_grad = (gate_prob[:, :, None] * picked).astype(BF16)
     return (hidden_grad, update)
 
 

time: 216 us -> 213 us (0.986)
  blocking collectives: 0 us -> 94.4 us
  waiting for transfers between devices: 85.9 us -> 19.1 us
  starting transfers between devices: 93.1 us -> 57.9 us
  Pallas kernels: 17.9 us -> 22.9 us
    all_to_all x0 -> x1, blocking collectives: none -> 94.4 us  [exchange(): return lax.all_to_all(value, axes, split_axis=0, concat_axis=0, tiled=True)]
    all_to_all x3, waiting for transfers between devices: 55.7 us -> 12.5 us  [exchange(): return lax.all_to_all(value, axes, split_axis=0, concat_axis=0, tiled=True)]
    ppermute x12 -> x6, starting transfers between devices: 41.2 us -> 17.4 us  [shift_y(): lax.ppermute(value, 'y', [(i, (i + step) % size) for i in range(size)])]
    ppermute x12 -> x6, waiting for transfers between devices: 29.4 us -> 6.61 us  [shift_y(): lax.ppermute(value, 'y', [(i, (i + step) % size) for i in range(size)])]
    all_to_all x3, starting transfers between devices: 33.2 us -> 21.3 us  [exchange(): return lax.all_to_all(value, axes, split_axis=0, concat_axis=0, tiled=True)]
    unnamed x11 -> x26, local copies, waits for them, and re-layouts: 3.12 us -> 8.44 us
    pallas_call x3 -> x7, Pallas kernels: 17.9 us -> 22.9 us  [call(): pl.pallas_call(kernel, out_shape=outs, in_specs=[smem_spec()] * scalars +...]
    reshape x7 -> x1, local copies, waits for them, and re-layouts: 4.22 us -> 0.07 us  [per_device(): returned = exchange(jnp.concatenate([summed[:main_count].reshape(experts,...]
  transfers between devices with their start and end apart: 19 -> 13, of which waited for: 12 -> 4; matrix products, arithmetic and copies ran while one was open for 5% -> 3% of each run, Pallas kernels for 8% -> 5%
where the time goes in v3:
time: 213 us; the launch traced here: 210 us
  blocking collectives  94.4 us (44%)
  starting transfers between devices  57.9 us (27%)
  Pallas kernels  22.9 us (11%)
  waiting for transfers between devices  19.1 us (9%)
  local copies, waits for them, and re-layouts  8.57 us (4%)
  other arithmetic  4.64 us (2%)
    all_to_all x1, blocking collectives, exchange(): return lax.all_to_all(value, axes, split_axis=0, concat_axis=0, tiled=True)  94.4 us
    pallas_call x7, Pallas kernels, call(): pl.pallas_call(kernel, out_shape=outs, in_specs=[smem_spec()] * scalars +...  22.9 us
    all_to_all x3, starting transfers between devices, exchange(): return lax.all_to_all(value, axes, split_axis=0, concat_axis=0, tiled=True)  21.3 us
    ppermute x4, starting transfers between devices, swap_core(): return lax.ppermute(value, 'c', [(0, 1), (1, 0)])  19.3 us
    ppermute x6, starting transfers between devices, shift_y(): lax.ppermute(value, 'y', [(i, (i + step) % size) for i in range(size)])  17.4 us
    all_to_all x3, waiting for transfers between devices, exchange(): return lax.all_to_all(value, axes, split_axis=0, concat_axis=0, tiled=True)  12.5 us
    unnamed x26, local copies, waits for them, and re-layouts  8.44 us
    ppermute x6, waiting for transfers between devices, shift_y(): lax.ppermute(value, 'y', [(i, (i + step) % size) for i in range(size)])  6.61 us
  transfers between devices with their start and end apart: 13, of which 4 were waited for; matrix products, arithmetic and copies ran while one was open for 3% of the time, Pallas kernels for 5%

profile of v3, /device:TPU:1, one launch (start us, length us, event | category | flops | bytes accessed | tf_op | source)
XLA Modules:
  0.0 209.7 jit_solution(15986683781070918599)
XLA Ops:
  2.8 3.1 %shard_map.68 = bf16[64,104,128]{2,1,0:T(8,128)(2,1)S(1)} custom-call(s32[1,1024]{1,0:T(1,128)S(1)} %get-tuple-element.22.main_ref, s32[1,1024]{1,0:T(1,128)S(1)} %get-tuple-element.21.left_ref, bf16[1024,128]{1,0:T(8,128)(2,1)S(1)} %bitcast.49, bf16[512,512]{1,0:T(8,128)(2,1)S(1)} %copy-done.8), custom_call_target="tpu_custom_call" | custom-call | tf_op jit(solution)/shard_map/pallas_call | solution.py:217
  6.0 94.4 %all_to_all.20.got_ref = bf16[64,104,128]{2,1,0:T(8,128)(2,1)S(1)} all-to-all(bf16[64,104,128]{2,1,0:T(8,128)(2,1)S(1)} %shard_map.68), channel_id=1, replica_groups=mesh['y'=4,'c'=2,'x'=4,'z'=16] {'x','z'}, dimensions={0} | all-to-all | bytes 3407872 | tf_op jit(solution)/shard_map/all_to_all | solution.py:265
  100.8 1.1 copy-done
  101.8 4.2 %all-to-all-start.1 = ((bf16[4,1280,128]{2,1,0:T(8,128)(2,1)}), bf16[4,1280,128]{2,1,0:T(8,128)(2,1)S(1)}, u32[]{:S(2)}, u32[]{:S(2)}) async-start(bf16[4,1280,128]{2,1,0:T(8,128)(2,1)} %copy-done), calls=%async_computation.1 | async-start | bytes 2621440 | tf_op jit(solution)/shard_map/all_to_all | solution.py:265
  106.2 1.2 copy-done.7
  107.4 4.5 %shard_map.69 = (bf16[4,1280,128]{2,1,0:T(8,128)(2,1)S(1)}, bf16[4,1280,128]{2,1,0:T(8,128)(2,1)}, bf16[1280,512]{1,0:T(8,128)(2,1)S(1)}) custom-call(s32[25]{0:T(128)S(1)} %pad_add_fusion.spot_ref.refs_0_, bf16[64,104,128]{2,1,0:T(8,128)(2,1)S(1)} %all_to_all.20.got_ref, bf16[1024,512]{1,0:T(8,128)(2,1)S(1)} %bitcast.50), custom_call_target="tpu_custom_call" | custom-call | tf_op jit(solution)/shard_map/pallas_call | solution.py:217
  111.9 1.1 copy-done.1
  113.0 1.1 copy-done.3
  114.0 9.2 %collective-permute-start = (bf16[4,1280,128]{2,1,0:T(8,128)(2,1)}, bf16[4,1280,128]{2,1,0:T(8,128)(2,1)S(1)}, u32[]{:S(2)}, u32[]{:S(2)}) collective-permute-start(bf16[4,1280,128]{2,1,0:T(8,128)(2,1)} %get-tuple-element.9), channel_id=1, source_target_pairs={{0,64},{64,0},{1,65},{65,1},{2,66},{66,2},{3,67},{67,3},{4,68},{68... | collective-permute-start | bytes 3932168 | tf_op jit(solution)/shard_map/ppermute | solution.py:27
  123.2 4.3 %collective-permute-start.1 = (bf16[4,1280,128]{2,1,0:T(8,128)(2,1)S(1)}, bf16[4,1280,128]{2,1,0:T(8,128)(2,1)}, u32[]{:S(2)}, u32[]{:S(2)}) collective-permute-start(bf16[4,1280,128]{2,1,0:T(8,128)(2,1)S(1)} %all-to-all-done.1.after_ref.part_ref), channel_id=1, source_target_pairs={{0,64},{64,0},{1,65},{65,1},{2,66},{66,2},{3,67},{67,3},{4,68},{68... | collective-permute-start | bytes 3932168 | tf_op jit(solution)/shard_map/ppermute | solution.py:27
  127.6 1.3 copy-done.4
  128.9 1.4 shard_map.71
  130.2 4.4 %all-to-all-start.2 = ((bf16[4,1280,128]{2,1,0:T(8,128)(2,1)}), bf16[4,1280,128]{2,1,0:T(8,128)(2,1)}, u32[]{:S(2)}, u32[]{:S(2)}) async-start(bf16[4,1280,128]{2,1,0:T(8,128)(2,1)} %shard_map.71), calls=%async_computation.2 | async-start | bytes 2621440 | tf_op jit(solution)/shard_map/all_to_all | solution.py:265
  134.7 1.0 shard_map.72.own_half_ref
  135.6 3.8 %shard_map.73 = (bf16[8,128,512]{2,1,0:T(8,128)(2,1)S(1)}, bf16[4,576,128]{2,1,0:T(8,128)(2,1)S(1)}, bf16[4,576,128]{2,1,0:T(8,128)(2,1)S(1)}) custom-call(s32[25]{0:T(128)S(1)} %pad_add_fusion.spot_ref.refs_0_, bf16[4,128,512]{2,1,0:T(8,128)(2,1)S(1)} %shard_map.72.own_half_ref, bf16[4,1280,128]{2,1,0:T(8,128)(2,1)} %collective-permute-done.1.part_ref, ...), custom_call_target="tpu_custom_call" | custom-call | tf_op jit(solution)/shard_map/pallas_call | solution.py:217
  139.5 1.0 copy-done.5
  140.5 2.1 collective-permute-start.2
  142.6 10.2 %all-to-all-done.2 = bf16[4,1280,128]{2,1,0:T(8,128)(2,1)} async-done(((bf16[4,1280,128]{2,1,0:T(8,128)(2,1)}), bf16[4,1280,128]{2,1,0:T(8,128)(2,1)}, u32[]{:S(2)}, u32[]{:S(2)}) %all-to-all-start.2) | async-done | bytes 1310752 | tf_op jit(solution)/shard_map/all_to_all | solution.py:265
  152.8 1.7 reduce_sum.22
  154.7 2.8 %collective-permute-start.5 = (bf16[576,128]{1,0:T(8,128)(2,1)S(1)}, bf16[576,128]{1,0:T(8,128)(2,1)S(1)}, u32[]{:S(2)}, u32[]{:S(2)}) collective-permute-start(bf16[576,128]{1,0:T(8,128)(2,1)S(1)} %get-tuple-element.19), channel_id=1, source_target_pairs={{0,384},{128,0},{256,128},{384,256},{1,385},{129,1},{257,129},{385... | collective-permute-start | bytes 442376 | tf_op jit(solution)/shard_map/ppermute | solution.py:23
  157.5 3.1 %collective-permute-start.4 = (bf16[576,128]{1,0:T(8,128)(2,1)S(1)}, bf16[576,128]{1,0:T(8,128)(2,1)S(1)}, u32[]{:S(2)}, u32[]{:S(2)}) collective-permute-start(bf16[576,128]{1,0:T(8,128)(2,1)S(1)} %get-tuple-element.20), channel_id=1, source_target_pairs={{0,256},{128,384},{256,0},{384,128},{1,257},{129,385},{257,1},{385... | collective-permute-start | bytes 442376 | tf_op jit(solution)/shard_map/ppermute | solution.py:23
  160.6 1.9 collective-permute-start.3
  163.3 12.6 %all-to-all-start.3 = ((bf16[64,20,128]{2,1,0:T(8,128)(2,1)}), bf16[64,20,128]{2,1,0:T(8,128)(2,1)S(1)}, u32[]{:S(2)}, u32[]{:S(2)}) async-start(bf16[64,20,128]{2,1,0:T(8,128)(2,1)} %pad_maximum_fusion.1), calls=%async_computation.3 | async-start | bytes 786432 | tf_op jit(solution)/shard_map/all_to_all | solution.py:265
  176.1 4.6 %collective-permute-start.8 = (bf16[576,128]{1,0:T(8,128)(2,1)S(1)}, bf16[576,128]{1,0:T(8,128)(2,1)S(1)}, u32[]{:S(2)}, u32[]{:S(2)}) collective-permute-start(bf16[576,128]{1,0:T(8,128)(2,1)S(1)} %fusion.7), channel_id=1, source_target_pairs={{0,384},{128,0},{256,128},{384,256},{1,385},{129,1},{257,129},{385... | collective-permute-start | bytes 442376 | tf_op jit(solution)/shard_map/ppermute | solution.py:23
  180.6 2.5 %collective-permute-start.7 = (bf16[576,128]{1,0:T(8,128)(2,1)S(1)}, bf16[576,128]{1,0:T(8,128)(2,1)S(1)}, u32[]{:S(2)}, u32[]{:S(2)}) collective-permute-start(bf16[576,128]{1,0:T(8,128)(2,1)S(1)} %fusion.7), channel_id=1, source_target_pairs={{0,256},{128,384},{256,0},{384,128},{1,257},{129,385},{257,1},{385... | collective-permute-start | bytes 442376 | tf_op jit(solution)/shard_map/ppermute | solution.py:23
  183.1 2.5 %collective-permute-start.6 = (bf16[576,128]{1,0:T(8,128)(2,1)S(1)}, bf16[576,128]{1,0:T(8,128)(2,1)S(1)}, u32[]{:S(2)}, u32[]{:S(2)}) collective-permute-start(bf16[576,128]{1,0:T(8,128)(2,1)S(1)} %fusion.7), channel_id=1, source_target_pairs={{0,128},{128,256},{256,384},{384,0},{1,129},{129,257},{257,385},{3... | collective-permute-start | bytes 442376 | tf_op jit(solution)/shard_map/ppermute | solution.py:23
  185.6 2.7 %collective-permute-done.7 = bf16[576,128]{1,0:T(8,128)(2,1)S(1)} collective-permute-done((bf16[576,128]{1,0:T(8,128)(2,1)S(1)}, bf16[576,128]{1,0:T(8,128)(2,1)S(1)}, u32[]{:S(2)}, u32[]{:S(2)}) %collective-permute-start.7) | collective-permute-done | bytes 147488 | tf_op jit(solution)/shard_map/ppermute | solution.py:23
  188.3 3.9 %collective-permute-done.6 = bf16[576,128]{1,0:T(8,128)(2,1)S(1)} collective-permute-done((bf16[576,128]{1,0:T(8,128)(2,1)S(1)}, bf16[576,128]{1,0:T(8,128)(2,1)S(1)}, u32[]{:S(2)}, u32[]{:S(2)}) %collective-permute-start.6) | collective-permute-done | bytes 147488 | tf_op jit(solution)/shard_map/ppermute | solution.py:23
  192.3 3.7 %collective-permute-start.9 = (bf16[4,576,128]{2,1,0:T(8,128)(2,1)S(1)}, bf16[4,576,128]{2,1,0:T(8,128)(2,1)S(1)}, u32[]{:S(2)}, u32[]{:S(2)}) collective-permute-start(bf16[4,576,128]{2,1,0:T(8,128)(2,1)S(1)} %pad_maximum_fusion.refs_1_), channel_id=1, source_target_pairs={{0,64},{64,0},{1,65},{65,1},{2,66},{66,2},{3,67},{67,3},{4,68},{68... | collective-permute-start | bytes 1769480 | tf_op jit(solution)/shard_map/ppermute | solution.py:27
  196.9 2.2 %all-to-all-done.3 = bf16[64,20,128]{2,1,0:T(8,128)(2,1)S(1)} async-done(((bf16[64,20,128]{2,1,0:T(8,128)(2,1)}), bf16[64,20,128]{2,1,0:T(8,128)(2,1)S(1)}, u32[]{:S(2)}, u32[]{:S(2)}) %all-to-all-start.3) | async-done | bytes 327712 | tf_op jit(solution)/shard_map/all_to_all | solution.py:265
  200.0 1.0 copy.10
  201.0 8.7 %shard_map.74 = f32[1,1024,512]{2,1,0:T(8,128)} custom-call(s32[25]{0:T(128)S(1)} %pad_add_fusion.spot_ref.refs_0_, bf16[4,576,128]{2,1,0:T(8,128)(2,1)S(1)} %pad_maximum_fusion.refs_1_, bf16[4,576,128]{2,1,0:T(8,128)(2,1)S(1)} %collective-permute-done.9.refs_2_, bf16[8,128,512]{2,1,0:T(8,128)(2,1)S(1)} %copy-done.6), custom_call_target="tpu_custom_call" | custom-call | tf_op jit(solution)/shard_map/pallas_call | solution.py:217
  (48 shorter events, 5.5 us)
Async XLA Ops:
  0.6 1.9 copy-start.9
  0.6 1.9 copy-start.10
  0.6 2.1 %copy-start.8 = (bf16[512,512]{1,0:T(8,128)(2,1)S(1)}, bf16[512,512]{1,0:T(8,128)(2,1)}, u32[]{:S(2)}) copy-start(bf16[512,512]{1,0:T(8,128)(2,1)} %grad_ref.1) | copy-start | bytes 1572868
  100.8 1.1 copy-start
  101.8 21.4 %all-to-all-start.1 = ((bf16[4,1280,128]{2,1,0:T(8,128)(2,1)}), bf16[4,1280,128]{2,1,0:T(8,128)(2,1)S(1)}, u32[]{:S(2)}, u32[]{:S(2)}) async-start(bf16[4,1280,128]{2,1,0:T(8,128)(2,1)} %copy-done), calls=%async_computation.1 | async-start | bytes 2621440 | tf_op jit(solution)/shard_map/all_to_all | solution.py:265
  106.1 1.2 copy-start.7
  111.9 1.1 copy-start.1
  113.0 1.1 copy-start.3
  114.0 13.5 %collective-permute-start = (bf16[4,1280,128]{2,1,0:T(8,128)(2,1)}, bf16[4,1280,128]{2,1,0:T(8,128)(2,1)S(1)}, u32[]{:S(2)}, u32[]{:S(2)}) collective-permute-start(bf16[4,1280,128]{2,1,0:T(8,128)(2,1)} %get-tuple-element.9), channel_id=1, source_target_pairs={{0,64},{64,0},{1,65},{65,1},{2,66},{66,2},{3,67},{67,3},{4,68},{68... | collective-permute-start | bytes 3932168 | tf_op jit(solution)/shard_map/ppermute | solution.py:27
  123.2 12.4 %collective-permute-start.1 = (bf16[4,1280,128]{2,1,0:T(8,128)(2,1)S(1)}, bf16[4,1280,128]{2,1,0:T(8,128)(2,1)}, u32[]{:S(2)}, u32[]{:S(2)}) collective-permute-start(bf16[4,1280,128]{2,1,0:T(8,128)(2,1)S(1)} %all-to-all-done.1.after_ref.part_ref), channel_id=1, source_target_pairs={{0,64},{64,0},{1,65},{65,1},{2,66},{66,2},{3,67},{67,3},{4,68},{68... | collective-permute-start | bytes 3932168 | tf_op jit(solution)/shard_map/ppermute | solution.py:27
  127.5 1.3 copy-start.4
  130.2 4.5 %copy-start.2 = (bf16[1280,512]{1,0:T(8,128)(2,1)S(1)}, bf16[1280,512]{1,0:T(8,128)(2,1)}, u32[]{:S(2)}) copy-start(bf16[1280,512]{1,0:T(8,128)(2,1)} %copy-done.1) | copy-start | bytes 3932164
  130.2 22.6 %all-to-all-start.2 = ((bf16[4,1280,128]{2,1,0:T(8,128)(2,1)}), bf16[4,1280,128]{2,1,0:T(8,128)(2,1)}, u32[]{:S(2)}, u32[]{:S(2)}) async-start(bf16[4,1280,128]{2,1,0:T(8,128)(2,1)} %shard_map.71), calls=%async_computation.2 | async-start | bytes 2621440 | tf_op jit(solution)/shard_map/all_to_all | solution.py:265
  139.4 1.0 copy-start.5
  140.5 14.0 %collective-permute-start.2 = (bf16[4,576,128]{2,1,0:T(8,128)(2,1)S(1)}, bf16[4,576,128]{2,1,0:T(8,128)(2,1)S(1)}, u32[]{:S(2)}, u32[]{:S(2)}) collective-permute-start(bf16[4,576,128]{2,1,0:T(8,128)(2,1)S(1)} %get-tuple-element.12), channel_id=1, source_target_pairs={{0,64},{64,0},{1,65},{65,1},{2,66},{66,2},{3,67},{67,3},{4,68},{68... | collective-permute-start | bytes 1769480 | tf_op jit(solution)/shard_map/ppermute | solution.py:27
  154.7 21.2 %collective-permute-start.5 = (bf16[576,128]{1,0:T(8,128)(2,1)S(1)}, bf16[576,128]{1,0:T(8,128)(2,1)S(1)}, u32[]{:S(2)}, u32[]{:S(2)}) collective-permute-start(bf16[576,128]{1,0:T(8,128)(2,1)S(1)} %get-tuple-element.19), channel_id=1, source_target_pairs={{0,384},{128,0},{256,128},{384,256},{1,385},{129,1},{257,129},{385... | collective-permute-start | bytes 442376 | tf_op jit(solution)/shard_map/ppermute | solution.py:23
  157.5 18.5 %collective-permute-start.4 = (bf16[576,128]{1,0:T(8,128)(2,1)S(1)}, bf16[576,128]{1,0:T(8,128)(2,1)S(1)}, u32[]{:S(2)}, u32[]{:S(2)}) collective-permute-start(bf16[576,128]{1,0:T(8,128)(2,1)S(1)} %get-tuple-element.20), channel_id=1, source_target_pairs={{0,256},{128,384},{256,0},{384,128},{1,257},{129,385},{257,1},{385... | collective-permute-start | bytes 442376 | tf_op jit(solution)/shard_map/ppermute | solution.py:23
  160.6 15.4 %collective-permute-start.3 = (bf16[576,128]{1,0:T(8,128)(2,1)S(1)}, bf16[576,128]{1,0:T(8,128)(2,1)S(1)}, u32[]{:S(2)}, u32[]{:S(2)}) collective-permute-start(bf16[576,128]{1,0:T(8,128)(2,1)S(1)} %get-tuple-element.18), channel_id=1, source_target_pairs={{0,128},{128,256},{256,384},{384,0},{1,129},{129,257},{257,385},{3... | collective-permute-start | bytes 442376 | tf_op jit(solution)/shard_map/ppermute | solution.py:23
  163.3 35.8 %all-to-all-start.3 = ((bf16[64,20,128]{2,1,0:T(8,128)(2,1)}), bf16[64,20,128]{2,1,0:T(8,128)(2,1)S(1)}, u32[]{:S(2)}, u32[]{:S(2)}) async-start(bf16[64,20,128]{2,1,0:T(8,128)(2,1)} %pad_maximum_fusion.1), calls=%async_computation.3 | async-start | bytes 786432 | tf_op jit(solution)/shard_map/all_to_all | solution.py:265
  176.1 9.6 %collective-permute-start.8 = (bf16[576,128]{1,0:T(8,128)(2,1)S(1)}, bf16[576,128]{1,0:T(8,128)(2,1)S(1)}, u32[]{:S(2)}, u32[]{:S(2)}) collective-permute-start(bf16[576,128]{1,0:T(8,128)(2,1)S(1)} %fusion.7), channel_id=1, source_target_pairs={{0,384},{128,0},{256,128},{384,256},{1,385},{129,1},{257,129},{385... | collective-permute-start | bytes 442376 | tf_op jit(solution)/shard_map/ppermute | solution.py:23
  180.6 7.7 %collective-permute-start.7 = (bf16[576,128]{1,0:T(8,128)(2,1)S(1)}, bf16[576,128]{1,0:T(8,128)(2,1)S(1)}, u32[]{:S(2)}, u32[]{:S(2)}) collective-permute-start(bf16[576,128]{1,0:T(8,128)(2,1)S(1)} %fusion.7), channel_id=1, source_target_pairs={{0,256},{128,384},{256,0},{384,128},{1,257},{129,385},{257,1},{385... | collective-permute-start | bytes 442376 | tf_op jit(solution)/shard_map/ppermute | solution.py:23
  183.1 9.1 %collective-permute-start.6 = (bf16[576,128]{1,0:T(8,128)(2,1)S(1)}, bf16[576,128]{1,0:T(8,128)(2,1)S(1)}, u32[]{:S(2)}, u32[]{:S(2)}) collective-permute-start(bf16[576,128]{1,0:T(8,128)(2,1)S(1)} %fusion.7), channel_id=1, source_target_pairs={{0,128},{128,256},{256,384},{384,0},{1,129},{129,257},{257,385},{3... | collective-permute-start | bytes 442376 | tf_op jit(solution)/shard_map/ppermute | solution.py:23
  192.3 8.7 %collective-permute-start.9 = (bf16[4,576,128]{2,1,0:T(8,128)(2,1)S(1)}, bf16[4,576,128]{2,1,0:T(8,128)(2,1)S(1)}, u32[]{:S(2)}, u32[]{:S(2)}) collective-permute-start(bf16[4,576,128]{2,1,0:T(8,128)(2,1)S(1)} %pad_maximum_fusion.refs_1_), channel_id=1, source_target_pairs={{0,64},{64,0},{1,65},{65,1},{2,66},{66,2},{3,67},{67,3},{4,68},{68... | collective-permute-start | bytes 1769480 | tf_op jit(solution)/shard_map/ppermute | solution.py:27
  199.2 1.8 copy-start.6

commit v4 on v1

v4 whole, which is shorter than its diff:
```python
import jax
import jax.numpy as jnp
from jax import lax
from jax.experimental import pallas as pl
from jax.experimental.pallas import tpu as pltpu
from jax.sharding import Mesh, PartitionSpec as P

EXPERT = ("x", "z")
MIB = 1024 * 1024
BF16 = jnp.bfloat16
F32 = jnp.float32
SMEM = pl.BlockSpec(memory_space=pltpu.SMEM)
LOOSE = pl.BlockSpec(memory_space=pl.ANY)


def shift_y(value, step, size):
    return lax.ppermute(value, "y", [(i, (i + step) % size) for i in range(size)])


def swap_core(value):
    return lax.ppermute(value, "c", [(0, 1), (1, 0)])


def exchange(value, axes):
    return lax.all_to_all(value, axes, split_axis=0, concat_axis=0, tiled=True)


def nt_dot(left, right):
    return lax.dot_general(left, right, (((1,), (1,)), ((), ())), preferred_element_type=F32)


def nn_dot(left, right):
    return jnp.dot(left, right, preferred_element_type=F32)


def one_hot(rows, index):
    return jnp.where(rows == index, 1.0, 0.0).astype(BF16)


def row_numbers(count):
    return lax.broadcasted_iota(jnp.int32, (count, 1), 0)


def lane_numbers(count):
    return lax.broadcasted_iota(jnp.int32, (1, count), 1)


def send_scaled_kernel(main_ref, left_ref, scaled_ref, out_ref):
    experts = out_ref.shape[0]
    scaled = scaled_ref[...]
    part = nn_dot(one_hot(row_numbers(experts * 16), main_ref[...]), scaled).astype(BF16)
    out_ref[:, 0:16, :] = part.reshape(experts, 16, 128)
    part = nn_dot(one_hot(row_numbers(experts * 8), left_ref[...]), scaled)
    out_ref[:, 16:24, :] = part.reshape(experts, 8, 128).astype(BF16)


def send_grad_kernel(main_ref, late_ref, grad_ref, out_ref):
    experts = out_ref.shape[0]
    tokens, width_part = grad_ref.shape
    blocks = width_part // 128
    grad = grad_ref[...]
    chosen = one_hot(row_numbers(experts * 16), main_ref[...])
    rows = nn_dot(chosen[:, :tokens] + chosen[:, tokens:], grad).astype(BF16)
    for b in range(blocks):
        out_ref[:, 16 * b : 16 * (b + 1), :] = rows[:, b * 128 : (b + 1) * 128].reshape(experts, 16, 128)
    number = row_numbers(experts * 16)
    chosen = one_hot((number & -16) + (number & 3), late_ref[...])
    rows = nn_dot(chosen[:, :tokens] + chosen[:, tokens:], grad)
    column = (number >> 2) & 3
    total = rows[:, 0:128]
    for b in range(1, blocks):
        total = jnp.where(column == b, rows[:, b * 128 : (b + 1) * 128], total)
    out_ref[:, 16 * blocks :, :] = total.astype(BF16).reshape(experts, 16, 128)


def unpack_kernel(got_ref, out_ref):
    experts = got_ref.shape[0]
    out_ref[: experts * 16] = got_ref[:, 0:16, :].reshape(experts * 16, 128)
    tail = got_ref[:, 16:24, :].astype(F32).reshape(experts * 8, 128).astype(BF16)
    number = row_numbers(experts * 4)
    take = one_hot((number >> 2) * 8 + (number & 3), lane_numbers(experts * 8))
    out_ref[experts * 16 :] = nn_dot(take, tail).astype(BF16)


def put_piece(spot, y_size, own_ref, other_ref, piece):
    @pl.when(spot < y_size)
    def _():
        own_ref[spot] = piece

    @pl.when(spot >= y_size)
    def _():
        other_ref[spot - y_size] = piece


def turn_kernel(spot_ref, own_ref, other_ref, out_ref):
    blocks = out_ref.shape[0] // 128
    y_size = blocks // 2
    for d in range(blocks):
        spot = spot_ref[blocks + d]

        @pl.when(spot < y_size)
        def _():
            out_ref[d * 128 : (d + 1) * 128, :] = own_ref[spot].T

        @pl.when(spot >= y_size)
        def _():
            out_ref[d * 128 : (d + 1) * 128, :] = other_ref[spot - y_size].T


def back_kernel(spot_ref, got_ref, weight_ref, after_ref, own_ref, other_ref, rows_ref):
    experts = got_ref.shape[0]
    columns = rows_ref.shape[1] // 128

    @pl.when(pl.program_id(0) == 0)
    def _():
        tail = got_ref[:, 16 * columns :, :].reshape(experts * 16, 128)
        number = row_numbers(experts * 4)
        base = (number >> 2) * 16 + (number & 3)
        for b in range(columns):
            lanes = slice(b * 128, (b + 1) * 128)
            rows_ref[: experts * 16, lanes] = got_ref[:, 16 * b : 16 * (b + 1), :].reshape(experts * 16, 128)
            take = one_hot(base + b * 4, lane_numbers(experts * 16))
            rows_ref[experts * 16 :, lanes] = nn_dot(take, tail).astype(BF16)

    term = nt_dot(rows_ref[...], weight_ref[...]).astype(BF16)
    core = spot_ref[spot_ref.shape[0] - 1]

    @pl.when(core == 0)
    def _():
        own_ref[0] = term[:, :128]
        other_ref[0] = term[:, 128:]

    @pl.when(core != 0)
    def _():
        own_ref[0] = term[:, 128:]
        other_ref[0] = term[:, :128]


def grad_kernel(spot_ref, turned_ref, rows_ref, gradb_ref, pack_own_ref, pack_other_ref):
    blocks = gradb_ref.shape[0] // 128
    y_size = blocks // 2
    half = blocks // 2
    step = pl.program_id(0)
    part = nn_dot(turned_ref[...], rows_ref[...]).astype(BF16)
    gradb_ref[pl.ds(pl.multiple_of(step * 256, 256), 256), :] = part

    @pl.when(step == pl.num_programs(0) - 1)
    def _():
        gradb = gradb_ref[...]
        gram = nt_dot(gradb, gradb).astype(BF16)
        for d in range(blocks):
            rows = slice(d * 128, (d + 1) * 128)
            pieces = []
            for k in range(half):
                j = (d + k) % blocks
                pieces.append(gram[rows, j * 128 : (j + 1) * 128])
            i = d % half
            top = i * 128 + (64 if d >= half else 0)
            pieces.append(gram[top : top + 64, (i + half) * 128 : (i + half + 1) * 128])
            spot = spot_ref[d]

            def put(ref, at):
                for k in range(half):
                    ref[at, k * 128 : (k + 1) * 128, :] = pieces[k]
                ref[at, half * 128 :, :] = pieces[half]

            @pl.when(spot < y_size)
            def _():
                put(pack_own_ref, spot)

            @pl.when(spot >= y_size)
            def _():
                put(pack_other_ref, spot - y_size)


def add_kernel(own_ref, other_ref, out_ref):
    out_ref[...] = (own_ref[...].astype(F32) + other_ref[...].astype(F32)).astype(BF16)


def pack_add_kernel(own_ref, other_ref, *out_refs):
    for k, out_ref in enumerate(out_refs):
        out_ref[...] = (own_ref[k].astype(F32) + other_ref[k].astype(F32)).astype(BF16)


def pack_sum_kernel(*refs):
    total = refs[0][...].astype(F32)
    for ref in refs[1:-1]:
        total = total + ref[...].astype(F32)
    refs[-1][...] = total.astype(BF16)


def return_kernel(part_ref, after_ref, out_ref):
    experts = out_ref.shape[0]
    total = part_ref[0].astype(F32)
    for k in range(1, part_ref.shape[0]):
        total = total + part_ref[k].astype(F32)
    total = total.astype(BF16)
    out_ref[:, 0:16, :] = total[: experts * 16].reshape(experts, 16, 128)
    number = row_numbers(experts * 8)
    wanted = jnp.where((number & 7) < 4, (number >> 3) * 4 + (number & 7), -1)
    left = nn_dot(one_hot(wanted, lane_numbers(experts * 4)), total[experts * 16 :])
    out_ref[:, 16:24, :] = left.reshape(experts, 8, 128).astype(BF16)


def ortho_kernel(width, spot_ref, own_ref, other_ref, gradb_ref, out_ref, gram_ref, norm_ref):
    blocks = gram_ref.shape[0] // 128
    y_size = blocks // 2
    half = blocks // 2

    @pl.when(pl.program_id(0) == 0)
    def _():
        unit = jnp.where(row_numbers(128) == lane_numbers(128), 1.0, 0.0).astype(BF16)
        for d in range(blocks):
            spot = spot_ref[blocks + d]

            def place(ref, at):
                for k in range(half):
                    j = (d + k) % blocks
                    gram_ref[d * 128 : (d + 1) * 128, j * 128 : (j + 1) * 128] = ref[at, k * 128 : (k + 1) * 128, :]
                turned = nt_dot(unit, ref[at, 128 : half * 128, :]).astype(BF16)
                for k in range(1, half):
                    j = (d + k) % blocks
                    gram_ref[j * 128 : (j + 1) * 128, d * 128 : (d + 1) * 128] = turned[:, (k - 1) * 128 : k * 128]
                i = d % half
                top = i * 128 + (64 if d >= half else 0)
                gram_ref[top : top + 64, (i + half) * 128 : (i + half + 1) * 128] = ref[at, half * 128 :, :]

            @pl.when(spot < y_size)
            def _():
                place(own_ref, spot)

            @pl.when(spot >= y_size)
            def _():
                place(other_ref, spot - y_size)

        for i in range(half):
            upper = gram_ref[i * 128 : (i + 1) * 128, (i + half) * 128 : (i + half + 1) * 128]
            gram_ref[(i + half) * 128 : (i + half + 1) * 128, i * 128 : (i + 1) * 128] = nt_dot(unit, upper).astype(BF16)
        squares = jnp.zeros((1, 1), F32)
        for ref in (own_ref, other_ref):
            whole = ref[...].astype(F32)
            diagonal = whole[:, :128, :]
            squares = squares + 2.0 * jnp.sum(whole * whole).reshape(1, 1) - jnp.sum(diagonal * diagonal).reshape(1, 1)
        norm_ref[...] = jnp.broadcast_to(jnp.sqrt(squares) + 1e-06, norm_ref.shape)

    norm_sq = norm_ref[0:1, 0:1]
    inverse = 1.0 / norm_sq
    gram = gram_ref[...]
    first = (gradb_ref[...].astype(F32) * lax.rsqrt(norm_sq)).astype(BF16)

    def apply(value):
        return nn_dot(gram, value) * inverse

    second = (1.5 * first.astype(F32) - 0.5 * apply(first)).astype(BF16)
    power_one = apply(second)
    power_two = apply(power_one.astype(BF16))
    power_three = apply(power_two.astype(BF16))
    total = 1.5 * second.astype(F32) - 0.5 * (2.25 * power_one - 1.5 * power_two + 0.25 * power_three)
    out_ref[0] = total * width**0.5


def whole(value):
    return pl.BlockSpec(value.shape, lambda *_: (0,) * len(value.shape))


def call(kernel, outs, ins, scratch=(), vmem=24, steps=(), specs=None, out_specs=None):
    specs = specs or {}
    out_specs = out_specs or {}
    flat, tree = jax.tree.flatten(outs)
    return pl.pallas_call(
        kernel,
        out_shape=outs,
        grid=steps,
        in_specs=[specs.get(i, whole(value)) for i, value in enumerate(ins)],
        out_specs=jax.tree.unflatten(tree, [out_specs.get(i, whole(value)) for i, value in enumerate(flat)]),
        scratch_shapes=list(scratch),
        compiler_params=pltpu.CompilerParams(vmem_limit_bytes=vmem * MIB),
    )(*ins)


def per_device(grad_out, hidden, gate_prob, expert_ids, weights):
    tokens, width_part = grad_out.shape
    top_count = expert_ids.shape[1]
    unit_part = hidden.shape[2]
    units = weights.shape[1]
    experts = lax.axis_size("x") * lax.axis_size("z")
    y_size = lax.axis_size("y")
    dp = y_size * 2
    width = width_part * dp
    capacity = 5 * tokens * top_count // (4 * experts)
    total_slots = experts * capacity
    pair_count = tokens * top_count
    y = lax.axis_index("y")
    c = lax.axis_index("c")
    block = jnp.arange(dp, dtype=jnp.int32)
    other_core = (block % 2) ^ c
    goes_to = other_core * y_size + (block // 2 - y) % y_size
    came_from = other_core * y_size + (y - block // 2) % y_size
    spots = jnp.concatenate([goes_to, came_from, jnp.full((1,), c)]).astype(jnp.int32)

    flat_ids = expert_ids.T.reshape(1, pair_count)
    named = (jnp.arange(experts, dtype=jnp.int32)[:, None] == flat_ids).astype(BF16)
    order = jnp.arange(pair_count, dtype=jnp.int32)
    earlier = (order[:, None] < order[None, :]).astype(BF16)
    before = jnp.dot(named, earlier, preferred_element_type=F32)
    rank_in = jnp.sum(before * named.astype(F32), axis=0, keepdims=True).astype(jnp.int32)
    late = rank_in >= 16
    main_index = jnp.where(late, -1, flat_ids * 16 + rank_in)
    left_index = jnp.where(late, flat_ids * 8 + rank_in - 16, -1)
    late_index = jnp.where(late, flat_ids * 16 + rank_in - 16, -1)

    scaled_part = (gate_prob[:, :, None] * hidden.astype(F32)).astype(BF16)
    scaled_part = scaled_part.transpose(1, 0, 2).reshape(pair_count, unit_part)
    columns = width_part // 128

    def shape(*dims):
        return jax.ShapeDtypeStruct(dims, BF16)

    got_scaled = exchange(
        call(send_scaled_kernel, shape(experts, 24, 128), (main_index, left_index, scaled_part)), EXPERT
    )
    got = exchange(
        call(send_grad_kernel, shape(experts, 20 * columns, 128), (main_index, late_index, grad_out)), EXPERT
    )

    scaled = call(unpack_kernel, shape(total_slots, unit_part), (got_scaled,), vmem=8)
    gathered = jnp.stack([scaled] + [shift_y(scaled, k, y_size) for k in range(1, y_size)])
    turned = call(
        turn_kernel, shape(units, total_slots), (spots, gathered, swap_core(gathered)), specs={0: SMEM}, vmem=20
    )

    piece = pl.BlockSpec((1, total_slots, 128), lambda i: (i, 0, 0))
    term_own, term_other, rows = call(
        back_kernel,
        (shape(y_size, total_slots, unit_part), shape(y_size, total_slots, unit_part), shape(total_slots, width_part)),
        (spots, got, pltpu.with_memory_space_constraint(weights[0], pltpu.HBM), turned),
        steps=(y_size,),
        specs={0: SMEM, 2: pl.BlockSpec((256, width_part), lambda i: (i, 0)), 3: LOOSE},
        out_specs={0: piece, 1: piece},
        vmem=20,
    )
    packs = shape(y_size, units // 2 + 64, 128)
    grad_bf16, pack_own, pack_other = call(
        grad_kernel,
        (shape(units, width_part), packs, packs),
        (spots, turned, rows),
        steps=(units // 256,),
        specs={0: SMEM, 1: pl.BlockSpec((256, total_slots), lambda i: (i, 0))},
        vmem=24,
    )
    both = call(
        add_kernel,
        shape(y_size, total_slots, unit_part),
        (term_own, swap_core(term_other)),
        steps=(y_size,),
        specs={0: piece, 1: piece},
        out_specs={0: piece},
        vmem=8,
    )
    parts = exchange(both, "y")

    pack = shape(units // 2 + 64, 128)
    pack_parts = call(pack_add_kernel, (pack,) * y_size, (pack_own, swap_core(pack_other)), vmem=8)
    pack_parts = [pack_parts[0]] + [shift_y(pack_parts[k], k, y_size) for k in range(1, y_size)]
    pack_total = call(pack_sum_kernel, pack, tuple(pack_parts), vmem=8)
    pack_all = jnp.stack([pack_total] + [shift_y(pack_total, k, y_size) for k in range(1, y_size)])
    pack_all_other = swap_core(pack_all)

    returned = exchange(
        call(return_kernel, shape(experts, 24, 128), (parts, pack_total), specs={1: LOOSE}, vmem=12), EXPERT
    ).reshape(experts * 24, unit_part)
    slot_index = flat_ids * 24 + rank_in
    chosen = (jnp.arange(experts * 24, dtype=jnp.int32)[:, None] == slot_index).astype(BF16)
    picked = lax.dot_general(chosen, returned, (((0,), (0,)), ((), ())), preferred_element_type=F32)
    picked = picked.reshape(top_count, tokens, unit_part).transpose(1, 0, 2)
    hidden_grad = (gate_prob[:, :, None] * picked).astype(BF16)

    half_width = width_part // 2
    update = call(
        lambda *refs: ortho_kernel(width, *refs),
        jax.ShapeDtypeStruct((1, units, width_part), F32),
        (spots, pack_all, pack_all_other, grad_bf16),
        (pltpu.VMEM((units, units), BF16), pltpu.VMEM((8, 128), F32)),
        steps=(2,),
        specs={0: SMEM, 3: pl.BlockSpec((units, half_width), lambda i: (0, i))},
        out_specs={0: pl.BlockSpec((1, units, half_width), lambda i: (0, 0, i))},
    )
    return (hidden_grad, update)


def solution(mesh):
    dp, experts = mesh.devices.shape
    x_size = 4
    split = Mesh(
        mesh.devices.reshape(dp // 2, 2, x_size, experts // x_size), ("y", "c", "x", "z")
    )
    rows, cols = ("x", "z"), ("y", "c")
    in_specs = (P(rows, cols), P(rows, None, cols), P(rows, None), P(rows, None), P(rows, None, cols))
    out_specs = (P(rows, None, cols), P(rows, None, cols))
    return jax.shard_map(per_device, mesh=split, in_specs=in_specs, out_specs=out_specs, check_vma=False)
```

time: 216 us -> 208 us (0.963)
  waiting for transfers between devices: 85.9 us -> 71.1 us
  Pallas kernels: 17.9 us -> 30.7 us
  starting transfers between devices: 93.1 us -> 90.3 us
    pallas_call x3 -> x11, Pallas kernels: 17.9 us -> 30.7 us  [call(): pl.pallas_call(kernel, out_shape=outs, grid=steps, in_specs=[specs.get(i,...]
    ppermute x12 -> x9, waiting for transfers between devices: 29.4 us -> 17.6 us  [shift_y(): lax.ppermute(value, 'y', [(i, (i + step) % size) for i in range(size)])]
    ppermute x12 -> x9, starting transfers between devices: 41.2 us -> 32.2 us  [shift_y(): lax.ppermute(value, 'y', [(i, (i + step) % size) for i in range(size)])]
    all_to_all x3 -> x4, waiting for transfers between devices: 55.7 us -> 47.5 us  [exchange(): return lax.all_to_all(value, axes, split_axis=0, concat_axis=0, tiled=True)]
    unnamed x11 -> x28, local copies, waits for them, and re-layouts: 3.12 us -> 9.89 us
    ppermute x4, waiting for transfers between devices: 0.81 us -> 5.93 us  [swap_core(): return lax.ppermute(value, 'c', [(0, 1), (1, 0)])]
    all_to_all x3 -> x4, starting transfers between devices: 33.2 us -> 37.7 us  [exchange(): return lax.all_to_all(value, axes, split_axis=0, concat_axis=0, tiled=True)]
    reshape x7 -> x0, local copies, waits for them, and re-layouts: 4.22 us -> none  [the longest x1 1.79 us: per_device(): send_grad = send_grad.reshape(experts, capacity, 2, width_part // 2).tran...]
  transfers between devices with their start and end apart: 19 -> 17, of which waited for: 12 -> 13; matrix products, arithmetic and copies ran while one was open for 5% -> 1% of each run, Pallas kernels for 8% -> 10%
where the time goes in v4:
time: 208 us; the launch traced here: 207 us
  starting transfers between devices  90.3 us (43%)
  waiting for transfers between devices  71.1 us (34%)
  Pallas kernels  30.7 us (15%)
  local copies, waits for them, and re-layouts  9.89 us (5%)
  other arithmetic  2.67 us (1%)
    all_to_all x4, waiting for transfers between devices, exchange(): return lax.all_to_all(value, axes, split_axis=0, concat_axis=0, tiled=True)  47.5 us
    all_to_all x4, starting transfers between devices, exchange(): return lax.all_to_all(value, axes, split_axis=0, concat_axis=0, tiled=True)  37.7 us
    ppermute x9, starting transfers between devices, shift_y(): lax.ppermute(value, 'y', [(i, (i + step) % size) for i in range(size)])  32.2 us
    pallas_call x11, Pallas kernels, call(): pl.pallas_call(kernel, out_shape=outs, grid=steps, in_specs=[specs.get(i,...  30.7 us
    ppermute x4, starting transfers between devices, swap_core(): return lax.ppermute(value, 'c', [(0, 1), (1, 0)])  20.4 us
    ppermute x9, waiting for transfers between devices, shift_y(): lax.ppermute(value, 'y', [(i, (i + step) % size) for i in range(size)])  17.6 us
    unnamed x28, local copies, waits for them, and re-layouts  9.89 us
    ppermute x4, waiting for transfers between devices, swap_core(): return lax.ppermute(value, 'c', [(0, 1), (1, 0)])  5.93 us
  transfers between devices with their start and end apart: 17, of which 13 were waited for; matrix products, arithmetic and copies ran while one was open for 1% of the time, Pallas kernels for 10%

profile of v4, /device:TPU:1, one launch (start us, length us, event | category | flops | bytes accessed | tf_op | source)
XLA Modules:
  0.0 207.0 jit_solution(11675728278737161346)
XLA Ops:
  2.8 1.7 shard_map.69
  4.5 19.1 %all-to-all-start.1 = ((bf16[64,24,128]{2,1,0:T(8,128)(2,1)}), bf16[64,24,128]{2,1,0:T(8,128)(2,1)S(1)}, u32[]{:S(2)}, u32[]{:S(2)}) async-start(bf16[64,24,128]{2,1,0:T(8,128)(2,1)} %shard_map.69), calls=%async_computation.1 | async-start | bytes 786432 | tf_op jit(solution)/shard_map/all_to_all | solution.py:25
  23.6 2.4 %shard_map.68 = bf16[64,80,128]{2,1,0:T(8,128)(2,1)} custom-call(s32[1,1024]{1,0:T(1,128)S(1)} %get-tuple-element.25.main_ref, s32[1,1024]{1,0:T(1,128)S(1)} %get-tuple-element.24.late_ref, bf16[512,512]{1,0:T(8,128)(2,1)S(1)} %copy-done.9), custom_call_target="tpu_custom_call" | custom-call | tf_op jit(solution)/shard_map/pallas_call | solution.py:270
  26.0 22.3 %all-to-all-done.1.got_ref = bf16[64,24,128]{2,1,0:T(8,128)(2,1)S(1)} async-done(((bf16[64,24,128]{2,1,0:T(8,128)(2,1)}), bf16[64,24,128]{2,1,0:T(8,128)(2,1)S(1)}, u32[]{:S(2)}, u32[]{:S(2)}) %all-to-all-start.1) | async-done | bytes 393248 | tf_op jit(solution)/shard_map/all_to_all | solution.py:25
  48.4 7.8 %all-to-all-start = ((bf16[64,80,128]{2,1,0:T(8,128)(2,1)}), bf16[64,80,128]{2,1,0:T(8,128)(2,1)}, u32[]{:S(2)}, u32[]{:S(2)}) async-start(bf16[64,80,128]{2,1,0:T(8,128)(2,1)} %shard_map.68), calls=%async_computation | async-start | bytes 2621440 | tf_op jit(solution)/shard_map/all_to_all | solution.py:25
  56.4 4.6 %collective-permute-start.2 = (bf16[1280,128]{1,0:T(8,128)(2,1)S(1)}, bf16[1280,128]{1,0:T(8,128)(2,1)S(1)}, u32[]{:S(2)}, u32[]{:S(2)}) collective-permute-start(bf16[1280,128]{1,0:T(8,128)(2,1)S(1)} %shard_map.70), channel_id=1, source_target_pairs={{0,384},{128,0},{256,128},{384,256},{1,385},{129,1},{257,129},{385... | collective-permute-start | bytes 983048 | tf_op jit(solution)/shard_map/ppermute | solution.py:17
  61.0 1.9 collective-permute-start
  63.0 3.5 %collective-permute-start.1 = (bf16[1280,128]{1,0:T(8,128)(2,1)S(1)}, bf16[1280,128]{1,0:T(8,128)(2,1)S(1)}, u32[]{:S(2)}, u32[]{:S(2)}) collective-permute-start(bf16[1280,128]{1,0:T(8,128)(2,1)S(1)} %shard_map.70), channel_id=1, source_target_pairs={{0,256},{128,384},{256,0},{384,128},{1,257},{129,385},{257,1},{385... | collective-permute-start | bytes 983048 | tf_op jit(solution)/shard_map/ppermute | solution.py:17
  66.5 6.1 %collective-permute-done = bf16[1280,128]{1,0:T(8,128)(2,1)S(1)} collective-permute-done((bf16[1280,128]{1,0:T(8,128)(2,1)S(1)}, bf16[1280,128]{1,0:T(8,128)(2,1)S(1)}, u32[]{:S(2)}, u32[]{:S(2)}) %collective-permute-start) | collective-permute-done | bytes 327712 | tf_op jit(solution)/shard_map/ppermute | solution.py:17
  72.6 5.0 %collective-permute-done.1 = bf16[1280,128]{1,0:T(8,128)(2,1)S(1)} collective-permute-done((bf16[1280,128]{1,0:T(8,128)(2,1)S(1)}, bf16[1280,128]{1,0:T(8,128)(2,1)S(1)}, u32[]{:S(2)}, u32[]{:S(2)}) %collective-permute-start.1) | collective-permute-done | bytes 327712 | tf_op jit(solution)/shard_map/ppermute | solution.py:17
  77.8 5.5 %collective-permute-start.3 = (bf16[4,1280,128]{2,1,0:T(8,128)(2,1)S(1)}, bf16[4,1280,128]{2,1,0:T(8,128)(2,1)S(1)}, u32[]{:S(2)}, u32[]{:S(2)}) collective-permute-start(bf16[4,1280,128]{2,1,0:T(8,128)(2,1)S(1)} %pad_maximum_fusion.own_ref), channel_id=1, source_target_pairs={{0,64},{64,0},{1,65},{65,1},{2,66},{66,2},{3,67},{67,3},{4,68},{68... | collective-permute-start | bytes 3932168 | tf_op jit(solution)/shard_map/ppermute | solution.py:21
  89.7 1.7 shard_map.71.after_ref.turned_ref
  91.4 25.2 %all-to-all-done.got_ref = bf16[64,80,128]{2,1,0:T(8,128)(2,1)} async-done(((bf16[64,80,128]{2,1,0:T(8,128)(2,1)}), bf16[64,80,128]{2,1,0:T(8,128)(2,1)}, u32[]{:S(2)}, u32[]{:S(2)}) %all-to-all-start) | async-done | bytes 1310752 | tf_op jit(solution)/shard_map/all_to_all | solution.py:25
  116.6 5.1 %shard_map.72 = (bf16[4,1280,128]{2,1,0:T(8,128)(2,1)S(1)}, bf16[4,1280,128]{2,1,0:T(8,128)(2,1)S(1)}, bf16[1280,512]{1,0:T(8,128)(2,1)S(1)}) custom-call(s32[17]{0:T(128)S(1)} %pad_add_fusion.spot_ref.refs_0_, bf16[64,80,128]{2,1,0:T(8,128)(2,1)} %all-to-all-done.got_ref, bf16[1024,512]{1,0:T(8,128)(2,1)} %bitcast.47, ...), custom_call_target="tpu_custom_call" | custom-call | tf_op jit(solution)/shard_map/pallas_call | solution.py:270
  122.8 7.6 %collective-permute-start.4 = (bf16[4,1280,128]{2,1,0:T(8,128)(2,1)S(1)}, bf16[4,1280,128]{2,1,0:T(8,128)(2,1)S(1)}, u32[]{:S(2)}, u32[]{:S(2)}) collective-permute-start(bf16[4,1280,128]{2,1,0:T(8,128)(2,1)S(1)} %get-tuple-element.13), channel_id=1, source_target_pairs={{0,64},{64,0},{1,65},{65,1},{2,66},{66,2},{3,67},{67,3},{4,68},{68... | collective-permute-start | bytes 3932168 | tf_op jit(solution)/shard_map/ppermute | solution.py:21
  130.4 2.6 %collective-permute-done.4.other_ref = bf16[4,1280,128]{2,1,0:T(8,128)(2,1)S(1)} collective-permute-done((bf16[4,1280,128]{2,1,0:T(8,128)(2,1)S(1)}, bf16[4,1280,128]{2,1,0:T(8,128)(2,1)S(1)}, u32[]{:S(2)}, u32[]{:S(2)}) %collective-permute-start.4) | collective-permute-done | bytes 1310752 | tf_op jit(solution)/shard_map/ppermute | solution.py:21
  134.4 4.3 %all-to-all-start.2 = ((bf16[4,1280,128]{2,1,0:T(8,128)(2,1)}), bf16[4,1280,128]{2,1,0:T(8,128)(2,1)}, u32[]{:S(2)}, u32[]{:S(2)}) async-start(bf16[4,1280,128]{2,1,0:T(8,128)(2,1)} %copy-done), calls=%async_computation.2 | async-start | bytes 2621440 | tf_op jit(solution)/shard_map/all_to_all | solution.py:25
  140.0 4.1 %shard_map.74 = (bf16[1024,512]{1,0:T(8,128)(2,1)S(1)}, bf16[4,576,128]{2,1,0:T(8,128)(2,1)S(1)}, bf16[4,576,128]{2,1,0:T(8,128)(2,1)S(1)}) custom-call(s32[17]{0:T(128)S(1)} %pad_add_fusion.spot_ref.refs_0_, bf16[1024,1280]{1,0:T(8,128)(2,1)S(1)} %shard_map.71.after_ref.turned_ref, bf16[1280,512]{1,0:T(8,128)(2,1)S(1)} %copy-done.4), custom_call_target="tpu_custom_call" | custom-call | tf_op jit(solution)/shard_map/pallas_call | solution.py:270
  144.1 2.4 %collective-permute-start.5 = (bf16[4,576,128]{2,1,0:T(8,128)(2,1)S(1)}, bf16[4,576,128]{2,1,0:T(8,128)(2,1)S(1)}, u32[]{:S(2)}, u32[]{:S(2)}) collective-permute-start(bf16[4,576,128]{2,1,0:T(8,128)(2,1)S(1)} %get-tuple-element.16), channel_id=1, source_target_pairs={{0,64},{64,0},{1,65},{65,1},{2,66},{66,2},{3,67},{67,3},{4,68},{68... | collective-permute-start | bytes 1769480 | tf_op jit(solution)/shard_map/ppermute | solution.py:21
  146.6 1.6 collective-permute-done.5.other_ref
  148.3 3.7 %collective-permute-start.6 = (bf16[576,128]{1,0:T(8,128)(2,1)S(1)}, bf16[576,128]{1,0:T(8,128)(2,1)S(1)}, u32[]{:S(2)}, u32[]{:S(2)}) collective-permute-start(bf16[576,128]{1,0:T(8,128)(2,1)S(1)} %get-tuple-element.18), channel_id=1, source_target_pairs={{0,128},{128,256},{256,384},{384,0},{1,129},{129,257},{257,385},{3... | collective-permute-start | bytes 442376 | tf_op jit(solution)/shard_map/ppermute | solution.py:17
  152.0 4.3 %collective-permute-start.7 = (bf16[576,128]{1,0:T(8,128)(2,1)S(1)}, bf16[576,128]{1,0:T(8,128)(2,1)S(1)}, u32[]{:S(2)}, u32[]{:S(2)}) collective-permute-start(bf16[576,128]{1,0:T(8,128)(2,1)S(1)} %get-tuple-element.19), channel_id=1, source_target_pairs={{0,256},{128,384},{256,0},{384,128},{1,257},{129,385},{257,1},{385... | collective-permute-start | bytes 442376 | tf_op jit(solution)/shard_map/ppermute | solution.py:17
  156.3 3.1 %collective-permute-start.8 = (bf16[576,128]{1,0:T(8,128)(2,1)S(1)}, bf16[576,128]{1,0:T(8,128)(2,1)S(1)}, u32[]{:S(2)}, u32[]{:S(2)}) collective-permute-start(bf16[576,128]{1,0:T(8,128)(2,1)S(1)} %get-tuple-element.20), channel_id=1, source_target_pairs={{0,384},{128,0},{256,128},{384,256},{1,385},{129,1},{257,129},{385... | collective-permute-start | bytes 442376 | tf_op jit(solution)/shard_map/ppermute | solution.py:17
  159.4 1.8 collective-permute-done.6.refs_1_
  162.7 2.5 %shard_map.77 = bf16[64,24,128]{2,1,0:T(8,128)(2,1)} custom-call(bf16[4,1280,128]{2,1,0:T(8,128)(2,1)} %all-to-all-done.2.part_ref, bf16[576,128]{1,0:T(8,128)(2,1)S(1)} %shard_map.76.after_ref), custom_call_target="tpu_custom_call" | custom-call | tf_op jit(solution)/shard_map/pallas_call | solution.py:270
  165.2 6.5 %all-to-all-start.3 = ((bf16[64,24,128]{2,1,0:T(8,128)(2,1)}), bf16[64,24,128]{2,1,0:T(8,128)(2,1)S(1)}, u32[]{:S(2)}, u32[]{:S(2)}) async-start(bf16[64,24,128]{2,1,0:T(8,128)(2,1)} %shard_map.77), calls=%async_computation.3 | async-start | bytes 786432 | tf_op jit(solution)/shard_map/all_to_all | solution.py:25
  171.7 4.8 %collective-permute-start.9 = (bf16[576,128]{1,0:T(8,128)(2,1)S(1)}, bf16[576,128]{1,0:T(8,128)(2,1)S(1)}, u32[]{:S(2)}, u32[]{:S(2)}) collective-permute-start(bf16[576,128]{1,0:T(8,128)(2,1)S(1)} %shard_map.76.after_ref), channel_id=1, source_target_pairs={{0,128},{128,256},{256,384},{384,0},{1,129},{129,257},{257,385},{3... | collective-permute-start | bytes 442376 | tf_op jit(solution)/shard_map/ppermute | solution.py:17
  176.5 2.6 %collective-permute-start.10 = (bf16[576,128]{1,0:T(8,128)(2,1)S(1)}, bf16[576,128]{1,0:T(8,128)(2,1)S(1)}, u32[]{:S(2)}, u32[]{:S(2)}) collective-permute-start(bf16[576,128]{1,0:T(8,128)(2,1)S(1)} %shard_map.76.after_ref), channel_id=1, source_target_pairs={{0,256},{128,384},{256,0},{384,128},{1,257},{129,385},{257,1},{385... | collective-permute-start | bytes 442376 | tf_op jit(solution)/shard_map/ppermute | solution.py:17
  179.1 3.6 %collective-permute-start.11 = (bf16[576,128]{1,0:T(8,128)(2,1)S(1)}, bf16[576,128]{1,0:T(8,128)(2,1)S(1)}, u32[]{:S(2)}, u32[]{:S(2)}) collective-permute-start(bf16[576,128]{1,0:T(8,128)(2,1)S(1)} %shard_map.76.after_ref), channel_id=1, source_target_pairs={{0,384},{128,0},{256,128},{384,256},{1,385},{129,1},{257,129},{385... | collective-permute-start | bytes 442376 | tf_op jit(solution)/shard_map/ppermute | solution.py:17
  184.2 1.8 collective-permute-done.11
  186.1 4.8 %collective-permute-start.12 = (bf16[4,576,128]{2,1,0:T(8,128)(2,1)S(1)}, bf16[4,576,128]{2,1,0:T(8,128)(2,1)S(1)}, u32[]{:S(2)}, u32[]{:S(2)}) collective-permute-start(bf16[4,576,128]{2,1,0:T(8,128)(2,1)S(1)} %pad_maximum_fusion.1.refs_1_), channel_id=1, source_target_pairs={{0,64},{64,0},{1,65},{65,1},{2,66},{66,2},{3,67},{67,3},{4,68},{68... | collective-permute-start | bytes 1769480 | tf_op jit(solution)/shard_map/ppermute | solution.py:21
  192.6 12.5 %shard_map.78 = f32[1,1024,512]{2,1,0:T(8,128)} custom-call(s32[17]{0:T(128)S(1)} %pad_add_fusion.spot_ref.refs_0_, bf16[4,576,128]{2,1,0:T(8,128)(2,1)S(1)} %pad_maximum_fusion.1.refs_1_, bf16[4,576,128]{2,1,0:T(8,128)(2,1)S(1)} %collective-permute-done.12.refs_2_, bf16[1024,512]{1,0:T(8,128)(2,1)S(1)} %copy-done.8), custom_call_target="tpu_custom_call" | custom-call | tf_op jit(solution)/shard_map/pallas_call | solution.py:270
  (53 shorter events, 19.3 us)
Async XLA Ops:
  0.6 1.9 copy-start.10
  0.6 1.9 copy-start.11
  2.5 21.1 %copy-start.9 = (bf16[512,512]{1,0:T(8,128)(2,1)S(1)}, bf16[512,512]{1,0:T(8,128)(2,1)}, u32[]{:S(2)}) copy-start(bf16[512,512]{1,0:T(8,128)(2,1)} %grad_ref.1) | copy-start | bytes 1572868
  4.5 43.9 %all-to-all-start.1 = ((bf16[64,24,128]{2,1,0:T(8,128)(2,1)}), bf16[64,24,128]{2,1,0:T(8,128)(2,1)S(1)}, u32[]{:S(2)}, u32[]{:S(2)}) async-start(bf16[64,24,128]{2,1,0:T(8,128)(2,1)} %shard_map.69), calls=%async_computation.1 | async-start | bytes 786432 | tf_op jit(solution)/shard_map/all_to_all | solution.py:25
  48.4 68.3 %all-to-all-start = ((bf16[64,80,128]{2,1,0:T(8,128)(2,1)}), bf16[64,80,128]{2,1,0:T(8,128)(2,1)}, u32[]{:S(2)}, u32[]{:S(2)}) async-start(bf16[64,80,128]{2,1,0:T(8,128)(2,1)} %shard_map.68), calls=%async_computation | async-start | bytes 2621440 | tf_op jit(solution)/shard_map/all_to_all | solution.py:25
  56.4 10.1 %collective-permute-start.2 = (bf16[1280,128]{1,0:T(8,128)(2,1)S(1)}, bf16[1280,128]{1,0:T(8,128)(2,1)S(1)}, u32[]{:S(2)}, u32[]{:S(2)}) collective-permute-start(bf16[1280,128]{1,0:T(8,128)(2,1)S(1)} %shard_map.70), channel_id=1, source_target_pairs={{0,384},{128,0},{256,128},{384,256},{1,385},{129,1},{257,129},{385... | collective-permute-start | bytes 983048 | tf_op jit(solution)/shard_map/ppermute | solution.py:17
  61.0 11.6 %collective-permute-start = (bf16[1280,128]{1,0:T(8,128)(2,1)S(1)}, bf16[1280,128]{1,0:T(8,128)(2,1)S(1)}, u32[]{:S(2)}, u32[]{:S(2)}) collective-permute-start(bf16[1280,128]{1,0:T(8,128)(2,1)S(1)} %shard_map.70), channel_id=1, source_target_pairs={{0,128},{128,256},{256,384},{384,0},{1,129},{129,257},{257,385},{3... | collective-permute-start | bytes 983048 | tf_op jit(solution)/shard_map/ppermute | solution.py:17
  63.0 14.7 %collective-permute-start.1 = (bf16[1280,128]{1,0:T(8,128)(2,1)S(1)}, bf16[1280,128]{1,0:T(8,128)(2,1)S(1)}, u32[]{:S(2)}, u32[]{:S(2)}) collective-permute-start(bf16[1280,128]{1,0:T(8,128)(2,1)S(1)} %shard_map.70), channel_id=1, source_target_pairs={{0,256},{128,384},{256,0},{384,128},{1,257},{129,385},{257,1},{385... | collective-permute-start | bytes 983048 | tf_op jit(solution)/shard_map/ppermute | solution.py:17
  77.8 8.2 %collective-permute-start.3 = (bf16[4,1280,128]{2,1,0:T(8,128)(2,1)S(1)}, bf16[4,1280,128]{2,1,0:T(8,128)(2,1)S(1)}, u32[]{:S(2)}, u32[]{:S(2)}) collective-permute-start(bf16[4,1280,128]{2,1,0:T(8,128)(2,1)S(1)} %pad_maximum_fusion.own_ref), channel_id=1, source_target_pairs={{0,64},{64,0},{1,65},{65,1},{2,66},{66,2},{3,67},{67,3},{4,68},{68... | collective-permute-start | bytes 3932168 | tf_op jit(solution)/shard_map/ppermute | solution.py:21
  83.4 1.1 copy-start.1
  86.0 1.1 copy-start.5
  87.1 1.3 copy-start.2
  88.4 1.3 copy-start.6
  121.7 1.1 copy-start.3
  122.8 10.2 %collective-permute-start.4 = (bf16[4,1280,128]{2,1,0:T(8,128)(2,1)S(1)}, bf16[4,1280,128]{2,1,0:T(8,128)(2,1)S(1)}, u32[]{:S(2)}, u32[]{:S(2)}) collective-permute-start(bf16[4,1280,128]{2,1,0:T(8,128)(2,1)S(1)} %get-tuple-element.13), channel_id=1, source_target_pairs={{0,64},{64,0},{1,65},{65,1},{2,66},{66,2},{3,67},{67,3},{4,68},{68... | collective-permute-start | bytes 3932168 | tf_op jit(solution)/shard_map/ppermute | solution.py:21
  133.3 1.1 copy-start
  134.4 28.3 %all-to-all-start.2 = ((bf16[4,1280,128]{2,1,0:T(8,128)(2,1)}), bf16[4,1280,128]{2,1,0:T(8,128)(2,1)}, u32[]{:S(2)}, u32[]{:S(2)}) async-start(bf16[4,1280,128]{2,1,0:T(8,128)(2,1)} %copy-done), calls=%async_computation.2 | async-start | bytes 2621440 | tf_op jit(solution)/shard_map/all_to_all | solution.py:25
  138.7 1.3 copy-start.4
  144.1 18.5 %copy-start.7 = (bf16[1024,512]{1,0:T(8,128)(2,1)}, bf16[1024,512]{1,0:T(8,128)(2,1)S(1)}, u32[]{:S(2)}) copy-start(bf16[1024,512]{1,0:T(8,128)(2,1)S(1)} %get-tuple-element.21.refs_3_) | copy-start | bytes 3145732
  144.1 4.0 %collective-permute-start.5 = (bf16[4,576,128]{2,1,0:T(8,128)(2,1)S(1)}, bf16[4,576,128]{2,1,0:T(8,128)(2,1)S(1)}, u32[]{:S(2)}, u32[]{:S(2)}) collective-permute-start(bf16[4,576,128]{2,1,0:T(8,128)(2,1)S(1)} %get-tuple-element.16), channel_id=1, source_target_pairs={{0,64},{64,0},{1,65},{65,1},{2,66},{66,2},{3,67},{67,3},{4,68},{68... | collective-permute-start | bytes 1769480 | tf_op jit(solution)/shard_map/ppermute | solution.py:21
  148.3 12.9 %collective-permute-start.6 = (bf16[576,128]{1,0:T(8,128)(2,1)S(1)}, bf16[576,128]{1,0:T(8,128)(2,1)S(1)}, u32[]{:S(2)}, u32[]{:S(2)}) collective-permute-start(bf16[576,128]{1,0:T(8,128)(2,1)S(1)} %get-tuple-element.18), channel_id=1, source_target_pairs={{0,128},{128,256},{256,384},{384,0},{1,129},{129,257},{257,385},{3... | collective-permute-start | bytes 442376 | tf_op jit(solution)/shard_map/ppermute | solution.py:17
  152.0 10.4 %collective-permute-start.7 = (bf16[576,128]{1,0:T(8,128)(2,1)S(1)}, bf16[576,128]{1,0:T(8,128)(2,1)S(1)}, u32[]{:S(2)}, u32[]{:S(2)}) collective-permute-start(bf16[576,128]{1,0:T(8,128)(2,1)S(1)} %get-tuple-element.19), channel_id=1, source_target_pairs={{0,256},{128,384},{256,0},{384,128},{1,257},{129,385},{257,1},{385... | collective-permute-start | bytes 442376 | tf_op jit(solution)/shard_map/ppermute | solution.py:17
  156.3 6.3 %collective-permute-start.8 = (bf16[576,128]{1,0:T(8,128)(2,1)S(1)}, bf16[576,128]{1,0:T(8,128)(2,1)S(1)}, u32[]{:S(2)}, u32[]{:S(2)}) collective-permute-start(bf16[576,128]{1,0:T(8,128)(2,1)S(1)} %get-tuple-element.20), channel_id=1, source_target_pairs={{0,384},{128,0},{256,128},{384,256},{1,385},{129,1},{257,129},{385... | collective-permute-start | bytes 442376 | tf_op jit(solution)/shard_map/ppermute | solution.py:17
  165.2 39.9 %all-to-all-start.3 = ((bf16[64,24,128]{2,1,0:T(8,128)(2,1)}), bf16[64,24,128]{2,1,0:T(8,128)(2,1)S(1)}, u32[]{:S(2)}, u32[]{:S(2)}) async-start(bf16[64,24,128]{2,1,0:T(8,128)(2,1)} %shard_map.77), calls=%async_computation.3 | async-start | bytes 786432 | tf_op jit(solution)/shard_map/all_to_all | solution.py:25
  171.7 11.0 %collective-permute-start.9 = (bf16[576,128]{1,0:T(8,128)(2,1)S(1)}, bf16[576,128]{1,0:T(8,128)(2,1)S(1)}, u32[]{:S(2)}, u32[]{:S(2)}) collective-permute-start(bf16[576,128]{1,0:T(8,128)(2,1)S(1)} %shard_map.76.after_ref), channel_id=1, source_target_pairs={{0,128},{128,256},{256,384},{384,0},{1,129},{129,257},{257,385},{3... | collective-permute-start | bytes 442376 | tf_op jit(solution)/shard_map/ppermute | solution.py:17
  176.5 7.7 %collective-permute-start.10 = (bf16[576,128]{1,0:T(8,128)(2,1)S(1)}, bf16[576,128]{1,0:T(8,128)(2,1)S(1)}, u32[]{:S(2)}, u32[]{:S(2)}) collective-permute-start(bf16[576,128]{1,0:T(8,128)(2,1)S(1)} %shard_map.76.after_ref), channel_id=1, source_target_pairs={{0,256},{128,384},{256,0},{384,128},{1,257},{129,385},{257,1},{385... | collective-permute-start | bytes 442376 | tf_op jit(solution)/shard_map/ppermute | solution.py:17
  179.1 6.9 %collective-permute-start.11 = (bf16[576,128]{1,0:T(8,128)(2,1)S(1)}, bf16[576,128]{1,0:T(8,128)(2,1)S(1)}, u32[]{:S(2)}, u32[]{:S(2)}) collective-permute-start(bf16[576,128]{1,0:T(8,128)(2,1)S(1)} %shard_map.76.after_ref), channel_id=1, source_target_pairs={{0,384},{128,0},{256,128},{384,256},{1,385},{129,1},{257,129},{385... | collective-permute-start | bytes 442376 | tf_op jit(solution)/shard_map/ppermute | solution.py:17
  186.0 6.5 %copy-start.8 = (bf16[1024,512]{1,0:T(8,128)(2,1)S(1)}, bf16[1024,512]{1,0:T(8,128)(2,1)}, u32[]{:S(2)}) copy-start(bf16[1024,512]{1,0:T(8,128)(2,1)} %copy-done.7) | copy-start | bytes 3145732
  186.1 6.5 %collective-permute-start.12 = (bf16[4,576,128]{2,1,0:T(8,128)(2,1)S(1)}, bf16[4,576,128]{2,1,0:T(8,128)(2,1)S(1)}, u32[]{:S(2)}, u32[]{:S(2)}) collective-permute-start(bf16[4,576,128]{2,1,0:T(8,128)(2,1)S(1)} %pad_maximum_fusion.1.refs_1_), channel_id=1, source_target_pairs={{0,64},{64,0},{1,65},{65,1},{2,66},{66,2},{3,67},{67,3},{4,68},{68... | collective-permute-start | bytes 1769480 | tf_op jit(solution)/shard_map/ppermute | solution.py:21

commit v5 on v4

v5 whole, which is shorter than its diff:
```python
import jax
import jax.numpy as jnp
from jax import lax
from jax.experimental import pallas as pl
from jax.experimental.pallas import tpu as pltpu
from jax.sharding import Mesh, PartitionSpec as P

EXPERT = ("x", "z")
MIB = 1024 * 1024
BF16 = jnp.bfloat16
F32 = jnp.float32
SMEM = pl.BlockSpec(memory_space=pltpu.SMEM)
LOOSE = pl.BlockSpec(memory_space=pl.ANY)
HBM = pl.BlockSpec(memory_space=pltpu.HBM)


def shift_y(value, step, size):
    return lax.ppermute(value, "y", [(i, (i + step) % size) for i in range(size)])


def swap_y(value, flip, size):
    return lax.ppermute(value, "y", [(i, i ^ flip) for i in range(size)])


def swap_core(value):
    return lax.ppermute(value, "c", [(0, 1), (1, 0)])


def exchange(value, axes):
    return lax.all_to_all(value, axes, split_axis=0, concat_axis=0, tiled=True)


def nt_dot(left, right):
    return lax.dot_general(left, right, (((1,), (1,)), ((), ())), preferred_element_type=F32)


def nn_dot(left, right):
    return jnp.dot(left, right, preferred_element_type=F32)


def one_hot(rows, index):
    return jnp.where(rows == index, 1.0, 0.0).astype(BF16)


def row_numbers(count):
    return lax.broadcasted_iota(jnp.int32, (count, 1), 0)


def lane_numbers(count):
    return lax.broadcasted_iota(jnp.int32, (1, count), 1)


def send_scaled_kernel(main_ref, left_ref, scaled_ref, out_ref):
    experts = out_ref.shape[0]
    scaled = scaled_ref[...]
    part = nn_dot(one_hot(row_numbers(experts * 16), main_ref[...]), scaled).astype(BF16)
    out_ref[:, 0:16, :] = part.reshape(experts, 16, 128)
    part = nn_dot(one_hot(row_numbers(experts * 8), left_ref[...]), scaled)
    out_ref[:, 16:24, :] = part.reshape(experts, 8, 128).astype(BF16)


def send_grad_kernel(main_ref, late_ref, grad_ref, out_ref):
    experts = out_ref.shape[0]
    tokens, width_part = grad_ref.shape
    blocks = width_part // 128
    grad = grad_ref[...]
    chosen = one_hot(row_numbers(experts * 16), main_ref[...])
    rows = nn_dot(chosen[:, :tokens] + chosen[:, tokens:], grad).astype(BF16)
    for b in range(blocks):
        out_ref[:, 16 * b : 16 * (b + 1), :] = rows[:, b * 128 : (b + 1) * 128].reshape(experts, 16, 128)
    number = row_numbers(experts * 16)
    chosen = one_hot((number & -16) + (number & 3), late_ref[...])
    rows = nn_dot(chosen[:, :tokens] + chosen[:, tokens:], grad)
    column = (number >> 2) & 3
    total = rows[:, 0:128]
    for b in range(1, blocks):
        total = jnp.where(column == b, rows[:, b * 128 : (b + 1) * 128], total)
    out_ref[:, 16 * blocks :, :] = total.astype(BF16).reshape(experts, 16, 128)


def unpack_kernel(got_ref, out_ref):
    experts = got_ref.shape[0]
    out_ref[: experts * 16] = got_ref[:, 0:16, :].reshape(experts * 16, 128)
    tail = got_ref[:, 16:24, :].astype(F32).reshape(experts * 8, 128).astype(BF16)
    number = row_numbers(experts * 4)
    take = one_hot((number >> 2) * 8 + (number & 3), lane_numbers(experts * 8))
    out_ref[experts * 16 :] = nn_dot(take, tail).astype(BF16)


def turn_kernel(spot_ref, own_ref, other_ref, out_ref):
    blocks = out_ref.shape[0] // 128
    y_size = blocks // 2
    for d in range(blocks):
        spot = spot_ref[d]

        @pl.when(spot < y_size)
        def _():
            out_ref[d * 128 : (d + 1) * 128, :] = own_ref[spot].T

        @pl.when(spot >= y_size)
        def _():
            out_ref[d * 128 : (d + 1) * 128, :] = other_ref[spot - y_size].T


def core_kernel(
    spot_ref, got_hbm, weight_hbm, turned_hbm, after_ref,
    own_ref, other_ref, gradb_hbm, pack_own_ref, pack_other_ref,
    rows_ref, got_ref, weight_ref, turned_ref, gradb_ref, sems,
):
    fetch_got = pltpu.make_async_copy(got_hbm, got_ref, sems.at[0])
    fetch_weight = pltpu.make_async_copy(weight_hbm, weight_ref, sems.at[1])
    fetch_turned = pltpu.make_async_copy(turned_hbm, turned_ref, sems.at[2])
    fetch_got.start()
    fetch_weight.start()
    fetch_turned.start()
    experts = got_ref.shape[0]
    columns = rows_ref.shape[1] // 128
    blocks = weight_ref.shape[0] // 128
    y_size = blocks // 2
    half = blocks // 2
    number = row_numbers(256)
    order = one_hot(((number >> 2) & 15) * 16 + (number >> 6) * 4 + (number & 3), lane_numbers(256))
    fetch_got.wait()
    for b in range(columns):
        rows_ref[: experts * 16, b * 128 : (b + 1) * 128] = got_ref[:, 16 * b : 16 * (b + 1), :].reshape(
            experts * 16, 128
        )
    for s in range(experts // 16):
        late = nn_dot(order, got_ref[16 * s : 16 * (s + 1), 16 * columns :, :].reshape(256, 128)).astype(BF16)
        for b in range(columns):
            rows_ref[experts * 16 + s * 64 : experts * 16 + (s + 1) * 64, b * 128 : (b + 1) * 128] = late[
                b * 64 : (b + 1) * 64
            ]
    rows = rows_ref[...]

    fetch_weight.wait()
    term = nt_dot(rows, weight_ref[...]).astype(BF16)
    core = spot_ref[blocks]

    def put_terms(own, other):
        for k in range(y_size):
            own_ref[k] = term[:, (2 * k + own) * 128 : (2 * k + own + 1) * 128]
            other_ref[k] = term[:, (2 * k + other) * 128 : (2 * k + other + 1) * 128]

    @pl.when(core == 0)
    def _():
        put_terms(0, 1)

    @pl.when(core != 0)
    def _():
        put_terms(1, 0)

    fetch_turned.wait()
    gradb = nn_dot(turned_ref[...], rows).astype(BF16)
    gradb_ref[...] = gradb
    store_grad = pltpu.make_async_copy(gradb_ref, gradb_hbm, sems.at[3])
    store_grad.start()
    gram = nt_dot(gradb, gradb).astype(BF16)
    for d in range(blocks):
        i = d % half
        top = i * 128 + (64 if d >= half else 0)
        spot = spot_ref[d]

        def put(ref, at):
            for k in range(half):
                j = (d + k) % blocks
                ref[at, k * 128 : (k + 1) * 128, :] = gram[d * 128 : (d + 1) * 128, j * 128 : (j + 1) * 128]
            ref[at, half * 128 :, :] = gram[top : top + 64, (i + half) * 128 : (i + half + 1) * 128]

        @pl.when(spot < y_size)
        def _():
            put(pack_own_ref, spot)

        @pl.when(spot >= y_size)
        def _():
            put(pack_other_ref, spot - y_size)

    store_grad.wait()


def add_kernel(own_ref, other_ref, out_ref):
    out_ref[...] = (own_ref[...].astype(F32) + other_ref[...].astype(F32)).astype(BF16)


def pack_add_kernel(own_ref, other_ref, keep_ref, send_ref):
    near = keep_ref.shape[0]
    keep_ref[...] = (own_ref[:near].astype(F32) + other_ref[:near].astype(F32)).astype(BF16)
    send_ref[...] = (own_ref[near:].astype(F32) + other_ref[near:].astype(F32)).astype(BF16)


def pack_pair_kernel(keep_ref, got_ref, mine_ref, send_ref):
    mine_ref[...] = (keep_ref[0].astype(F32) + got_ref[0].astype(F32)).astype(BF16)
    send_ref[...] = (keep_ref[1].astype(F32) + got_ref[1].astype(F32)).astype(BF16)


def return_kernel(part_ref, after_ref, out_ref):
    experts = out_ref.shape[0]
    total = part_ref[0].astype(F32)
    for k in range(1, part_ref.shape[0]):
        total = total + part_ref[k].astype(F32)
    total = total.astype(BF16)
    out_ref[:, 0:16, :] = total[: experts * 16].reshape(experts, 16, 128)
    number = row_numbers(128)
    take = one_hot(jnp.where((number & 7) < 4, (number >> 3) * 4 + (number & 7), -1), lane_numbers(64))
    for s in range(experts // 16):
        left = nn_dot(take, total[experts * 16 + s * 64 : experts * 16 + (s + 1) * 64])
        out_ref[16 * s : 16 * (s + 1), 16:24, :] = left.reshape(16, 8, 128).astype(BF16)


def ortho_kernel(
    width, spot_ref, own_near_ref, own_far_ref, other_near_ref, other_far_ref, gradb_hbm, out_ref,
    gram_ref, pack_ref, gradb_ref, sem,
):
    fetch_grad = pltpu.make_async_copy(gradb_hbm, gradb_ref, sem)
    fetch_grad.start()
    blocks = gram_ref.shape[0] // 128
    half = blocks // 2
    squares = jnp.zeros((8, 128), F32)
    for i, ref in enumerate((own_near_ref, own_far_ref, other_near_ref, other_far_ref)):
        for k in range(2):
            pack = ref[k]
            pack_ref[2 * i + k] = pack
            square = pack.astype(F32)
            square = square * square
            squares = squares + 2.0 * jnp.sum(square.reshape(-1, 8, 128), axis=0)
            squares = squares - jnp.sum(square[:128].reshape(-1, 8, 128), axis=0)
    norm_sq = jnp.sqrt(jnp.sum(squares, keepdims=True)) + 1e-06
    for d in range(blocks):
        spot = spot_ref[d]
        rows = slice(d * 128, (d + 1) * 128)
        for k in range(half):
            lanes = slice((d + k) % blocks * 128, ((d + k) % blocks + 1) * 128)
            block = pack_ref[spot, k * 128 : (k + 1) * 128, :]
            gram_ref[rows, lanes] = block
            if k > 0:
                gram_ref[lanes, rows] = block.T
        i = d % half
        top = i * 128 + (64 if d >= half else 0)
        gram_ref[top : top + 64, (i + half) * 128 : (i + half + 1) * 128] = pack_ref[spot, half * 128 :, :]
    for i in range(half):
        upper = gram_ref[i * 128 : (i + 1) * 128, (i + half) * 128 : (i + half + 1) * 128]
        gram_ref[(i + half) * 128 : (i + half + 1) * 128, i * 128 : (i + 1) * 128] = upper.T

    inverse = 1.0 / norm_sq
    gram = gram_ref[...]
    fetch_grad.wait()
    first = (gradb_ref[...].astype(F32) * lax.rsqrt(norm_sq)).astype(BF16)

    def apply(value):
        return nn_dot(gram, value) * inverse

    second = (1.5 * first.astype(F32) - 0.5 * apply(first)).astype(BF16)
    power_one = apply(second).astype(BF16)
    power_two = apply(power_one).astype(BF16)
    power_three = apply(power_two)
    total = 1.5 * second.astype(F32)
    total = total - 0.5 * (2.25 * power_one.astype(F32) - 1.5 * power_two.astype(F32) + 0.25 * power_three)
    out_ref[0] = total * width**0.5


def in_hbm(value):
    return pltpu.with_memory_space_constraint(value, pltpu.HBM)


def whole(value):
    return pl.BlockSpec(value.shape, lambda *_: (0,) * len(value.shape))


def call(kernel, outs, ins, scratch=(), vmem=24, steps=(), specs=None, out_specs=None):
    specs = specs or {}
    out_specs = out_specs or {}
    flat, tree = jax.tree.flatten(outs)
    return pl.pallas_call(
        kernel,
        out_shape=outs,
        grid=steps,
        in_specs=[specs.get(i, whole(value)) for i, value in enumerate(ins)],
        out_specs=jax.tree.unflatten(tree, [out_specs.get(i, whole(value)) for i, value in enumerate(flat)]),
        scratch_shapes=list(scratch),
        compiler_params=pltpu.CompilerParams(vmem_limit_bytes=vmem * MIB),
    )(*ins)


def per_device(grad_out, hidden, gate_prob, expert_ids, weights):
    tokens, width_part = grad_out.shape
    top_count = expert_ids.shape[1]
    unit_part = hidden.shape[2]
    units = weights.shape[1]
    experts = lax.axis_size("x") * lax.axis_size("z")
    y_size = lax.axis_size("y")
    dp = y_size * 2
    width = width_part * dp
    capacity = 5 * tokens * top_count // (4 * experts)
    total_slots = experts * capacity
    pair_count = tokens * top_count
    y = lax.axis_index("y")
    c = lax.axis_index("c")
    block = jnp.arange(dp, dtype=jnp.int32)
    other_core = (block % 2) ^ c
    flip = y ^ (block // 2)
    pair_spot = other_core * y_size + (flip ^ (flip >> 1))
    came_from = other_core * y_size + (y - block // 2) % y_size
    core = jnp.full((1,), c)
    pair_spots = jnp.concatenate([pair_spot, core]).astype(jnp.int32)

    flat_ids = expert_ids.T.reshape(1, pair_count)
    named = (jnp.arange(experts, dtype=jnp.int32)[:, None] == flat_ids).astype(BF16)
    order = jnp.arange(pair_count, dtype=jnp.int32)
    earlier = (order[:, None] < order[None, :]).astype(BF16)
    before = jnp.dot(named, earlier, preferred_element_type=F32)
    rank_in = jnp.sum(before * named.astype(F32), axis=0, keepdims=True).astype(jnp.int32)
    late = rank_in >= 16
    main_index = jnp.where(late, -1, flat_ids * 16 + rank_in)
    left_index = jnp.where(late, flat_ids * 8 + rank_in - 16, -1)
    late_index = jnp.where(late, flat_ids * 16 + rank_in - 16, -1)

    scaled_part = (gate_prob[:, :, None] * hidden.astype(F32)).astype(BF16)
    scaled_part = scaled_part.transpose(1, 0, 2).reshape(pair_count, unit_part)
    columns = width_part // 128

    def shape(*dims):
        return jax.ShapeDtypeStruct(dims, BF16)

    got_scaled = exchange(
        call(send_scaled_kernel, shape(experts, 24, 128), (main_index, left_index, scaled_part)), EXPERT
    )
    got = exchange(
        call(send_grad_kernel, shape(experts, 20 * columns, 128), (main_index, late_index, grad_out)), EXPERT
    )

    scaled = call(unpack_kernel, shape(total_slots, unit_part), (got_scaled,), vmem=8)
    gathered = jnp.stack([scaled] + [shift_y(scaled, k, y_size) for k in range(1, y_size)])
    turned = call(
        turn_kernel, pltpu.HBM((units, total_slots), BF16), (came_from.astype(jnp.int32), gathered, swap_core(gathered)),
        specs={0: SMEM},
        vmem=20,
    )

    slot_index = flat_ids.reshape(pair_count, 1) * 24 + rank_in.reshape(pair_count, 1)
    chosen = (slot_index == jnp.arange(experts * 24, dtype=jnp.int32)[None, :]).astype(BF16)
    chosen = lax.optimization_barrier(chosen)

    dp_parts = shape(y_size, total_slots, unit_part)
    packs = shape(y_size, units // 2 + 64, 128)
    term_own, term_other, grad_bf16, pack_own, pack_other = call(
        core_kernel,
        (dp_parts, dp_parts, pltpu.HBM((units, width_part), BF16), pltpu.HBM(packs.shape, BF16), packs),
        (pair_spots, in_hbm(got), in_hbm(weights[0]), in_hbm(turned), chosen),
        (
            pltpu.VMEM((total_slots, width_part), BF16),
            pltpu.VMEM(got.shape, BF16),
            pltpu.VMEM((units, width_part), BF16),
            pltpu.VMEM((units, total_slots), BF16),
            pltpu.VMEM((units, width_part), BF16),
            pltpu.SemaphoreType.DMA((4,)),
        ),
        specs={0: SMEM, 1: HBM, 2: HBM, 3: HBM, 4: LOOSE},
        out_specs={2: HBM},
        vmem=32,
    )
    pack_swapped = swap_core(pack_other)
    piece = pl.BlockSpec((1, total_slots, 128), lambda i: (i, 0, 0))
    both = call(
        add_kernel,
        pltpu.HBM(dp_parts.shape, BF16),
        (term_own, swap_core(term_other)),
        steps=(y_size,),
        specs={0: piece, 1: piece},
        out_specs={0: piece},
        vmem=8,
    )
    parts = exchange(both, "y")

    pack = shape(units // 2 + 64, 128)
    pair = shape(2, units // 2 + 64, 128)
    keep, send = call(pack_add_kernel, (pair, pair), (in_hbm(pack_own), pack_swapped), vmem=8)
    mine, send = call(pack_pair_kernel, (pack, pack), (keep, swap_y(send, 3, y_size)), vmem=8)
    mine = call(add_kernel, pack, (mine, swap_y(send, 1, y_size)), vmem=8)

    returned = exchange(
        call(return_kernel, shape(experts, 24, 128), (parts, mine), specs={1: LOOSE}, vmem=12), EXPERT
    ).reshape(experts * 24, unit_part)
    picked = jnp.dot(chosen, returned, preferred_element_type=F32)
    picked = picked.reshape(top_count, tokens, unit_part).transpose(1, 0, 2)
    hidden_grad = (gate_prob[:, :, None] * picked).astype(BF16)

    near = jnp.stack([mine, swap_y(mine, 1, y_size)])
    far = swap_y(near, 3, y_size)
    update = call(
        lambda *refs: ortho_kernel(width, *refs),
        jax.ShapeDtypeStruct((1, units, width_part), F32),
        (pair_spots, near, far, swap_core(near), swap_core(far), in_hbm(grad_bf16)),
        (
            pltpu.VMEM((units, units), BF16),
            pltpu.VMEM((dp, units // 2 + 64, 128), BF16),
            pltpu.VMEM((units, width_part), BF16),
            pltpu.SemaphoreType.DMA,
        ),
        specs={0: SMEM, 5: HBM},
        vmem=32,
    )
    return (hidden_grad, update)


def solution(mesh):
    dp, experts = mesh.devices.shape
    x_size = 4
    split = Mesh(
        mesh.devices.reshape(dp // 2, 2, x_size, experts // x_size), ("y", "c", "x", "z")
    )
    rows, cols = ("x", "z"), ("y", "c")
    in_specs = (P(rows, cols), P(rows, None, cols), P(rows, None), P(rows, None), P(rows, None, cols))
    out_specs = (P(rows, None, cols), P(rows, None, cols))
    return jax.shard_map(per_device, mesh=split, in_specs=in_specs, out_specs=out_specs, check_vma=False)
```

time: 208 us -> 215 us (1.034)
  waiting for transfers between devices: 71.1 us -> 92.8 us
  local copies, waits for them, and re-layouts: 9.89 us -> 1.69 us
  starting transfers between devices: 90.3 us -> 82.2 us
    ppermute x0 -> x4, waiting for transfers between devices: none -> 26.5 us  [swap_y(): return lax.ppermute(value, 'y', [(i, i ^ flip) for i in range(size)])]
    ppermute x9 -> x3, starting transfers between devices: 32.2 us -> 9.5 us  [shift_y(): lax.ppermute(value, 'y', [(i, (i + step) % size) for i in range(size)])]
    ppermute x0 -> x4, starting transfers between devices: none -> 11 us  [swap_y(): return lax.ppermute(value, 'y', [(i, i ^ flip) for i in range(size)])]
    unnamed x28 -> x10, local copies, waits for them, and re-layouts: 9.89 us -> 1.69 us
    ppermute x4 -> x5, starting transfers between devices: 20.4 us -> 23.9 us  [swap_core(): return lax.ppermute(value, 'c', [(0, 1), (1, 0)])]
    ppermute x9 -> x3, waiting for transfers between devices: 17.6 us -> 15.3 us  [shift_y(): lax.ppermute(value, 'y', [(i, (i + step) % size) for i in range(size)])]
    ppermute x4 -> x5, waiting for transfers between devices: 5.93 us -> 4.18 us  [swap_core(): return lax.ppermute(value, 'c', [(0, 1), (1, 0)])]
  transfers between devices with their start and end apart: 17 -> 16, of which waited for: 13 -> 12; matrix products, arithmetic and copies ran while one was open for 1% -> 1% of each run, Pallas kernels for 10% -> 8%
where the time goes in v5:
time: 215 us; the launch traced here: 214 us
  waiting for transfers between devices  92.8 us (43%)
  starting transfers between devices  82.2 us (38%)
  Pallas kernels  30.7 us (14%)
  other arithmetic  2.91 us (1%)
  matrix products  2.36 us (1%)
    all_to_all x4, waiting for transfers between devices, exchange(): return lax.all_to_all(value, axes, split_axis=0, concat_axis=0, tiled=True)  46.9 us
    all_to_all x4, starting transfers between devices, exchange(): return lax.all_to_all(value, axes, split_axis=0, concat_axis=0, tiled=True)  37.8 us
    pallas_call x11, Pallas kernels, call(): pl.pallas_call(kernel, out_shape=outs, grid=steps, in_specs=[specs.get(i,...  30.7 us
    ppermute x4, waiting for transfers between devices, swap_y(): return lax.ppermute(value, 'y', [(i, i ^ flip) for i in range(size)])  26.5 us
    ppermute x5, starting transfers between devices, swap_core(): return lax.ppermute(value, 'c', [(0, 1), (1, 0)])  23.9 us
    ppermute x3, waiting for transfers between devices, shift_y(): lax.ppermute(value, 'y', [(i, (i + step) % size) for i in range(size)])  15.3 us
    ppermute x4, starting transfers between devices, swap_y(): return lax.ppermute(value, 'y', [(i, i ^ flip) for i in range(size)])  11 us
    ppermute x3, starting transfers between devices, shift_y(): lax.ppermute(value, 'y', [(i, (i + step) % size) for i in range(size)])  9.5 us
  transfers between devices with their start and end apart: 16, of which 12 were waited for; matrix products, arithmetic and copies ran while one was open for 1% of the time, Pallas kernels for 8%

profile of v5, /device:TPU:1, one launch (start us, length us, event | category | flops | bytes accessed | tf_op | source)
XLA Modules:
  0.0 213.6 jit_solution(7243576734881721190)
XLA Ops:
  2.8 1.7 shard_map.69
  4.5 19.1 %all-to-all-start.1 = ((bf16[64,24,128]{2,1,0:T(8,128)(2,1)}), bf16[64,24,128]{2,1,0:T(8,128)(2,1)S(1)}, u32[]{:S(2)}, u32[]{:S(2)}) async-start(bf16[64,24,128]{2,1,0:T(8,128)(2,1)} %shard_map.69), calls=%async_computation.1 | async-start | bytes 786432 | tf_op jit(solution)/shard_map/all_to_all | solution.py:30
  23.6 2.4 %shard_map.68 = bf16[64,80,128]{2,1,0:T(8,128)(2,1)} custom-call(s32[1,1024]{1,0:T(1,128)S(1)} %get-tuple-element.23.main_ref, s32[1,1024]{1,0:T(1,128)S(1)} %get-tuple-element.22.late_ref, bf16[512,512]{1,0:T(8,128)(2,1)S(1)} %copy-done), custom_call_target="tpu_custom_call" | custom-call | tf_op jit(solution)/shard_map/pallas_call | solution.py:273
  26.0 22.3 %all-to-all-done.1.got_ref = bf16[64,24,128]{2,1,0:T(8,128)(2,1)S(1)} async-done(((bf16[64,24,128]{2,1,0:T(8,128)(2,1)}), bf16[64,24,128]{2,1,0:T(8,128)(2,1)S(1)}, u32[]{:S(2)}, u32[]{:S(2)}) %all-to-all-start.1) | async-done | bytes 393248 | tf_op jit(solution)/shard_map/all_to_all | solution.py:30
  48.4 7.8 %all-to-all-start = ((bf16[64,80,128]{2,1,0:T(8,128)(2,1)}), bf16[64,80,128]{2,1,0:T(8,128)(2,1)}, u32[]{:S(2)}, u32[]{:S(2)}) async-start(bf16[64,80,128]{2,1,0:T(8,128)(2,1)} %shard_map.68), calls=%async_computation | async-start | bytes 2621440 | tf_op jit(solution)/shard_map/all_to_all | solution.py:30
  56.4 4.6 %collective-permute-start.2 = (bf16[1280,128]{1,0:T(8,128)(2,1)S(1)}, bf16[1280,128]{1,0:T(8,128)(2,1)S(1)}, u32[]{:S(2)}, u32[]{:S(2)}) collective-permute-start(bf16[1280,128]{1,0:T(8,128)(2,1)S(1)} %shard_map.70), channel_id=1, source_target_pairs={{0,384},{128,0},{256,128},{384,256},{1,385},{129,1},{257,129},{385... | collective-permute-start | bytes 983048 | tf_op jit(solution)/shard_map/ppermute | solution.py:18
  61.1 2.3 %collective-permute-start.1 = (bf16[1280,128]{1,0:T(8,128)(2,1)S(1)}, bf16[1280,128]{1,0:T(8,128)(2,1)S(1)}, u32[]{:S(2)}, u32[]{:S(2)}) collective-permute-start(bf16[1280,128]{1,0:T(8,128)(2,1)S(1)} %shard_map.70), channel_id=1, source_target_pairs={{0,256},{128,384},{256,0},{384,128},{1,257},{129,385},{257,1},{385... | collective-permute-start | bytes 983048 | tf_op jit(solution)/shard_map/ppermute | solution.py:18
  63.3 2.6 %collective-permute-start = (bf16[1280,128]{1,0:T(8,128)(2,1)S(1)}, bf16[1280,128]{1,0:T(8,128)(2,1)S(1)}, u32[]{:S(2)}, u32[]{:S(2)}) collective-permute-start(bf16[1280,128]{1,0:T(8,128)(2,1)S(1)} %shard_map.70), channel_id=1, source_target_pairs={{0,128},{128,256},{256,384},{384,0},{1,129},{129,257},{257,385},{3... | collective-permute-start | bytes 983048 | tf_op jit(solution)/shard_map/ppermute | solution.py:18
  67.5 4.4 %collective-permute-done.1 = bf16[1280,128]{1,0:T(8,128)(2,1)S(1)} collective-permute-done((bf16[1280,128]{1,0:T(8,128)(2,1)S(1)}, bf16[1280,128]{1,0:T(8,128)(2,1)S(1)}, u32[]{:S(2)}, u32[]{:S(2)}) %collective-permute-start.1) | collective-permute-done | bytes 327712 | tf_op jit(solution)/shard_map/ppermute | solution.py:18
  72.0 9.2 %collective-permute-done = bf16[1280,128]{1,0:T(8,128)(2,1)S(1)} collective-permute-done((bf16[1280,128]{1,0:T(8,128)(2,1)S(1)}, bf16[1280,128]{1,0:T(8,128)(2,1)S(1)}, u32[]{:S(2)}, u32[]{:S(2)}) %collective-permute-start) | collective-permute-done | bytes 327712 | tf_op jit(solution)/shard_map/ppermute | solution.py:18
  82.5 2.3 %collective-permute-start.3 = (bf16[4,1280,128]{2,1,0:T(8,128)(2,1)}, bf16[4,1280,128]{2,1,0:T(8,128)(2,1)}, u32[]{:S(2)}, u32[]{:S(2)}) collective-permute-start(bf16[4,1280,128]{2,1,0:T(8,128)(2,1)} %pad_maximum_fusion.own_ref), channel_id=1, source_target_pairs={{0,64},{64,0},{1,65},{65,1},{2,66},{66,2},{3,67},{67,3},{4,68},{68... | collective-permute-start | bytes 3932168 | tf_op jit(solution)/shard_map/ppermute | solution.py:26
  85.5 2.3 %collective-permute-done.3.other_ref = bf16[4,1280,128]{2,1,0:T(8,128)(2,1)} collective-permute-done((bf16[4,1280,128]{2,1,0:T(8,128)(2,1)}, bf16[4,1280,128]{2,1,0:T(8,128)(2,1)}, u32[]{:S(2)}, u32[]{:S(2)}) %collective-permute-start.3) | collective-permute-done | bytes 1310752 | tf_op jit(solution)/shard_map/ppermute | solution.py:26
  87.7 4.4 %shard_map.71.turned_hbm = bf16[1024,1280]{1,0:T(8,128)(2,1)} custom-call(s32[8]{0:T(128)S(1)} %get-tuple-element.27.spot_ref, bf16[4,1280,128]{2,1,0:T(8,128)(2,1)} %pad_maximum_fusion.own_ref, bf16[4,1280,128]{2,1,0:T(8,128)(2,1)} %collective-permute-done.3.other_ref), custom_call_target="tpu_custom_call" | custom-call | tf_op jit(solution)/shard_map/pallas_call | solution.py:273
  92.1 24.5 %all-to-all-done.got_hbm = bf16[64,80,128]{2,1,0:T(8,128)(2,1)} async-done(((bf16[64,80,128]{2,1,0:T(8,128)(2,1)}), bf16[64,80,128]{2,1,0:T(8,128)(2,1)}, u32[]{:S(2)}, u32[]{:S(2)}) %all-to-all-start) | async-done | bytes 1310752 | tf_op jit(solution)/shard_map/all_to_all | solution.py:30
  116.6 8.6 %shard_map.72 = (bf16[4,1280,128]{2,1,0:T(8,128)(2,1)S(1)}, bf16[4,1280,128]{2,1,0:T(8,128)(2,1)S(1)}, bf16[1024,512]{1,0:T(8,128)(2,1)}, bf16[4,576,128]{2,1,0:T(8,128)(2,1)}, bf16[4,576,128]{2,1,0:T(8,128)(2,1)}) custom-call(s32[9]{0:T(128)S(1)} %pad_add_fusion.spot_ref.refs_0_, bf16[64,80,128]{2,1,0:T(8,128)(2,1)} %all-to-all-done.got_hbm, ...), custom_call_target="tpu_custom_call" | custom-call | tf_op jit(solution)/shard_map/pallas_call | solution.py:273
  125.2 7.6 %collective-permute-start.4 = (bf16[4,1280,128]{2,1,0:T(8,128)(2,1)S(1)}, bf16[4,1280,128]{2,1,0:T(8,128)(2,1)S(1)}, u32[]{:S(2)}, u32[]{:S(2)}) collective-permute-start(bf16[4,1280,128]{2,1,0:T(8,128)(2,1)S(1)} %get-tuple-element.12), channel_id=1, source_target_pairs={{0,64},{64,0},{1,65},{65,1},{2,66},{66,2},{3,67},{67,3},{4,68},{68... | collective-permute-start | bytes 3932168 | tf_op jit(solution)/shard_map/ppermute | solution.py:26
  132.8 1.9 collective-permute-start.5
  135.4 1.7 shard_map.73
  137.2 4.3 %all-to-all-start.2 = ((bf16[4,1280,128]{2,1,0:T(8,128)(2,1)}), bf16[4,1280,128]{2,1,0:T(8,128)(2,1)}, u32[]{:S(2)}, u32[]{:S(2)}) async-start(bf16[4,1280,128]{2,1,0:T(8,128)(2,1)} %shard_map.73), calls=%async_computation.2 | async-start | bytes 2621440 | tf_op jit(solution)/shard_map/all_to_all | solution.py:30
  142.9 4.6 %collective-permute-start.6 = (bf16[2,576,128]{2,1,0:T(8,128)(2,1)S(1)}, bf16[2,576,128]{2,1,0:T(8,128)(2,1)S(1)}, u32[]{:S(2)}, u32[]{:S(2)}) collective-permute-start(bf16[2,576,128]{2,1,0:T(8,128)(2,1)S(1)} %get-tuple-element.16), channel_id=1, source_target_pairs={{0,384},{128,256},{256,128},{384,0},{1,385},{129,257},{257,129},{3... | collective-permute-start | bytes 884744 | tf_op jit(solution)/shard_map/ppermute | solution.py:22
  147.5 17.5 %collective-permute-done.6.got_ref = bf16[2,576,128]{2,1,0:T(8,128)(2,1)S(1)} collective-permute-done((bf16[2,576,128]{2,1,0:T(8,128)(2,1)S(1)}, bf16[2,576,128]{2,1,0:T(8,128)(2,1)S(1)}, u32[]{:S(2)}, u32[]{:S(2)}) %collective-permute-start.6) | collective-permute-done | bytes 294944 | tf_op jit(solution)/shard_map/ppermute | solution.py:22
  165.1 1.9 collective-permute-start.7
  167.0 4.0 %collective-permute-done.7.other_ref = bf16[576,128]{1,0:T(8,128)(2,1)S(1)} collective-permute-done((bf16[576,128]{1,0:T(8,128)(2,1)S(1)}, bf16[576,128]{1,0:T(8,128)(2,1)S(1)}, u32[]{:S(2)}, u32[]{:S(2)}) %collective-permute-start.7) | collective-permute-done | bytes 147488 | tf_op jit(solution)/shard_map/ppermute | solution.py:22
  171.0 2.4 %shard_map.77 = bf16[64,24,128]{2,1,0:T(8,128)(2,1)} custom-call(bf16[4,1280,128]{2,1,0:T(8,128)(2,1)} %all-to-all-done.2.part_ref, bf16[576,128]{1,0:T(8,128)(2,1)S(1)} %shard_map.76.after_ref), custom_call_target="tpu_custom_call" | custom-call | tf_op jit(solution)/shard_map/pallas_call | solution.py:273
  173.4 6.6 %all-to-all-start.3 = ((bf16[64,24,128]{2,1,0:T(8,128)(2,1)}), bf16[64,24,128]{2,1,0:T(8,128)(2,1)}, u32[]{:S(2)}, u32[]{:S(2)}) async-start(bf16[64,24,128]{2,1,0:T(8,128)(2,1)} %shard_map.77), calls=%async_computation.3 | async-start | bytes 786432 | tf_op jit(solution)/shard_map/all_to_all | solution.py:30
  180.0 1.9 collective-permute-start.8
  181.9 4.0 %collective-permute-done.8 = bf16[576,128]{1,0:T(8,128)(2,1)S(1)} collective-permute-done((bf16[576,128]{1,0:T(8,128)(2,1)S(1)}, bf16[576,128]{1,0:T(8,128)(2,1)S(1)}, u32[]{:S(2)}, u32[]{:S(2)}) %collective-permute-start.8) | collective-permute-done | bytes 147488 | tf_op jit(solution)/shard_map/ppermute | solution.py:22
  185.9 2.5 %collective-permute-start.9 = (bf16[2,576,128]{2,1,0:T(8,128)(2,1)S(1)}, bf16[2,576,128]{2,1,0:T(8,128)(2,1)S(1)}, u32[]{:S(2)}, u32[]{:S(2)}) collective-permute-start(bf16[2,576,128]{2,1,0:T(8,128)(2,1)S(1)} %pad_maximum_fusion.1.refs_1_), channel_id=1, source_target_pairs={{0,384},{128,256},{256,128},{384,0},{1,385},{129,257},{257,129},{3... | collective-permute-start | bytes 884744 | tf_op jit(solution)/shard_map/ppermute | solution.py:22
  188.5 5.5 %collective-permute-start.10 = (bf16[2,576,128]{2,1,0:T(8,128)(2,1)S(1)}, bf16[2,576,128]{2,1,0:T(8,128)(2,1)S(1)}, u32[]{:S(2)}, u32[]{:S(2)}) collective-permute-start(bf16[2,576,128]{2,1,0:T(8,128)(2,1)S(1)} %pad_maximum_fusion.1.refs_1_), channel_id=1, source_target_pairs={{0,64},{64,0},{1,65},{65,1},{2,66},{66,2},{3,67},{67,3},{4,68},{68... | collective-permute-start | bytes 884744 | tf_op jit(solution)/shard_map/ppermute | solution.py:26
  195.0 6.6 %collective-permute-start.11 = (bf16[2,576,128]{2,1,0:T(8,128)(2,1)S(1)}, bf16[2,576,128]{2,1,0:T(8,128)(2,1)S(1)}, u32[]{:S(2)}, u32[]{:S(2)}) collective-permute-start(bf16[2,576,128]{2,1,0:T(8,128)(2,1)S(1)} %collective-permute-done.9.refs_2_), channel_id=1, source_target_pairs={{0,64},{64,0},{1,65},{65,1},{2,66},{66,2},{3,67},{67,3},{4,68},{68... | collective-permute-start | bytes 884744 | tf_op jit(solution)/shard_map/ppermute | solution.py:26
  202.8 7.9 %shard_map.78 = f32[1,1024,512]{2,1,0:T(8,128)} custom-call(s32[9]{0:T(128)S(1)} %pad_add_fusion.spot_ref.refs_0_, bf16[2,576,128]{2,1,0:T(8,128)(2,1)S(1)} %pad_maximum_fusion.1.refs_1_, bf16[2,576,128]{2,1,0:T(8,128)(2,1)S(1)} %collective-permute-done.9.refs_2_, bf16[2,576,128]{2,1,0:T(8,128)(2,1)S(1)} %collective-permute-done.10.refs_3_, ...), custom_call_target="tpu_custom_call" | custom-call | tf_op jit(solution)/shard_map/pallas_call | solution.py:273
  210.7 2.0 fusion.3
  (33 shorter events, 11.2 us)
Async XLA Ops:
  0.6 1.9 copy-start.2
  0.6 1.9 copy-start.1
  2.5 21.2 %copy-start = (bf16[512,512]{1,0:T(8,128)(2,1)S(1)}, bf16[512,512]{1,0:T(8,128)(2,1)}, u32[]{:S(2)}) copy-start(bf16[512,512]{1,0:T(8,128)(2,1)} %grad_ref.1) | copy-start | bytes 1572868
  4.5 43.9 %all-to-all-start.1 = ((bf16[64,24,128]{2,1,0:T(8,128)(2,1)}), bf16[64,24,128]{2,1,0:T(8,128)(2,1)S(1)}, u32[]{:S(2)}, u32[]{:S(2)}) async-start(bf16[64,24,128]{2,1,0:T(8,128)(2,1)} %shard_map.69), calls=%async_computation.1 | async-start | bytes 786432 | tf_op jit(solution)/shard_map/all_to_all | solution.py:30
  48.4 68.3 %all-to-all-start = ((bf16[64,80,128]{2,1,0:T(8,128)(2,1)}), bf16[64,80,128]{2,1,0:T(8,128)(2,1)}, u32[]{:S(2)}, u32[]{:S(2)}) async-start(bf16[64,80,128]{2,1,0:T(8,128)(2,1)} %shard_map.68), calls=%async_computation | async-start | bytes 2621440 | tf_op jit(solution)/shard_map/all_to_all | solution.py:30
  56.4 11.1 %collective-permute-start.2 = (bf16[1280,128]{1,0:T(8,128)(2,1)S(1)}, bf16[1280,128]{1,0:T(8,128)(2,1)S(1)}, u32[]{:S(2)}, u32[]{:S(2)}) collective-permute-start(bf16[1280,128]{1,0:T(8,128)(2,1)S(1)} %shard_map.70), channel_id=1, source_target_pairs={{0,384},{128,0},{256,128},{384,256},{1,385},{129,1},{257,129},{385... | collective-permute-start | bytes 983048 | tf_op jit(solution)/shard_map/ppermute | solution.py:18
  61.1 10.9 %collective-permute-start.1 = (bf16[1280,128]{1,0:T(8,128)(2,1)S(1)}, bf16[1280,128]{1,0:T(8,128)(2,1)S(1)}, u32[]{:S(2)}, u32[]{:S(2)}) collective-permute-start(bf16[1280,128]{1,0:T(8,128)(2,1)S(1)} %shard_map.70), channel_id=1, source_target_pairs={{0,256},{128,384},{256,0},{384,128},{1,257},{129,385},{257,1},{385... | collective-permute-start | bytes 983048 | tf_op jit(solution)/shard_map/ppermute | solution.py:18
  63.3 17.9 %collective-permute-start = (bf16[1280,128]{1,0:T(8,128)(2,1)S(1)}, bf16[1280,128]{1,0:T(8,128)(2,1)S(1)}, u32[]{:S(2)}, u32[]{:S(2)}) collective-permute-start(bf16[1280,128]{1,0:T(8,128)(2,1)S(1)} %shard_map.70), channel_id=1, source_target_pairs={{0,128},{128,256},{256,384},{384,0},{1,129},{129,257},{257,385},{3... | collective-permute-start | bytes 983048 | tf_op jit(solution)/shard_map/ppermute | solution.py:18
  82.5 5.3 %collective-permute-start.3 = (bf16[4,1280,128]{2,1,0:T(8,128)(2,1)}, bf16[4,1280,128]{2,1,0:T(8,128)(2,1)}, u32[]{:S(2)}, u32[]{:S(2)}) collective-permute-start(bf16[4,1280,128]{2,1,0:T(8,128)(2,1)} %pad_maximum_fusion.own_ref), channel_id=1, source_target_pairs={{0,64},{64,0},{1,65},{65,1},{2,66},{66,2},{3,67},{67,3},{4,68},{68... | collective-permute-start | bytes 3932168 | tf_op jit(solution)/shard_map/ppermute | solution.py:26
  125.2 10.2 %collective-permute-start.4 = (bf16[4,1280,128]{2,1,0:T(8,128)(2,1)S(1)}, bf16[4,1280,128]{2,1,0:T(8,128)(2,1)S(1)}, u32[]{:S(2)}, u32[]{:S(2)}) collective-permute-start(bf16[4,1280,128]{2,1,0:T(8,128)(2,1)S(1)} %get-tuple-element.12), channel_id=1, source_target_pairs={{0,64},{64,0},{1,65},{65,1},{2,66},{66,2},{3,67},{67,3},{4,68},{68... | collective-permute-start | bytes 3932168 | tf_op jit(solution)/shard_map/ppermute | solution.py:26
  132.8 8.7 %collective-permute-start.5 = (bf16[4,576,128]{2,1,0:T(8,128)(2,1)}, bf16[4,576,128]{2,1,0:T(8,128)(2,1)}, u32[]{:S(2)}, u32[]{:S(2)}) collective-permute-start(bf16[4,576,128]{2,1,0:T(8,128)(2,1)} %get-tuple-element.14), channel_id=1, source_target_pairs={{0,64},{64,0},{1,65},{65,1},{2,66},{66,2},{3,67},{67,3},{4,68},{68... | collective-permute-start | bytes 1769480 | tf_op jit(solution)/shard_map/ppermute | solution.py:26
  137.2 33.8 %all-to-all-start.2 = ((bf16[4,1280,128]{2,1,0:T(8,128)(2,1)}), bf16[4,1280,128]{2,1,0:T(8,128)(2,1)}, u32[]{:S(2)}, u32[]{:S(2)}) async-start(bf16[4,1280,128]{2,1,0:T(8,128)(2,1)} %shard_map.73), calls=%async_computation.2 | async-start | bytes 2621440 | tf_op jit(solution)/shard_map/all_to_all | solution.py:30
  142.9 22.1 %collective-permute-start.6 = (bf16[2,576,128]{2,1,0:T(8,128)(2,1)S(1)}, bf16[2,576,128]{2,1,0:T(8,128)(2,1)S(1)}, u32[]{:S(2)}, u32[]{:S(2)}) collective-permute-start(bf16[2,576,128]{2,1,0:T(8,128)(2,1)S(1)} %get-tuple-element.16), channel_id=1, source_target_pairs={{0,384},{128,256},{256,128},{384,0},{1,385},{129,257},{257,129},{3... | collective-permute-start | bytes 884744 | tf_op jit(solution)/shard_map/ppermute | solution.py:22
  165.1 5.9 %collective-permute-start.7 = (bf16[576,128]{1,0:T(8,128)(2,1)S(1)}, bf16[576,128]{1,0:T(8,128)(2,1)S(1)}, u32[]{:S(2)}, u32[]{:S(2)}) collective-permute-start(bf16[576,128]{1,0:T(8,128)(2,1)S(1)} %get-tuple-element.18), channel_id=1, source_target_pairs={{0,128},{128,0},{256,384},{384,256},{1,129},{129,1},{257,385},{385... | collective-permute-start | bytes 442376 | tf_op jit(solution)/shard_map/ppermute | solution.py:22
  173.4 37.2 %all-to-all-start.3 = ((bf16[64,24,128]{2,1,0:T(8,128)(2,1)}), bf16[64,24,128]{2,1,0:T(8,128)(2,1)}, u32[]{:S(2)}, u32[]{:S(2)}) async-start(bf16[64,24,128]{2,1,0:T(8,128)(2,1)} %shard_map.77), calls=%async_computation.3 | async-start | bytes 786432 | tf_op jit(solution)/shard_map/all_to_all | solution.py:30
  180.0 5.9 %collective-permute-start.8 = (bf16[576,128]{1,0:T(8,128)(2,1)S(1)}, bf16[576,128]{1,0:T(8,128)(2,1)S(1)}, u32[]{:S(2)}, u32[]{:S(2)}) collective-permute-start(bf16[576,128]{1,0:T(8,128)(2,1)S(1)} %shard_map.76.after_ref), channel_id=1, source_target_pairs={{0,128},{128,0},{256,384},{384,256},{1,129},{129,1},{257,385},{385... | collective-permute-start | bytes 442376 | tf_op jit(solution)/shard_map/ppermute | solution.py:22
  185.9 9.1 %collective-permute-start.9 = (bf16[2,576,128]{2,1,0:T(8,128)(2,1)S(1)}, bf16[2,576,128]{2,1,0:T(8,128)(2,1)S(1)}, u32[]{:S(2)}, u32[]{:S(2)}) collective-permute-start(bf16[2,576,128]{2,1,0:T(8,128)(2,1)S(1)} %pad_maximum_fusion.1.refs_1_), channel_id=1, source_target_pairs={{0,384},{128,256},{256,128},{384,0},{1,385},{129,257},{257,129},{3... | collective-permute-start | bytes 884744 | tf_op jit(solution)/shard_map/ppermute | solution.py:22
  188.5 13.1 %collective-permute-start.10 = (bf16[2,576,128]{2,1,0:T(8,128)(2,1)S(1)}, bf16[2,576,128]{2,1,0:T(8,128)(2,1)S(1)}, u32[]{:S(2)}, u32[]{:S(2)}) collective-permute-start(bf16[2,576,128]{2,1,0:T(8,128)(2,1)S(1)} %pad_maximum_fusion.1.refs_1_), channel_id=1, source_target_pairs={{0,64},{64,0},{1,65},{65,1},{2,66},{66,2},{3,67},{67,3},{4,68},{68... | collective-permute-start | bytes 884744 | tf_op jit(solution)/shard_map/ppermute | solution.py:26
  195.0 7.8 %collective-permute-start.11 = (bf16[2,576,128]{2,1,0:T(8,128)(2,1)S(1)}, bf16[2,576,128]{2,1,0:T(8,128)(2,1)S(1)}, u32[]{:S(2)}, u32[]{:S(2)}) collective-permute-start(bf16[2,576,128]{2,1,0:T(8,128)(2,1)S(1)} %collective-permute-done.9.refs_2_), channel_id=1, source_target_pairs={{0,64},{64,0},{1,65},{65,1},{2,66},{66,2},{3,67},{67,3},{4,68},{68... | collective-permute-start | bytes 884744 | tf_op jit(solution)/shard_map/ppermute | solution.py:26

commit v6 on v5

--- a/solution.py
+++ b/solution.py
@@ -103,39 +103,46 @@
 
 
 def core_kernel(
-    spot_ref, got_hbm, weight_hbm, turned_hbm, after_ref,
+    spot_ref, got_hbm, weight_hbm, turned_hbm,
     own_ref, other_ref, gradb_hbm, pack_own_ref, pack_other_ref,
     rows_ref, got_ref, weight_ref, turned_ref, gradb_ref, sems,
 ):
-    fetch_got = pltpu.make_async_copy(got_hbm, got_ref, sems.at[0])
-    fetch_weight = pltpu.make_async_copy(weight_hbm, weight_ref, sems.at[1])
-    fetch_turned = pltpu.make_async_copy(turned_hbm, turned_ref, sems.at[2])
-    fetch_got.start()
-    fetch_weight.start()
-    fetch_turned.start()
     experts = got_ref.shape[0]
     columns = rows_ref.shape[1] // 128
     blocks = weight_ref.shape[0] // 128
     y_size = blocks // 2
     half = blocks // 2
+    groups = experts // 16
+    part = weight_ref.shape[0] // groups
+
+    def fetch(source, target, size, first):
+        copies = []
+        for s in range(groups):
+            here = slice(s * size, (s + 1) * size)
+            copies.append(pltpu.make_async_copy(source.at[here], target.at[here], sems.at[first + s]))
+            copies[-1].start()
+        return copies
+
+    fetch_got = fetch(got_hbm, got_ref, 16, 0)
+    fetch_weight = fetch(weight_hbm, weight_ref, part, groups)
+    fetch_turned = fetch(turned_hbm, turned_ref, part, 2 * groups)
+
     number = row_numbers(256)
     order = one_hot(((number >> 2) & 15) * 16 + (number >> 6) * 4 + (number & 3), lane_numbers(256))
-    fetch_got.wait()
-    for b in range(columns):
-        rows_ref[: experts * 16, b * 128 : (b + 1) * 128] = got_ref[:, 16 * b : 16 * (b + 1), :].reshape(
-            experts * 16, 128
-        )
-    for s in range(experts // 16):
-        late = nn_dot(order, got_ref[16 * s : 16 * (s + 1), 16 * columns :, :].reshape(256, 128)).astype(BF16)
+    for s in range(groups):
+        fetch_got[s].wait()
+        here = slice(16 * s, 16 * (s + 1))
+        late = nn_dot(order, got_ref[here, 16 * columns :, :].reshape(256, 128)).astype(BF16)
         for b in range(columns):
-            rows_ref[experts * 16 + s * 64 : experts * 16 + (s + 1) * 64, b * 128 : (b + 1) * 128] = late[
-                b * 64 : (b + 1) * 64
-            ]
+            lanes = slice(b * 128, (b + 1) * 128)
+            rows_ref[256 * s : 256 * (s + 1), lanes] = got_ref[here, 16 * b : 16 * (b + 1), :].reshape(256, 128)
+            rows_ref[experts * 16 + s * 64 : experts * 16 + (s + 1) * 64, lanes] = late[b * 64 : (b + 1) * 64]
     rows = rows_ref[...]
-
-    fetch_weight.wait()
+    core = spot_ref[blocks]
+
+    for copy in fetch_weight:
+        copy.wait()
     term = nt_dot(rows, weight_ref[...]).astype(BF16)
-    core = spot_ref[blocks]
 
     def put_terms(own, other):
         for k in range(y_size):
@@ -150,58 +157,60 @@
     def _():
         put_terms(1, 0)
 
-    fetch_turned.wait()
+    for copy in fetch_turned:
+        copy.wait()
     gradb = nn_dot(turned_ref[...], rows).astype(BF16)
     gradb_ref[...] = gradb
-    store_grad = pltpu.make_async_copy(gradb_ref, gradb_hbm, sems.at[3])
+    store_grad = pltpu.make_async_copy(gradb_ref, gradb_hbm, sems.at[3 * groups])
     store_grad.start()
     gram = nt_dot(gradb, gradb).astype(BF16)
-    for d in range(blocks):
-        i = d % half
-        top = i * 128 + (64 if d >= half else 0)
-        spot = spot_ref[d]
-
-        def put(ref, at):
+
+    def put_packs(ref, side):
+        for n in range(y_size):
+            d = 2 * n + side
+            i = d % half
+            top = i * 128 + (64 if d >= half else 0)
             for k in range(half):
                 j = (d + k) % blocks
-                ref[at, k * 128 : (k + 1) * 128, :] = gram[d * 128 : (d + 1) * 128, j * 128 : (j + 1) * 128]
-            ref[at, half * 128 :, :] = gram[top : top + 64, (i + half) * 128 : (i + half + 1) * 128]
-
-        @pl.when(spot < y_size)
-        def _():
-            put(pack_own_ref, spot)
-
-        @pl.when(spot >= y_size)
-        def _():
-            put(pack_other_ref, spot - y_size)
+                ref[n, k * 128 : (k + 1) * 128, :] = gram[d * 128 : (d + 1) * 128, j * 128 : (j + 1) * 128]
+            ref[n, half * 128 :, :] = gram[top : top + 64, (i + half) * 128 : (i + half + 1) * 128]
+
+    @pl.when(core == 0)
+    def _():
+        put_packs(pack_own_ref, 0)
+        put_packs(pack_other_ref, 1)
+
+    @pl.when(core != 0)
+    def _():
+        put_packs(pack_own_ref, 1)
+        put_packs(pack_other_ref, 0)
 
     store_grad.wait()
 
 
-def add_kernel(own_ref, other_ref, out_ref):
-    out_ref[...] = (own_ref[...].astype(F32) + other_ref[...].astype(F32)).astype(BF16)
-
-
-def pack_add_kernel(own_ref, other_ref, keep_ref, send_ref):
-    near = keep_ref.shape[0]
-    keep_ref[...] = (own_ref[:near].astype(F32) + other_ref[:near].astype(F32)).astype(BF16)
-    send_ref[...] = (own_ref[near:].astype(F32) + other_ref[near:].astype(F32)).astype(BF16)
-
-
-def pack_pair_kernel(keep_ref, got_ref, mine_ref, send_ref):
-    mine_ref[...] = (keep_ref[0].astype(F32) + got_ref[0].astype(F32)).astype(BF16)
-    send_ref[...] = (keep_ref[1].astype(F32) + got_ref[1].astype(F32)).astype(BF16)
-
-
-def return_kernel(part_ref, after_ref, out_ref):
+def add_kernel(own_ref, other_ref, pack_own_ref, pack_other_ref, out_ref):
+    count = own_ref.shape[1]
+    out_ref[:, :count] = (own_ref[...].astype(F32) + other_ref[...].astype(F32)).astype(BF16)
+    out_ref[:, count:] = (pack_own_ref[...].astype(F32) + pack_other_ref[...].astype(F32)).astype(BF16)
+
+
+def return_kernel(part_hbm, out_ref, pack_ref, part_ref, sems):
     experts = out_ref.shape[0]
+    count = part_ref.shape[1] - pack_ref.shape[0]
+    copies = []
+    for k in range(part_ref.shape[0]):
+        copies.append(pltpu.make_async_copy(part_hbm.at[k], part_ref.at[k], sems.at[k]))
+        copies[-1].start()
+    number = row_numbers(128)
+    take = one_hot(jnp.where((number & 7) < 4, (number >> 3) * 4 + (number & 7), -1), lane_numbers(64))
+    for copy in copies:
+        copy.wait()
     total = part_ref[0].astype(F32)
     for k in range(1, part_ref.shape[0]):
         total = total + part_ref[k].astype(F32)
     total = total.astype(BF16)
+    pack_ref[...] = total[count:]
     out_ref[:, 0:16, :] = total[: experts * 16].reshape(experts, 16, 128)
-    number = row_numbers(128)
-    take = one_hot(jnp.where((number & 7) < 4, (number >> 3) * 4 + (number & 7), -1), lane_numbers(64))
     for s in range(experts // 16):
         left = nn_dot(take, total[experts * 16 + s * 64 : experts * 16 + (s + 1) * 64])
         out_ref[16 * s : 16 * (s + 1), 16:24, :] = left.reshape(16, 8, 128).astype(BF16)
@@ -336,51 +345,52 @@
         vmem=20,
     )
 
-    slot_index = flat_ids.reshape(pair_count, 1) * 24 + rank_in.reshape(pair_count, 1)
-    chosen = (slot_index == jnp.arange(experts * 24, dtype=jnp.int32)[None, :]).astype(BF16)
-    chosen = lax.optimization_barrier(chosen)
-
     dp_parts = shape(y_size, total_slots, unit_part)
-    packs = shape(y_size, units // 2 + 64, 128)
+    pack_rows = units // 2 + 64
+    packs = shape(y_size, pack_rows, 128)
+    groups = experts // 16
     term_own, term_other, grad_bf16, pack_own, pack_other = call(
         core_kernel,
-        (dp_parts, dp_parts, pltpu.HBM((units, width_part), BF16), pltpu.HBM(packs.shape, BF16), packs),
-        (pair_spots, in_hbm(got), in_hbm(weights[0]), in_hbm(turned), chosen),
+        (dp_parts, dp_parts, pltpu.HBM((units, width_part), BF16), packs, packs),
+        (pair_spots, in_hbm(got), in_hbm(weights[0]), in_hbm(turned)),
         (
             pltpu.VMEM((total_slots, width_part), BF16),
             pltpu.VMEM(got.shape, BF16),
             pltpu.VMEM((units, width_part), BF16),
             pltpu.VMEM((units, total_slots), BF16),
             pltpu.VMEM((units, width_part), BF16),
-            pltpu.SemaphoreType.DMA((4,)),
+            pltpu.SemaphoreType.DMA((3 * groups + 1,)),
         ),
-        specs={0: SMEM, 1: HBM, 2: HBM, 3: HBM, 4: LOOSE},
+        specs={0: SMEM, 1: HBM, 2: HBM, 3: HBM},
         out_specs={2: HBM},
         vmem=32,
     )
-    pack_swapped = swap_core(pack_other)
-    piece = pl.BlockSpec((1, total_slots, 128), lambda i: (i, 0, 0))
+
+    def piece(count):
+        return pl.BlockSpec((1, count, 128), lambda i: (i, 0, 0))
+
     both = call(
         add_kernel,
-        pltpu.HBM(dp_parts.shape, BF16),
-        (term_own, swap_core(term_other)),
+        pltpu.HBM((y_size, total_slots + pack_rows, 128), BF16),
+        (term_own, swap_core(term_other), pack_own, swap_core(pack_other)),
         steps=(y_size,),
-        specs={0: piece, 1: piece},
-        out_specs={0: piece},
-        vmem=8,
+        specs={0: piece(total_slots), 1: piece(total_slots), 2: piece(pack_rows), 3: piece(pack_rows)},
+        out_specs={0: piece(total_slots + pack_rows)},
+        vmem=12,
     )
     parts = exchange(both, "y")
-
-    pack = shape(units // 2 + 64, 128)
-    pair = shape(2, units // 2 + 64, 128)
-    keep, send = call(pack_add_kernel, (pair, pair), (in_hbm(pack_own), pack_swapped), vmem=8)
-    mine, send = call(pack_pair_kernel, (pack, pack), (keep, swap_y(send, 3, y_size)), vmem=8)
-    mine = call(add_kernel, pack, (mine, swap_y(send, 1, y_size)), vmem=8)
-
-    returned = exchange(
-        call(return_kernel, shape(experts, 24, 128), (parts, mine), specs={1: LOOSE}, vmem=12), EXPERT
-    ).reshape(experts * 24, unit_part)
-    picked = jnp.dot(chosen, returned, preferred_element_type=F32)
+    sent_back, mine = call(
+        return_kernel,
+        (pltpu.HBM((experts, 24, 128), BF16), shape(pack_rows, 128)),
+        (in_hbm(parts),),
+        (pltpu.VMEM(parts.shape, BF16), pltpu.SemaphoreType.DMA((y_size,))),
+        specs={0: HBM},
+        vmem=16,
+    )
+    returned = exchange(sent_back, EXPERT).reshape(experts * 24, unit_part)
+    slot_index = flat_ids * 24 + rank_in
+    chosen = (jnp.arange(experts * 24, dtype=jnp.int32)[:, None] == slot_index).astype(BF16)
+    picked = lax.dot_general(chosen, returned, (((0,), (0,)), ((), ())), preferred_element_type=F32)
     picked = picked.reshape(top_count, tokens, unit_part).transpose(1, 0, 2)
     hidden_grad = (gate_prob[:, :, None] * picked).astype(BF16)
 

time: 215 us -> 208 us (0.967)
  blocking collectives: 0 us -> 28.2 us
  waiting for transfers between devices: 92.8 us -> 74.3 us
  starting transfers between devices: 82.2 us -> 70.1 us
  Pallas kernels: 30.7 us -> 27.7 us
    all_to_all x0 -> x1, blocking collectives: none -> 28.2 us  [exchange(): return lax.all_to_all(value, axes, split_axis=0, concat_axis=0, tiled=True)]
    ppermute x4 -> x2, waiting for transfers between devices: 26.5 us -> 5.07 us  [swap_y(): return lax.ppermute(value, 'y', [(i, i ^ flip) for i in range(size)])]
    ppermute x4 -> x2, starting transfers between devices: 11 us -> 5.43 us  [swap_y(): return lax.ppermute(value, 'y', [(i, i ^ flip) for i in range(size)])]
    all_to_all x4 -> x3, starting transfers between devices: 37.8 us -> 33.3 us  [exchange(): return lax.all_to_all(value, axes, split_axis=0, concat_axis=0, tiled=True)]
    pallas_call x11 -> x8, Pallas kernels: 30.7 us -> 27.7 us  [call(): pl.pallas_call(kernel, out_shape=outs, grid=steps, in_specs=[specs.get(i,...]
    all_to_all x4 -> x3, waiting for transfers between devices: 46.9 us -> 49.5 us  [exchange(): return lax.all_to_all(value, axes, split_axis=0, concat_axis=0, tiled=True)]
  transfers between devices with their start and end apart: 16 -> 13, of which waited for: 12 -> 9; matrix products, arithmetic and copies ran while one was open for 1% -> 1% of each run, Pallas kernels for 8% -> 7%
where the time goes in v6:
time: 208 us; the launch traced here: 207 us
  waiting for transfers between devices  74.3 us (36%)
  starting transfers between devices  70.1 us (34%)
  blocking collectives  28.2 us (14%)
  Pallas kernels  27.7 us (13%)
  other arithmetic  2.63 us (1%)
    all_to_all x3, waiting for transfers between devices, exchange(): return lax.all_to_all(value, axes, split_axis=0, concat_axis=0, tiled=True)  49.5 us
    all_to_all x3, starting transfers between devices, exchange(): return lax.all_to_all(value, axes, split_axis=0, concat_axis=0, tiled=True)  33.3 us
    all_to_all x1, blocking collectives, exchange(): return lax.all_to_all(value, axes, split_axis=0, concat_axis=0, tiled=True)  28.2 us
    pallas_call x8, Pallas kernels, call(): pl.pallas_call(kernel, out_shape=outs, grid=steps, in_specs=[specs.get(i,...  27.7 us
    ppermute x5, starting transfers between devices, swap_core(): return lax.ppermute(value, 'c', [(0, 1), (1, 0)])  21.9 us
    ppermute x3, waiting for transfers between devices, shift_y(): lax.ppermute(value, 'y', [(i, (i + step) % size) for i in range(size)])  15.3 us
    ppermute x3, starting transfers between devices, shift_y(): lax.ppermute(value, 'y', [(i, (i + step) % size) for i in range(size)])  9.5 us
    ppermute x2, starting transfers between devices, swap_y(): return lax.ppermute(value, 'y', [(i, i ^ flip) for i in range(size)])  5.43 us
  transfers between devices with their start and end apart: 13, of which 9 were waited for; matrix products, arithmetic and copies ran while one was open for 1% of the time, Pallas kernels for 7%

profile of v6, /device:TPU:1, one launch (start us, length us, event | category | flops | bytes accessed | tf_op | source)
XLA Modules:
  0.0 206.9 jit_solution(6495496643573668443)
XLA Ops:
  2.8 1.7 shard_map.69
  4.5 19.1 %all-to-all-start.1 = ((bf16[64,24,128]{2,1,0:T(8,128)(2,1)}), bf16[64,24,128]{2,1,0:T(8,128)(2,1)S(1)}, u32[]{:S(2)}, u32[]{:S(2)}) async-start(bf16[64,24,128]{2,1,0:T(8,128)(2,1)} %shard_map.69), calls=%async_computation.1 | async-start | bytes 786432 | tf_op jit(solution)/shard_map/all_to_all | solution.py:30
  23.6 2.4 %shard_map.68 = bf16[64,80,128]{2,1,0:T(8,128)(2,1)} custom-call(s32[1,1024]{1,0:T(1,128)S(1)} %get-tuple-element.19.main_ref, s32[1,1024]{1,0:T(1,128)S(1)} %get-tuple-element.18.late_ref, bf16[512,512]{1,0:T(8,128)(2,1)S(1)} %copy-done), custom_call_target="tpu_custom_call" | custom-call | tf_op jit(solution)/shard_map/pallas_call | solution.py:282
  26.0 22.3 %all-to-all-done.1.got_ref = bf16[64,24,128]{2,1,0:T(8,128)(2,1)S(1)} async-done(((bf16[64,24,128]{2,1,0:T(8,128)(2,1)}), bf16[64,24,128]{2,1,0:T(8,128)(2,1)S(1)}, u32[]{:S(2)}, u32[]{:S(2)}) %all-to-all-start.1) | async-done | bytes 393248 | tf_op jit(solution)/shard_map/all_to_all | solution.py:30
  48.4 7.8 %all-to-all-start = ((bf16[64,80,128]{2,1,0:T(8,128)(2,1)}), bf16[64,80,128]{2,1,0:T(8,128)(2,1)}, u32[]{:S(2)}, u32[]{:S(2)}) async-start(bf16[64,80,128]{2,1,0:T(8,128)(2,1)} %shard_map.68), calls=%async_computation | async-start | bytes 2621440 | tf_op jit(solution)/shard_map/all_to_all | solution.py:30
  56.4 4.6 %collective-permute-start.2 = (bf16[1280,128]{1,0:T(8,128)(2,1)S(1)}, bf16[1280,128]{1,0:T(8,128)(2,1)S(1)}, u32[]{:S(2)}, u32[]{:S(2)}) collective-permute-start(bf16[1280,128]{1,0:T(8,128)(2,1)S(1)} %shard_map.70), channel_id=1, source_target_pairs={{0,384},{128,0},{256,128},{384,256},{1,385},{129,1},{257,129},{385... | collective-permute-start | bytes 983048 | tf_op jit(solution)/shard_map/ppermute | solution.py:18
  61.0 2.3 %collective-permute-start.1 = (bf16[1280,128]{1,0:T(8,128)(2,1)S(1)}, bf16[1280,128]{1,0:T(8,128)(2,1)S(1)}, u32[]{:S(2)}, u32[]{:S(2)}) collective-permute-start(bf16[1280,128]{1,0:T(8,128)(2,1)S(1)} %shard_map.70), channel_id=1, source_target_pairs={{0,256},{128,384},{256,0},{384,128},{1,257},{129,385},{257,1},{385... | collective-permute-start | bytes 983048 | tf_op jit(solution)/shard_map/ppermute | solution.py:18
  63.3 2.6 %collective-permute-start = (bf16[1280,128]{1,0:T(8,128)(2,1)S(1)}, bf16[1280,128]{1,0:T(8,128)(2,1)S(1)}, u32[]{:S(2)}, u32[]{:S(2)}) collective-permute-start(bf16[1280,128]{1,0:T(8,128)(2,1)S(1)} %shard_map.70), channel_id=1, source_target_pairs={{0,128},{128,256},{256,384},{384,0},{1,129},{129,257},{257,385},{3... | collective-permute-start | bytes 983048 | tf_op jit(solution)/shard_map/ppermute | solution.py:18
  65.9 1.6 collective-permute-done.2
  67.5 4.4 %collective-permute-done.1 = bf16[1280,128]{1,0:T(8,128)(2,1)S(1)} collective-permute-done((bf16[1280,128]{1,0:T(8,128)(2,1)S(1)}, bf16[1280,128]{1,0:T(8,128)(2,1)S(1)}, u32[]{:S(2)}, u32[]{:S(2)}) %collective-permute-start.1) | collective-permute-done | bytes 327712 | tf_op jit(solution)/shard_map/ppermute | solution.py:18
  72.0 9.2 %collective-permute-done = bf16[1280,128]{1,0:T(8,128)(2,1)S(1)} collective-permute-done((bf16[1280,128]{1,0:T(8,128)(2,1)S(1)}, bf16[1280,128]{1,0:T(8,128)(2,1)S(1)}, u32[]{:S(2)}, u32[]{:S(2)}) %collective-permute-start) | collective-permute-done | bytes 327712 | tf_op jit(solution)/shard_map/ppermute | solution.py:18
  81.4 2.3 %collective-permute-start.3 = (bf16[4,1280,128]{2,1,0:T(8,128)(2,1)S(1)}, bf16[4,1280,128]{2,1,0:T(8,128)(2,1)S(1)}, u32[]{:S(2)}, u32[]{:S(2)}) collective-permute-start(bf16[4,1280,128]{2,1,0:T(8,128)(2,1)S(1)} %pad_maximum_fusion.own_ref), channel_id=1, source_target_pairs={{0,64},{64,0},{1,65},{65,1},{2,66},{66,2},{3,67},{67,3},{4,68},{68... | collective-permute-start | bytes 3932168 | tf_op jit(solution)/shard_map/ppermute | solution.py:26
  83.8 2.5 %collective-permute-done.3.other_ref = bf16[4,1280,128]{2,1,0:T(8,128)(2,1)S(1)} collective-permute-done((bf16[4,1280,128]{2,1,0:T(8,128)(2,1)S(1)}, bf16[4,1280,128]{2,1,0:T(8,128)(2,1)S(1)}, u32[]{:S(2)}, u32[]{:S(2)}) %collective-permute-start.3) | collective-permute-done | bytes 1310752 | tf_op jit(solution)/shard_map/ppermute | solution.py:26
  86.3 3.2 %shard_map.71.turned_hbm = bf16[1024,1280]{1,0:T(8,128)(2,1)} custom-call(s32[8]{0:T(128)S(1)} %get-tuple-element.23.spot_ref, bf16[4,1280,128]{2,1,0:T(8,128)(2,1)S(1)} %pad_maximum_fusion.own_ref, bf16[4,1280,128]{2,1,0:T(8,128)(2,1)S(1)} %collective-permute-done.3.other_ref), custom_call_target="tpu_custom_call" | custom-call | tf_op jit(solution)/shard_map/pallas_call | solution.py:282
  89.5 27.1 %all-to-all-done.got_hbm = bf16[64,80,128]{2,1,0:T(8,128)(2,1)} async-done(((bf16[64,80,128]{2,1,0:T(8,128)(2,1)}), bf16[64,80,128]{2,1,0:T(8,128)(2,1)}, u32[]{:S(2)}, u32[]{:S(2)}) %all-to-all-start) | async-done | bytes 1310752 | tf_op jit(solution)/shard_map/all_to_all | solution.py:30
  116.6 7.7 %shard_map.72 = (bf16[4,1280,128]{2,1,0:T(8,128)(2,1)S(1)}, bf16[4,1280,128]{2,1,0:T(8,128)(2,1)S(1)}, bf16[1024,512]{1,0:T(8,128)(2,1)}, bf16[4,576,128]{2,1,0:T(8,128)(2,1)S(1)}, bf16[4,576,128]{2,1,0:T(8,128)(2,1)S(1)}) custom-call(s32[9]{0:T(128)S(1)} %pad_add_fusion.spot_ref.refs_0_, bf16[64,80,128]{2,1,0:T(8,128)(2,1)} %all-to-all-done.got_hbm, ...), custom_call_target="tpu_custom_call" | custom-call | tf_op jit(solution)/shard_map/pallas_call | solution.py:282
  124.3 7.6 %collective-permute-start.4 = (bf16[4,1280,128]{2,1,0:T(8,128)(2,1)S(1)}, bf16[4,1280,128]{2,1,0:T(8,128)(2,1)S(1)}, u32[]{:S(2)}, u32[]{:S(2)}) collective-permute-start(bf16[4,1280,128]{2,1,0:T(8,128)(2,1)S(1)} %get-tuple-element.10), channel_id=1, source_target_pairs={{0,64},{64,0},{1,65},{65,1},{2,66},{66,2},{3,67},{67,3},{4,68},{68... | collective-permute-start | bytes 3932168 | tf_op jit(solution)/shard_map/ppermute | solution.py:26
  131.9 1.9 collective-permute-start.5
  133.8 2.0 collective-permute-done.5.pack_other_ref
  135.8 1.9 shard_map.73
  137.7 28.2 %all_to_all.20.part_hbm = bf16[4,1856,128]{2,1,0:T(8,128)(2,1)} all-to-all(bf16[4,1856,128]{2,1,0:T(8,128)(2,1)} %shard_map.73), channel_id=1, replica_groups=mesh['y'=4,'c'=2,'x'=4,'z'=16] {'y'}, dimensions={0} | all-to-all | bytes 3801088 | tf_op jit(solution)/shard_map/all_to_all | solution.py:30
  165.9 2.7 %shard_map.74 = (bf16[64,24,128]{2,1,0:T(8,128)(2,1)}, bf16[576,128]{1,0:T(8,128)(2,1)S(1)}) custom-call(bf16[4,1856,128]{2,1,0:T(8,128)(2,1)} %all_to_all.20.part_hbm), custom_call_target="tpu_custom_call" | custom-call | tf_op jit(solution)/shard_map/pallas_call | solution.py:282
  168.6 6.3 %all-to-all-start.3 = ((bf16[64,24,128]{2,1,0:T(8,128)(2,1)}), bf16[64,24,128]{2,1,0:T(8,128)(2,1)S(1)}, u32[]{:S(2)}, u32[]{:S(2)}) async-start(bf16[64,24,128]{2,1,0:T(8,128)(2,1)} %get-tuple-element.13), calls=%async_computation.3 | async-start | bytes 786432 | tf_op jit(solution)/shard_map/all_to_all | solution.py:30
  175.0 2.6 %collective-permute-start.6 = (bf16[576,128]{1,0:T(8,128)(2,1)S(1)}, bf16[576,128]{1,0:T(8,128)(2,1)S(1)}, u32[]{:S(2)}, u32[]{:S(2)}) collective-permute-start(bf16[576,128]{1,0:T(8,128)(2,1)S(1)} %get-tuple-element.14), channel_id=1, source_target_pairs={{0,128},{128,0},{256,384},{384,256},{1,129},{129,1},{257,385},{385... | collective-permute-start | bytes 442376 | tf_op jit(solution)/shard_map/ppermute | solution.py:22
  177.6 3.5 %collective-permute-done.6 = bf16[576,128]{1,0:T(8,128)(2,1)S(1)} collective-permute-done((bf16[576,128]{1,0:T(8,128)(2,1)S(1)}, bf16[576,128]{1,0:T(8,128)(2,1)S(1)}, u32[]{:S(2)}, u32[]{:S(2)}) %collective-permute-start.6) | collective-permute-done | bytes 147488 | tf_op jit(solution)/shard_map/ppermute | solution.py:22
  181.2 2.8 %collective-permute-start.7 = (bf16[2,576,128]{2,1,0:T(8,128)(2,1)S(1)}, bf16[2,576,128]{2,1,0:T(8,128)(2,1)S(1)}, u32[]{:S(2)}, u32[]{:S(2)}) collective-permute-start(bf16[2,576,128]{2,1,0:T(8,128)(2,1)S(1)} %pad_maximum_fusion.1.refs_1_), channel_id=1, source_target_pairs={{0,384},{128,256},{256,128},{384,0},{1,385},{129,257},{257,129},{3... | collective-permute-start | bytes 884744 | tf_op jit(solution)/shard_map/ppermute | solution.py:22
  184.0 4.7 %collective-permute-start.8 = (bf16[2,576,128]{2,1,0:T(8,128)(2,1)S(1)}, bf16[2,576,128]{2,1,0:T(8,128)(2,1)S(1)}, u32[]{:S(2)}, u32[]{:S(2)}) collective-permute-start(bf16[2,576,128]{2,1,0:T(8,128)(2,1)S(1)} %pad_maximum_fusion.1.refs_1_), channel_id=1, source_target_pairs={{0,64},{64,0},{1,65},{65,1},{2,66},{66,2},{3,67},{67,3},{4,68},{68... | collective-permute-start | bytes 884744 | tf_op jit(solution)/shard_map/ppermute | solution.py:26
  188.7 1.5 collective-permute-done.7.refs_2_
  190.3 5.4 %collective-permute-start.9 = (bf16[2,576,128]{2,1,0:T(8,128)(2,1)S(1)}, bf16[2,576,128]{2,1,0:T(8,128)(2,1)S(1)}, u32[]{:S(2)}, u32[]{:S(2)}) collective-permute-start(bf16[2,576,128]{2,1,0:T(8,128)(2,1)S(1)} %collective-permute-done.7.refs_2_), channel_id=1, source_target_pairs={{0,64},{64,0},{1,65},{65,1},{2,66},{66,2},{3,67},{67,3},{4,68},{68... | collective-permute-start | bytes 884744 | tf_op jit(solution)/shard_map/ppermute | solution.py:26
  195.6 1.4 iota_compare_fusion
  197.0 7.9 %shard_map.75 = f32[1,1024,512]{2,1,0:T(8,128)} custom-call(s32[9]{0:T(128)S(1)} %pad_add_fusion.spot_ref.refs_0_, bf16[2,576,128]{2,1,0:T(8,128)(2,1)S(1)} %pad_maximum_fusion.1.refs_1_, bf16[2,576,128]{2,1,0:T(8,128)(2,1)S(1)} %collective-permute-done.7.refs_2_, bf16[2,576,128]{2,1,0:T(8,128)(2,1)S(1)} %collective-permute-done.8.refs_3_, ...), custom_call_target="tpu_custom_call" | custom-call | tf_op jit(solution)/shard_map/pallas_call | solution.py:282
  204.9 1.0 fusion.2
  (25 shorter events, 3.6 us)
Async XLA Ops:
  0.6 1.9 copy-start.2
  0.6 1.9 copy-start.1
  2.1 21.5 %copy-start = (bf16[512,512]{1,0:T(8,128)(2,1)S(1)}, bf16[512,512]{1,0:T(8,128)(2,1)}, u32[]{:S(2)}) copy-start(bf16[512,512]{1,0:T(8,128)(2,1)} %grad_ref.1) | copy-start | bytes 1572868
  4.5 43.9 %all-to-all-start.1 = ((bf16[64,24,128]{2,1,0:T(8,128)(2,1)}), bf16[64,24,128]{2,1,0:T(8,128)(2,1)S(1)}, u32[]{:S(2)}, u32[]{:S(2)}) async-start(bf16[64,24,128]{2,1,0:T(8,128)(2,1)} %shard_map.69), calls=%async_computation.1 | async-start | bytes 786432 | tf_op jit(solution)/shard_map/all_to_all | solution.py:30
  48.4 68.3 %all-to-all-start = ((bf16[64,80,128]{2,1,0:T(8,128)(2,1)}), bf16[64,80,128]{2,1,0:T(8,128)(2,1)}, u32[]{:S(2)}, u32[]{:S(2)}) async-start(bf16[64,80,128]{2,1,0:T(8,128)(2,1)} %shard_map.68), calls=%async_computation | async-start | bytes 2621440 | tf_op jit(solution)/shard_map/all_to_all | solution.py:30
  56.4 11.1 %collective-permute-start.2 = (bf16[1280,128]{1,0:T(8,128)(2,1)S(1)}, bf16[1280,128]{1,0:T(8,128)(2,1)S(1)}, u32[]{:S(2)}, u32[]{:S(2)}) collective-permute-start(bf16[1280,128]{1,0:T(8,128)(2,1)S(1)} %shard_map.70), channel_id=1, source_target_pairs={{0,384},{128,0},{256,128},{384,256},{1,385},{129,1},{257,129},{385... | collective-permute-start | bytes 983048 | tf_op jit(solution)/shard_map/ppermute | solution.py:18
  61.0 10.9 %collective-permute-start.1 = (bf16[1280,128]{1,0:T(8,128)(2,1)S(1)}, bf16[1280,128]{1,0:T(8,128)(2,1)S(1)}, u32[]{:S(2)}, u32[]{:S(2)}) collective-permute-start(bf16[1280,128]{1,0:T(8,128)(2,1)S(1)} %shard_map.70), channel_id=1, source_target_pairs={{0,256},{128,384},{256,0},{384,128},{1,257},{129,385},{257,1},{385... | collective-permute-start | bytes 983048 | tf_op jit(solution)/shard_map/ppermute | solution.py:18
  63.3 17.9 %collective-permute-start = (bf16[1280,128]{1,0:T(8,128)(2,1)S(1)}, bf16[1280,128]{1,0:T(8,128)(2,1)S(1)}, u32[]{:S(2)}, u32[]{:S(2)}) collective-permute-start(bf16[1280,128]{1,0:T(8,128)(2,1)S(1)} %shard_map.70), channel_id=1, source_target_pairs={{0,128},{128,256},{256,384},{384,0},{1,129},{129,257},{257,385},{3... | collective-permute-start | bytes 983048 | tf_op jit(solution)/shard_map/ppermute | solution.py:18
  81.4 4.9 %collective-permute-start.3 = (bf16[4,1280,128]{2,1,0:T(8,128)(2,1)S(1)}, bf16[4,1280,128]{2,1,0:T(8,128)(2,1)S(1)}, u32[]{:S(2)}, u32[]{:S(2)}) collective-permute-start(bf16[4,1280,128]{2,1,0:T(8,128)(2,1)S(1)} %pad_maximum_fusion.own_ref), channel_id=1, source_target_pairs={{0,64},{64,0},{1,65},{65,1},{2,66},{66,2},{3,67},{67,3},{4,68},{68... | collective-permute-start | bytes 3932168 | tf_op jit(solution)/shard_map/ppermute | solution.py:26
  124.3 11.5 %collective-permute-start.4 = (bf16[4,1280,128]{2,1,0:T(8,128)(2,1)S(1)}, bf16[4,1280,128]{2,1,0:T(8,128)(2,1)S(1)}, u32[]{:S(2)}, u32[]{:S(2)}) collective-permute-start(bf16[4,1280,128]{2,1,0:T(8,128)(2,1)S(1)} %get-tuple-element.10), channel_id=1, source_target_pairs={{0,64},{64,0},{1,65},{65,1},{2,66},{66,2},{3,67},{67,3},{4,68},{68... | collective-permute-start | bytes 3932168 | tf_op jit(solution)/shard_map/ppermute | solution.py:26
  131.9 3.9 %collective-permute-start.5 = (bf16[4,576,128]{2,1,0:T(8,128)(2,1)S(1)}, bf16[4,576,128]{2,1,0:T(8,128)(2,1)S(1)}, u32[]{:S(2)}, u32[]{:S(2)}) collective-permute-start(bf16[4,576,128]{2,1,0:T(8,128)(2,1)S(1)} %get-tuple-element.12), channel_id=1, source_target_pairs={{0,64},{64,0},{1,65},{65,1},{2,66},{66,2},{3,67},{67,3},{4,68},{68... | collective-permute-start | bytes 1769480 | tf_op jit(solution)/shard_map/ppermute | solution.py:26
  168.6 36.3 %all-to-all-start.3 = ((bf16[64,24,128]{2,1,0:T(8,128)(2,1)}), bf16[64,24,128]{2,1,0:T(8,128)(2,1)S(1)}, u32[]{:S(2)}, u32[]{:S(2)}) async-start(bf16[64,24,128]{2,1,0:T(8,128)(2,1)} %get-tuple-element.13), calls=%async_computation.3 | async-start | bytes 786432 | tf_op jit(solution)/shard_map/all_to_all | solution.py:30
  175.0 6.2 %collective-permute-start.6 = (bf16[576,128]{1,0:T(8,128)(2,1)S(1)}, bf16[576,128]{1,0:T(8,128)(2,1)S(1)}, u32[]{:S(2)}, u32[]{:S(2)}) collective-permute-start(bf16[576,128]{1,0:T(8,128)(2,1)S(1)} %get-tuple-element.14), channel_id=1, source_target_pairs={{0,128},{128,0},{256,384},{384,256},{1,129},{129,1},{257,385},{385... | collective-permute-start | bytes 442376 | tf_op jit(solution)/shard_map/ppermute | solution.py:22
  181.2 9.1 %collective-permute-start.7 = (bf16[2,576,128]{2,1,0:T(8,128)(2,1)S(1)}, bf16[2,576,128]{2,1,0:T(8,128)(2,1)S(1)}, u32[]{:S(2)}, u32[]{:S(2)}) collective-permute-start(bf16[2,576,128]{2,1,0:T(8,128)(2,1)S(1)} %pad_maximum_fusion.1.refs_1_), channel_id=1, source_target_pairs={{0,384},{128,256},{256,128},{384,0},{1,385},{129,257},{257,129},{3... | collective-permute-start | bytes 884744 | tf_op jit(solution)/shard_map/ppermute | solution.py:22
  184.0 13.0 %collective-permute-start.8 = (bf16[2,576,128]{2,1,0:T(8,128)(2,1)S(1)}, bf16[2,576,128]{2,1,0:T(8,128)(2,1)S(1)}, u32[]{:S(2)}, u32[]{:S(2)}) collective-permute-start(bf16[2,576,128]{2,1,0:T(8,128)(2,1)S(1)} %pad_maximum_fusion.1.refs_1_), channel_id=1, source_target_pairs={{0,64},{64,0},{1,65},{65,1},{2,66},{66,2},{3,67},{67,3},{4,68},{68... | collective-permute-start | bytes 884744 | tf_op jit(solution)/shard_map/ppermute | solution.py:26
  190.3 6.8 %collective-permute-start.9 = (bf16[2,576,128]{2,1,0:T(8,128)(2,1)S(1)}, bf16[2,576,128]{2,1,0:T(8,128)(2,1)S(1)}, u32[]{:S(2)}, u32[]{:S(2)}) collective-permute-start(bf16[2,576,128]{2,1,0:T(8,128)(2,1)S(1)} %collective-permute-done.7.refs_2_), channel_id=1, source_target_pairs={{0,64},{64,0},{1,65},{65,1},{2,66},{66,2},{3,67},{67,3},{4,68},{68... | collective-permute-start | bytes 884744 | tf_op jit(solution)/shard_map/ppermute | solution.py:26

commit v7 on v6

--- a/solution.py
+++ b/solution.py
@@ -50,12 +50,31 @@
     return lax.broadcasted_iota(jnp.int32, (1, count), 1)
 
 
-def send_scaled_kernel(main_ref, left_ref, scaled_ref, out_ref):
+def send_scaled_kernel(ids_ref, scaled_ref, out_ref, main_ref, late_ref, slot_ref):
     experts = out_ref.shape[0]
+    count, tokens = ids_ref.shape
+    earlier = jnp.where(row_numbers(tokens) < lane_numbers(tokens), 1.0, 0.0).astype(BF16)
+    passed = jnp.zeros((experts, 1), F32)
+    ids, ranks = [], []
+    for k in range(count):
+        ids.append(ids_ref[k : k + 1, :])
+        named = one_hot(row_numbers(experts), ids[k])
+        wide = named.astype(F32)
+        before = nn_dot(named, earlier) + passed
+        ranks.append(jnp.sum(wide * before, axis=0, keepdims=True).astype(jnp.int32))
+        passed = passed + jnp.sum(wide, axis=1, keepdims=True)
+    expert = jnp.concatenate(ids, axis=1)
+    rank = jnp.concatenate(ranks, axis=1)
+    late = rank >= 16
+    main_index = jnp.where(late, -1, expert * 16 + rank)
+    main_ref[...] = main_index
+    late_ref[...] = jnp.where(late, expert * 16 + rank - 16, -1)
+    slot_ref[...] = expert * 24 + rank
+    left_index = jnp.where(late, expert * 8 + rank - 16, -1)
     scaled = scaled_ref[...]
-    part = nn_dot(one_hot(row_numbers(experts * 16), main_ref[...]), scaled).astype(BF16)
+    part = nn_dot(one_hot(row_numbers(experts * 16), main_index), scaled).astype(BF16)
     out_ref[:, 0:16, :] = part.reshape(experts, 16, 128)
-    part = nn_dot(one_hot(row_numbers(experts * 8), left_ref[...]), scaled)
+    part = nn_dot(one_hot(row_numbers(experts * 8), left_index), scaled)
     out_ref[:, 16:24, :] = part.reshape(experts, 8, 128).astype(BF16)
 
 
@@ -104,7 +123,7 @@
 
 def core_kernel(
     spot_ref, got_hbm, weight_hbm, turned_hbm,
-    own_ref, other_ref, gradb_hbm, pack_own_ref, pack_other_ref,
+    own_ref, other_ref, gradb_hbm,
     rows_ref, got_ref, weight_ref, turned_ref, gradb_ref, sems,
 ):
     experts = got_ref.shape[0]
@@ -139,6 +158,7 @@
             rows_ref[experts * 16 + s * 64 : experts * 16 + (s + 1) * 64, lanes] = late[b * 64 : (b + 1) * 64]
     rows = rows_ref[...]
     core = spot_ref[blocks]
+    count = rows_ref.shape[0]
 
     for copy in fetch_weight:
         copy.wait()
@@ -146,8 +166,8 @@
 
     def put_terms(own, other):
         for k in range(y_size):
-            own_ref[k] = term[:, (2 * k + own) * 128 : (2 * k + own + 1) * 128]
-            other_ref[k] = term[:, (2 * k + other) * 128 : (2 * k + other + 1) * 128]
+            own_ref[k, :count] = term[:, (2 * k + own) * 128 : (2 * k + own + 1) * 128]
+            other_ref[k, :count] = term[:, (2 * k + other) * 128 : (2 * k + other + 1) * 128]
 
     @pl.when(core == 0)
     def _():
@@ -172,39 +192,31 @@
             top = i * 128 + (64 if d >= half else 0)
             for k in range(half):
                 j = (d + k) % blocks
-                ref[n, k * 128 : (k + 1) * 128, :] = gram[d * 128 : (d + 1) * 128, j * 128 : (j + 1) * 128]
-            ref[n, half * 128 :, :] = gram[top : top + 64, (i + half) * 128 : (i + half + 1) * 128]
+                ref[n, count + k * 128 : count + (k + 1) * 128, :] = gram[d * 128 : (d + 1) * 128, j * 128 : (j + 1) * 128]
+            ref[n, count + half * 128 :, :] = gram[top : top + 64, (i + half) * 128 : (i + half + 1) * 128]
 
     @pl.when(core == 0)
     def _():
-        put_packs(pack_own_ref, 0)
-        put_packs(pack_other_ref, 1)
+        put_packs(own_ref, 0)
+        put_packs(other_ref, 1)
 
     @pl.when(core != 0)
     def _():
-        put_packs(pack_own_ref, 1)
-        put_packs(pack_other_ref, 0)
+        put_packs(own_ref, 1)
+        put_packs(other_ref, 0)
 
     store_grad.wait()
 
 
-def add_kernel(own_ref, other_ref, pack_own_ref, pack_other_ref, out_ref):
-    count = own_ref.shape[1]
-    out_ref[:, :count] = (own_ref[...].astype(F32) + other_ref[...].astype(F32)).astype(BF16)
-    out_ref[:, count:] = (pack_own_ref[...].astype(F32) + pack_other_ref[...].astype(F32)).astype(BF16)
-
-
-def return_kernel(part_hbm, out_ref, pack_ref, part_ref, sems):
+def add_kernel(own_ref, other_ref, out_ref):
+    out_ref[...] = (own_ref[...].astype(F32) + other_ref[...].astype(F32)).astype(BF16)
+
+
+def return_kernel(part_ref, out_ref, pack_ref):
     experts = out_ref.shape[0]
     count = part_ref.shape[1] - pack_ref.shape[0]
-    copies = []
-    for k in range(part_ref.shape[0]):
-        copies.append(pltpu.make_async_copy(part_hbm.at[k], part_ref.at[k], sems.at[k]))
-        copies[-1].start()
     number = row_numbers(128)
     take = one_hot(jnp.where((number & 7) < 4, (number >> 3) * 4 + (number & 7), -1), lane_numbers(64))
-    for copy in copies:
-        copy.wait()
     total = part_ref[0].astype(F32)
     for k in range(1, part_ref.shape[0]):
         total = total + part_ref[k].astype(F32)
@@ -312,17 +324,6 @@
     core = jnp.full((1,), c)
     pair_spots = jnp.concatenate([pair_spot, core]).astype(jnp.int32)
 
-    flat_ids = expert_ids.T.reshape(1, pair_count)
-    named = (jnp.arange(experts, dtype=jnp.int32)[:, None] == flat_ids).astype(BF16)
-    order = jnp.arange(pair_count, dtype=jnp.int32)
-    earlier = (order[:, None] < order[None, :]).astype(BF16)
-    before = jnp.dot(named, earlier, preferred_element_type=F32)
-    rank_in = jnp.sum(before * named.astype(F32), axis=0, keepdims=True).astype(jnp.int32)
-    late = rank_in >= 16
-    main_index = jnp.where(late, -1, flat_ids * 16 + rank_in)
-    left_index = jnp.where(late, flat_ids * 8 + rank_in - 16, -1)
-    late_index = jnp.where(late, flat_ids * 16 + rank_in - 16, -1)
-
     scaled_part = (gate_prob[:, :, None] * hidden.astype(F32)).astype(BF16)
     scaled_part = scaled_part.transpose(1, 0, 2).reshape(pair_count, unit_part)
     columns = width_part // 128
@@ -330,9 +331,11 @@
     def shape(*dims):
         return jax.ShapeDtypeStruct(dims, BF16)
 
-    got_scaled = exchange(
-        call(send_scaled_kernel, shape(experts, 24, 128), (main_index, left_index, scaled_part)), EXPERT
-    )
+    row = jax.ShapeDtypeStruct((1, pair_count), jnp.int32)
+    sent_scaled, main_index, late_index, slot_index = call(
+        send_scaled_kernel, (shape(experts, 24, 128), row, row, row), (expert_ids.T, scaled_part)
+    )
+    got_scaled = exchange(sent_scaled, EXPERT)
     got = exchange(
         call(send_grad_kernel, shape(experts, 20 * columns, 128), (main_index, late_index, grad_out)), EXPERT
     )
@@ -345,13 +348,12 @@
         vmem=20,
     )
 
-    dp_parts = shape(y_size, total_slots, unit_part)
     pack_rows = units // 2 + 64
-    packs = shape(y_size, pack_rows, 128)
+    dp_parts = shape(y_size, total_slots + pack_rows, 128)
     groups = experts // 16
-    term_own, term_other, grad_bf16, pack_own, pack_other = call(
+    own, other, grad_bf16 = call(
         core_kernel,
-        (dp_parts, dp_parts, pltpu.HBM((units, width_part), BF16), packs, packs),
+        (dp_parts, dp_parts, pltpu.HBM((units, width_part), BF16)),
         (pair_spots, in_hbm(got), in_hbm(weights[0]), in_hbm(turned)),
         (
             pltpu.VMEM((total_slots, width_part), BF16),
@@ -365,30 +367,12 @@
         out_specs={2: HBM},
         vmem=32,
     )
-
-    def piece(count):
-        return pl.BlockSpec((1, count, 128), lambda i: (i, 0, 0))
-
-    both = call(
-        add_kernel,
-        pltpu.HBM((y_size, total_slots + pack_rows, 128), BF16),
-        (term_own, swap_core(term_other), pack_own, swap_core(pack_other)),
-        steps=(y_size,),
-        specs={0: piece(total_slots), 1: piece(total_slots), 2: piece(pack_rows), 3: piece(pack_rows)},
-        out_specs={0: piece(total_slots + pack_rows)},
-        vmem=12,
-    )
+    both = call(add_kernel, dp_parts, (own, swap_core(other)), vmem=12)
     parts = exchange(both, "y")
     sent_back, mine = call(
-        return_kernel,
-        (pltpu.HBM((experts, 24, 128), BF16), shape(pack_rows, 128)),
-        (in_hbm(parts),),
-        (pltpu.VMEM(parts.shape, BF16), pltpu.SemaphoreType.DMA((y_size,))),
-        specs={0: HBM},
-        vmem=16,
+        return_kernel, (pltpu.HBM((experts, 24, 128), BF16), shape(pack_rows, 128)), (parts,), vmem=12
     )
     returned = exchange(sent_back, EXPERT).reshape(experts * 24, unit_part)
-    slot_index = flat_ids * 24 + rank_in
     chosen = (jnp.arange(experts * 24, dtype=jnp.int32)[:, None] == slot_index).astype(BF16)
     picked = lax.dot_general(chosen, returned, (((0,), (0,)), ((), ())), preferred_element_type=F32)
     picked = picked.reshape(top_count, tokens, unit_part).transpose(1, 0, 2)

time: 208 us -> 204 us (0.981)
  Pallas kernels: 27.7 us -> 25 us
  starting transfers between devices: 70.1 us -> 67.9 us
    pallas_call x8, Pallas kernels: 27.7 us -> 25 us  [call(): pl.pallas_call(kernel, out_shape=outs, grid=steps, in_specs=[specs.get(i,...]
    ppermute x5 -> x4, starting transfers between devices: 21.9 us -> 20.2 us  [swap_core(): return lax.ppermute(value, 'c', [(0, 1), (1, 0)])]
    ppermute x5 -> x4, waiting for transfers between devices: 4.52 us -> 6.03 us  [swap_core(): return lax.ppermute(value, 'c', [(0, 1), (1, 0)])]
  transfers between devices with their start and end apart: 13 -> 12, of which waited for: 9 -> 9; matrix products, arithmetic and copies ran while one was open for 1% -> 1% of each run, Pallas kernels for 7% -> 7%
where the time goes in v7:
time: 204 us; the launch traced here: 203 us
  waiting for transfers between devices  76.1 us (37%)
  starting transfers between devices  67.9 us (33%)
  blocking collectives  27.6 us (14%)
  Pallas kernels  25 us (12%)
  other arithmetic  2.87 us (1%)
    all_to_all x3, waiting for transfers between devices, exchange(): return lax.all_to_all(value, axes, split_axis=0, concat_axis=0, tiled=True)  49.5 us
    all_to_all x3, starting transfers between devices, exchange(): return lax.all_to_all(value, axes, split_axis=0, concat_axis=0, tiled=True)  33.3 us
    all_to_all x1, blocking collectives, exchange(): return lax.all_to_all(value, axes, split_axis=0, concat_axis=0, tiled=True)  27.6 us
    pallas_call x8, Pallas kernels, call(): pl.pallas_call(kernel, out_shape=outs, grid=steps, in_specs=[specs.get(i,...  25 us
    ppermute x4, starting transfers between devices, swap_core(): return lax.ppermute(value, 'c', [(0, 1), (1, 0)])  20.2 us
    ppermute x3, waiting for transfers between devices, shift_y(): lax.ppermute(value, 'y', [(i, (i + step) % size) for i in range(size)])  15.3 us
    ppermute x3, starting transfers between devices, shift_y(): lax.ppermute(value, 'y', [(i, (i + step) % size) for i in range(size)])  9.5 us
    ppermute x4, waiting for transfers between devices, swap_core(): return lax.ppermute(value, 'c', [(0, 1), (1, 0)])  6.03 us
  transfers between devices with their start and end apart: 12, of which 9 were waited for; matrix products, arithmetic and copies ran while one was open for 1% of the time, Pallas kernels for 7%

profile of v7, /device:TPU:1, one launch (start us, length us, event | category | flops | bytes accessed | tf_op | source)
XLA Modules:
  0.0 202.9 jit_solution(9469724621551456908)
XLA Ops:
  0.6 1.2 multiply_convert_fusion
  2.5 2.0 shard_map.68
  4.5 19.1 %all-to-all-start.1 = ((bf16[64,24,128]{2,1,0:T(8,128)(2,1)}), bf16[64,24,128]{2,1,0:T(8,128)(2,1)S(1)}, u32[]{:S(2)}, u32[]{:S(2)}) async-start(bf16[64,24,128]{2,1,0:T(8,128)(2,1)} %get-tuple-element.14), calls=%async_computation.1 | async-start | bytes 786432 | tf_op jit(solution)/shard_map/all_to_all | solution.py:30
  23.6 2.4 %shard_map.69 = bf16[64,80,128]{2,1,0:T(8,128)(2,1)} custom-call(s32[1,1024]{1,0:T(1,128)S(1)} %get-tuple-element.12.main_ref, s32[1,1024]{1,0:T(1,128)S(1)} %get-tuple-element.13.late_ref, bf16[512,512]{1,0:T(8,128)(2,1)S(1)} %copy-done), custom_call_target="tpu_custom_call" | custom-call | tf_op jit(solution)/shard_map/pallas_call | solution.py:294
  26.0 22.3 %all-to-all-done.1.got_ref = bf16[64,24,128]{2,1,0:T(8,128)(2,1)S(1)} async-done(((bf16[64,24,128]{2,1,0:T(8,128)(2,1)}), bf16[64,24,128]{2,1,0:T(8,128)(2,1)S(1)}, u32[]{:S(2)}, u32[]{:S(2)}) %all-to-all-start.1) | async-done | bytes 393248 | tf_op jit(solution)/shard_map/all_to_all | solution.py:30
  48.4 7.8 %all-to-all-start = ((bf16[64,80,128]{2,1,0:T(8,128)(2,1)}), bf16[64,80,128]{2,1,0:T(8,128)(2,1)}, u32[]{:S(2)}, u32[]{:S(2)}) async-start(bf16[64,80,128]{2,1,0:T(8,128)(2,1)} %shard_map.69), calls=%async_computation | async-start | bytes 2621440 | tf_op jit(solution)/shard_map/all_to_all | solution.py:30
  56.4 4.6 %collective-permute-start.2 = (bf16[1280,128]{1,0:T(8,128)(2,1)S(1)}, bf16[1280,128]{1,0:T(8,128)(2,1)S(1)}, u32[]{:S(2)}, u32[]{:S(2)}) collective-permute-start(bf16[1280,128]{1,0:T(8,128)(2,1)S(1)} %shard_map.70), channel_id=1, source_target_pairs={{0,384},{128,0},{256,128},{384,256},{1,385},{129,1},{257,129},{385... | collective-permute-start | bytes 983048 | tf_op jit(solution)/shard_map/ppermute | solution.py:18
  61.1 2.3 %collective-permute-start.1 = (bf16[1280,128]{1,0:T(8,128)(2,1)S(1)}, bf16[1280,128]{1,0:T(8,128)(2,1)S(1)}, u32[]{:S(2)}, u32[]{:S(2)}) collective-permute-start(bf16[1280,128]{1,0:T(8,128)(2,1)S(1)} %shard_map.70), channel_id=1, source_target_pairs={{0,256},{128,384},{256,0},{384,128},{1,257},{129,385},{257,1},{385... | collective-permute-start | bytes 983048 | tf_op jit(solution)/shard_map/ppermute | solution.py:18
  63.3 2.6 %collective-permute-start = (bf16[1280,128]{1,0:T(8,128)(2,1)S(1)}, bf16[1280,128]{1,0:T(8,128)(2,1)S(1)}, u32[]{:S(2)}, u32[]{:S(2)}) collective-permute-start(bf16[1280,128]{1,0:T(8,128)(2,1)S(1)} %shard_map.70), channel_id=1, source_target_pairs={{0,128},{128,256},{256,384},{384,0},{1,129},{129,257},{257,385},{3... | collective-permute-start | bytes 983048 | tf_op jit(solution)/shard_map/ppermute | solution.py:18
  65.9 1.6 collective-permute-done.2
  67.5 4.4 %collective-permute-done.1 = bf16[1280,128]{1,0:T(8,128)(2,1)S(1)} collective-permute-done((bf16[1280,128]{1,0:T(8,128)(2,1)S(1)}, bf16[1280,128]{1,0:T(8,128)(2,1)S(1)}, u32[]{:S(2)}, u32[]{:S(2)}) %collective-permute-start.1) | collective-permute-done | bytes 327712 | tf_op jit(solution)/shard_map/ppermute | solution.py:18
  72.0 9.2 %collective-permute-done = bf16[1280,128]{1,0:T(8,128)(2,1)S(1)} collective-permute-done((bf16[1280,128]{1,0:T(8,128)(2,1)S(1)}, bf16[1280,128]{1,0:T(8,128)(2,1)S(1)}, u32[]{:S(2)}, u32[]{:S(2)}) %collective-permute-start) | collective-permute-done | bytes 327712 | tf_op jit(solution)/shard_map/ppermute | solution.py:18
  81.4 2.3 %collective-permute-start.3 = (bf16[4,1280,128]{2,1,0:T(8,128)(2,1)S(1)}, bf16[4,1280,128]{2,1,0:T(8,128)(2,1)S(1)}, u32[]{:S(2)}, u32[]{:S(2)}) collective-permute-start(bf16[4,1280,128]{2,1,0:T(8,128)(2,1)S(1)} %pad_maximum_fusion.own_ref), channel_id=1, source_target_pairs={{0,64},{64,0},{1,65},{65,1},{2,66},{66,2},{3,67},{67,3},{4,68},{68... | collective-permute-start | bytes 3932168 | tf_op jit(solution)/shard_map/ppermute | solution.py:26
  83.8 2.5 %collective-permute-done.3.other_ref = bf16[4,1280,128]{2,1,0:T(8,128)(2,1)S(1)} collective-permute-done((bf16[4,1280,128]{2,1,0:T(8,128)(2,1)S(1)}, bf16[4,1280,128]{2,1,0:T(8,128)(2,1)S(1)}, u32[]{:S(2)}, u32[]{:S(2)}) %collective-permute-start.3) | collective-permute-done | bytes 1310752 | tf_op jit(solution)/shard_map/ppermute | solution.py:26
  86.3 3.2 %shard_map.71.turned_hbm = bf16[1024,1280]{1,0:T(8,128)(2,1)} custom-call(s32[8]{0:T(128)S(1)} %get-tuple-element.22.spot_ref, bf16[4,1280,128]{2,1,0:T(8,128)(2,1)S(1)} %pad_maximum_fusion.own_ref, bf16[4,1280,128]{2,1,0:T(8,128)(2,1)S(1)} %collective-permute-done.3.other_ref), custom_call_target="tpu_custom_call" | custom-call | tf_op jit(solution)/shard_map/pallas_call | solution.py:294
  89.5 27.1 %all-to-all-done.got_hbm = bf16[64,80,128]{2,1,0:T(8,128)(2,1)} async-done(((bf16[64,80,128]{2,1,0:T(8,128)(2,1)}), bf16[64,80,128]{2,1,0:T(8,128)(2,1)}, u32[]{:S(2)}, u32[]{:S(2)}) %all-to-all-start) | async-done | bytes 1310752 | tf_op jit(solution)/shard_map/all_to_all | solution.py:30
  116.6 7.7 %shard_map.72 = (bf16[4,1856,128]{2,1,0:T(8,128)(2,1)S(1)}, bf16[4,1856,128]{2,1,0:T(8,128)(2,1)S(1)}, bf16[1024,512]{1,0:T(8,128)(2,1)}) custom-call(s32[9]{0:T(128)S(1)} %pad_add_fusion.spot_ref.refs_0_, bf16[64,80,128]{2,1,0:T(8,128)(2,1)} %all-to-all-done.got_hbm, bf16[1024,512]{1,0:T(8,128)(2,1)} %bitcast.31, bf16[1024,1280]{1,0:T(8,128)(2,1)} %shard_map.71.turned_hbm), custom_call_target="tpu_custom_call" | custom-call | tf_op jit(solution)/shard_map/pallas_call | solution.py:294
  124.3 7.6 %collective-permute-start.4 = (bf16[4,1856,128]{2,1,0:T(8,128)(2,1)S(1)}, bf16[4,1856,128]{2,1,0:T(8,128)(2,1)S(1)}, u32[]{:S(2)}, u32[]{:S(2)}) collective-permute-start(bf16[4,1856,128]{2,1,0:T(8,128)(2,1)S(1)} %get-tuple-element.16), channel_id=1, source_target_pairs={{0,64},{64,0},{1,65},{65,1},{2,66},{66,2},{3,67},{67,3},{4,68},{68... | collective-permute-start | bytes 5701640 | tf_op jit(solution)/shard_map/ppermute | solution.py:26
  131.9 3.5 %collective-permute-done.4.other_ref = bf16[4,1856,128]{2,1,0:T(8,128)(2,1)S(1)} collective-permute-done((bf16[4,1856,128]{2,1,0:T(8,128)(2,1)S(1)}, bf16[4,1856,128]{2,1,0:T(8,128)(2,1)S(1)}, u32[]{:S(2)}, u32[]{:S(2)}) %collective-permute-start.4) | collective-permute-done | bytes 1900576 | tf_op jit(solution)/shard_map/ppermute | solution.py:26
  135.8 27.6 %all_to_all.20.part_ref = bf16[4,1856,128]{2,1,0:T(8,128)(2,1)S(1)} all-to-all(bf16[4,1856,128]{2,1,0:T(8,128)(2,1)S(1)} %shard_map.73), channel_id=1, replica_groups=mesh['y'=4,'c'=2,'x'=4,'z'=16] {'y'}, dimensions={0} | all-to-all | bytes 3801088 | tf_op jit(solution)/shard_map/all_to_all | solution.py:30
  163.5 1.2 shard_map.74
  164.7 6.3 %all-to-all-start.3 = ((bf16[64,24,128]{2,1,0:T(8,128)(2,1)}), bf16[64,24,128]{2,1,0:T(8,128)(2,1)S(1)}, u32[]{:S(2)}, u32[]{:S(2)}) async-start(bf16[64,24,128]{2,1,0:T(8,128)(2,1)} %get-tuple-element.17), calls=%async_computation.3 | async-start | bytes 786432 | tf_op jit(solution)/shard_map/all_to_all | solution.py:30
  171.0 2.2 %collective-permute-start.5 = (bf16[576,128]{1,0:T(8,128)(2,1)S(1)}, bf16[576,128]{1,0:T(8,128)(2,1)S(1)}, u32[]{:S(2)}, u32[]{:S(2)}) collective-permute-start(bf16[576,128]{1,0:T(8,128)(2,1)S(1)} %get-tuple-element.18), channel_id=1, source_target_pairs={{0,128},{128,0},{256,384},{384,256},{1,129},{129,1},{257,385},{385... | collective-permute-start | bytes 442376 | tf_op jit(solution)/shard_map/ppermute | solution.py:22
  173.2 4.0 %collective-permute-done.5 = bf16[576,128]{1,0:T(8,128)(2,1)S(1)} collective-permute-done((bf16[576,128]{1,0:T(8,128)(2,1)S(1)}, bf16[576,128]{1,0:T(8,128)(2,1)S(1)}, u32[]{:S(2)}, u32[]{:S(2)}) %collective-permute-start.5) | collective-permute-done | bytes 147488 | tf_op jit(solution)/shard_map/ppermute | solution.py:22
  177.2 2.8 %collective-permute-start.6 = (bf16[2,576,128]{2,1,0:T(8,128)(2,1)S(1)}, bf16[2,576,128]{2,1,0:T(8,128)(2,1)S(1)}, u32[]{:S(2)}, u32[]{:S(2)}) collective-permute-start(bf16[2,576,128]{2,1,0:T(8,128)(2,1)S(1)} %pad_maximum_fusion.1.refs_1_), channel_id=1, source_target_pairs={{0,384},{128,256},{256,128},{384,0},{1,385},{129,257},{257,129},{3... | collective-permute-start | bytes 884744 | tf_op jit(solution)/shard_map/ppermute | solution.py:22
  180.0 4.8 %collective-permute-start.7 = (bf16[2,576,128]{2,1,0:T(8,128)(2,1)S(1)}, bf16[2,576,128]{2,1,0:T(8,128)(2,1)S(1)}, u32[]{:S(2)}, u32[]{:S(2)}) collective-permute-start(bf16[2,576,128]{2,1,0:T(8,128)(2,1)S(1)} %pad_maximum_fusion.1.refs_1_), channel_id=1, source_target_pairs={{0,64},{64,0},{1,65},{65,1},{2,66},{66,2},{3,67},{67,3},{4,68},{68... | collective-permute-start | bytes 884744 | tf_op jit(solution)/shard_map/ppermute | solution.py:26
  184.9 1.3 collective-permute-done.6.refs_2_
  186.2 5.5 %collective-permute-start.8 = (bf16[2,576,128]{2,1,0:T(8,128)(2,1)S(1)}, bf16[2,576,128]{2,1,0:T(8,128)(2,1)S(1)}, u32[]{:S(2)}, u32[]{:S(2)}) collective-permute-start(bf16[2,576,128]{2,1,0:T(8,128)(2,1)S(1)} %collective-permute-done.6.refs_2_), channel_id=1, source_target_pairs={{0,64},{64,0},{1,65},{65,1},{2,66},{66,2},{3,67},{67,3},{4,68},{68... | collective-permute-start | bytes 884744 | tf_op jit(solution)/shard_map/ppermute | solution.py:26
  191.7 1.4 iota_compare_fusion
  193.1 7.9 %shard_map.75 = f32[1,1024,512]{2,1,0:T(8,128)} custom-call(s32[9]{0:T(128)S(1)} %pad_add_fusion.spot_ref.refs_0_, bf16[2,576,128]{2,1,0:T(8,128)(2,1)S(1)} %pad_maximum_fusion.1.refs_1_, bf16[2,576,128]{2,1,0:T(8,128)(2,1)S(1)} %collective-permute-done.6.refs_2_, bf16[2,576,128]{2,1,0:T(8,128)(2,1)S(1)} %collective-permute-done.7.refs_3_, ...), custom_call_target="tpu_custom_call" | custom-call | tf_op jit(solution)/shard_map/pallas_call | solution.py:294
  201.0 1.0 fusion.1
  202.0 1.0 copy.8
  (15 shorter events, 1.6 us)
Async XLA Ops:
  0.6 23.0 %copy-start = (bf16[512,512]{1,0:T(8,128)(2,1)S(1)}, bf16[512,512]{1,0:T(8,128)(2,1)}, u32[]{:S(2)}) copy-start(bf16[512,512]{1,0:T(8,128)(2,1)} %grad_ref.1) | copy-start | bytes 1572868
  1.9 0.7 copy-start.1
  4.5 43.9 %all-to-all-start.1 = ((bf16[64,24,128]{2,1,0:T(8,128)(2,1)}), bf16[64,24,128]{2,1,0:T(8,128)(2,1)S(1)}, u32[]{:S(2)}, u32[]{:S(2)}) async-start(bf16[64,24,128]{2,1,0:T(8,128)(2,1)} %get-tuple-element.14), calls=%async_computation.1 | async-start | bytes 786432 | tf_op jit(solution)/shard_map/all_to_all | solution.py:30
  48.4 68.3 %all-to-all-start = ((bf16[64,80,128]{2,1,0:T(8,128)(2,1)}), bf16[64,80,128]{2,1,0:T(8,128)(2,1)}, u32[]{:S(2)}, u32[]{:S(2)}) async-start(bf16[64,80,128]{2,1,0:T(8,128)(2,1)} %shard_map.69), calls=%async_computation | async-start | bytes 2621440 | tf_op jit(solution)/shard_map/all_to_all | solution.py:30
  56.4 11.1 %collective-permute-start.2 = (bf16[1280,128]{1,0:T(8,128)(2,1)S(1)}, bf16[1280,128]{1,0:T(8,128)(2,1)S(1)}, u32[]{:S(2)}, u32[]{:S(2)}) collective-permute-start(bf16[1280,128]{1,0:T(8,128)(2,1)S(1)} %shard_map.70), channel_id=1, source_target_pairs={{0,384},{128,0},{256,128},{384,256},{1,385},{129,1},{257,129},{385... | collective-permute-start | bytes 983048 | tf_op jit(solution)/shard_map/ppermute | solution.py:18
  61.1 10.9 %collective-permute-start.1 = (bf16[1280,128]{1,0:T(8,128)(2,1)S(1)}, bf16[1280,128]{1,0:T(8,128)(2,1)S(1)}, u32[]{:S(2)}, u32[]{:S(2)}) collective-permute-start(bf16[1280,128]{1,0:T(8,128)(2,1)S(1)} %shard_map.70), channel_id=1, source_target_pairs={{0,256},{128,384},{256,0},{384,128},{1,257},{129,385},{257,1},{385... | collective-permute-start | bytes 983048 | tf_op jit(solution)/shard_map/ppermute | solution.py:18
  63.3 17.9 %collective-permute-start = (bf16[1280,128]{1,0:T(8,128)(2,1)S(1)}, bf16[1280,128]{1,0:T(8,128)(2,1)S(1)}, u32[]{:S(2)}, u32[]{:S(2)}) collective-permute-start(bf16[1280,128]{1,0:T(8,128)(2,1)S(1)} %shard_map.70), channel_id=1, source_target_pairs={{0,128},{128,256},{256,384},{384,0},{1,129},{129,257},{257,385},{3... | collective-permute-start | bytes 983048 | tf_op jit(solution)/shard_map/ppermute | solution.py:18
  81.4 4.9 %collective-permute-start.3 = (bf16[4,1280,128]{2,1,0:T(8,128)(2,1)S(1)}, bf16[4,1280,128]{2,1,0:T(8,128)(2,1)S(1)}, u32[]{:S(2)}, u32[]{:S(2)}) collective-permute-start(bf16[4,1280,128]{2,1,0:T(8,128)(2,1)S(1)} %pad_maximum_fusion.own_ref), channel_id=1, source_target_pairs={{0,64},{64,0},{1,65},{65,1},{2,66},{66,2},{3,67},{67,3},{4,68},{68... | collective-permute-start | bytes 3932168 | tf_op jit(solution)/shard_map/ppermute | solution.py:26
  124.3 11.1 %collective-permute-start.4 = (bf16[4,1856,128]{2,1,0:T(8,128)(2,1)S(1)}, bf16[4,1856,128]{2,1,0:T(8,128)(2,1)S(1)}, u32[]{:S(2)}, u32[]{:S(2)}) collective-permute-start(bf16[4,1856,128]{2,1,0:T(8,128)(2,1)S(1)} %get-tuple-element.16), channel_id=1, source_target_pairs={{0,64},{64,0},{1,65},{65,1},{2,66},{66,2},{3,67},{67,3},{4,68},{68... | collective-permute-start | bytes 5701640 | tf_op jit(solution)/shard_map/ppermute | solution.py:26
  164.7 36.3 %all-to-all-start.3 = ((bf16[64,24,128]{2,1,0:T(8,128)(2,1)}), bf16[64,24,128]{2,1,0:T(8,128)(2,1)S(1)}, u32[]{:S(2)}, u32[]{:S(2)}) async-start(bf16[64,24,128]{2,1,0:T(8,128)(2,1)} %get-tuple-element.17), calls=%async_computation.3 | async-start | bytes 786432 | tf_op jit(solution)/shard_map/all_to_all | solution.py:30
  171.0 6.2 %collective-permute-start.5 = (bf16[576,128]{1,0:T(8,128)(2,1)S(1)}, bf16[576,128]{1,0:T(8,128)(2,1)S(1)}, u32[]{:S(2)}, u32[]{:S(2)}) collective-permute-start(bf16[576,128]{1,0:T(8,128)(2,1)S(1)} %get-tuple-element.18), channel_id=1, source_target_pairs={{0,128},{128,0},{256,384},{384,256},{1,129},{129,1},{257,385},{385... | collective-permute-start | bytes 442376 | tf_op jit(solution)/shard_map/ppermute | solution.py:22
  177.2 9.0 %collective-permute-start.6 = (bf16[2,576,128]{2,1,0:T(8,128)(2,1)S(1)}, bf16[2,576,128]{2,1,0:T(8,128)(2,1)S(1)}, u32[]{:S(2)}, u32[]{:S(2)}) collective-permute-start(bf16[2,576,128]{2,1,0:T(8,128)(2,1)S(1)} %pad_maximum_fusion.1.refs_1_), channel_id=1, source_target_pairs={{0,384},{128,256},{256,128},{384,0},{1,385},{129,257},{257,129},{3... | collective-permute-start | bytes 884744 | tf_op jit(solution)/shard_map/ppermute | solution.py:22
  180.0 13.0 %collective-permute-start.7 = (bf16[2,576,128]{2,1,0:T(8,128)(2,1)S(1)}, bf16[2,576,128]{2,1,0:T(8,128)(2,1)S(1)}, u32[]{:S(2)}, u32[]{:S(2)}) collective-permute-start(bf16[2,576,128]{2,1,0:T(8,128)(2,1)S(1)} %pad_maximum_fusion.1.refs_1_), channel_id=1, source_target_pairs={{0,64},{64,0},{1,65},{65,1},{2,66},{66,2},{3,67},{67,3},{4,68},{68... | collective-permute-start | bytes 884744 | tf_op jit(solution)/shard_map/ppermute | solution.py:26
  186.2 6.9 %collective-permute-start.8 = (bf16[2,576,128]{2,1,0:T(8,128)(2,1)S(1)}, bf16[2,576,128]{2,1,0:T(8,128)(2,1)S(1)}, u32[]{:S(2)}, u32[]{:S(2)}) collective-permute-start(bf16[2,576,128]{2,1,0:T(8,128)(2,1)S(1)} %collective-permute-done.6.refs_2_), channel_id=1, source_target_pairs={{0,64},{64,0},{1,65},{65,1},{2,66},{66,2},{3,67},{67,3},{4,68},{68... | collective-permute-start | bytes 884744 | tf_op jit(solution)/shard_map/ppermute | solution.py:26
  193.1 7.9 %copy-start.2 = (f32[512,2]{0,1:T(2,128)S(1)}, f32[512,2]{0,1:T(2,128)}, u32[]{:S(2)}) copy-start(f32[512,2]{0,1:T(2,128)} %param.7) | copy-start | bytes 12292

commit v8 on v7

v8 whole, which is shorter than its diff:
```python
import jax
import jax.numpy as jnp
from jax import lax
from jax.experimental import pallas as pl
from jax.experimental.pallas import tpu as pltpu
from jax.sharding import Mesh, PartitionSpec as P

EXPERT = ("x", "z")
MIB = 1024 * 1024
BF16 = jnp.bfloat16
F32 = jnp.float32
SMEM = pl.BlockSpec(memory_space=pltpu.SMEM)
LOOSE = pl.BlockSpec(memory_space=pl.ANY)
HBM = pl.BlockSpec(memory_space=pltpu.HBM)


def shift_y(value, step, size):
    return lax.ppermute(value, "y", [(i, (i + step) % size) for i in range(size)])


def swap_y(value, flip, size):
    return lax.ppermute(value, "y", [(i, i ^ flip) for i in range(size)])


def swap_core(value):
    return lax.ppermute(value, "c", [(0, 1), (1, 0)])


def exchange(value, axes):
    return lax.all_to_all(value, axes, split_axis=0, concat_axis=0, tiled=True)


def nt_dot(left, right):
    return lax.dot_general(left, right, (((1,), (1,)), ((), ())), preferred_element_type=F32)


def nn_dot(left, right):
    return jnp.dot(left, right, preferred_element_type=F32)


def one_hot(rows, index):
    return jnp.where(rows == index, 1.0, 0.0).astype(BF16)


def row_numbers(count):
    return lax.broadcasted_iota(jnp.int32, (count, 1), 0)


def lane_numbers(count):
    return lax.broadcasted_iota(jnp.int32, (1, count), 1)


def fetch(source, target, size, sems, first):
    copies = []
    for s in range(source.shape[0] // size):
        here = slice(s * size, (s + 1) * size)
        copies.append(pltpu.make_async_copy(source.at[here], target.at[here], sems.at[first + s]))
        copies[-1].start()
    return copies


def send_kernel(ids_ref, scaled_ref, grad_ref, out_ref, slot_ref):
    experts, height, _ = out_ref.shape
    count, tokens = ids_ref.shape
    blocks = grad_ref.shape[1] // 128
    main = 16 * (blocks + 1)
    tail = height - main
    earlier = jnp.where(row_numbers(tokens) < lane_numbers(tokens), 1.0, 0.0).astype(BF16)
    passed = jnp.zeros((experts, 1), F32)
    ids, ranks = [], []
    for k in range(count):
        ids.append(ids_ref[k : k + 1, :])
        named = one_hot(row_numbers(experts), ids[k])
        wide = named.astype(F32)
        before = nn_dot(named, earlier) + passed
        ranks.append(jnp.sum(wide * before, axis=0, keepdims=True).astype(jnp.int32))
        passed = passed + jnp.sum(wide, axis=1, keepdims=True)
    owner = jnp.concatenate(ids, axis=1)
    rank = jnp.concatenate(ranks, axis=1)
    late = rank >= 16
    slot_ref[...] = owner * 24 + rank

    scaled = scaled_ref[...]
    grad = grad_ref[...]
    chosen = one_hot(row_numbers(experts * 16), jnp.where(late, -1, owner * 16 + rank))
    part = nn_dot(chosen, scaled).astype(BF16)
    out_ref[:, 0:16, :] = part.reshape(experts, 16, 128)
    rows = nn_dot(chosen[:, :tokens] + chosen[:, tokens:], grad).astype(BF16)
    for b in range(blocks):
        out_ref[:, 16 * (b + 1) : 16 * (b + 2), :] = rows[:, b * 128 : (b + 1) * 128].reshape(experts, 16, 128)
    expert = lax.broadcasted_iota(jnp.int32, (experts, tail, 1), 0)
    place = lax.broadcasted_iota(jnp.int32, (experts, tail, 1), 1)
    number = (expert * tail + (place & 3)).reshape(experts * tail, 1)
    kind = (place >> 2).reshape(experts * tail, 1)
    chosen = one_hot(number, jnp.where(late, owner * tail + rank - 16, -1))
    part = nn_dot(chosen, scaled)
    total = jnp.where(kind == 0, part, 0.0)
    rows = nn_dot(chosen[:, :tokens] + chosen[:, tokens:], grad)
    for b in range(blocks):
        total = jnp.where(kind == b + 1, rows[:, b * 128 : (b + 1) * 128], total)
    out_ref[:, main:, :] = total.reshape(experts, tail, 128).astype(BF16)


def late_rows(got_ref, main, s, kinds):
    tail = got_ref.shape[1] - main
    group = got_ref[8 * s : 8 * (s + 1), main:, :].astype(F32).reshape(8 * tail, 128).astype(BF16)
    number = row_numbers(32 * kinds)
    order = one_hot(((number >> 2) & 7) * tail + (number >> 5) * 4 + (number & 3), lane_numbers(8 * tail))
    return nn_dot(order, group).astype(BF16)


def unpack_kernel(got_ref, out_hbm, scaled_ref, sems):
    experts, height, _ = got_ref.shape
    main = (height // 16 - 1) * 16
    scaled_ref[: experts * 16] = got_ref[:, 0:16, :].reshape(experts * 16, 128)
    for s in range(experts // 8):
        scaled_ref[experts * 16 + 32 * s : experts * 16 + 32 * (s + 1)] = late_rows(got_ref, main, s, 1)
    copies = []
    for k in range(out_hbm.shape[0]):
        copies.append(pltpu.make_async_copy(scaled_ref, out_hbm.at[k], sems.at[k]))
        copies[-1].start()
    for copy in copies:
        copy.wait()


def back_kernel(
    spot_ref, got_ref, weight_hbm, own_hbm, other_ref, rows_hbm, own_ref, rows_ref, weight_ref, sems
):
    experts, height, _ = got_ref.shape
    columns = rows_ref.shape[1] // 128
    blocks = weight_ref.shape[0] // 128
    y_size = blocks // 2
    main = 16 * (columns + 1)
    fetch_weight = fetch(weight_hbm, weight_ref, weight_ref.shape[0] // y_size, sems, 0)
    for b in range(columns):
        lanes = slice(b * 128, (b + 1) * 128)
        rows_ref[: experts * 16, lanes] = got_ref[:, 16 * (b + 1) : 16 * (b + 2), :].reshape(experts * 16, 128)
    for s in range(experts // 8):
        late = late_rows(got_ref, main, s, columns + 1)
        for b in range(columns):
            rows_ref[experts * 16 + 32 * s : experts * 16 + 32 * (s + 1), b * 128 : (b + 1) * 128] = late[
                32 * (b + 1) : 32 * (b + 2)
            ]
    store_rows = pltpu.make_async_copy(rows_ref, rows_hbm, sems.at[y_size])
    store_rows.start()
    for copy in fetch_weight:
        copy.wait()
    term = nt_dot(rows_ref[...], weight_ref[...]).astype(BF16)
    core = spot_ref[blocks]

    def put_terms(own, other):
        for k in range(y_size):
            own_ref[k] = term[:, (2 * k + own) * 128 : (2 * k + own + 1) * 128]
            other_ref[k] = term[:, (2 * k + other) * 128 : (2 * k + other + 1) * 128]

    @pl.when(core == 0)
    def _():
        put_terms(0, 1)

    @pl.when(core != 0)
    def _():
        put_terms(1, 0)

    stores = fetch(own_ref, own_hbm, 1, sems, y_size + 1)
    for copy in stores:
        copy.wait()
    store_rows.wait()


def grad_kernel(
    spot_ref, own_hbm, other_hbm, rows_hbm, gradb_hbm, pack_own_ref, pack_other_ref,
    own_ref, other_ref, rows_ref, wide_ref, gradb_ref, sems,
):
    blocks = gradb_ref.shape[0] // 128
    y_size = blocks // 2
    half = blocks // 2
    copies = fetch(own_hbm, own_ref, 1, sems, 0)
    copies += fetch(other_hbm, other_ref, 1, sems, y_size)
    copies += fetch(rows_hbm, rows_ref, rows_ref.shape[0] // y_size, sems, 2 * y_size)
    for copy in copies:
        copy.wait()
    core = spot_ref[blocks]

    def put_units(ref, side):
        for n in range(y_size):
            wide_ref[:, (2 * n + side) * 128 : (2 * n + side + 1) * 128] = ref[n]

    @pl.when(core == 0)
    def _():
        put_units(own_ref, 0)
        put_units(other_ref, 1)

    @pl.when(core != 0)
    def _():
        put_units(own_ref, 1)
        put_units(other_ref, 0)

    gradb = lax.dot_general(
        wide_ref[...], rows_ref[...], (((0,), (0,)), ((), ())), preferred_element_type=F32
    ).astype(BF16)
    gradb_ref[...] = gradb
    store_grad = pltpu.make_async_copy(gradb_ref, gradb_hbm, sems.at[3 * y_size])
    store_grad.start()
    gram = nt_dot(gradb, gradb).astype(BF16)

    def put_packs(ref, side):
        for n in range(y_size):
            d = 2 * n + side
            i = d % half
            top = i * 128 + (64 if d >= half else 0)
            for k in range(half):
                j = (d + k) % blocks
                ref[n, k * 128 : (k + 1) * 128, :] = gram[d * 128 : (d + 1) * 128, j * 128 : (j + 1) * 128]
            ref[n, half * 128 :, :] = gram[top : top + 64, (i + half) * 128 : (i + half + 1) * 128]

    @pl.when(core == 0)
    def _():
        put_packs(pack_own_ref, 0)
        put_packs(pack_other_ref, 1)

    @pl.when(core != 0)
    def _():
        put_packs(pack_own_ref, 1)
        put_packs(pack_other_ref, 0)

    store_grad.wait()


def add_kernel(own_ref, other_ref, after_ref, out_ref):
    out_ref[...] = (own_ref[...].astype(F32) + other_ref[...].astype(F32)).astype(BF16)


def sum_parts(part_ref):
    total = part_ref[0].astype(F32)
    for k in range(1, part_ref.shape[0]):
        total = total + part_ref[k].astype(F32)
    return total.astype(BF16)


def return_kernel(part_ref, pack_part_ref, out_ref, pack_ref):
    experts = out_ref.shape[0]
    number = row_numbers(128)
    take = one_hot(jnp.where((number & 7) < 4, (number >> 3) * 4 + (number & 7), -1), lane_numbers(64))
    pack_ref[...] = sum_parts(pack_part_ref)
    total = sum_parts(part_ref)
    out_ref[:, 0:16, :] = total[: experts * 16].reshape(experts, 16, 128)
    for s in range(experts // 16):
        left = nn_dot(take, total[experts * 16 + s * 64 : experts * 16 + (s + 1) * 64])
        out_ref[16 * s : 16 * (s + 1), 16:24, :] = left.reshape(16, 8, 128).astype(BF16)


def ortho_kernel(
    width, spot_ref, own_near_ref, own_far_ref, other_near_ref, other_far_ref, gradb_hbm, out_ref,
    gram_ref, pack_ref, gradb_ref, sem,
):
    fetch_grad = pltpu.make_async_copy(gradb_hbm, gradb_ref, sem)
    fetch_grad.start()
    blocks = gram_ref.shape[0] // 128
    half = blocks // 2
    squares = jnp.zeros((8, 128), F32)
    for i, ref in enumerate((own_near_ref, own_far_ref, other_near_ref, other_far_ref)):
        for k in range(2):
            pack = ref[k]
            pack_ref[2 * i + k] = pack
            square = pack.astype(F32)
            square = square * square
            squares = squares + 2.0 * jnp.sum(square.reshape(-1, 8, 128), axis=0)
            squares = squares - jnp.sum(square[:128].reshape(-1, 8, 128), axis=0)
    norm_sq = jnp.sqrt(jnp.sum(squares, keepdims=True)) + 1e-06
    for d in range(blocks):
        spot = spot_ref[d]
        rows = slice(d * 128, (d + 1) * 128)
        for k in range(half):
            lanes = slice((d + k) % blocks * 128, ((d + k) % blocks + 1) * 128)
            block = pack_ref[spot, k * 128 : (k + 1) * 128, :]
            gram_ref[rows, lanes] = block
            if k > 0:
                gram_ref[lanes, rows] = block.T
        i = d % half
        top = i * 128 + (64 if d >= half else 0)
        gram_ref[top : top + 64, (i + half) * 128 : (i + half + 1) * 128] = pack_ref[spot, half * 128 :, :]
    for i in range(half):
        upper = gram_ref[i * 128 : (i + 1) * 128, (i + half) * 128 : (i + half + 1) * 128]
        gram_ref[(i + half) * 128 : (i + half + 1) * 128, i * 128 : (i + 1) * 128] = upper.T

    inverse = 1.0 / norm_sq
    gram = gram_ref[...]
    fetch_grad.wait()
    first = (gradb_ref[...].astype(F32) * lax.rsqrt(norm_sq)).astype(BF16)

    def apply(value):
        return nn_dot(gram, value) * inverse

    second = (1.5 * first.astype(F32) - 0.5 * apply(first)).astype(BF16)
    power_one = apply(second).astype(BF16)
    power_two = apply(power_one).astype(BF16)
    power_three = apply(power_two)
    total = 1.5 * second.astype(F32)
    total = total - 0.5 * (2.25 * power_one.astype(F32) - 1.5 * power_two.astype(F32) + 0.25 * power_three)
    out_ref[0] = total * width**0.5


def in_hbm(value):
    return pltpu.with_memory_space_constraint(value, pltpu.HBM)


def whole(value):
    return pl.BlockSpec(value.shape, lambda *_: (0,) * len(value.shape))


def call(kernel, outs, ins, scratch=(), vmem=24, steps=(), specs=None, out_specs=None):
    specs = specs or {}
    out_specs = out_specs or {}
    flat, tree = jax.tree.flatten(outs)
    return pl.pallas_call(
        kernel,
        out_shape=outs,
        grid=steps,
        in_specs=[specs.get(i, whole(value)) for i, value in enumerate(ins)],
        out_specs=jax.tree.unflatten(tree, [out_specs.get(i, whole(value)) for i, value in enumerate(flat)]),
        scratch_shapes=list(scratch),
        compiler_params=pltpu.CompilerParams(vmem_limit_bytes=vmem * MIB),
    )(*ins)


def per_device(grad_out, hidden, gate_prob, expert_ids, weights):
    tokens, width_part = grad_out.shape
    top_count = expert_ids.shape[1]
    unit_part = hidden.shape[2]
    units = weights.shape[1]
    experts = lax.axis_size("x") * lax.axis_size("z")
    y_size = lax.axis_size("y")
    dp = y_size * 2
    width = width_part * dp
    capacity = 5 * tokens * top_count // (4 * experts)
    total_slots = experts * capacity
    pair_count = tokens * top_count
    y = lax.axis_index("y")
    c = lax.axis_index("c")
    block = jnp.arange(dp, dtype=jnp.int32)
    other_core = (block % 2) ^ c
    flip = y ^ (block // 2)
    pair_spot = other_core * y_size + (flip ^ (flip >> 1))
    core = jnp.full((1,), c)
    pair_spots = jnp.concatenate([pair_spot, core]).astype(jnp.int32)

    scaled_part = (gate_prob[:, :, None] * hidden.astype(F32)).astype(BF16)
    scaled_part = scaled_part.transpose(1, 0, 2).reshape(pair_count, unit_part)
    columns = width_part // 128
    main_rows = 16 * (columns + 1)
    tail = -(-4 * (columns + 1) // 8) * 8

    def shape(*dims):
        return jax.ShapeDtypeStruct(dims, BF16)

    sent, slot_index = call(
        send_kernel,
        (shape(experts, main_rows + tail, 128), jax.ShapeDtypeStruct((1, pair_count), jnp.int32)),
        (expert_ids.T, scaled_part, grad_out),
    )
    got = exchange(sent, EXPERT)

    parts_shape = (y_size, total_slots, unit_part)
    gathered = exchange(
        call(
            unpack_kernel,
            pltpu.HBM(parts_shape, BF16),
            (got,),
            (pltpu.VMEM((total_slots, unit_part), BF16), pltpu.SemaphoreType.DMA((y_size,))),
            out_specs={0: HBM},
            vmem=12,
        ),
        "y",
    )
    gathered_other = swap_core(gathered)
    term_own, term_other, rows = call(
        back_kernel,
        (pltpu.HBM(parts_shape, BF16), shape(*parts_shape), pltpu.HBM((total_slots, width_part), BF16)),
        (pair_spots, got, in_hbm(weights[0])),
        (
            pltpu.VMEM(parts_shape, BF16),
            pltpu.VMEM((total_slots, width_part), BF16),
            pltpu.VMEM((units, width_part), BF16),
            pltpu.SemaphoreType.DMA((2 * y_size + 1,)),
        ),
        specs={0: SMEM, 2: HBM},
        out_specs={0: HBM, 2: HBM},
        vmem=24,
    )

    def piece(count):
        return pl.BlockSpec((1, count, 128), lambda i: (i, 0, 0))

    both = call(
        add_kernel,
        pltpu.HBM(parts_shape, BF16),
        (in_hbm(term_own), swap_core(term_other), gathered),
        steps=(y_size,),
        specs={0: piece(total_slots), 1: piece(total_slots), 2: LOOSE},
        out_specs={0: piece(total_slots)},
        vmem=8,
    )
    parts = exchange(both, "y")

    pack_rows = units // 2 + 64
    packs = shape(y_size, pack_rows, 128)
    grad_bf16, pack_own, pack_other = call(
        grad_kernel,
        (pltpu.HBM((units, width_part), BF16), packs, packs),
        (pair_spots, in_hbm(gathered), in_hbm(gathered_other), in_hbm(rows)),
        (
            pltpu.VMEM(parts_shape, BF16),
            pltpu.VMEM(parts_shape, BF16),
            pltpu.VMEM((total_slots, width_part), BF16),
            pltpu.VMEM((total_slots, units), BF16),
            pltpu.VMEM((units, width_part), BF16),
            pltpu.SemaphoreType.DMA((3 * y_size + 1,)),
        ),
        specs={0: SMEM, 1: HBM, 2: HBM, 3: HBM},
        out_specs={0: HBM},
        vmem=32,
    )
    pack_both = call(add_kernel, packs, (pack_own, swap_core(pack_other), parts), specs={2: LOOSE}, vmem=8)
    pack_parts = exchange(pack_both, "y")
    sent_back, mine = call(
        return_kernel,
        (pltpu.HBM((experts, 24, 128), BF16), shape(pack_rows, 128)),
        (parts, pack_parts),
        vmem=12,
    )
    returned = exchange(sent_back, EXPERT).reshape(experts * 24, unit_part)
    chosen = (jnp.arange(experts * 24, dtype=jnp.int32)[:, None] == slot_index).astype(BF16)
    picked = lax.dot_general(chosen, returned, (((0,), (0,)), ((), ())), preferred_element_type=F32)
    picked = picked.reshape(top_count, tokens, unit_part).transpose(1, 0, 2)
    hidden_grad = (gate_prob[:, :, None] * picked).astype(BF16)

    near = jnp.stack([mine, swap_y(mine, 1, y_size)])
    far = swap_y(near, 3, y_size)
    update = call(
        lambda *refs: ortho_kernel(width, *refs),
        jax.ShapeDtypeStruct((1, units, width_part), F32),
        (pair_spots, near, far, swap_core(near), swap_core(far), in_hbm(grad_bf16)),
        (
            pltpu.VMEM((units, units), BF16),
            pltpu.VMEM((dp, units // 2 + 64, 128), BF16),
            pltpu.VMEM((units, width_part), BF16),
            pltpu.SemaphoreType.DMA,
        ),
        specs={0: SMEM, 5: HBM},
        vmem=32,
    )
    return (hidden_grad, update)


def solution(mesh):
    dp, experts = mesh.devices.shape
    x_size = 4
    split = Mesh(
        mesh.devices.reshape(dp // 2, 2, x_size, experts // x_size), ("y", "c", "x", "z")
    )
    rows, cols = ("x", "z"), ("y", "c")
    in_specs = (P(rows, cols), P(rows, None, cols), P(rows, None), P(rows, None), P(rows, None, cols))
    out_specs = (P(rows, None, cols), P(rows, None, cols))
    return jax.shard_map(per_device, mesh=split, in_specs=in_specs, out_specs=out_specs, check_vma=False)
```

time: 204 us -> 212 us (1.039)
  blocking collectives: 27.6 us -> 106 us
  waiting for transfers between devices: 76.1 us -> 14.2 us
  starting transfers between devices: 67.9 us -> 53.2 us
  Pallas kernels: 25 us -> 30.7 us
    all_to_all x1 -> x2, blocking collectives: 27.6 us -> 106 us  [exchange(): return lax.all_to_all(value, axes, split_axis=0, concat_axis=0, tiled=True)]
    all_to_all x3, waiting for transfers between devices: 49.5 us -> 9.04 us  [exchange(): return lax.all_to_all(value, axes, split_axis=0, concat_axis=0, tiled=True)]
    ppermute x3 -> x0, waiting for transfers between devices: 15.3 us -> none  [shift_y(): lax.ppermute(value, 'y', [(i, (i + step) % size) for i in range(size)])]
    all_to_all x3, starting transfers between devices: 33.3 us -> 20.3 us  [exchange(): return lax.all_to_all(value, axes, split_axis=0, concat_axis=0, tiled=True)]
    ppermute x3 -> x0, starting transfers between devices: 9.5 us -> none  [shift_y(): lax.ppermute(value, 'y', [(i, (i + step) % size) for i in range(size)])]
    ppermute x4 -> x5, starting transfers between devices: 20.2 us -> 28 us  [swap_core(): return lax.ppermute(value, 'c', [(0, 1), (1, 0)])]
    ppermute x4 -> x5, waiting for transfers between devices: 6.03 us -> 0.01 us  [swap_core(): return lax.ppermute(value, 'c', [(0, 1), (1, 0)])]
    pallas_call x8, Pallas kernels: 25 us -> 30.7 us  [call(): pl.pallas_call(kernel, out_shape=outs, grid=steps, in_specs=[specs.get(i,...]
  transfers between devices with their start and end apart: 12 -> 10, of which waited for: 9 -> 3; matrix products, arithmetic and copies ran while one was open for 1% -> 1% of each run, Pallas kernels for 7% -> 12%
where the time goes in v8:
time: 212 us
  blocking collectives  106 us (50%)
  starting transfers between devices  53.2 us (25%)
  Pallas kernels  30.7 us (14%)
  waiting for transfers between devices  14.2 us (7%)
  local copies, waits for them, and re-layouts  2.71 us (1%)
  other arithmetic  2.64 us (1%)
    all_to_all x2, blocking collectives, exchange(): return lax.all_to_all(value, axes, split_axis=0, concat_axis=0, tiled=True)  106 us
    pallas_call x8, Pallas kernels, call(): pl.pallas_call(kernel, out_shape=outs, grid=steps, in_specs=[specs.get(i,...  30.7 us
    ppermute x5, starting transfers between devices, swap_core(): return lax.ppermute(value, 'c', [(0, 1), (1, 0)])  28 us
    all_to_all x3, starting transfers between devices, exchange(): return lax.all_to_all(value, axes, split_axis=0, concat_axis=0, tiled=True)  20.3 us
    all_to_all x3, waiting for transfers between devices, exchange(): return lax.all_to_all(value, axes, split_axis=0, concat_axis=0, tiled=True)  9.04 us
    ppermute x2, waiting for transfers between devices, swap_y(): return lax.ppermute(value, 'y', [(i, i ^ flip) for i in range(size)])  5.13 us
    ppermute x2, starting transfers between devices, swap_y(): return lax.ppermute(value, 'y', [(i, i ^ flip) for i in range(size)])  4.99 us
  transfers between devices with their start and end apart: 10, of which 3 were waited for; matrix products, arithmetic and copies ran while one was open for 1% of the time, Pallas kernels for 12%

profile of v8, /device:TPU:1, one launch (start us, length us, event | category | flops | bytes accessed | tf_op | source)
XLA Modules:
  0.0 211.5 jit_solution(14906972171262980485)
XLA Ops:
  0.6 1.2 multiply_convert_fusion
  1.8 0.0 copy-start.1
  1.8 1.0 copy-done.1
  2.8 0.7 copy-done.2
  3.5 3.5 %shard_map.68 = (bf16[64,104,128]{2,1,0:T(8,128)(2,1)S(1)}, s32[1,1024]{1,0:T(1,128)S(1)}) custom-call(s32[2,512]{1,0:T(2,128)S(1)} %bitcast.23, bf16[1024,128]{1,0:T(8,128)(2,1)S(1)} %bitcast.21, bf16[512,512]{1,0:T(8,128)(2,1)S(1)} %copy-done.1), custom_call_target="tpu_custom_call" | custom-call | tf_op jit(solution)/shard_map/pallas_call | solution.py:315
  7.0 94.4 %all_to_all.25.got_ref = bf16[64,104,128]{2,1,0:T(8,128)(2,1)S(1)} all-to-all(bf16[64,104,128]{2,1,0:T(8,128)(2,1)S(1)} %get-tuple-element.13), channel_id=1, replica_groups=mesh['y'=4,'c'=2,'x'=4,'z'=16] {'x','z'}, dimensions={0} | all-to-all | bytes 3407872 | tf_op jit(solution)/shard_map/all_to_all | solution.py:30
  101.4 1.4 shard_map.70
  102.8 4.2 %all-to-all-start.1 = ((bf16[4,1280,128]{2,1,0:T(8,128)(2,1)}), bf16[4,1280,128]{2,1,0:T(8,128)(2,1)S(1)}, u32[]{:S(2)}, u32[]{:S(2)}) async-start(bf16[4,1280,128]{2,1,0:T(8,128)(2,1)} %shard_map.70), calls=%async_computation.1 | async-start | bytes 2621440 | tf_op jit(solution)/shard_map/all_to_all | solution.py:30
  107.0 0.1 pad_add_fusion.spot_ref.refs_0_
  107.0 6.0 %shard_map.69 = (bf16[4,1280,128]{2,1,0:T(8,128)(2,1)}, bf16[4,1280,128]{2,1,0:T(8,128)(2,1)}, bf16[1280,512]{1,0:T(8,128)(2,1)}) custom-call(s32[9]{0:T(128)S(1)} %pad_add_fusion.spot_ref.refs_0_, bf16[64,104,128]{2,1,0:T(8,128)(2,1)S(1)} %all_to_all.25.got_ref, bf16[1024,512]{1,0:T(8,128)(2,1)} %bitcast.26), custom_call_target="tpu_custom_call" | custom-call | tf_op jit(solution)/shard_map/pallas_call | solution.py:315
  113.0 9.3 %collective-permute-start = (bf16[4,1280,128]{2,1,0:T(8,128)(2,1)}, bf16[4,1280,128]{2,1,0:T(8,128)(2,1)S(1)}, u32[]{:S(2)}, u32[]{:S(2)}) collective-permute-start(bf16[4,1280,128]{2,1,0:T(8,128)(2,1)} %get-tuple-element.15), channel_id=1, source_target_pairs={{0,64},{64,0},{1,65},{65,1},{2,66},{66,2},{3,67},{67,3},{4,68},{68... | collective-permute-start | bytes 3932168 | tf_op jit(solution)/shard_map/ppermute | solution.py:26
  122.3 6.2 %collective-permute-start.1 = (bf16[4,1280,128]{2,1,0:T(8,128)(2,1)S(1)}, bf16[4,1280,128]{2,1,0:T(8,128)(2,1)}, u32[]{:S(2)}, u32[]{:S(2)}) collective-permute-start(bf16[4,1280,128]{2,1,0:T(8,128)(2,1)S(1)} %all-to-all-done.1.after_ref.own_hbm), channel_id=1, source_target_pairs={{0,64},{64,0},{1,65},{65,1},{2,66},{66,2},{3,67},{67,3},{4,68},{68... | collective-permute-start | bytes 3932168 | tf_op jit(solution)/shard_map/ppermute | solution.py:26
  128.5 3.6 %shard_map.71 = bf16[4,1280,128]{2,1,0:T(8,128)(2,1)} custom-call(bf16[4,1280,128]{2,1,0:T(8,128)(2,1)} %get-tuple-element.14.own_ref, bf16[4,1280,128]{2,1,0:T(8,128)(2,1)S(1)} %collective-permute-done.other_ref, bf16[4,1280,128]{2,1,0:T(8,128)(2,1)S(1)} %all-to-all-done.1.after_ref.own_hbm), custom_call_target="tpu_custom_call" | custom-call | tf_op jit(solution)/shard_map/pallas_call | solution.py:315
  132.2 3.5 %all-to-all-start.2 = ((bf16[4,1280,128]{2,1,0:T(8,128)(2,1)}), bf16[4,1280,128]{2,1,0:T(8,128)(2,1)S(1)}, u32[]{:S(2)}, u32[]{:S(2)}) async-start(bf16[4,1280,128]{2,1,0:T(8,128)(2,1)} %shard_map.71), calls=%async_computation.2 | async-start | bytes 2621440 | tf_op jit(solution)/shard_map/all_to_all | solution.py:30
  135.7 7.0 %shard_map.72 = (bf16[1024,512]{1,0:T(8,128)(2,1)}, bf16[4,576,128]{2,1,0:T(8,128)(2,1)S(1)}, bf16[4,576,128]{2,1,0:T(8,128)(2,1)}) custom-call(s32[9]{0:T(128)S(1)} %pad_add_fusion.spot_ref.refs_0_, bf16[4,1280,128]{2,1,0:T(8,128)(2,1)} %copy-done, bf16[4,1280,128]{2,1,0:T(8,128)(2,1)} %collective-permute-done.1.other_hbm, ...), custom_call_target="tpu_custom_call" | custom-call | tf_op jit(solution)/shard_map/pallas_call | solution.py:315
  142.8 1.9 collective-permute-start.2
  144.7 9.0 %all-to-all-done.2.after_ref.part_ref = bf16[4,1280,128]{2,1,0:T(8,128)(2,1)S(1)} async-done(((bf16[4,1280,128]{2,1,0:T(8,128)(2,1)}), bf16[4,1280,128]{2,1,0:T(8,128)(2,1)S(1)}, u32[]{:S(2)}, u32[]{:S(2)}) %all-to-all-start.2) | async-done | bytes 1310752 | tf_op jit(solution)/shard_map/all_to_all | solution.py:30
  153.8 0.1 shard_map.73
  153.9 11.8 %all_to_all.26.pack_part_ref = bf16[4,576,128]{2,1,0:T(8,128)(2,1)S(1)} all-to-all(bf16[4,576,128]{2,1,0:T(8,128)(2,1)S(1)} %shard_map.73), channel_id=1, replica_groups=mesh['y'=4,'c'=2,'x'=4,'z'=16] {'y'}, dimensions={0} | all-to-all | bytes 1179648 | tf_op jit(solution)/shard_map/all_to_all | solution.py:30
  165.7 1.2 shard_map.74
  166.9 12.5 %all-to-all-start.4 = ((bf16[64,24,128]{2,1,0:T(8,128)(2,1)}), bf16[64,24,128]{2,1,0:T(8,128)(2,1)S(1)}, u32[]{:S(2)}, u32[]{:S(2)}) async-start(bf16[64,24,128]{2,1,0:T(8,128)(2,1)} %get-tuple-element.19), calls=%async_computation.4 | async-start | bytes 786432 | tf_op jit(solution)/shard_map/all_to_all | solution.py:30
  179.5 2.2 %collective-permute-start.3 = (bf16[576,128]{1,0:T(8,128)(2,1)S(1)}, bf16[576,128]{1,0:T(8,128)(2,1)S(1)}, u32[]{:S(2)}, u32[]{:S(2)}) collective-permute-start(bf16[576,128]{1,0:T(8,128)(2,1)S(1)} %get-tuple-element.20), channel_id=1, source_target_pairs={{0,128},{128,0},{256,384},{384,256},{1,129},{129,1},{257,385},{385... | collective-permute-start | bytes 442376 | tf_op jit(solution)/shard_map/ppermute | solution.py:22
  181.7 4.0 %collective-permute-done.3 = bf16[576,128]{1,0:T(8,128)(2,1)S(1)} collective-permute-done((bf16[576,128]{1,0:T(8,128)(2,1)S(1)}, bf16[576,128]{1,0:T(8,128)(2,1)S(1)}, u32[]{:S(2)}, u32[]{:S(2)}) %collective-permute-start.3) | collective-permute-done | bytes 147488 | tf_op jit(solution)/shard_map/ppermute | solution.py:22
  185.7 2.8 %collective-permute-start.4 = (bf16[2,576,128]{2,1,0:T(8,128)(2,1)S(1)}, bf16[2,576,128]{2,1,0:T(8,128)(2,1)S(1)}, u32[]{:S(2)}, u32[]{:S(2)}) collective-permute-start(bf16[2,576,128]{2,1,0:T(8,128)(2,1)S(1)} %pad_maximum_fusion.refs_1_), channel_id=1, source_target_pairs={{0,384},{128,256},{256,128},{384,0},{1,385},{129,257},{257,129},{3... | collective-permute-start | bytes 884744 | tf_op jit(solution)/shard_map/ppermute | solution.py:22
  188.5 5.0 %collective-permute-start.5 = (bf16[2,576,128]{2,1,0:T(8,128)(2,1)S(1)}, bf16[2,576,128]{2,1,0:T(8,128)(2,1)S(1)}, u32[]{:S(2)}, u32[]{:S(2)}) collective-permute-start(bf16[2,576,128]{2,1,0:T(8,128)(2,1)S(1)} %pad_maximum_fusion.refs_1_), channel_id=1, source_target_pairs={{0,64},{64,0},{1,65},{65,1},{2,66},{66,2},{3,67},{67,3},{4,68},{68... | collective-permute-start | bytes 884744 | tf_op jit(solution)/shard_map/ppermute | solution.py:26
  193.5 1.2 collective-permute-done.4.refs_2_
  194.7 5.6 %collective-permute-start.6 = (bf16[2,576,128]{2,1,0:T(8,128)(2,1)S(1)}, bf16[2,576,128]{2,1,0:T(8,128)(2,1)S(1)}, u32[]{:S(2)}, u32[]{:S(2)}) collective-permute-start(bf16[2,576,128]{2,1,0:T(8,128)(2,1)S(1)} %collective-permute-done.4.refs_2_), channel_id=1, source_target_pairs={{0,64},{64,0},{1,65},{65,1},{2,66},{66,2},{3,67},{67,3},{4,68},{68... | collective-permute-start | bytes 884744 | tf_op jit(solution)/shard_map/ppermute | solution.py:26
  200.3 1.4 iota_compare_fusion
  201.7 0.0 copy-start.3
  201.7 7.9 %shard_map.75 = f32[1,1024,512]{2,1,0:T(8,128)} custom-call(s32[9]{0:T(128)S(1)} %pad_add_fusion.spot_ref.refs_0_, bf16[2,576,128]{2,1,0:T(8,128)(2,1)S(1)} %pad_maximum_fusion.refs_1_, bf16[2,576,128]{2,1,0:T(8,128)(2,1)S(1)} %collective-permute-done.4.refs_2_, bf16[2,576,128]{2,1,0:T(8,128)(2,1)S(1)} %collective-permute-done.5.refs_3_, ...), custom_call_target="tpu_custom_call" | custom-call | tf_op jit(solution)/shard_map/pallas_call | solution.py:315
  209.6 1.0 fusion.1
  210.6 1.0 copy.8
  (13 shorter events, 0.1 us)
Async XLA Ops:
  1.8 1.0 copy-start.1
  2.8 0.7 copy-start.2
  102.8 19.6 %all-to-all-start.1 = ((bf16[4,1280,128]{2,1,0:T(8,128)(2,1)}), bf16[4,1280,128]{2,1,0:T(8,128)(2,1)S(1)}, u32[]{:S(2)}, u32[]{:S(2)}) async-start(bf16[4,1280,128]{2,1,0:T(8,128)(2,1)} %shard_map.70), calls=%async_computation.1 | async-start | bytes 2621440 | tf_op jit(solution)/shard_map/all_to_all | solution.py:30
  113.0 15.5 %collective-permute-start = (bf16[4,1280,128]{2,1,0:T(8,128)(2,1)}, bf16[4,1280,128]{2,1,0:T(8,128)(2,1)S(1)}, u32[]{:S(2)}, u32[]{:S(2)}) collective-permute-start(bf16[4,1280,128]{2,1,0:T(8,128)(2,1)} %get-tuple-element.15), channel_id=1, source_target_pairs={{0,64},{64,0},{1,65},{65,1},{2,66},{66,2},{3,67},{67,3},{4,68},{68... | collective-permute-start | bytes 3932168 | tf_op jit(solution)/shard_map/ppermute | solution.py:26
  122.3 9.8 %copy-start = (bf16[4,1280,128]{2,1,0:T(8,128)(2,1)}, bf16[4,1280,128]{2,1,0:T(8,128)(2,1)S(1)}, u32[]{:S(2)}) copy-start(bf16[4,1280,128]{2,1,0:T(8,128)(2,1)S(1)} %all-to-all-done.1.after_ref.own_hbm) | copy-start | bytes 3932164
  122.3 13.4 %collective-permute-start.1 = (bf16[4,1280,128]{2,1,0:T(8,128)(2,1)S(1)}, bf16[4,1280,128]{2,1,0:T(8,128)(2,1)}, u32[]{:S(2)}, u32[]{:S(2)}) collective-permute-start(bf16[4,1280,128]{2,1,0:T(8,128)(2,1)S(1)} %all-to-all-done.1.after_ref.own_hbm), channel_id=1, source_target_pairs={{0,64},{64,0},{1,65},{65,1},{2,66},{66,2},{3,67},{67,3},{4,68},{68... | collective-permute-start | bytes 3932168 | tf_op jit(solution)/shard_map/ppermute | solution.py:26
  132.2 21.6 %all-to-all-start.2 = ((bf16[4,1280,128]{2,1,0:T(8,128)(2,1)}), bf16[4,1280,128]{2,1,0:T(8,128)(2,1)S(1)}, u32[]{:S(2)}, u32[]{:S(2)}) async-start(bf16[4,1280,128]{2,1,0:T(8,128)(2,1)} %shard_map.71), calls=%async_computation.2 | async-start | bytes 2621440 | tf_op jit(solution)/shard_map/all_to_all | solution.py:30
  142.8 11.0 %collective-permute-start.2 = (bf16[4,576,128]{2,1,0:T(8,128)(2,1)}, bf16[4,576,128]{2,1,0:T(8,128)(2,1)S(1)}, u32[]{:S(2)}, u32[]{:S(2)}) collective-permute-start(bf16[4,576,128]{2,1,0:T(8,128)(2,1)} %get-tuple-element.18), channel_id=1, source_target_pairs={{0,64},{64,0},{1,65},{65,1},{2,66},{66,2},{3,67},{67,3},{4,68},{68... | collective-permute-start | bytes 1769480 | tf_op jit(solution)/shard_map/ppermute | solution.py:26
  166.9 42.6 %all-to-all-start.4 = ((bf16[64,24,128]{2,1,0:T(8,128)(2,1)}), bf16[64,24,128]{2,1,0:T(8,128)(2,1)S(1)}, u32[]{:S(2)}, u32[]{:S(2)}) async-start(bf16[64,24,128]{2,1,0:T(8,128)(2,1)} %get-tuple-element.19), calls=%async_computation.4 | async-start | bytes 786432 | tf_op jit(solution)/shard_map/all_to_all | solution.py:30
  179.5 6.2 %collective-permute-start.3 = (bf16[576,128]{1,0:T(8,128)(2,1)S(1)}, bf16[576,128]{1,0:T(8,128)(2,1)S(1)}, u32[]{:S(2)}, u32[]{:S(2)}) collective-permute-start(bf16[576,128]{1,0:T(8,128)(2,1)S(1)} %get-tuple-element.20), channel_id=1, source_target_pairs={{0,128},{128,0},{256,384},{384,256},{1,129},{129,1},{257,385},{385... | collective-permute-start | bytes 442376 | tf_op jit(solution)/shard_map/ppermute | solution.py:22
  185.7 9.0 %collective-permute-start.4 = (bf16[2,576,128]{2,1,0:T(8,128)(2,1)S(1)}, bf16[2,576,128]{2,1,0:T(8,128)(2,1)S(1)}, u32[]{:S(2)}, u32[]{:S(2)}) collective-permute-start(bf16[2,576,128]{2,1,0:T(8,128)(2,1)S(1)} %pad_maximum_fusion.refs_1_), channel_id=1, source_target_pairs={{0,384},{128,256},{256,128},{384,0},{1,385},{129,257},{257,129},{3... | collective-permute-start | bytes 884744 | tf_op jit(solution)/shard_map/ppermute | solution.py:22
  188.5 13.1 %collective-permute-start.5 = (bf16[2,576,128]{2,1,0:T(8,128)(2,1)S(1)}, bf16[2,576,128]{2,1,0:T(8,128)(2,1)S(1)}, u32[]{:S(2)}, u32[]{:S(2)}) collective-permute-start(bf16[2,576,128]{2,1,0:T(8,128)(2,1)S(1)} %pad_maximum_fusion.refs_1_), channel_id=1, source_target_pairs={{0,64},{64,0},{1,65},{65,1},{2,66},{66,2},{3,67},{67,3},{4,68},{68... | collective-permute-start | bytes 884744 | tf_op jit(solution)/shard_map/ppermute | solution.py:26
  194.7 7.0 %collective-permute-start.6 = (bf16[2,576,128]{2,1,0:T(8,128)(2,1)S(1)}, bf16[2,576,128]{2,1,0:T(8,128)(2,1)S(1)}, u32[]{:S(2)}, u32[]{:S(2)}) collective-permute-start(bf16[2,576,128]{2,1,0:T(8,128)(2,1)S(1)} %collective-permute-done.4.refs_2_), channel_id=1, source_target_pairs={{0,64},{64,0},{1,65},{65,1},{2,66},{66,2},{3,67},{67,3},{4,68},{68... | collective-permute-start | bytes 884744 | tf_op jit(solution)/shard_map/ppermute | solution.py:26
  201.7 7.9 %copy-start.3 = (f32[512,2]{0,1:T(2,128)S(1)}, f32[512,2]{0,1:T(2,128)}, u32[]{:S(2)}) copy-start(f32[512,2]{0,1:T(2,128)} %param.7) | copy-start | bytes 12292

commit v9 on v7

--- a/solution.py
+++ b/solution.py
@@ -144,7 +144,6 @@
 
     fetch_got = fetch(got_hbm, got_ref, 16, 0)
     fetch_weight = fetch(weight_hbm, weight_ref, part, groups)
-    fetch_turned = fetch(turned_hbm, turned_ref, part, 2 * groups)
 
     number = row_numbers(256)
     order = one_hot(((number >> 2) & 15) * 16 + (number >> 6) * 4 + (number & 3), lane_numbers(256))
@@ -156,6 +155,7 @@
             lanes = slice(b * 128, (b + 1) * 128)
             rows_ref[256 * s : 256 * (s + 1), lanes] = got_ref[here, 16 * b : 16 * (b + 1), :].reshape(256, 128)
             rows_ref[experts * 16 + s * 64 : experts * 16 + (s + 1) * 64, lanes] = late[b * 64 : (b + 1) * 64]
+    fetch_turned = fetch(turned_hbm, turned_ref, part, 2 * groups)
     rows = rows_ref[...]
     core = spot_ref[blocks]
     count = rows_ref.shape[0]
@@ -212,7 +212,18 @@
     out_ref[...] = (own_ref[...].astype(F32) + other_ref[...].astype(F32)).astype(BF16)
 
 
-def return_kernel(part_ref, out_ref, pack_ref):
+def store_pieces(source, target, count, sems):
+    size = source.shape[0] // count
+    copies = []
+    for k in range(count):
+        piece = slice(k * size, (k + 1) * size)
+        copies.append(pltpu.make_async_copy(source.at[piece], target.at[piece], sems.at[k]))
+        copies[-1].start()
+    for copy in copies:
+        copy.wait()
+
+
+def return_kernel(part_ref, out_hbm, pack_ref, out_ref, sems):
     experts = out_ref.shape[0]
     count = part_ref.shape[1] - pack_ref.shape[0]
     number = row_numbers(128)
@@ -226,11 +237,12 @@
     for s in range(experts // 16):
         left = nn_dot(take, total[experts * 16 + s * 64 : experts * 16 + (s + 1) * 64])
         out_ref[16 * s : 16 * (s + 1), 16:24, :] = left.reshape(16, 8, 128).astype(BF16)
+    store_pieces(out_ref, out_hbm, 4, sems)
 
 
 def ortho_kernel(
-    width, spot_ref, own_near_ref, own_far_ref, other_near_ref, other_far_ref, gradb_hbm, out_ref,
-    gram_ref, pack_ref, gradb_ref, sem,
+    width, spot_ref, own_near_ref, own_far_ref, other_near_ref, other_far_ref, gradb_hbm, out_hbm,
+    gram_ref, pack_ref, gradb_ref, out_ref, sem, sems,
 ):
     fetch_grad = pltpu.make_async_copy(gradb_hbm, gradb_ref, sem)
     fetch_grad.start()
@@ -273,10 +285,20 @@
     second = (1.5 * first.astype(F32) - 0.5 * apply(first)).astype(BF16)
     power_one = apply(second).astype(BF16)
     power_two = apply(power_one).astype(BF16)
-    power_three = apply(power_two)
-    total = 1.5 * second.astype(F32)
-    total = total - 0.5 * (2.25 * power_one.astype(F32) - 1.5 * power_two.astype(F32) + 0.25 * power_three)
-    out_ref[0] = total * width**0.5
+    near_terms = 1.5 * second.astype(F32) - 0.5 * (2.25 * power_one.astype(F32) - 1.5 * power_two.astype(F32))
+    size = gram.shape[0] // 2
+    part = size // 2
+    stores = []
+    for h in range(2):
+        rows = slice(h * size, (h + 1) * size)
+        power_three = nn_dot(gram[rows], power_two) * inverse
+        out_ref[rows] = (near_terms[rows] - 0.125 * power_three) * width**0.5
+        for q in range(2):
+            piece = slice(h * size + q * part, h * size + (q + 1) * part)
+            stores.append(pltpu.make_async_copy(out_ref.at[piece], out_hbm.at[0, piece], sems.at[2 * h + q]))
+            stores[-1].start()
+    for copy in stores:
+        copy.wait()
 
 
 def in_hbm(value):
@@ -370,7 +392,12 @@
     both = call(add_kernel, dp_parts, (own, swap_core(other)), vmem=12)
     parts = exchange(both, "y")
     sent_back, mine = call(
-        return_kernel, (pltpu.HBM((experts, 24, 128), BF16), shape(pack_rows, 128)), (parts,), vmem=12
+        return_kernel,
+        (pltpu.HBM((experts, 24, 128), BF16), shape(pack_rows, 128)),
+        (parts,),
+        (pltpu.VMEM((experts, 24, 128), BF16), pltpu.SemaphoreType.DMA((4,))),
+        out_specs={0: HBM},
+        vmem=12,
     )
     returned = exchange(sent_back, EXPERT).reshape(experts * 24, unit_part)
     chosen = (jnp.arange(experts * 24, dtype=jnp.int32)[:, None] == slot_index).astype(BF16)
@@ -388,9 +415,12 @@
             pltpu.VMEM((units, units), BF16),
             pltpu.VMEM((dp, units // 2 + 64, 128), BF16),
             pltpu.VMEM((units, width_part), BF16),
+            pltpu.VMEM((units, width_part), F32),
             pltpu.SemaphoreType.DMA,
+            pltpu.SemaphoreType.DMA((4,)),
         ),
         specs={0: SMEM, 5: HBM},
+        out_specs={0: HBM},
         vmem=32,
     )
     return (hidden_grad, update)

time: 204 us -> 203 us (level)
  no operation moved by 1% of the time
where the time goes in v9:
time: 203 us
  waiting for transfers between devices  76.1 us (37%)
  starting transfers between devices  67.9 us (33%)
  blocking collectives  27.6 us (14%)
  Pallas kernels  24.5 us (12%)
  other arithmetic  2.87 us (1%)
    all_to_all x3, waiting for transfers between devices, exchange(): return lax.all_to_all(value, axes, split_axis=0, concat_axis=0, tiled=True)  49.5 us
    all_to_all x3, starting transfers between devices, exchange(): return lax.all_to_all(value, axes, split_axis=0, concat_axis=0, tiled=True)  33.3 us
    all_to_all x1, blocking collectives, exchange(): return lax.all_to_all(value, axes, split_axis=0, concat_axis=0, tiled=True)  27.6 us
    pallas_call x8, Pallas kernels, call(): pl.pallas_call(kernel, out_shape=outs, grid=steps, in_specs=[specs.get(i,...  24.5 us
    ppermute x4, starting transfers between devices, swap_core(): return lax.ppermute(value, 'c', [(0, 1), (1, 0)])  20.2 us
    ppermute x3, waiting for transfers between devices, shift_y(): lax.ppermute(value, 'y', [(i, (i + step) % size) for i in range(size)])  15.3 us
    ppermute x3, starting transfers between devices, shift_y(): lax.ppermute(value, 'y', [(i, (i + step) % size) for i in range(size)])  9.5 us
    ppermute x4, waiting for transfers between devices, swap_core(): return lax.ppermute(value, 'c', [(0, 1), (1, 0)])  6.03 us
  transfers between devices with their start and end apart: 12, of which 9 were waited for; matrix products, arithmetic and copies ran while one was open for 1% of the time, Pallas kernels for 7%

profile of v9, /device:TPU:1, one launch (start us, length us, event | category | flops | bytes accessed | tf_op | source)
XLA Modules:
  0.0 202.5 jit_solution(8442227097622571192)
XLA Ops:
  0.6 1.2 multiply_convert_fusion
  2.5 2.0 shard_map.68
  4.5 19.1 %all-to-all-start.1 = ((bf16[64,24,128]{2,1,0:T(8,128)(2,1)}), bf16[64,24,128]{2,1,0:T(8,128)(2,1)S(1)}, u32[]{:S(2)}, u32[]{:S(2)}) async-start(bf16[64,24,128]{2,1,0:T(8,128)(2,1)} %get-tuple-element.14), calls=%async_computation.1 | async-start | bytes 786432 | tf_op jit(solution)/shard_map/all_to_all | solution.py:30
  23.6 2.4 %shard_map.69 = bf16[64,80,128]{2,1,0:T(8,128)(2,1)} custom-call(s32[1,1024]{1,0:T(1,128)S(1)} %get-tuple-element.12.main_ref, s32[1,1024]{1,0:T(1,128)S(1)} %get-tuple-element.13.late_ref, bf16[512,512]{1,0:T(8,128)(2,1)S(1)} %copy-done), custom_call_target="tpu_custom_call" | custom-call | tf_op jit(solution)/shard_map/pallas_call | solution.py:316
  26.0 22.3 %all-to-all-done.1.got_ref = bf16[64,24,128]{2,1,0:T(8,128)(2,1)S(1)} async-done(((bf16[64,24,128]{2,1,0:T(8,128)(2,1)}), bf16[64,24,128]{2,1,0:T(8,128)(2,1)S(1)}, u32[]{:S(2)}, u32[]{:S(2)}) %all-to-all-start.1) | async-done | bytes 393248 | tf_op jit(solution)/shard_map/all_to_all | solution.py:30
  48.4 7.8 %all-to-all-start = ((bf16[64,80,128]{2,1,0:T(8,128)(2,1)}), bf16[64,80,128]{2,1,0:T(8,128)(2,1)}, u32[]{:S(2)}, u32[]{:S(2)}) async-start(bf16[64,80,128]{2,1,0:T(8,128)(2,1)} %shard_map.69), calls=%async_computation | async-start | bytes 2621440 | tf_op jit(solution)/shard_map/all_to_all | solution.py:30
  56.4 4.6 %collective-permute-start.2 = (bf16[1280,128]{1,0:T(8,128)(2,1)S(1)}, bf16[1280,128]{1,0:T(8,128)(2,1)S(1)}, u32[]{:S(2)}, u32[]{:S(2)}) collective-permute-start(bf16[1280,128]{1,0:T(8,128)(2,1)S(1)} %shard_map.70), channel_id=1, source_target_pairs={{0,384},{128,0},{256,128},{384,256},{1,385},{129,1},{257,129},{385... | collective-permute-start | bytes 983048 | tf_op jit(solution)/shard_map/ppermute | solution.py:18
  61.1 2.3 %collective-permute-start.1 = (bf16[1280,128]{1,0:T(8,128)(2,1)S(1)}, bf16[1280,128]{1,0:T(8,128)(2,1)S(1)}, u32[]{:S(2)}, u32[]{:S(2)}) collective-permute-start(bf16[1280,128]{1,0:T(8,128)(2,1)S(1)} %shard_map.70), channel_id=1, source_target_pairs={{0,256},{128,384},{256,0},{384,128},{1,257},{129,385},{257,1},{385... | collective-permute-start | bytes 983048 | tf_op jit(solution)/shard_map/ppermute | solution.py:18
  63.3 2.6 %collective-permute-start = (bf16[1280,128]{1,0:T(8,128)(2,1)S(1)}, bf16[1280,128]{1,0:T(8,128)(2,1)S(1)}, u32[]{:S(2)}, u32[]{:S(2)}) collective-permute-start(bf16[1280,128]{1,0:T(8,128)(2,1)S(1)} %shard_map.70), channel_id=1, source_target_pairs={{0,128},{128,256},{256,384},{384,0},{1,129},{129,257},{257,385},{3... | collective-permute-start | bytes 983048 | tf_op jit(solution)/shard_map/ppermute | solution.py:18
  65.9 1.6 collective-permute-done.2
  67.5 4.4 %collective-permute-done.1 = bf16[1280,128]{1,0:T(8,128)(2,1)S(1)} collective-permute-done((bf16[1280,128]{1,0:T(8,128)(2,1)S(1)}, bf16[1280,128]{1,0:T(8,128)(2,1)S(1)}, u32[]{:S(2)}, u32[]{:S(2)}) %collective-permute-start.1) | collective-permute-done | bytes 327712 | tf_op jit(solution)/shard_map/ppermute | solution.py:18
  72.0 9.2 %collective-permute-done = bf16[1280,128]{1,0:T(8,128)(2,1)S(1)} collective-permute-done((bf16[1280,128]{1,0:T(8,128)(2,1)S(1)}, bf16[1280,128]{1,0:T(8,128)(2,1)S(1)}, u32[]{:S(2)}, u32[]{:S(2)}) %collective-permute-start) | collective-permute-done | bytes 327712 | tf_op jit(solution)/shard_map/ppermute | solution.py:18
  81.4 2.3 %collective-permute-start.3 = (bf16[4,1280,128]{2,1,0:T(8,128)(2,1)S(1)}, bf16[4,1280,128]{2,1,0:T(8,128)(2,1)S(1)}, u32[]{:S(2)}, u32[]{:S(2)}) collective-permute-start(bf16[4,1280,128]{2,1,0:T(8,128)(2,1)S(1)} %pad_maximum_fusion.own_ref), channel_id=1, source_target_pairs={{0,64},{64,0},{1,65},{65,1},{2,66},{66,2},{3,67},{67,3},{4,68},{68... | collective-permute-start | bytes 3932168 | tf_op jit(solution)/shard_map/ppermute | solution.py:26
  83.8 2.5 %collective-permute-done.3.other_ref = bf16[4,1280,128]{2,1,0:T(8,128)(2,1)S(1)} collective-permute-done((bf16[4,1280,128]{2,1,0:T(8,128)(2,1)S(1)}, bf16[4,1280,128]{2,1,0:T(8,128)(2,1)S(1)}, u32[]{:S(2)}, u32[]{:S(2)}) %collective-permute-start.3) | collective-permute-done | bytes 1310752 | tf_op jit(solution)/shard_map/ppermute | solution.py:26
  86.3 3.2 %shard_map.71.turned_hbm = bf16[1024,1280]{1,0:T(8,128)(2,1)} custom-call(s32[8]{0:T(128)S(1)} %get-tuple-element.22.spot_ref, bf16[4,1280,128]{2,1,0:T(8,128)(2,1)S(1)} %pad_maximum_fusion.own_ref, bf16[4,1280,128]{2,1,0:T(8,128)(2,1)S(1)} %collective-permute-done.3.other_ref), custom_call_target="tpu_custom_call" | custom-call | tf_op jit(solution)/shard_map/pallas_call | solution.py:316
  89.5 27.1 %all-to-all-done.got_hbm = bf16[64,80,128]{2,1,0:T(8,128)(2,1)} async-done(((bf16[64,80,128]{2,1,0:T(8,128)(2,1)}), bf16[64,80,128]{2,1,0:T(8,128)(2,1)}, u32[]{:S(2)}, u32[]{:S(2)}) %all-to-all-start) | async-done | bytes 1310752 | tf_op jit(solution)/shard_map/all_to_all | solution.py:30
  116.6 7.7 %shard_map.72 = (bf16[4,1856,128]{2,1,0:T(8,128)(2,1)S(1)}, bf16[4,1856,128]{2,1,0:T(8,128)(2,1)S(1)}, bf16[1024,512]{1,0:T(8,128)(2,1)}) custom-call(s32[9]{0:T(128)S(1)} %pad_add_fusion.spot_ref.refs_0_, bf16[64,80,128]{2,1,0:T(8,128)(2,1)} %all-to-all-done.got_hbm, bf16[1024,512]{1,0:T(8,128)(2,1)} %bitcast.31, bf16[1024,1280]{1,0:T(8,128)(2,1)} %shard_map.71.turned_hbm), custom_call_target="tpu_custom_call" | custom-call | tf_op jit(solution)/shard_map/pallas_call | solution.py:316
  124.3 7.6 %collective-permute-start.4 = (bf16[4,1856,128]{2,1,0:T(8,128)(2,1)S(1)}, bf16[4,1856,128]{2,1,0:T(8,128)(2,1)S(1)}, u32[]{:S(2)}, u32[]{:S(2)}) collective-permute-start(bf16[4,1856,128]{2,1,0:T(8,128)(2,1)S(1)} %get-tuple-element.16), channel_id=1, source_target_pairs={{0,64},{64,0},{1,65},{65,1},{2,66},{66,2},{3,67},{67,3},{4,68},{68... | collective-permute-start | bytes 5701640 | tf_op jit(solution)/shard_map/ppermute | solution.py:26
  131.9 3.5 %collective-permute-done.4.other_ref = bf16[4,1856,128]{2,1,0:T(8,128)(2,1)S(1)} collective-permute-done((bf16[4,1856,128]{2,1,0:T(8,128)(2,1)S(1)}, bf16[4,1856,128]{2,1,0:T(8,128)(2,1)S(1)}, u32[]{:S(2)}, u32[]{:S(2)}) %collective-permute-start.4) | collective-permute-done | bytes 1900576 | tf_op jit(solution)/shard_map/ppermute | solution.py:26
  135.8 27.6 %all_to_all.20.part_ref = bf16[4,1856,128]{2,1,0:T(8,128)(2,1)S(1)} all-to-all(bf16[4,1856,128]{2,1,0:T(8,128)(2,1)S(1)} %shard_map.73), channel_id=1, replica_groups=mesh['y'=4,'c'=2,'x'=4,'z'=16] {'y'}, dimensions={0} | all-to-all | bytes 3801088 | tf_op jit(solution)/shard_map/all_to_all | solution.py:30
  163.5 1.3 shard_map.74
  164.7 6.3 %all-to-all-start.3 = ((bf16[64,24,128]{2,1,0:T(8,128)(2,1)}), bf16[64,24,128]{2,1,0:T(8,128)(2,1)S(1)}, u32[]{:S(2)}, u32[]{:S(2)}) async-start(bf16[64,24,128]{2,1,0:T(8,128)(2,1)} %get-tuple-element.17), calls=%async_computation.3 | async-start | bytes 786432 | tf_op jit(solution)/shard_map/all_to_all | solution.py:30
  171.1 2.2 %collective-permute-start.5 = (bf16[576,128]{1,0:T(8,128)(2,1)S(1)}, bf16[576,128]{1,0:T(8,128)(2,1)S(1)}, u32[]{:S(2)}, u32[]{:S(2)}) collective-permute-start(bf16[576,128]{1,0:T(8,128)(2,1)S(1)} %get-tuple-element.18), channel_id=1, source_target_pairs={{0,128},{128,0},{256,384},{384,256},{1,129},{129,1},{257,385},{385... | collective-permute-start | bytes 442376 | tf_op jit(solution)/shard_map/ppermute | solution.py:22
  173.3 4.0 %collective-permute-done.5 = bf16[576,128]{1,0:T(8,128)(2,1)S(1)} collective-permute-done((bf16[576,128]{1,0:T(8,128)(2,1)S(1)}, bf16[576,128]{1,0:T(8,128)(2,1)S(1)}, u32[]{:S(2)}, u32[]{:S(2)}) %collective-permute-start.5) | collective-permute-done | bytes 147488 | tf_op jit(solution)/shard_map/ppermute | solution.py:22
  177.3 2.8 %collective-permute-start.6 = (bf16[2,576,128]{2,1,0:T(8,128)(2,1)S(1)}, bf16[2,576,128]{2,1,0:T(8,128)(2,1)S(1)}, u32[]{:S(2)}, u32[]{:S(2)}) collective-permute-start(bf16[2,576,128]{2,1,0:T(8,128)(2,1)S(1)} %pad_maximum_fusion.1.refs_1_), channel_id=1, source_target_pairs={{0,384},{128,256},{256,128},{384,0},{1,385},{129,257},{257,129},{3... | collective-permute-start | bytes 884744 | tf_op jit(solution)/shard_map/ppermute | solution.py:22
  180.1 4.8 %collective-permute-start.7 = (bf16[2,576,128]{2,1,0:T(8,128)(2,1)S(1)}, bf16[2,576,128]{2,1,0:T(8,128)(2,1)S(1)}, u32[]{:S(2)}, u32[]{:S(2)}) collective-permute-start(bf16[2,576,128]{2,1,0:T(8,128)(2,1)S(1)} %pad_maximum_fusion.1.refs_1_), channel_id=1, source_target_pairs={{0,64},{64,0},{1,65},{65,1},{2,66},{66,2},{3,67},{67,3},{4,68},{68... | collective-permute-start | bytes 884744 | tf_op jit(solution)/shard_map/ppermute | solution.py:26
  185.0 1.3 collective-permute-done.6.refs_2_
  186.3 5.5 %collective-permute-start.8 = (bf16[2,576,128]{2,1,0:T(8,128)(2,1)S(1)}, bf16[2,576,128]{2,1,0:T(8,128)(2,1)S(1)}, u32[]{:S(2)}, u32[]{:S(2)}) collective-permute-start(bf16[2,576,128]{2,1,0:T(8,128)(2,1)S(1)} %collective-permute-done.6.refs_2_), channel_id=1, source_target_pairs={{0,64},{64,0},{1,65},{65,1},{2,66},{66,2},{3,67},{67,3},{4,68},{68... | collective-permute-start | bytes 884744 | tf_op jit(solution)/shard_map/ppermute | solution.py:26
  191.7 1.4 iota_compare_fusion
  193.1 7.4 %shard_map.75 = f32[1,1024,512]{2,1,0:T(8,128)} custom-call(s32[9]{0:T(128)S(1)} %pad_add_fusion.spot_ref.refs_0_, bf16[2,576,128]{2,1,0:T(8,128)(2,1)S(1)} %pad_maximum_fusion.1.refs_1_, bf16[2,576,128]{2,1,0:T(8,128)(2,1)S(1)} %collective-permute-done.6.refs_2_, bf16[2,576,128]{2,1,0:T(8,128)(2,1)S(1)} %collective-permute-done.7.refs_3_, ...), custom_call_target="tpu_custom_call" | custom-call | tf_op jit(solution)/shard_map/pallas_call | solution.py:316
  200.6 1.0 fusion.1
  201.5 1.0 copy.8
  (15 shorter events, 1.6 us)
Async XLA Ops:
  0.6 23.0 %copy-start = (bf16[512,512]{1,0:T(8,128)(2,1)S(1)}, bf16[512,512]{1,0:T(8,128)(2,1)}, u32[]{:S(2)}) copy-start(bf16[512,512]{1,0:T(8,128)(2,1)} %grad_ref.1) | copy-start | bytes 1572868
  1.9 0.7 copy-start.1
  4.5 43.9 %all-to-all-start.1 = ((bf16[64,24,128]{2,1,0:T(8,128)(2,1)}), bf16[64,24,128]{2,1,0:T(8,128)(2,1)S(1)}, u32[]{:S(2)}, u32[]{:S(2)}) async-start(bf16[64,24,128]{2,1,0:T(8,128)(2,1)} %get-tuple-element.14), calls=%async_computation.1 | async-start | bytes 786432 | tf_op jit(solution)/shard_map/all_to_all | solution.py:30
  48.4 68.3 %all-to-all-start = ((bf16[64,80,128]{2,1,0:T(8,128)(2,1)}), bf16[64,80,128]{2,1,0:T(8,128)(2,1)}, u32[]{:S(2)}, u32[]{:S(2)}) async-start(bf16[64,80,128]{2,1,0:T(8,128)(2,1)} %shard_map.69), calls=%async_computation | async-start | bytes 2621440 | tf_op jit(solution)/shard_map/all_to_all | solution.py:30
  56.4 11.1 %collective-permute-start.2 = (bf16[1280,128]{1,0:T(8,128)(2,1)S(1)}, bf16[1280,128]{1,0:T(8,128)(2,1)S(1)}, u32[]{:S(2)}, u32[]{:S(2)}) collective-permute-start(bf16[1280,128]{1,0:T(8,128)(2,1)S(1)} %shard_map.70), channel_id=1, source_target_pairs={{0,384},{128,0},{256,128},{384,256},{1,385},{129,1},{257,129},{385... | collective-permute-start | bytes 983048 | tf_op jit(solution)/shard_map/ppermute | solution.py:18
  61.1 10.9 %collective-permute-start.1 = (bf16[1280,128]{1,0:T(8,128)(2,1)S(1)}, bf16[1280,128]{1,0:T(8,128)(2,1)S(1)}, u32[]{:S(2)}, u32[]{:S(2)}) collective-permute-start(bf16[1280,128]{1,0:T(8,128)(2,1)S(1)} %shard_map.70), channel_id=1, source_target_pairs={{0,256},{128,384},{256,0},{384,128},{1,257},{129,385},{257,1},{385... | collective-permute-start | bytes 983048 | tf_op jit(solution)/shard_map/ppermute | solution.py:18
  63.3 17.9 %collective-permute-start = (bf16[1280,128]{1,0:T(8,128)(2,1)S(1)}, bf16[1280,128]{1,0:T(8,128)(2,1)S(1)}, u32[]{:S(2)}, u32[]{:S(2)}) collective-permute-start(bf16[1280,128]{1,0:T(8,128)(2,1)S(1)} %shard_map.70), channel_id=1, source_target_pairs={{0,128},{128,256},{256,384},{384,0},{1,129},{129,257},{257,385},{3... | collective-permute-start | bytes 983048 | tf_op jit(solution)/shard_map/ppermute | solution.py:18
  81.4 4.9 %collective-permute-start.3 = (bf16[4,1280,128]{2,1,0:T(8,128)(2,1)S(1)}, bf16[4,1280,128]{2,1,0:T(8,128)(2,1)S(1)}, u32[]{:S(2)}, u32[]{:S(2)}) collective-permute-start(bf16[4,1280,128]{2,1,0:T(8,128)(2,1)S(1)} %pad_maximum_fusion.own_ref), channel_id=1, source_target_pairs={{0,64},{64,0},{1,65},{65,1},{2,66},{66,2},{3,67},{67,3},{4,68},{68... | collective-permute-start | bytes 3932168 | tf_op jit(solution)/shard_map/ppermute | solution.py:26
  124.3 11.1 %collective-permute-start.4 = (bf16[4,1856,128]{2,1,0:T(8,128)(2,1)S(1)}, bf16[4,1856,128]{2,1,0:T(8,128)(2,1)S(1)}, u32[]{:S(2)}, u32[]{:S(2)}) collective-permute-start(bf16[4,1856,128]{2,1,0:T(8,128)(2,1)S(1)} %get-tuple-element.16), channel_id=1, source_target_pairs={{0,64},{64,0},{1,65},{65,1},{2,66},{66,2},{3,67},{67,3},{4,68},{68... | collective-permute-start | bytes 5701640 | tf_op jit(solution)/shard_map/ppermute | solution.py:26
  164.7 35.8 %all-to-all-start.3 = ((bf16[64,24,128]{2,1,0:T(8,128)(2,1)}), bf16[64,24,128]{2,1,0:T(8,128)(2,1)S(1)}, u32[]{:S(2)}, u32[]{:S(2)}) async-start(bf16[64,24,128]{2,1,0:T(8,128)(2,1)} %get-tuple-element.17), calls=%async_computation.3 | async-start | bytes 786432 | tf_op jit(solution)/shard_map/all_to_all | solution.py:30
  171.1 6.2 %collective-permute-start.5 = (bf16[576,128]{1,0:T(8,128)(2,1)S(1)}, bf16[576,128]{1,0:T(8,128)(2,1)S(1)}, u32[]{:S(2)}, u32[]{:S(2)}) collective-permute-start(bf16[576,128]{1,0:T(8,128)(2,1)S(1)} %get-tuple-element.18), channel_id=1, source_target_pairs={{0,128},{128,0},{256,384},{384,256},{1,129},{129,1},{257,385},{385... | collective-permute-start | bytes 442376 | tf_op jit(solution)/shard_map/ppermute | solution.py:22
  177.3 9.0 %collective-permute-start.6 = (bf16[2,576,128]{2,1,0:T(8,128)(2,1)S(1)}, bf16[2,576,128]{2,1,0:T(8,128)(2,1)S(1)}, u32[]{:S(2)}, u32[]{:S(2)}) collective-permute-start(bf16[2,576,128]{2,1,0:T(8,128)(2,1)S(1)} %pad_maximum_fusion.1.refs_1_), channel_id=1, source_target_pairs={{0,384},{128,256},{256,128},{384,0},{1,385},{129,257},{257,129},{3... | collective-permute-start | bytes 884744 | tf_op jit(solution)/shard_map/ppermute | solution.py:22
  180.1 13.0 %collective-permute-start.7 = (bf16[2,576,128]{2,1,0:T(8,128)(2,1)S(1)}, bf16[2,576,128]{2,1,0:T(8,128)(2,1)S(1)}, u32[]{:S(2)}, u32[]{:S(2)}) collective-permute-start(bf16[2,576,128]{2,1,0:T(8,128)(2,1)S(1)} %pad_maximum_fusion.1.refs_1_), channel_id=1, source_target_pairs={{0,64},{64,0},{1,65},{65,1},{2,66},{66,2},{3,67},{67,3},{4,68},{68... | collective-permute-start | bytes 884744 | tf_op jit(solution)/shard_map/ppermute | solution.py:26
  186.3 6.9 %collective-permute-start.8 = (bf16[2,576,128]{2,1,0:T(8,128)(2,1)S(1)}, bf16[2,576,128]{2,1,0:T(8,128)(2,1)S(1)}, u32[]{:S(2)}, u32[]{:S(2)}) collective-permute-start(bf16[2,576,128]{2,1,0:T(8,128)(2,1)S(1)} %collective-permute-done.6.refs_2_), channel_id=1, source_target_pairs={{0,64},{64,0},{1,65},{65,1},{2,66},{66,2},{3,67},{67,3},{4,68},{68... | collective-permute-start | bytes 884744 | tf_op jit(solution)/shard_map/ppermute | solution.py:26
  193.1 7.4 %copy-start.2 = (f32[512,2]{0,1:T(2,128)S(1)}, f32[512,2]{0,1:T(2,128)}, u32[]{:S(2)}) copy-start(f32[512,2]{0,1:T(2,128)} %param.7) | copy-start | bytes 12292

commit v10 on v9

--- a/solution.py
+++ b/solution.py
@@ -50,11 +50,14 @@
     return lax.broadcasted_iota(jnp.int32, (1, count), 1)
 
 
-def send_scaled_kernel(ids_ref, scaled_ref, out_ref, main_ref, late_ref, slot_ref):
+def send_scaled_kernel(ids_hbm, scaled_ref, out_hbm, main_ref, late_ref, slot_ref, out_ref, ids_ref, sem, sems):
+    fetch_ids = pltpu.make_async_copy(ids_hbm, ids_ref, sem)
+    fetch_ids.start()
     experts = out_ref.shape[0]
     count, tokens = ids_ref.shape
     earlier = jnp.where(row_numbers(tokens) < lane_numbers(tokens), 1.0, 0.0).astype(BF16)
     passed = jnp.zeros((experts, 1), F32)
+    fetch_ids.wait()
     ids, ranks = [], []
     for k in range(count):
         ids.append(ids_ref[k : k + 1, :])
@@ -76,6 +79,7 @@
     out_ref[:, 0:16, :] = part.reshape(experts, 16, 128)
     part = nn_dot(one_hot(row_numbers(experts * 8), left_index), scaled)
     out_ref[:, 16:24, :] = part.reshape(experts, 8, 128).astype(BF16)
+    store_pieces(out_ref, out_hbm, 4, sems)
 
 
 def send_grad_kernel(main_ref, late_ref, grad_ref, out_ref):
@@ -355,7 +359,17 @@
 
     row = jax.ShapeDtypeStruct((1, pair_count), jnp.int32)
     sent_scaled, main_index, late_index, slot_index = call(
-        send_scaled_kernel, (shape(experts, 24, 128), row, row, row), (expert_ids.T, scaled_part)
+        send_scaled_kernel,
+        (pltpu.HBM((experts, 24, 128), BF16), row, row, row),
+        (in_hbm(expert_ids.T), scaled_part),
+        (
+            pltpu.VMEM((experts, 24, 128), BF16),
+            pltpu.VMEM((top_count, tokens), jnp.int32),
+            pltpu.SemaphoreType.DMA,
+            pltpu.SemaphoreType.DMA((4,)),
+        ),
+        specs={0: HBM},
+        out_specs={0: HBM},
     )
     got_scaled = exchange(sent_scaled, EXPERT)
     got = exchange(

time: 203 us -> 203 us (level)
  no operation moved by 1% of the time
where the time goes in v10:
time: 203 us
  waiting for transfers between devices  76.1 us (37%)
  starting transfers between devices  68 us (33%)
  blocking collectives  27.6 us (14%)
  Pallas kernels  25.2 us (12%)
  other arithmetic  2.87 us (1%)
    all_to_all x3, waiting for transfers between devices, exchange(): return lax.all_to_all(value, axes, split_axis=0, concat_axis=0, tiled=True)  49.5 us
    all_to_all x3, starting transfers between devices, exchange(): return lax.all_to_all(value, axes, split_axis=0, concat_axis=0, tiled=True)  33.3 us
    all_to_all x1, blocking collectives, exchange(): return lax.all_to_all(value, axes, split_axis=0, concat_axis=0, tiled=True)  27.6 us
    pallas_call x8, Pallas kernels, call(): pl.pallas_call(kernel, out_shape=outs, grid=steps, in_specs=[specs.get(i,...  25.2 us
    ppermute x4, starting transfers between devices, swap_core(): return lax.ppermute(value, 'c', [(0, 1), (1, 0)])  20.2 us
    ppermute x3, waiting for transfers between devices, shift_y(): lax.ppermute(value, 'y', [(i, (i + step) % size) for i in range(size)])  15.3 us
    ppermute x3, starting transfers between devices, shift_y(): lax.ppermute(value, 'y', [(i, (i + step) % size) for i in range(size)])  9.5 us
    ppermute x4, waiting for transfers between devices, swap_core(): return lax.ppermute(value, 'c', [(0, 1), (1, 0)])  6.03 us
  transfers between devices with their start and end apart: 12, of which 9 were waited for; matrix products, arithmetic and copies ran while one was open for 1% of the time, Pallas kernels for 7%

profile of v10, /device:TPU:1, one launch (start us, length us, event | category | flops | bytes accessed | tf_op | source)
XLA Modules:
  0.0 202.6 jit_solution(13050949463920889084)
XLA Ops:
  0.6 1.2 multiply_convert_fusion
  1.9 2.7 %shard_map.68 = (bf16[64,24,128]{2,1,0:T(8,128)(2,1)}, s32[1,1024]{1,0:T(1,128)S(1)}, s32[1,1024]{1,0:T(1,128)S(1)}, s32[1,1024]{1,0:T(1,128)S(1)}) custom-call(s32[2,512]{1,0:T(2,128)} %bitcast.36, bf16[1024,128]{1,0:T(8,128)(2,1)S(1)} %bitcast.26), custom_call_target="tpu_custom_call" | custom-call | tf_op jit(solution)/shard_map/pallas_call | solution.py:320
  4.5 19.1 %all-to-all-start.1 = ((bf16[64,24,128]{2,1,0:T(8,128)(2,1)}), bf16[64,24,128]{2,1,0:T(8,128)(2,1)S(1)}, u32[]{:S(2)}, u32[]{:S(2)}) async-start(bf16[64,24,128]{2,1,0:T(8,128)(2,1)} %get-tuple-element.14), calls=%async_computation.1 | async-start | bytes 786432 | tf_op jit(solution)/shard_map/all_to_all | solution.py:30
  23.7 2.4 %shard_map.69 = bf16[64,80,128]{2,1,0:T(8,128)(2,1)} custom-call(s32[1,1024]{1,0:T(1,128)S(1)} %get-tuple-element.12.main_ref, s32[1,1024]{1,0:T(1,128)S(1)} %get-tuple-element.13.late_ref, bf16[512,512]{1,0:T(8,128)(2,1)S(1)} %copy-done), custom_call_target="tpu_custom_call" | custom-call | tf_op jit(solution)/shard_map/pallas_call | solution.py:320
  26.1 22.3 %all-to-all-done.1.got_ref = bf16[64,24,128]{2,1,0:T(8,128)(2,1)S(1)} async-done(((bf16[64,24,128]{2,1,0:T(8,128)(2,1)}), bf16[64,24,128]{2,1,0:T(8,128)(2,1)S(1)}, u32[]{:S(2)}, u32[]{:S(2)}) %all-to-all-start.1) | async-done | bytes 393248 | tf_op jit(solution)/shard_map/all_to_all | solution.py:30
  48.4 7.8 %all-to-all-start = ((bf16[64,80,128]{2,1,0:T(8,128)(2,1)}), bf16[64,80,128]{2,1,0:T(8,128)(2,1)}, u32[]{:S(2)}, u32[]{:S(2)}) async-start(bf16[64,80,128]{2,1,0:T(8,128)(2,1)} %shard_map.69), calls=%async_computation | async-start | bytes 2621440 | tf_op jit(solution)/shard_map/all_to_all | solution.py:30
  56.5 4.6 %collective-permute-start.2 = (bf16[1280,128]{1,0:T(8,128)(2,1)S(1)}, bf16[1280,128]{1,0:T(8,128)(2,1)S(1)}, u32[]{:S(2)}, u32[]{:S(2)}) collective-permute-start(bf16[1280,128]{1,0:T(8,128)(2,1)S(1)} %shard_map.70), channel_id=1, source_target_pairs={{0,384},{128,0},{256,128},{384,256},{1,385},{129,1},{257,129},{385... | collective-permute-start | bytes 983048 | tf_op jit(solution)/shard_map/ppermute | solution.py:18
  61.1 2.3 %collective-permute-start.1 = (bf16[1280,128]{1,0:T(8,128)(2,1)S(1)}, bf16[1280,128]{1,0:T(8,128)(2,1)S(1)}, u32[]{:S(2)}, u32[]{:S(2)}) collective-permute-start(bf16[1280,128]{1,0:T(8,128)(2,1)S(1)} %shard_map.70), channel_id=1, source_target_pairs={{0,256},{128,384},{256,0},{384,128},{1,257},{129,385},{257,1},{385... | collective-permute-start | bytes 983048 | tf_op jit(solution)/shard_map/ppermute | solution.py:18
  63.4 2.6 %collective-permute-start = (bf16[1280,128]{1,0:T(8,128)(2,1)S(1)}, bf16[1280,128]{1,0:T(8,128)(2,1)S(1)}, u32[]{:S(2)}, u32[]{:S(2)}) collective-permute-start(bf16[1280,128]{1,0:T(8,128)(2,1)S(1)} %shard_map.70), channel_id=1, source_target_pairs={{0,128},{128,256},{256,384},{384,0},{1,129},{129,257},{257,385},{3... | collective-permute-start | bytes 983048 | tf_op jit(solution)/shard_map/ppermute | solution.py:18
  66.0 1.6 collective-permute-done.2
  67.6 4.4 %collective-permute-done.1 = bf16[1280,128]{1,0:T(8,128)(2,1)S(1)} collective-permute-done((bf16[1280,128]{1,0:T(8,128)(2,1)S(1)}, bf16[1280,128]{1,0:T(8,128)(2,1)S(1)}, u32[]{:S(2)}, u32[]{:S(2)}) %collective-permute-start.1) | collective-permute-done | bytes 327712 | tf_op jit(solution)/shard_map/ppermute | solution.py:18
  72.0 9.2 %collective-permute-done = bf16[1280,128]{1,0:T(8,128)(2,1)S(1)} collective-permute-done((bf16[1280,128]{1,0:T(8,128)(2,1)S(1)}, bf16[1280,128]{1,0:T(8,128)(2,1)S(1)}, u32[]{:S(2)}, u32[]{:S(2)}) %collective-permute-start) | collective-permute-done | bytes 327712 | tf_op jit(solution)/shard_map/ppermute | solution.py:18
  81.4 2.3 %collective-permute-start.3 = (bf16[4,1280,128]{2,1,0:T(8,128)(2,1)S(1)}, bf16[4,1280,128]{2,1,0:T(8,128)(2,1)S(1)}, u32[]{:S(2)}, u32[]{:S(2)}) collective-permute-start(bf16[4,1280,128]{2,1,0:T(8,128)(2,1)S(1)} %pad_maximum_fusion.own_ref), channel_id=1, source_target_pairs={{0,64},{64,0},{1,65},{65,1},{2,66},{66,2},{3,67},{67,3},{4,68},{68... | collective-permute-start | bytes 3932168 | tf_op jit(solution)/shard_map/ppermute | solution.py:26
  83.8 2.5 %collective-permute-done.3.other_ref = bf16[4,1280,128]{2,1,0:T(8,128)(2,1)S(1)} collective-permute-done((bf16[4,1280,128]{2,1,0:T(8,128)(2,1)S(1)}, bf16[4,1280,128]{2,1,0:T(8,128)(2,1)S(1)}, u32[]{:S(2)}, u32[]{:S(2)}) %collective-permute-start.3) | collective-permute-done | bytes 1310752 | tf_op jit(solution)/shard_map/ppermute | solution.py:26
  86.4 3.2 %shard_map.71.turned_hbm = bf16[1024,1280]{1,0:T(8,128)(2,1)} custom-call(s32[8]{0:T(128)S(1)} %get-tuple-element.22.spot_ref, bf16[4,1280,128]{2,1,0:T(8,128)(2,1)S(1)} %pad_maximum_fusion.own_ref, bf16[4,1280,128]{2,1,0:T(8,128)(2,1)S(1)} %collective-permute-done.3.other_ref), custom_call_target="tpu_custom_call" | custom-call | tf_op jit(solution)/shard_map/pallas_call | solution.py:320
  89.6 27.1 %all-to-all-done.got_hbm = bf16[64,80,128]{2,1,0:T(8,128)(2,1)} async-done(((bf16[64,80,128]{2,1,0:T(8,128)(2,1)}), bf16[64,80,128]{2,1,0:T(8,128)(2,1)}, u32[]{:S(2)}, u32[]{:S(2)}) %all-to-all-start) | async-done | bytes 1310752 | tf_op jit(solution)/shard_map/all_to_all | solution.py:30
  116.7 7.7 %shard_map.72 = (bf16[4,1856,128]{2,1,0:T(8,128)(2,1)S(1)}, bf16[4,1856,128]{2,1,0:T(8,128)(2,1)S(1)}, bf16[1024,512]{1,0:T(8,128)(2,1)}) custom-call(s32[9]{0:T(128)S(1)} %pad_add_fusion.spot_ref.refs_0_, bf16[64,80,128]{2,1,0:T(8,128)(2,1)} %all-to-all-done.got_hbm, bf16[1024,512]{1,0:T(8,128)(2,1)} %bitcast.30, bf16[1024,1280]{1,0:T(8,128)(2,1)} %shard_map.71.turned_hbm), custom_call_target="tpu_custom_call" | custom-call | tf_op jit(solution)/shard_map/pallas_call | solution.py:320
  124.4 7.6 %collective-permute-start.4 = (bf16[4,1856,128]{2,1,0:T(8,128)(2,1)S(1)}, bf16[4,1856,128]{2,1,0:T(8,128)(2,1)S(1)}, u32[]{:S(2)}, u32[]{:S(2)}) collective-permute-start(bf16[4,1856,128]{2,1,0:T(8,128)(2,1)S(1)} %get-tuple-element.16), channel_id=1, source_target_pairs={{0,64},{64,0},{1,65},{65,1},{2,66},{66,2},{3,67},{67,3},{4,68},{68... | collective-permute-start | bytes 5701640 | tf_op jit(solution)/shard_map/ppermute | solution.py:26
  132.0 3.5 %collective-permute-done.4.other_ref = bf16[4,1856,128]{2,1,0:T(8,128)(2,1)S(1)} collective-permute-done((bf16[4,1856,128]{2,1,0:T(8,128)(2,1)S(1)}, bf16[4,1856,128]{2,1,0:T(8,128)(2,1)S(1)}, u32[]{:S(2)}, u32[]{:S(2)}) %collective-permute-start.4) | collective-permute-done | bytes 1900576 | tf_op jit(solution)/shard_map/ppermute | solution.py:26
  135.9 27.6 %all_to_all.20.part_ref = bf16[4,1856,128]{2,1,0:T(8,128)(2,1)S(1)} all-to-all(bf16[4,1856,128]{2,1,0:T(8,128)(2,1)S(1)} %shard_map.73), channel_id=1, replica_groups=mesh['y'=4,'c'=2,'x'=4,'z'=16] {'y'}, dimensions={0} | all-to-all | bytes 3801088 | tf_op jit(solution)/shard_map/all_to_all | solution.py:30
  163.5 1.3 shard_map.74
  164.8 6.3 %all-to-all-start.3 = ((bf16[64,24,128]{2,1,0:T(8,128)(2,1)}), bf16[64,24,128]{2,1,0:T(8,128)(2,1)S(1)}, u32[]{:S(2)}, u32[]{:S(2)}) async-start(bf16[64,24,128]{2,1,0:T(8,128)(2,1)} %get-tuple-element.17), calls=%async_computation.3 | async-start | bytes 786432 | tf_op jit(solution)/shard_map/all_to_all | solution.py:30
  171.1 2.2 %collective-permute-start.5 = (bf16[576,128]{1,0:T(8,128)(2,1)S(1)}, bf16[576,128]{1,0:T(8,128)(2,1)S(1)}, u32[]{:S(2)}, u32[]{:S(2)}) collective-permute-start(bf16[576,128]{1,0:T(8,128)(2,1)S(1)} %get-tuple-element.18), channel_id=1, source_target_pairs={{0,128},{128,0},{256,384},{384,256},{1,129},{129,1},{257,385},{385... | collective-permute-start | bytes 442376 | tf_op jit(solution)/shard_map/ppermute | solution.py:22
  173.3 4.0 %collective-permute-done.5 = bf16[576,128]{1,0:T(8,128)(2,1)S(1)} collective-permute-done((bf16[576,128]{1,0:T(8,128)(2,1)S(1)}, bf16[576,128]{1,0:T(8,128)(2,1)S(1)}, u32[]{:S(2)}, u32[]{:S(2)}) %collective-permute-start.5) | collective-permute-done | bytes 147488 | tf_op jit(solution)/shard_map/ppermute | solution.py:22
  177.3 2.8 %collective-permute-start.6 = (bf16[2,576,128]{2,1,0:T(8,128)(2,1)S(1)}, bf16[2,576,128]{2,1,0:T(8,128)(2,1)S(1)}, u32[]{:S(2)}, u32[]{:S(2)}) collective-permute-start(bf16[2,576,128]{2,1,0:T(8,128)(2,1)S(1)} %pad_maximum_fusion.1.refs_1_), channel_id=1, source_target_pairs={{0,384},{128,256},{256,128},{384,0},{1,385},{129,257},{257,129},{3... | collective-permute-start | bytes 884744 | tf_op jit(solution)/shard_map/ppermute | solution.py:22
  180.2 4.8 %collective-permute-start.7 = (bf16[2,576,128]{2,1,0:T(8,128)(2,1)S(1)}, bf16[2,576,128]{2,1,0:T(8,128)(2,1)S(1)}, u32[]{:S(2)}, u32[]{:S(2)}) collective-permute-start(bf16[2,576,128]{2,1,0:T(8,128)(2,1)S(1)} %pad_maximum_fusion.1.refs_1_), channel_id=1, source_target_pairs={{0,64},{64,0},{1,65},{65,1},{2,66},{66,2},{3,67},{67,3},{4,68},{68... | collective-permute-start | bytes 884744 | tf_op jit(solution)/shard_map/ppermute | solution.py:26
  185.0 1.3 collective-permute-done.6.refs_2_
  186.3 5.5 %collective-permute-start.8 = (bf16[2,576,128]{2,1,0:T(8,128)(2,1)S(1)}, bf16[2,576,128]{2,1,0:T(8,128)(2,1)S(1)}, u32[]{:S(2)}, u32[]{:S(2)}) collective-permute-start(bf16[2,576,128]{2,1,0:T(8,128)(2,1)S(1)} %collective-permute-done.6.refs_2_), channel_id=1, source_target_pairs={{0,64},{64,0},{1,65},{65,1},{2,66},{66,2},{3,67},{67,3},{4,68},{68... | collective-permute-start | bytes 884744 | tf_op jit(solution)/shard_map/ppermute | solution.py:26
  191.8 1.4 iota_compare_fusion
  193.2 7.4 %shard_map.75 = f32[1,1024,512]{2,1,0:T(8,128)} custom-call(s32[9]{0:T(128)S(1)} %pad_add_fusion.spot_ref.refs_0_, bf16[2,576,128]{2,1,0:T(8,128)(2,1)S(1)} %pad_maximum_fusion.1.refs_1_, bf16[2,576,128]{2,1,0:T(8,128)(2,1)S(1)} %collective-permute-done.6.refs_2_, bf16[2,576,128]{2,1,0:T(8,128)(2,1)S(1)} %collective-permute-done.7.refs_3_, ...), custom_call_target="tpu_custom_call" | custom-call | tf_op jit(solution)/shard_map/pallas_call | solution.py:320
  200.6 1.0 fusion.1
  201.6 1.0 copy.8
  (13 shorter events, 1.0 us)
Async XLA Ops:
  0.6 23.1 %copy-start = (bf16[512,512]{1,0:T(8,128)(2,1)S(1)}, bf16[512,512]{1,0:T(8,128)(2,1)}, u32[]{:S(2)}) copy-start(bf16[512,512]{1,0:T(8,128)(2,1)} %grad_ref.1) | copy-start | bytes 1572868
  4.5 43.9 %all-to-all-start.1 = ((bf16[64,24,128]{2,1,0:T(8,128)(2,1)}), bf16[64,24,128]{2,1,0:T(8,128)(2,1)S(1)}, u32[]{:S(2)}, u32[]{:S(2)}) async-start(bf16[64,24,128]{2,1,0:T(8,128)(2,1)} %get-tuple-element.14), calls=%async_computation.1 | async-start | bytes 786432 | tf_op jit(solution)/shard_map/all_to_all | solution.py:30
  48.4 68.3 %all-to-all-start = ((bf16[64,80,128]{2,1,0:T(8,128)(2,1)}), bf16[64,80,128]{2,1,0:T(8,128)(2,1)}, u32[]{:S(2)}, u32[]{:S(2)}) async-start(bf16[64,80,128]{2,1,0:T(8,128)(2,1)} %shard_map.69), calls=%async_computation | async-start | bytes 2621440 | tf_op jit(solution)/shard_map/all_to_all | solution.py:30
  56.5 11.1 %collective-permute-start.2 = (bf16[1280,128]{1,0:T(8,128)(2,1)S(1)}, bf16[1280,128]{1,0:T(8,128)(2,1)S(1)}, u32[]{:S(2)}, u32[]{:S(2)}) collective-permute-start(bf16[1280,128]{1,0:T(8,128)(2,1)S(1)} %shard_map.70), channel_id=1, source_target_pairs={{0,384},{128,0},{256,128},{384,256},{1,385},{129,1},{257,129},{385... | collective-permute-start | bytes 983048 | tf_op jit(solution)/shard_map/ppermute | solution.py:18
  61.1 10.9 %collective-permute-start.1 = (bf16[1280,128]{1,0:T(8,128)(2,1)S(1)}, bf16[1280,128]{1,0:T(8,128)(2,1)S(1)}, u32[]{:S(2)}, u32[]{:S(2)}) collective-permute-start(bf16[1280,128]{1,0:T(8,128)(2,1)S(1)} %shard_map.70), channel_id=1, source_target_pairs={{0,256},{128,384},{256,0},{384,128},{1,257},{129,385},{257,1},{385... | collective-permute-start | bytes 983048 | tf_op jit(solution)/shard_map/ppermute | solution.py:18
  63.4 17.9 %collective-permute-start = (bf16[1280,128]{1,0:T(8,128)(2,1)S(1)}, bf16[1280,128]{1,0:T(8,128)(2,1)S(1)}, u32[]{:S(2)}, u32[]{:S(2)}) collective-permute-start(bf16[1280,128]{1,0:T(8,128)(2,1)S(1)} %shard_map.70), channel_id=1, source_target_pairs={{0,128},{128,256},{256,384},{384,0},{1,129},{129,257},{257,385},{3... | collective-permute-start | bytes 983048 | tf_op jit(solution)/shard_map/ppermute | solution.py:18
  81.4 4.9 %collective-permute-start.3 = (bf16[4,1280,128]{2,1,0:T(8,128)(2,1)S(1)}, bf16[4,1280,128]{2,1,0:T(8,128)(2,1)S(1)}, u32[]{:S(2)}, u32[]{:S(2)}) collective-permute-start(bf16[4,1280,128]{2,1,0:T(8,128)(2,1)S(1)} %pad_maximum_fusion.own_ref), channel_id=1, source_target_pairs={{0,64},{64,0},{1,65},{65,1},{2,66},{66,2},{3,67},{67,3},{4,68},{68... | collective-permute-start | bytes 3932168 | tf_op jit(solution)/shard_map/ppermute | solution.py:26
  124.4 11.1 %collective-permute-start.4 = (bf16[4,1856,128]{2,1,0:T(8,128)(2,1)S(1)}, bf16[4,1856,128]{2,1,0:T(8,128)(2,1)S(1)}, u32[]{:S(2)}, u32[]{:S(2)}) collective-permute-start(bf16[4,1856,128]{2,1,0:T(8,128)(2,1)S(1)} %get-tuple-element.16), channel_id=1, source_target_pairs={{0,64},{64,0},{1,65},{65,1},{2,66},{66,2},{3,67},{67,3},{4,68},{68... | collective-permute-start | bytes 5701640 | tf_op jit(solution)/shard_map/ppermute | solution.py:26
  164.8 35.8 %all-to-all-start.3 = ((bf16[64,24,128]{2,1,0:T(8,128)(2,1)}), bf16[64,24,128]{2,1,0:T(8,128)(2,1)S(1)}, u32[]{:S(2)}, u32[]{:S(2)}) async-start(bf16[64,24,128]{2,1,0:T(8,128)(2,1)} %get-tuple-element.17), calls=%async_computation.3 | async-start | bytes 786432 | tf_op jit(solution)/shard_map/all_to_all | solution.py:30
  171.1 6.2 %collective-permute-start.5 = (bf16[576,128]{1,0:T(8,128)(2,1)S(1)}, bf16[576,128]{1,0:T(8,128)(2,1)S(1)}, u32[]{:S(2)}, u32[]{:S(2)}) collective-permute-start(bf16[576,128]{1,0:T(8,128)(2,1)S(1)} %get-tuple-element.18), channel_id=1, source_target_pairs={{0,128},{128,0},{256,384},{384,256},{1,129},{129,1},{257,385},{385... | collective-permute-start | bytes 442376 | tf_op jit(solution)/shard_map/ppermute | solution.py:22
  177.3 9.0 %collective-permute-start.6 = (bf16[2,576,128]{2,1,0:T(8,128)(2,1)S(1)}, bf16[2,576,128]{2,1,0:T(8,128)(2,1)S(1)}, u32[]{:S(2)}, u32[]{:S(2)}) collective-permute-start(bf16[2,576,128]{2,1,0:T(8,128)(2,1)S(1)} %pad_maximum_fusion.1.refs_1_), channel_id=1, source_target_pairs={{0,384},{128,256},{256,128},{384,0},{1,385},{129,257},{257,129},{3... | collective-permute-start | bytes 884744 | tf_op jit(solution)/shard_map/ppermute | solution.py:22
  180.2 13.0 %collective-permute-start.7 = (bf16[2,576,128]{2,1,0:T(8,128)(2,1)S(1)}, bf16[2,576,128]{2,1,0:T(8,128)(2,1)S(1)}, u32[]{:S(2)}, u32[]{:S(2)}) collective-permute-start(bf16[2,576,128]{2,1,0:T(8,128)(2,1)S(1)} %pad_maximum_fusion.1.refs_1_), channel_id=1, source_target_pairs={{0,64},{64,0},{1,65},{65,1},{2,66},{66,2},{3,67},{67,3},{4,68},{68... | collective-permute-start | bytes 884744 | tf_op jit(solution)/shard_map/ppermute | solution.py:26
  186.3 6.9 %collective-permute-start.8 = (bf16[2,576,128]{2,1,0:T(8,128)(2,1)S(1)}, bf16[2,576,128]{2,1,0:T(8,128)(2,1)S(1)}, u32[]{:S(2)}, u32[]{:S(2)}) collective-permute-start(bf16[2,576,128]{2,1,0:T(8,128)(2,1)S(1)} %collective-permute-done.6.refs_2_), channel_id=1, source_target_pairs={{0,64},{64,0},{1,65},{65,1},{2,66},{66,2},{3,67},{67,3},{4,68},{68... | collective-permute-start | bytes 884744 | tf_op jit(solution)/shard_map/ppermute | solution.py:26
  193.2 7.4 %copy-start.1 = (f32[512,2]{0,1:T(2,128)S(1)}, f32[512,2]{0,1:T(2,128)}, u32[]{:S(2)}) copy-start(f32[512,2]{0,1:T(2,128)} %param.7) | copy-start | bytes 12292
